TPU v7x, 32 devices: a whole 2x2x4 slice. The times are simulated.
32 devices in a mesh: pipe: 2 (over core), expert: 16 (over z, y, x).
Axes of the slice: x: 2, y: 2, z: 4, core: 2. Of those that a mesh axis runs over, the one named last changes fastest.
Arguments:
- tokens: bfloat16 [4096, 2048], P(('pipe', 'expert')), may hold values from -6 to 6
- routes: int32 [4096, 8], P(('pipe', 'expert')), may hold values from 0 to 15, all different within a row; in each aligned block of 128 rows (0 to 127, 128 to 255, ...) at most 64 rows name the same one
- gates: float32 [4096, 8], P(('pipe', 'expert')), may hold values from 0.1 to 1
- cotangent: bfloat16 [4096, 2048], P(('pipe', 'expert')), may hold values from -1.5 to 1.5
- w_gate: bfloat16 [16, 2048, 384], P('expert'), may hold values from -0.125 to 0.125
- w_up: bfloat16 [16, 2048, 384], P('expert'), may hold values from -0.125 to 0.125
- w_down: bfloat16 [16, 384, 2048], P('expert'), may hold values from -0.3125 to 0.3125
Outputs:
- mixed: bfloat16 [4096, 2048], P(('pipe', 'expert'))
- input_grad: bfloat16 [4096, 2048], P(('pipe', 'expert'))
- gate_weight_grad: bfloat16 [16, 2048, 384], P('expert')
- up_weight_grad: bfloat16 [16, 2048, 384], P('expert')
- down_weight_grad: bfloat16 [16, 384, 2048], P('expert')
Inputs may be any that keep to these rules, and one draw needn't show every extreme that they name: `routes`: each row names 8 different experts. Within the rows of one device (aligned blocks of 128 rows, device order pipe then expert) each expert is named exactly 64 times.
All inputs are finite; a program needn't handle non-finite values.
Results may differ from a plain program's by a relative error of at most 0.009.
Values may be sent and summed in bfloat16 or wider, within the bound.
No kernel may reach another device: no remote copies, remote signals or barrier semaphores. Data moves between devices by JAX's collectives and lax.ppermute only.
A program may use at most 128 MiB of HBM per device.

v0:
```python
import jax
import jax.numpy as jnp
from jax import lax
from jax.sharding import PartitionSpec as P


def slot_index(block_routes, expert_count, capacity):
    flat = block_routes.reshape(-1)
    onehot = (flat[:, None] == jnp.arange(expert_count, dtype=jnp.int32)[None, :]).astype(jnp.int32)
    before = jnp.cumsum(onehot, axis=0) - onehot
    ranks = jnp.sum(before * onehot, axis=1)
    return flat * capacity + ranks


def expert_forward(block, gate_mat, up_mat, down_mat):
    inputs = block.reshape(-1, block.shape[2])
    gate_pre = jnp.dot(inputs, gate_mat, preferred_element_type=jnp.float32)
    up_pre = jnp.dot(inputs, up_mat, preferred_element_type=jnp.float32)
    sigma = jax.nn.sigmoid(gate_pre)
    hidden = (gate_pre * sigma * up_pre).astype(jnp.bfloat16)
    outputs = jnp.dot(hidden, down_mat, preferred_element_type=jnp.float32).astype(jnp.bfloat16)
    return (gate_pre, up_pre, hidden, outputs)


def on_device(tokens, routes, gates, cotangent, w_gate, w_up, w_down):
    rows_dev, width = tokens.shape
    picks = routes.shape[1]
    experts = lax.axis_size("expert")
    capacity = rows_dev * picks // experts
    gate_mat = w_gate[0]
    up_mat = w_up[0]
    down_mat = w_down[0]
    inner = gate_mat.shape[1]
    slots = slot_index(routes, experts, capacity)
    flat_rows = jnp.arange(rows_dev * picks, dtype=jnp.int32) // picks
    token_of = jnp.full((experts * capacity,), rows_dev, jnp.int32).at[slots].set(flat_rows)
    weight_of = jnp.zeros((experts * capacity,), jnp.float32).at[slots].set(gates.reshape(-1))
    token_pad = jnp.concatenate([tokens, jnp.zeros((1, width), tokens.dtype)], axis=0)
    send = token_pad[token_of].reshape(experts, capacity, width)
    block = lax.all_to_all(send, "expert", split_axis=0, concat_axis=0, tiled=True)
    items = block.shape[1]
    gate_pre, up_pre, hidden, outputs = expert_forward(block, gate_mat, up_mat, down_mat)
    back_items = lax.all_to_all(
        outputs.reshape(experts, items, width), "expert", split_axis=0, concat_axis=0, tiled=True
    )
    gate_three = gate_pre.reshape(experts, items, inner)
    up_three = up_pre.reshape(experts, items, inner)
    hidden_three = hidden.reshape(experts, items, inner)
    inputs = block.reshape(-1, width)
    gate_pre = gate_three.reshape(-1, inner)
    up_pre = up_three.reshape(-1, inner)
    hidden = hidden_three.reshape(-1, inner)
    gathered = back_items.reshape(-1, width)[slots].reshape(rows_dev, picks, width)
    mixed = jnp.sum(gates[:, :, None] * gathered.astype(jnp.float32), axis=1).astype(jnp.bfloat16)
    cot_pad = jnp.concatenate([cotangent, jnp.zeros((1, width), cotangent.dtype)], axis=0)
    cot_send = (weight_of[:, None] * cot_pad[token_of].astype(jnp.float32)).astype(jnp.bfloat16)
    slot_cot = lax.all_to_all(
        cot_send.reshape(experts, capacity, width),
        "expert",
        split_axis=0,
        concat_axis=0,
        tiled=True,
    ).reshape(-1, width)
    down_part = jnp.dot(hidden.T, slot_cot, preferred_element_type=jnp.float32)
    hidden_grad = jnp.dot(slot_cot, down_mat.T, preferred_element_type=jnp.float32)
    sigma = jax.nn.sigmoid(gate_pre)
    gate_grad = (hidden_grad * up_pre * sigma * (1.0 + gate_pre * (1.0 - sigma))).astype(
        jnp.bfloat16
    )
    up_grad = (hidden_grad * gate_pre * sigma).astype(jnp.bfloat16)
    slot_grads = (
        jnp.dot(gate_grad, gate_mat.T, preferred_element_type=jnp.float32)
        + jnp.dot(up_grad, up_mat.T, preferred_element_type=jnp.float32)
    ).astype(jnp.bfloat16)
    grads_back = lax.all_to_all(
        slot_grads.reshape(experts, capacity, width),
        "expert",
        split_axis=0,
        concat_axis=0,
        tiled=True,
    )
    gate_part = jnp.dot(inputs.T, gate_grad, preferred_element_type=jnp.float32)
    up_part = jnp.dot(inputs.T, up_grad, preferred_element_type=jnp.float32)
    gate_total, up_total, down_total = (
        lax.psum(gate_part.astype(jnp.bfloat16), "pipe").astype(jnp.float32),
        lax.psum(up_part.astype(jnp.bfloat16), "pipe").astype(jnp.float32),
        lax.psum(down_part.astype(jnp.bfloat16), "pipe").astype(jnp.float32),
    )
    grad_rows = grads_back.reshape(-1, width)[slots].reshape(rows_dev, picks, width)
    input_grad = jnp.sum(grad_rows.astype(jnp.float32), axis=1).astype(jnp.bfloat16)
    return (
        mixed,
        input_grad,
        gate_total.astype(jnp.bfloat16)[None],
        up_total.astype(jnp.bfloat16)[None],
        down_total.astype(jnp.bfloat16)[None],
    )


def solution(mesh):
    in_specs = (
        P(("pipe", "expert"), None),
        P(("pipe", "expert"), None),
        P(("pipe", "expert"), None),
        P(("pipe", "expert"), None),
        P("expert", None, None),
        P("expert", None, None),
        P("expert", None, None),
    )
    out_specs = (
        P(("pipe", "expert"), None),
        P(("pipe", "expert"), None),
        P("expert", None, None),
        P("expert", None, None),
        P("expert", None, None),
    )
    return jax.shard_map(
        on_device, mesh=mesh, in_specs=in_specs, out_specs=out_specs, check_vma=False
    )
```

profile of v0, /device:TPU:14, one launch (start us, length us, event | category | flops | bytes accessed | tf_op | source)
XLA Modules:
  0.0 467.3 jit_solution(10504910093243393587)
XLA Ops:
  7.2 0.0 copy-start
  7.2 0.8 broadcast_multiply_fusion
  8.0 0.8 copy.17
  8.8 0.1 eq.29
  8.9 0.1 eq.25
  9.0 0.1 copy.16
  9.1 0.1 mul.65
  9.2 4.5 reduce-window.6
  13.7 0.1 slice.16
  13.8 0.1 copy.19
  13.9 0.1 copy.20
  14.0 0.1 broadcast_add_fusion
  14.2 4.3 scatter_custom_fusion
  18.5 1.1 concatenate.6
  19.6 6.1 %gather_fusion = bf16[1024,2048]{1,0:T(8,128)(2,1)} fusion(bf16[129,2048]{1,0:T(8,128)(2,1)S(1)} %concatenate.6, s32[1024]{0:T(1024)S(1)} %fusion.21), kind=kCustom, calls=%fused_computation | custom fusion | bytes 8392704 | tf_op jit(solution)/shard_map/gather | solution.py:39
  25.7 0.0 copy-start.10
  25.7 7.3 %all-to-all-start = ((bf16[16,64,2048]{2,1,0:T(8,128)(2,1)}), bf16[16,64,2048]{2,1,0:T(8,128)(2,1)}, u32[]{:S(2)}, u32[]{:S(2)}) async-start(bf16[16,64,2048]{2,1,0:T(8,128)(2,1)} %bitcast.73), calls=%async_computation | async-start | bytes 8388608 | tf_op jit(solution)/shard_map/all_to_all | solution.py:40
  32.9 0.0 copy-done.11
  32.9 0.1 copy.15
  33.0 0.1 reshape.154
  33.1 4.3 scatter_custom_fusion.1
  37.4 0.1 mul.70
  37.5 0.0 copy-done.10
  37.6 6.0 %gather_fusion.2 = bf16[1024,2048]{1,0:T(8,128)(2,1)} fusion(bf16[129,2048]{1,0:T(8,128)(2,1)S(1)} %concatenate.7, s32[1024]{0:T(1024)S(1)} %fusion.21), kind=kCustom, calls=%fused_computation.2 | custom fusion | bytes 8392704 | tf_op jit(solution)/shard_map/gather | solution.py:56
  43.6 4.9 %fusion = bf16[16,64,2048]{2,1,0:T(8,128)(2,1)} fusion(bf16[16,64,2048]{2,1,0:T(8,128)(2,1)} %bitcast.71, f32[16,64]{1,0:T(8,128)S(1)} %mul.70), kind=kLoop, calls=%fused_computation.7 | loop fusion | flops 6291456 | bytes 8392704 | tf_op jit(solution)/shard_map/convert_element_type | solution.py:56
  48.5 79.1 %all-to-all-done = bf16[16,64,2048]{2,1,0:T(8,128)(2,1)} async-done(((bf16[16,64,2048]{2,1,0:T(8,128)(2,1)}), bf16[16,64,2048]{2,1,0:T(8,128)(2,1)}, u32[]{:S(2)}, u32[]{:S(2)}) %all-to-all-start) | async-done | bytes 4194336 | tf_op jit(solution)/shard_map/all_to_all | solution.py:40
  127.6 5.1 %all-to-all-start.2 = ((bf16[16,64,2048]{2,1,0:T(8,128)(2,1)}), bf16[16,64,2048]{2,1,0:T(8,128)(2,1)}, u32[]{:S(2)}, u32[]{:S(2)}) async-start(bf16[16,64,2048]{2,1,0:T(8,128)(2,1)} %fusion), calls=%async_computation.2 | async-start | bytes 8388608 | tf_op jit(solution)/shard_map/all_to_all | solution.py:57
  132.7 0.0 copy-start.3
  132.7 6.2 %fusion.9 = f32[1024,384]{1,0:T(8,128)} fusion(bf16[1024,2048]{1,0:T(8,128)(2,1)} %bitcast.5, bf16[1,2048,384]{2,1,0:T(8,128)(2,1)} %param.12), kind=kOutput, calls=%fused_computation.23 | convolution fusion | flops 1610612736 | bytes 7340032 | tf_op jit(solution)/shard_map/dot_general | solution.py:18
  139.0 0.0 copy-done.3
  139.0 5.7 %fusion.13 = f32[1024,384]{1,0:T(8,128)} fusion(bf16[1024,2048]{1,0:T(8,128)(2,1)} %bitcast.5, bf16[1,2048,384]{2,1,0:T(8,128)(2,1)S(1)} %copy-done.3), kind=kOutput, calls=%fused_computation.27 | convolution fusion | flops 1610612736 | bytes 7340032 | tf_op jit(solution)/shard_map/dot_general | solution.py:17
  144.6 80.7 %all-to-all-done.2 = bf16[16,64,2048]{2,1,0:T(8,128)(2,1)} async-done(((bf16[16,64,2048]{2,1,0:T(8,128)(2,1)}), bf16[16,64,2048]{2,1,0:T(8,128)(2,1)}, u32[]{:S(2)}, u32[]{:S(2)}) %all-to-all-start.2) | async-done | bytes 4194336 | tf_op jit(solution)/shard_map/all_to_all | solution.py:57
  225.4 0.0 copy-done
  225.4 7.2 %multiply_convert_fusion = (bf16[1024,384]{1,0:T(8,128)(2,1)}, bf16[1024,384]{1,0:T(8,128)(2,1)}, bf16[1024,384]{1,0:T(8,128)(2,1)S(1)}) fusion(f32[1024,384]{1,0:T(8,128)} %fusion.13, f32[1024,384]{1,0:T(8,128)} %fusion.9, bf16[1024,2048]{1,0:T(8,128)(2,1)} %bitcast.13, bf16[1,384,2048]{2,1,0:T(8,128)(2,1)S(1)} %copy-done), kind=kOutput, calls=%fused_computation.29 | convolution fusion | flops 1616904192 | bytes 11272192 | tf_op jit(solution)/shard_map/dot_general | solution.py:65
  232.6 4.3 convolution_convert_fusion
  236.9 0.0 copy-done.12
  236.9 5.1 %all-to-all-start.1 = ((bf16[16,64,2048]{2,1,0:T(8,128)(2,1)}), bf16[16,64,2048]{2,1,0:T(8,128)(2,1)}, u32[]{:S(2)}, u32[]{:S(2)}) async-start(bf16[16,64,2048]{2,1,0:T(8,128)(2,1)} %bitcast.74), calls=%async_computation.1 | async-start | bytes 8388608 | tf_op jit(solution)/shard_map/all_to_all | solution.py:43
  242.0 0.0 copy-start.8
  242.0 3.6 fusion.11
  245.6 0.0 copy-done.4
  245.7 0.0 copy-done.8
  245.7 4.3 add_convert_fusion
  250.0 84.6 %all-to-all-done.1 = bf16[16,64,2048]{2,1,0:T(8,128)(2,1)} async-done(((bf16[16,64,2048]{2,1,0:T(8,128)(2,1)}), bf16[16,64,2048]{2,1,0:T(8,128)(2,1)}, u32[]{:S(2)}, u32[]{:S(2)}) %all-to-all-start.1) | async-done | bytes 4194336 | tf_op jit(solution)/shard_map/all_to_all | solution.py:43
  334.6 5.2 %all-to-all-start.3 = ((bf16[16,64,2048]{2,1,0:T(8,128)(2,1)}), bf16[16,64,2048]{2,1,0:T(8,128)(2,1)}, u32[]{:S(2)}, u32[]{:S(2)}) async-start(bf16[16,64,2048]{2,1,0:T(8,128)(2,1)} %bitcast.72), calls=%async_computation.3 | async-start | bytes 8388608 | tf_op jit(solution)/shard_map/all_to_all | solution.py:75
  339.9 0.0 all-reduce.5.cloned.1.call-start
  339.9 0.0 copy-done.13
  339.9 5.2 %fusion.4 = bf16[1,384,2048]{2,1,0:T(8,128)(2,1)} fusion(bf16[1024,384]{1,0:T(8,128)(2,1)S(1)} %copy-done.13, bf16[1024,2048]{1,0:T(8,128)(2,1)} %bitcast.13), kind=kOutput, calls=%fused_computation.18 | convolution fusion | flops 1611399168 | bytes 6553600 | tf_op jit(solution)/shard_map/dot_general | solution.py:64
  345.2 0.0 copy-done.9
  345.2 5.8 %fusion.3 = bf16[1,2048,384]{2,1,0:T(8,128)(2,1)} fusion(bf16[1024,2048]{1,0:T(8,128)(2,1)} %bitcast.5, bf16[1024,384]{1,0:T(8,128)(2,1)S(1)} %copy-done.9), kind=kOutput, calls=%fused_computation.17 | convolution fusion | flops 1611399168 | bytes 6553600 | tf_op jit(solution)/shard_map/dot_general | solution.py:83
  350.9 0.0 copy-done.7
  351.0 5.7 %fusion.2 = bf16[1,2048,384]{2,1,0:T(8,128)(2,1)} fusion(bf16[1024,2048]{1,0:T(8,128)(2,1)} %bitcast.5, bf16[1024,384]{1,0:T(8,128)(2,1)S(1)} %copy-done.7), kind=kOutput, calls=%fused_computation.16 | convolution fusion | flops 1611399168 | bytes 6553600 | tf_op jit(solution)/shard_map/dot_general | solution.py:82
  356.7 0.0 all-reduce.5.cloned.1.call-update
  356.7 11.8 %gather_fusion.1 = bf16[1024,2048]{1,0:T(8,128)(2,1)} fusion(bf16[1024,2048]{1,0:T(8,128)(2,1)} %bitcast.10, s32[1024]{0:T(1024)S(1)} %broadcast_clamp_fusion), kind=kCustom, calls=%fused_computation.1 | custom fusion | bytes 8392704 | tf_op jit(solution)/shard_map/gather | solution.py:53
  368.5 64.0 %all-to-all-done.3 = bf16[16,64,2048]{2,1,0:T(8,128)(2,1)} async-done(((bf16[16,64,2048]{2,1,0:T(8,128)(2,1)}), bf16[16,64,2048]{2,1,0:T(8,128)(2,1)}, u32[]{:S(2)}, u32[]{:S(2)}) %all-to-all-start.3) | async-done | bytes 4194336 | tf_op jit(solution)/shard_map/all_to_all | solution.py:75
  432.5 11.6 %gather_fusion.3 = bf16[1024,2048]{1,0:T(8,128)(2,1)} fusion(bf16[1024,2048]{1,0:T(8,128)(2,1)} %bitcast.15, s32[1024]{0:T(1024)S(1)} %broadcast_clamp_fusion), kind=kCustom, calls=%fused_computation.3 | custom fusion | bytes 8392704 | tf_op jit(solution)/shard_map/gather | solution.py:89
  444.1 6.0 %bitcast_reduce_fusion = bf16[128,2048]{1,0:T(8,128)(2,1)} fusion(bf16[1024,2048]{1,0:T(8,128)(2,1)} %gather_fusion.3), kind=kLoop, calls=%fused_computation.11 | loop fusion | flops 1835008 | bytes 4718592 | tf_op jit(solution)/shard_map/reduce_sum | solution.py:90
  450.1 0.0 copy-done.2
  450.1 5.2 %fusion.1 = bf16[128,2048]{1,0:T(8,128)(2,1)} fusion(bf16[1024,2048]{1,0:T(8,128)(2,1)S(1)} %copy-done.2, f32[128,8]{1,0:T(8,128)S(1)} %copy.15), kind=kLoop, calls=%fused_computation.9 | loop fusion | flops 6029312 | bytes 4722688 | tf_op jit(solution)/shard_map/reduce_sum | solution.py:54
  455.3 2.9 copy.27
  458.2 0.0 copy-done.6
  458.2 1.1 copy.28
  459.3 0.0 copy-done.5
  459.3 1.1 copy.29
  460.5 0.0 copy-done.1
  (20 shorter events, 0.2 us)
Async XLA Ops:
  7.2 218.2 %copy-start = (bf16[1,384,2048]{2,1,0:T(8,128)(2,1)S(1)}, bf16[1,384,2048]{2,1,0:T(8,128)(2,1)}, u32[]{:S(2)}) copy-start(bf16[1,384,2048]{2,1,0:T(8,128)(2,1)} %param.13) | copy-start | bytes 4718596
  25.7 7.3 %copy-start.11 = (f32[128,8]{0,1:T(8,128)S(1)}, f32[128,8]{0,1:T(8,128)}, u32[]{:S(2)}) copy-start(f32[128,8]{0,1:T(8,128)} %param.9) | copy-start | bytes 12292
  25.7 11.9 %copy-start.10 = (bf16[128,2048]{1,0:T(8,128)(2,1)S(1)}, bf16[128,2048]{1,0:T(8,128)(2,1)}, u32[]{:S(2)}) copy-start(bf16[128,2048]{1,0:T(8,128)(2,1)} %param.10) | copy-start | bytes 1572868
  25.7 101.9 %all-to-all-start = ((bf16[16,64,2048]{2,1,0:T(8,128)(2,1)}), bf16[16,64,2048]{2,1,0:T(8,128)(2,1)}, u32[]{:S(2)}, u32[]{:S(2)}) async-start(bf16[16,64,2048]{2,1,0:T(8,128)(2,1)} %bitcast.73), calls=%async_computation | async-start | bytes 8388608 | tf_op jit(solution)/shard_map/all_to_all | solution.py:40
  127.6 97.8 %all-to-all-start.2 = ((bf16[16,64,2048]{2,1,0:T(8,128)(2,1)}), bf16[16,64,2048]{2,1,0:T(8,128)(2,1)}, u32[]{:S(2)}, u32[]{:S(2)}) async-start(bf16[16,64,2048]{2,1,0:T(8,128)(2,1)} %fusion), calls=%async_computation.2 | async-start | bytes 8388608 | tf_op jit(solution)/shard_map/all_to_all | solution.py:57
  132.7 6.3 %copy-start.3 = (bf16[1,2048,384]{2,1,0:T(8,128)(2,1)S(1)}, bf16[1,2048,384]{2,1,0:T(8,128)(2,1)}, u32[]{:S(2)}) copy-start(bf16[1,2048,384]{2,1,0:T(8,128)(2,1)} %param.11) | copy-start | bytes 4718596
  232.6 4.3 copy-start.12
  236.9 97.8 %all-to-all-start.1 = ((bf16[16,64,2048]{2,1,0:T(8,128)(2,1)}), bf16[16,64,2048]{2,1,0:T(8,128)(2,1)}, u32[]{:S(2)}, u32[]{:S(2)}) async-start(bf16[16,64,2048]{2,1,0:T(8,128)(2,1)} %bitcast.74), calls=%async_computation.1 | async-start | bytes 8388608 | tf_op jit(solution)/shard_map/all_to_all | solution.py:43
  242.0 3.7 copy-start.4
  242.0 3.7 copy-start.8
  334.6 5.3 %copy-start.13 = (bf16[1024,384]{1,0:T(8,128)(2,1)S(1)}, bf16[1024,384]{1,0:T(8,128)(2,1)}, u32[]{:S(2)}) copy-start(bf16[1024,384]{1,0:T(8,128)(2,1)} %copy-done.12) | copy-start | bytes 2359300
  334.6 97.9 %all-to-all-start.3 = ((bf16[16,64,2048]{2,1,0:T(8,128)(2,1)}), bf16[16,64,2048]{2,1,0:T(8,128)(2,1)}, u32[]{:S(2)}, u32[]{:S(2)}) async-start(bf16[16,64,2048]{2,1,0:T(8,128)(2,1)} %bitcast.72), calls=%async_computation.3 | async-start | bytes 8388608 | tf_op jit(solution)/shard_map/all_to_all | solution.py:75
  339.9 5.3 %copy-start.9 = (bf16[1024,384]{1,0:T(8,128)(2,1)S(1)}, bf16[1024,384]{1,0:T(8,128)(2,1)}, u32[]{:S(2)}) copy-start(bf16[1024,384]{1,0:T(8,128)(2,1)} %get-tuple-element.8) | copy-start | bytes 2359300
  339.9 115.4 %all-reduce.5.cloned.1.call-start = ((), (), s32[]{:S(2)}) async-start(), calls=%async_computation.4 | async-start | bytes 9437184 | tf_op jit(solution)/shard_map/psum | solution.py:85
  345.2 5.8 %copy-start.7 = (bf16[1024,384]{1,0:T(8,128)(2,1)S(1)}, bf16[1024,384]{1,0:T(8,128)(2,1)}, u32[]{:S(2)}) copy-start(bf16[1024,384]{1,0:T(8,128)(2,1)} %get-tuple-element.9) | copy-start | bytes 2359300
  444.1 6.0 %copy-start.2 = (bf16[1024,2048]{1,0:T(8,128)(2,1)S(1)}, bf16[1024,2048]{1,0:T(8,128)(2,1)}, u32[]{:S(2)}) copy-start(bf16[1024,2048]{1,0:T(8,128)(2,1)} %gather_fusion.1) | copy-start | bytes 12582916
  455.3 2.9 copy-start.6
  455.3 4.0 copy-start.5
  455.3 5.2 %copy-start.1 = (bf16[1,384,2048]{2,1,0:T(8,128)(2,1)S(1)}, bf16[1,384,2048]{2,1,0:T(8,128)(2,1)}, u32[]{:S(2)}) copy-start(bf16[1,384,2048]{2,1,0:T(8,128)(2,1)} %param.13) | copy-start | bytes 4718596
Sparse Core Ops, SparseCore 0:
  356.8 30.5 all-reduce.4
where the time goes:
time: 468 us; the launch traced here: 467 us
  waiting for transfers between devices  309 us (66%)
  local copies, waits for them, and re-layouts  52.1 us (11%)
  matrix products  48.1 us (10%)
  starting transfers between devices  22.8 us (5%)
  other arithmetic  21.6 us (5%)
  between operations  14.2 us (3%)
    all_to_all x1, waiting for transfers between devices, on_device(): lax.all_to_all(outputs.reshape(experts, items, width), 'expert', split_ax...  84.6 us
    all_to_all x1, waiting for transfers between devices, on_device(): lax.all_to_all(cot_send.reshape(experts, capacity, width), 'expert', spli...  80.7 us
    all_to_all x1, waiting for transfers between devices, on_device(): lax.all_to_all(send, 'expert', split_axis=0, concat_axis=0, tiled=True)  79.1 us
    all_to_all x1, waiting for transfers between devices, on_device(): lax.all_to_all(slot_grads.reshape(experts, capacity, width), 'expert', sp...  64 us
    gather x1, local copies, waits for them, and re-layouts, on_device(): back_items.reshape(-1, width)[slots].reshape(rows_dev, picks, width)  11.8 us
    gather x1, local copies, waits for them, and re-layouts, on_device(): grads_back.reshape(-1, width)[slots].reshape(rows_dev, picks, width)  11.6 us
  transfers between devices with their start and end apart: 5, of which 4 were waited for; matrix products, arithmetic and copies ran while one was open for 19% of the time, Pallas kernels for 0%

commit v1 on v0

v1 whole, which is shorter than its diff:
```python
import functools

import jax
import jax.numpy as jnp
from jax import lax
from jax.experimental import pallas as pl
from jax.experimental.pallas import tpu as pltpu
from jax.sharding import PartitionSpec as P

PLANE = 4
BF = jnp.bfloat16
F32 = jnp.float32


def slot_index(block_routes, expert_count, capacity):
    flat = block_routes.reshape(-1)
    onehot = (flat[:, None] == jnp.arange(expert_count, dtype=jnp.int32)[None, :]).astype(jnp.int32)
    before = jnp.cumsum(onehot, axis=0) - onehot
    ranks = jnp.sum(before * onehot, axis=1)
    return flat * capacity + ranks


def expert_forward(block, gate_mat, up_mat, down_mat):
    inputs = block.reshape(-1, block.shape[2])
    gate_pre = jnp.dot(inputs, gate_mat, preferred_element_type=jnp.float32)
    up_pre = jnp.dot(inputs, up_mat, preferred_element_type=jnp.float32)
    sigma = jax.nn.sigmoid(gate_pre)
    hidden = (gate_pre * sigma * up_pre).astype(jnp.bfloat16)
    outputs = jnp.dot(hidden, down_mat, preferred_element_type=jnp.float32).astype(jnp.bfloat16)
    return (gate_pre, up_pre, hidden, outputs)


def direct_plan(tokens, routes, gates, cotangent, w_gate, w_up, w_down):
    rows_dev, width = tokens.shape
    picks = routes.shape[1]
    experts = lax.axis_size("expert")
    capacity = rows_dev * picks // experts
    gate_mat = w_gate[0]
    up_mat = w_up[0]
    down_mat = w_down[0]
    slots = slot_index(routes, experts, capacity)
    flat_rows = jnp.arange(rows_dev * picks, dtype=jnp.int32) // picks
    token_of = jnp.full((experts * capacity,), rows_dev, jnp.int32).at[slots].set(flat_rows)
    weight_of = jnp.zeros((experts * capacity,), jnp.float32).at[slots].set(gates.reshape(-1))
    token_pad = jnp.concatenate([tokens, jnp.zeros((1, width), tokens.dtype)], axis=0)
    send = token_pad[token_of].reshape(experts, capacity, width)

    def exchange(rows):
        return lax.all_to_all(
            rows.reshape(experts, capacity, width), "expert", split_axis=0, concat_axis=0, tiled=True
        )

    block = exchange(send)
    gate_pre, up_pre, hidden, outputs = expert_forward(block, gate_mat, up_mat, down_mat)
    back_items = exchange(outputs)
    inputs = block.reshape(-1, width)
    gathered = back_items.reshape(-1, width)[slots].reshape(rows_dev, picks, width)
    mixed = jnp.sum(gates[:, :, None] * gathered.astype(jnp.float32), axis=1).astype(jnp.bfloat16)
    cot_pad = jnp.concatenate([cotangent, jnp.zeros((1, width), cotangent.dtype)], axis=0)
    cot_send = (weight_of[:, None] * cot_pad[token_of].astype(jnp.float32)).astype(jnp.bfloat16)
    slot_cot = exchange(cot_send).reshape(-1, width)
    down_part = jnp.dot(hidden.T, slot_cot, preferred_element_type=jnp.float32)
    hidden_grad = jnp.dot(slot_cot, down_mat.T, preferred_element_type=jnp.float32)
    sigma = jax.nn.sigmoid(gate_pre)
    gate_grad = (hidden_grad * up_pre * sigma * (1.0 + gate_pre * (1.0 - sigma))).astype(
        jnp.bfloat16
    )
    up_grad = (hidden_grad * gate_pre * sigma).astype(jnp.bfloat16)
    slot_grads = (
        jnp.dot(gate_grad, gate_mat.T, preferred_element_type=jnp.float32)
        + jnp.dot(up_grad, up_mat.T, preferred_element_type=jnp.float32)
    ).astype(jnp.bfloat16)
    grads_back = exchange(slot_grads)
    gate_part = jnp.dot(inputs.T, gate_grad, preferred_element_type=jnp.float32)
    up_part = jnp.dot(inputs.T, up_grad, preferred_element_type=jnp.float32)
    grad_rows = grads_back.reshape(-1, width)[slots].reshape(rows_dev, picks, width)
    input_grad = jnp.sum(grad_rows.astype(jnp.float32), axis=1).astype(jnp.bfloat16)
    return (mixed, input_grad) + relay_sums(gate_part, up_part, down_part)


def relay_sums(*parts):
    relays = lax.axis_size("pipe")
    sums = []
    for part in parts:
        part = part.astype(BF)
        if relays == 2:
            other = lax.ppermute(part, "pipe", [(0, 1), (1, 0)])
            total = (part.astype(F32) + other.astype(F32)).astype(BF)
        else:
            total = lax.psum(part, "pipe")
        sums.append(total[None])
    return tuple(sums)


def pick_matrix(ids_ref, meta, k, capacity):
    picks, rows = meta.shape[0] // 2, meta.shape[1]
    hit = meta[:picks] == ids_ref[k].astype(F32)
    weight = jnp.sum(jnp.where(hit, meta[picks:], 0.0), axis=0, keepdims=True)
    member = jnp.sum(jnp.where(hit, 1.0, 0.0), axis=0, keepdims=True)
    first = lax.broadcasted_iota(jnp.int32, (rows, rows), 0)
    second = lax.broadcasted_iota(jnp.int32, (rows, rows), 1)
    ahead = jnp.where(first < second, 1.0, 0.0).astype(BF)
    member8 = jnp.broadcast_to(member, (16, rows)).astype(BF)
    rank = jnp.dot(member8, ahead, preferred_element_type=F32)[0:1]
    place = jnp.where(member > 0.5, rank, -1.0)
    slot = lax.broadcasted_iota(jnp.int32, (capacity, rows), 0).astype(F32)
    return slot == place, weight


def compact_kernel(ids_ref, meta_ref, rows_ref, *out_refs, weighted):
    capacity = out_refs[0].shape[1]
    meta = meta_ref[0]
    block = rows_ref[0]
    for k, out_ref in enumerate(out_refs):
        chosen, weight = pick_matrix(ids_ref, meta, k, capacity)
        matrix = jnp.where(chosen, 1.0, 0.0).astype(BF)
        picked = jnp.dot(matrix, block, preferred_element_type=F32)
        if weighted:
            picked = picked * jnp.sum(jnp.where(chosen, weight, 0.0), axis=1, keepdims=True)
        out_ref[0] = picked.astype(BF)


def compact(ids, meta, rows, capacity, weighted):
    blocks, rows_dev, width = rows.shape
    half = width // 2
    return pl.pallas_call(
        functools.partial(compact_kernel, weighted=weighted),
        grid=(blocks, 2),
        in_specs=[
            pl.BlockSpec(memory_space=pltpu.SMEM),
            pl.BlockSpec((1,) + meta.shape[1:], lambda b, h: (b, 0, 0)),
            pl.BlockSpec((1, rows_dev, half), lambda b, h: (b, 0, h)),
        ],
        out_specs=[pl.BlockSpec((1, capacity, half), lambda b, h: (b, 0, h))] * PLANE,
        out_shape=[jax.ShapeDtypeStruct((blocks, capacity, width), BF)] * PLANE,
        name="compact",
    )(ids, meta, rows)


def expand_kernel(ids_ref, meta_ref, *refs, weighted):
    row_refs, out_ref = refs[:PLANE], refs[-1]
    capacity = row_refs[0].shape[1]
    meta = meta_ref[0]
    total = jnp.zeros(out_ref.shape[1:], F32)
    for k, row_ref in enumerate(row_refs):
        chosen, weight = pick_matrix(ids_ref, meta, k, capacity)
        rows = row_ref[0]
        if weighted:
            high = weight.astype(BF).astype(F32)
            parts = [high, weight - high]
        else:
            parts = [1.0]
        for part in parts:
            matrix = jnp.where(chosen, part, 0.0).T.astype(BF)
            total += jnp.dot(matrix, rows, preferred_element_type=F32)
    for extra_ref in refs[PLANE:-1]:
        total += extra_ref[...].astype(F32)
    out_ref[0] = total.astype(BF)


def expand(ids, meta, rows, weighted, extras=()):
    blocks, capacity, width = rows[0].shape
    rows_dev = meta.shape[2]
    half = width // 2
    return pl.pallas_call(
        functools.partial(expand_kernel, weighted=weighted),
        grid=(blocks, 2),
        in_specs=[
            pl.BlockSpec(memory_space=pltpu.SMEM),
            pl.BlockSpec((1,) + meta.shape[1:], lambda b, h: (b, 0, 0)),
        ]
        + [pl.BlockSpec((1, capacity, half), lambda b, h: (b, 0, h))] * PLANE
        + [pl.BlockSpec((rows_dev, half), lambda b, h: (0, h))] * len(extras),
        out_specs=pl.BlockSpec((1, rows_dev, half), lambda b, h: (b, 0, h)),
        out_shape=jax.ShapeDtypeStruct((blocks, rows_dev, width), BF),
        name="expand",
    )(ids, meta, *rows, *extras)


def plane_plan(tokens, routes, gates, cotangent, w_gate, w_up, w_down):
    rows_dev, width = tokens.shape
    picks = routes.shape[1]
    experts = lax.axis_size("expert")
    planes = experts // PLANE
    capacity = rows_dev * picks // experts
    gate_mat, up_mat, down_mat = w_gate[0], w_up[0], w_down[0]
    inner = gate_mat.shape[1]
    here = lax.axis_index("expert")
    level, place = here // PLANE, here % PLANE
    ids = level * PLANE + (place ^ jnp.arange(PLANE, dtype=jnp.int32))
    groups = [[0]] + [sorted({r, planes - r}) for r in range(1, planes // 2 + 1)]

    def rotate(value, turn):
        return lax.ppermute(
            value, "expert", [(i, (i - PLANE * turn) % experts) for i in range(experts)]
        )

    def across(value, bits):
        return lax.ppermute(value, "expert", [(i, i ^ bits) for i in range(experts)])

    def spread(value):
        return {r: value if r == 0 else rotate(value, r) for g in groups for r in g}

    meta_of = spread(jnp.concatenate([routes.astype(F32).T, gates.T], axis=0))
    metas = [jnp.stack([meta_of[r] for r in g]) for g in groups]

    def dispatch(value, weighted):
        block_of = spread(value)
        out = []
        for g, meta in zip(groups, metas):
            rows = compact(ids, meta, jnp.stack([block_of[r] for r in g]), capacity, weighted)
            out.append([rows[0]] + [across(rows[k], k) for k in (3, 1, 2)])
        return out

    def flat(chunks):
        return jnp.concatenate([piece.reshape(-1, width) for chunk in chunks for piece in chunk])

    order = (0, 3, 1, 2)

    def collect(value, weighted):
        start = 0
        pieces = []
        for g in groups:
            count = len(g) * capacity
            chunk = []
            for k in order:
                chunk.append(value[start : start + count].reshape(len(g), capacity, width))
                start += count
            pieces.append(chunk)
        arrived = []
        for at in reversed(range(len(groups))):
            chunk = pieces[at]
            rows = {0: chunk[0]}
            for k, piece in zip(order[1:], chunk[1:]):
                rows[k] = across(piece, k)
            rows = [rows[k] for k in range(PLANE)]
            if at:
                part = expand(ids, metas[at], rows, weighted)
                arrived += [rotate(part[n], -r) for n, r in enumerate(groups[at])]
            else:
                return expand(ids, metas[0], rows, weighted, arrived)[0]

    inputs = flat(dispatch(tokens, False))
    slot_cot = flat(dispatch(cotangent, True))
    gate_pre = jnp.dot(inputs, gate_mat, preferred_element_type=F32)
    up_pre = jnp.dot(inputs, up_mat, preferred_element_type=F32)
    sigma = jax.nn.sigmoid(gate_pre)
    hidden = (gate_pre * sigma * up_pre).astype(BF)
    outputs = jnp.dot(hidden, down_mat, preferred_element_type=F32).astype(BF)
    mixed = collect(outputs, True)
    hidden_grad = jnp.dot(slot_cot, down_mat.T, preferred_element_type=F32)
    gate_grad = (hidden_grad * up_pre * sigma * (1.0 + gate_pre * (1.0 - sigma))).astype(BF)
    up_grad = (hidden_grad * gate_pre * sigma).astype(BF)
    slot_grads = (
        jnp.dot(gate_grad, gate_mat.T, preferred_element_type=F32)
        + jnp.dot(up_grad, up_mat.T, preferred_element_type=F32)
    ).astype(BF)
    input_grad = collect(slot_grads, False)
    down_part = jnp.dot(hidden.T, slot_cot, preferred_element_type=F32)
    gate_part = jnp.dot(inputs.T, gate_grad, preferred_element_type=F32)
    up_part = jnp.dot(inputs.T, up_grad, preferred_element_type=F32)
    return (mixed, input_grad) + relay_sums(gate_part, up_part, down_part)


def on_device(tokens, routes, *rest):
    experts, picks = lax.axis_size("expert"), routes.shape[1]
    if experts % PLANE == 0 and experts <= 2 * picks:
        return plane_plan(tokens, routes, *rest)
    return direct_plan(tokens, routes, *rest)


def solution(mesh):
    rows, stack = P(("pipe", "expert"), None), P("expert", None, None)
    return jax.shard_map(
        on_device,
        mesh=mesh,
        in_specs=(rows, rows, rows, rows, stack, stack, stack),
        out_specs=(rows, rows, stack, stack, stack),
        check_vma=False,
    )
```

time: 468 us -> 349 us (0.75)
  waiting for transfers between devices: 309 us -> 112 us
  starting transfers between devices: 22.8 us -> 96.3 us
  Pallas kernels: 0 us -> 56.5 us
  local copies, waits for them, and re-layouts: 52.1 us -> 32 us
  matrix products: 48.1 us -> 30.3 us
  between operations: 14.2 us -> 1.12 us
  other arithmetic: 21.6 us -> 16.7 us
    all_to_all x4 -> x0, waiting for transfers between devices: 309 us -> none  [the longest x1 84.6 us: on_device(): lax.all_to_all(outputs.reshape(experts, items, width), 'expert', split_ax...]
    ppermute x0 -> x54, waiting for transfers between devices: none -> 112 us  [the longest x36 82.2 us: across(): lax.ppermute(value, 'expert', [(i, i ^ bits) for i in range(experts)])]
    ppermute x0 -> x54, starting transfers between devices: none -> 96.3 us  [the longest x15 51.7 us: rotate(): lax.ppermute(value, 'expert', [(i, (i - PLANE * turn) % experts) for i in...]
    pallas_call x0 -> x12, Pallas kernels: none -> 56.5 us  [the longest x6 33 us: expand(): pl.pallas_call(functools.partial(expand_kernel, weighted=weighted), grid=...]
    gather x4 -> x0, local copies, waits for them, and re-layouts: 35.4 us -> none  [the longest x1 11.8 us: on_device(): back_items.reshape(-1, width)[slots].reshape(rows_dev, picks, width)]
    all_to_all x4 -> x0, starting transfers between devices: 22.7 us -> none  [the longest x1 7.27 us: on_device(): lax.all_to_all(send, 'expert', split_axis=0, concat_axis=0, tiled=True)]
    dot_general x9, matrix products: 48.1 us -> 30.3 us  [the longest x1 5.72 us: plane_plan(): up_part = jnp.dot(inputs.T, up_grad, preferred_element_type=F32)]
    unnamed x33 -> x86, local copies, waits for them, and re-layouts: 6.09 us -> 22.2 us
  transfers between devices with their start and end apart: 5 -> 54, of which waited for: 4 -> 21; matrix products, arithmetic and copies ran while one was open for 19% -> 19% of each run, Pallas kernels for 0% -> 16%
where the time goes in v1:
time: 349 us; the launch traced here: 345 us
  waiting for transfers between devices  112 us (32%)
  starting transfers between devices  96.3 us (28%)
  Pallas kernels  56.5 us (16%)
  local copies, waits for them, and re-layouts  32 us (9%)
  matrix products  30.3 us (9%)
  other arithmetic  16.7 us (5%)
    ppermute x36, waiting for transfers between devices, across(): lax.ppermute(value, 'expert', [(i, i ^ bits) for i in range(experts)])  82.2 us
    ppermute x15, starting transfers between devices, rotate(): lax.ppermute(value, 'expert', [(i, (i - PLANE * turn) % experts) for i in...  51.7 us
    ppermute x36, starting transfers between devices, across(): lax.ppermute(value, 'expert', [(i, i ^ bits) for i in range(experts)])  44.5 us
    pallas_call x6, Pallas kernels, expand(): pl.pallas_call(functools.partial(expand_kernel, weighted=weighted), grid=...  33 us
    ppermute x15, waiting for transfers between devices, rotate(): lax.ppermute(value, 'expert', [(i, (i - PLANE * turn) % experts) for i in...  29.9 us
    pallas_call x6, Pallas kernels, compact(): pl.pallas_call(functools.partial(compact_kernel, weighted=weighted), grid...  23.5 us
    unnamed x86, local copies, waits for them, and re-layouts  22.2 us
    broadcast_in_dim x3, other arithmetic, relay_sums(): sums.append(total[None])  10.1 us
  transfers between devices with their start and end apart: 54, of which 21 were waited for; matrix products, arithmetic and copies ran while one was open for 19% of the time, Pallas kernels for 16%

profile of v1, /device:TPU:14, one launch (start us, length us, event | category | flops | bytes accessed | tf_op | source)
XLA Modules:
  0.0 345.0 jit_solution(6803273224729407916)
XLA Ops:
  4.8 2.0 collective-permute-start.30
  7.4 3.3 compact.9
  12.8 3.3 compact.6
  17.7 3.8 %collective-permute-start.5 = (bf16[128,2048]{1,0:T(8,128)(2,1)}, bf16[128,2048]{1,0:T(8,128)(2,1)S(1)}, u32[]{:S(2)}, u32[]{:S(2)}) collective-permute-start(bf16[128,2048]{1,0:T(8,128)(2,1)} %param.7), channel_id=1, source_target_pairs={{0,12},{1,13},{2,14},{3,15},{4,0},{5,1},{6,2},{7,3},{8,4},{9,5},{1... | collective-permute-start | bytes 1572872 | tf_op jit(solution)/shard_map/ppermute | solution.py:194
  24.4 4.6 %collective-permute-done.28 = bf16[1,64,2048]{2,1,0:T(8,128)(2,1)S(1)} collective-permute-done((bf16[1,64,2048]{2,1,0:T(8,128)(2,1)}, bf16[1,64,2048]{2,1,0:T(8,128)(2,1)S(1)}, u32[]{:S(2)}, u32[]{:S(2)}) %collective-permute-start.28) | collective-permute-done | bytes 262176 | tf_op jit(solution)/shard_map/ppermute | solution.py:199
  31.2 4.3 %collective-permute-done.29 = bf16[1,64,2048]{2,1,0:T(8,128)(2,1)S(1)} collective-permute-done((bf16[1,64,2048]{2,1,0:T(8,128)(2,1)}, bf16[1,64,2048]{2,1,0:T(8,128)(2,1)S(1)}, u32[]{:S(2)}, u32[]{:S(2)}) %collective-permute-start.29) | collective-permute-done | bytes 262176 | tf_op jit(solution)/shard_map/ppermute | solution.py:199
  35.6 2.4 collective-permute-start
  38.8 5.0 %collective-permute-done = bf16[1,64,2048]{2,1,0:T(8,128)(2,1)S(1)} collective-permute-done((bf16[1,64,2048]{2,1,0:T(8,128)(2,1)}, bf16[1,64,2048]{2,1,0:T(8,128)(2,1)S(1)}, u32[]{:S(2)}, u32[]{:S(2)}) %collective-permute-start) | collective-permute-done | bytes 262176 | tf_op jit(solution)/shard_map/ppermute | solution.py:199
  45.7 4.6 %collective-permute-done.1 = bf16[1,64,2048]{2,1,0:T(8,128)(2,1)S(1)} collective-permute-done((bf16[1,64,2048]{2,1,0:T(8,128)(2,1)}, bf16[1,64,2048]{2,1,0:T(8,128)(2,1)S(1)}, u32[]{:S(2)}, u32[]{:S(2)}) %collective-permute-start.1) | collective-permute-done | bytes 262176 | tf_op jit(solution)/shard_map/ppermute | solution.py:199
  50.3 2.3 collective-permute-start.2
  53.4 3.8 %collective-permute-done.2 = bf16[1,64,2048]{2,1,0:T(8,128)(2,1)S(1)} collective-permute-done((bf16[1,64,2048]{2,1,0:T(8,128)(2,1)}, bf16[1,64,2048]{2,1,0:T(8,128)(2,1)S(1)}, u32[]{:S(2)}, u32[]{:S(2)}) %collective-permute-start.2) | collective-permute-done | bytes 262176 | tf_op jit(solution)/shard_map/ppermute | solution.py:199
  57.2 6.3 %collective-permute-start.10 = (f32[16,128]{1,0:T(8,128)S(1)}, f32[16,128]{1,0:T(8,128)S(1)}, u32[]{:S(2)}, u32[]{:S(2)}) collective-permute-start(f32[16,128]{1,0:T(8,128)S(1)} %get-tuple-element.84), channel_id=1, source_target_pairs={{0,8},{1,9},{2,10},{3,11},{4,12},{5,13},{6,14},{7,15},{8,0},{9,1},... | collective-permute-start | bytes 24584 | tf_op jit(solution)/shard_map/ppermute | solution.py:194
  64.2 2.9 collective-permute-start.11
  68.2 5.1 %compact.7 = (bf16[2,64,2048]{2,1,0:T(8,128)(2,1)}, bf16[2,64,2048]{2,1,0:T(8,128)(2,1)}, bf16[2,64,2048]{2,1,0:T(8,128)(2,1)}, bf16[2,64,2048]{2,1,0:T(8,128)(2,1)}) custom-call(s32[4]{0:T(128)} %xor_add_fusion.ids_ref, f32[2,16,128]{2,1,0:T(8,128)} %pad_maximum_fusion.2.meta_ref, bf16[2,128,2048]{2,1,0:T(8,128)(2,1)} %pad_maximum_fusion.rows_ref), custom_call_target="tpu_custom_call" | custom-call | tf_op jit(solution)/shard_map/compact/pallas_call | solution.py:126
  73.3 3.0 collective-permute-start.7
  76.4 2.3 pad_maximum_fusion.1.rows_ref
  78.6 5.1 %compact.10 = (bf16[2,64,2048]{2,1,0:T(8,128)(2,1)}, bf16[2,64,2048]{2,1,0:T(8,128)(2,1)}, bf16[2,64,2048]{2,1,0:T(8,128)(2,1)}, bf16[2,64,2048]{2,1,0:T(8,128)(2,1)}) custom-call(s32[4]{0:T(128)} %xor_add_fusion.ids_ref, f32[2,16,128]{2,1,0:T(8,128)} %pad_maximum_fusion.2.meta_ref, bf16[2,128,2048]{2,1,0:T(8,128)(2,1)} %pad_maximum_fusion.1.rows_ref), custom_call_target="tpu_custom_call" | custom-call | tf_op jit(solution)/shard_map/compact/pallas_call | solution.py:126
  84.3 1.9 constant_dynamic-update-slice_fusion.7
  87.2 5.1 %collective-permute-done.35 = bf16[128,2048]{1,0:T(8,128)(2,1)S(1)} collective-permute-done((bf16[128,2048]{1,0:T(8,128)(2,1)S(1)}, bf16[128,2048]{1,0:T(8,128)(2,1)S(1)}, u32[]{:S(2)}, u32[]{:S(2)}) %collective-permute-start.35) | collective-permute-done | bytes 524320 | tf_op jit(solution)/shard_map/ppermute | solution.py:194
  93.7 3.4 compact.11
  97.1 6.3 %collective-permute-done.11 = bf16[128,2048]{1,0:T(8,128)(2,1)} collective-permute-done((bf16[128,2048]{1,0:T(8,128)(2,1)}, bf16[128,2048]{1,0:T(8,128)(2,1)}, u32[]{:S(2)}, u32[]{:S(2)}) %collective-permute-start.11) | collective-permute-done | bytes 524320 | tf_op jit(solution)/shard_map/ppermute | solution.py:194
  104.9 3.3 compact.8
  108.8 2.2 constant_dynamic-update-slice_fusion.2
  112.2 1.9 constant_dynamic-update-slice_fusion.1
  114.1 1.8 collective-permute-start.12
  115.8 1.9 constant_dynamic-update-slice_fusion
  119.4 10.2 %collective-permute-done.12 = bf16[1,64,2048]{2,1,0:T(8,128)(2,1)S(1)} collective-permute-done((bf16[1,64,2048]{2,1,0:T(8,128)(2,1)}, bf16[1,64,2048]{2,1,0:T(8,128)(2,1)S(1)}, u32[]{:S(2)}, u32[]{:S(2)}) %collective-permute-start.12) | collective-permute-done | bytes 262176 | tf_op jit(solution)/shard_map/ppermute | solution.py:199
  131.8 5.5 %collective-permute-done.13 = bf16[1,64,2048]{2,1,0:T(8,128)(2,1)S(1)} collective-permute-done((bf16[1,64,2048]{2,1,0:T(8,128)(2,1)}, bf16[1,64,2048]{2,1,0:T(8,128)(2,1)S(1)}, u32[]{:S(2)}, u32[]{:S(2)}) %collective-permute-start.13) | collective-permute-done | bytes 262176 | tf_op jit(solution)/shard_map/ppermute | solution.py:199
  143.8 5.0 %collective-permute-done.14 = bf16[1,64,2048]{2,1,0:T(8,128)(2,1)S(1)} collective-permute-done((bf16[1,64,2048]{2,1,0:T(8,128)(2,1)}, bf16[1,64,2048]{2,1,0:T(8,128)(2,1)S(1)}, u32[]{:S(2)}, u32[]{:S(2)}) %collective-permute-start.14) | collective-permute-done | bytes 262176 | tf_op jit(solution)/shard_map/ppermute | solution.py:199
  149.5 4.7 %fusion.11 = f32[1024,384]{1,0:T(8,128)S(1)} fusion(bf16[1024,2048]{1,0:T(8,128)(2,1)} %bitcast_dynamic-update-slice_fusion.8, bf16[1,2048,384]{2,1,0:T(8,128)(2,1)S(1)} %copy-done.2), kind=kOutput, calls=%fused_computation.19 | convolution fusion | flops 1610612736 | bytes 7340032 | tf_op jit(solution)/shard_map/dot_general | solution.py:245
  154.2 2.3 fusion.7
  156.8 3.0 multiply_convert_fusion
  159.7 2.4 fusion.9
  162.1 2.4 add_convert_fusion
  166.4 2.6 collective-permute-start.44
  169.9 2.3 convolution_convert_fusion
  176.3 2.1 collective-permute-start.46
  180.1 1.7 collective-permute-start.47
  181.8 4.2 %collective-permute-done.39.refs_1_ = bf16[1,64,2048]{2,1,0:T(8,128)(2,1)S(1)} collective-permute-done((bf16[1,64,2048]{2,1,0:T(8,128)(2,1)S(1)}, bf16[1,64,2048]{2,1,0:T(8,128)(2,1)S(1)}, u32[]{:S(2)}, u32[]{:S(2)}) %collective-permute-start.39) | collective-permute-done | bytes 262176 | tf_op jit(solution)/shard_map/ppermute | solution.py:199
  188.0 3.6 %collective-permute-done.18.refs_1_ = bf16[1,64,2048]{2,1,0:T(8,128)(2,1)S(1)} collective-permute-done((bf16[1,64,2048]{2,1,0:T(8,128)(2,1)S(1)}, bf16[1,64,2048]{2,1,0:T(8,128)(2,1)S(1)}, u32[]{:S(2)}, u32[]{:S(2)}) %collective-permute-start.18) | collective-permute-done | bytes 262176 | tf_op jit(solution)/shard_map/ppermute | solution.py:199
  193.4 20.2 %collective-permute-done.19.refs_2_ = bf16[1,64,2048]{2,1,0:T(8,128)(2,1)S(1)} collective-permute-done((bf16[1,64,2048]{2,1,0:T(8,128)(2,1)S(1)}, bf16[1,64,2048]{2,1,0:T(8,128)(2,1)S(1)}, u32[]{:S(2)}, u32[]{:S(2)}) %collective-permute-start.19) | collective-permute-done | bytes 262176 | tf_op jit(solution)/shard_map/ppermute | solution.py:199
  213.7 2.5 collective-permute-start.41
  216.1 3.3 collective-permute-done.20.refs_3_
  223.6 1.9 convolution_convert_fusion.1
  225.6 4.0 %expand.9 = bf16[1,128,2048]{2,1,0:T(8,128)(2,1)} custom-call(s32[4]{0:T(128)} %xor_add_fusion.ids_ref, f32[1,16,128]{2,1,0:T(8,128)} %bitcast.161, bf16[1,64,2048]{2,1,0:T(8,128)(2,1)} %get-tuple-element.60.refs_0_, bf16[1,64,2048]{2,1,0:T(8,128)(2,1)} %copy-done.18, bf16[1,64,2048]{2,1,0:T(8,128)(2,1)} %copy-done.19, bf16[1,64,2048]{2,1,0:T(8,128)(2,1)} %copy-done.20), custom_call_target="tpu_custom_call" | custom-call | tf_op jit(solution)/shard_map/expand/pallas_call | solution.py:165
  229.6 4.9 %expand.6 = bf16[1,128,2048]{2,1,0:T(8,128)(2,1)} custom-call(s32[4]{0:T(128)} %xor_add_fusion.ids_ref, f32[1,16,128]{2,1,0:T(8,128)} %bitcast.162, bf16[1,64,2048]{2,1,0:T(8,128)(2,1)} %get-tuple-element.72.refs_0_, bf16[1,64,2048]{2,1,0:T(8,128)(2,1)} %copy-done.21, bf16[1,64,2048]{2,1,0:T(8,128)(2,1)} %copy-done.22, bf16[1,64,2048]{2,1,0:T(8,128)(2,1)} %copy-done.23), custom_call_target="tpu_custom_call" | custom-call | tf_op jit(solution)/shard_map/expand/pallas_call | solution.py:165
  234.5 6.2 %expand.10 = bf16[2,128,2048]{2,1,0:T(8,128)(2,1)} custom-call(s32[4]{0:T(128)} %xor_add_fusion.ids_ref, f32[2,16,128]{2,1,0:T(8,128)} %pad_maximum_fusion.2.meta_ref, bf16[2,64,2048]{2,1,0:T(8,128)(2,1)} %bitcast.144, bf16[2,64,2048]{2,1,0:T(8,128)(2,1)} %copy-done.12, bf16[2,64,2048]{2,1,0:T(8,128)(2,1)} %copy-done.13, bf16[2,64,2048]{2,1,0:T(8,128)(2,1)} %copy-done.14), custom_call_target="tpu_custom_call" | custom-call | tf_op jit(solution)/shard_map/expand/pallas_call | solution.py:165
  242.4 4.7 %collective-permute-done.15.refs_1_ = bf16[1,64,2048]{2,1,0:T(8,128)(2,1)} collective-permute-done((bf16[1,64,2048]{2,1,0:T(8,128)(2,1)}, bf16[1,64,2048]{2,1,0:T(8,128)(2,1)}, u32[]{:S(2)}, u32[]{:S(2)}) %collective-permute-start.15) | collective-permute-done | bytes 262176 | tf_op jit(solution)/shard_map/ppermute | solution.py:199
  247.1 3.4 collective-permute-start.45
  250.5 2.3 slice_bitcast_fusion
  253.6 5.7 %convolution_convert_fusion.2 = bf16[2048,384]{1,0:T(8,128)(2,1)} fusion(bf16[1024,2048]{1,0:T(8,128)(2,1)} %bitcast_dynamic-update-slice_fusion.8, bf16[1024,384]{1,0:T(8,128)(2,1)S(1)} %copy-done.7), kind=kOutput, calls=%fused_computation.6 | convolution fusion | flops 1611399168 | bytes 6553600 | tf_op jit(solution)/shard_map/dot_general | solution.py:261
  259.3 8.1 %expand.7 = bf16[2,128,2048]{2,1,0:T(8,128)(2,1)} custom-call(s32[4]{0:T(128)} %xor_add_fusion.ids_ref, f32[2,16,128]{2,1,0:T(8,128)} %pad_maximum_fusion.2.meta_ref, bf16[2,64,2048]{2,1,0:T(8,128)(2,1)} %bitcast.143, bf16[2,64,2048]{2,1,0:T(8,128)(2,1)} %collective-permute-done.22.refs_1_, bf16[2,64,2048]{2,1,0:T(8,128)(2,1)} %collective-permute-done.23.refs_2_, ...), custom_call_target="tpu_custom_call" | custom-call | tf_op jit(solution)/shard_map/expand/pallas_call | solution.py:165
  267.5 5.6 %collective-permute-done.45.refs_4_ = bf16[128,2048]{1,0:T(8,128)(2,1)} collective-permute-done((bf16[128,2048]{1,0:T(8,128)(2,1)}, bf16[128,2048]{1,0:T(8,128)(2,1)}, u32[]{:S(2)}, u32[]{:S(2)}) %collective-permute-start.45) | collective-permute-done | bytes 524320 | tf_op jit(solution)/shard_map/ppermute | solution.py:194
  273.1 18.7 %collective-permute-start.50 = (bf16[128,2048]{1,0:T(8,128)(2,1)}, bf16[128,2048]{1,0:T(8,128)(2,1)}, u32[]{:S(2)}, u32[]{:S(2)}) collective-permute-start(bf16[128,2048]{1,0:T(8,128)(2,1)} %get-tuple-element.80), channel_id=1, source_target_pairs={{0,12},{1,13},{2,14},{3,15},{4,0},{5,1},{6,2},{7,3},{8,4},{9,5},{1... | collective-permute-start | bytes 1572872 | tf_op jit(solution)/shard_map/ppermute | solution.py:194
  291.7 2.3 slice_bitcast_fusion.2
  294.0 12.5 %collective-permute-start.25 = (bf16[128,2048]{1,0:T(8,128)(2,1)}, bf16[128,2048]{1,0:T(8,128)(2,1)S(1)}, u32[]{:S(2)}, u32[]{:S(2)}) collective-permute-start(bf16[128,2048]{1,0:T(8,128)(2,1)} %get-tuple-element.83), channel_id=1, source_target_pairs={{0,4},{1,5},{2,6},{3,7},{4,8},{5,9},{6,10},{7,11},{8,12},{9,13},{1... | collective-permute-start | bytes 1572872 | tf_op jit(solution)/shard_map/ppermute | solution.py:194
  306.5 5.9 %collective-permute-done.49.refs_5_ = bf16[128,2048]{1,0:T(8,128)(2,1)} collective-permute-done((bf16[128,2048]{1,0:T(8,128)(2,1)}, bf16[128,2048]{1,0:T(8,128)(2,1)}, u32[]{:S(2)}, u32[]{:S(2)}) %collective-permute-start.49) | collective-permute-done | bytes 524320 | tf_op jit(solution)/shard_map/ppermute | solution.py:194
  312.4 5.7 %convolution_convert_fusion.3 = bf16[2048,384]{1,0:T(8,128)(2,1)} fusion(bf16[1024,2048]{1,0:T(8,128)(2,1)} %bitcast_dynamic-update-slice_fusion.8, bf16[1024,384]{1,0:T(8,128)(2,1)S(1)} %copy-done.5), kind=kOutput, calls=%fused_computation.7 | convolution fusion | flops 1611399168 | bytes 6553600 | tf_op jit(solution)/shard_map/dot_general | solution.py:260
  318.1 4.5 %expand.11 = bf16[1,128,2048]{2,1,0:T(8,128)(2,1)} custom-call(s32[4]{0:T(128)} %xor_add_fusion.ids_ref, f32[1,16,128]{2,1,0:T(8,128)} %get-tuple-element.85.meta_ref, bf16[1,64,2048]{2,1,0:T(8,128)(2,1)} %get-tuple-element.64.refs_0_, bf16[1,64,2048]{2,1,0:T(8,128)(2,1)} %copy-done.24, bf16[1,64,2048]{2,1,0:T(8,128)(2,1)} %copy-done.25, ...), custom_call_target="tpu_custom_call" | custom-call | tf_op jit(solution)/shard_map/expand/pallas_call | solution.py:165
  322.6 6.0 %collective-permute-done.25.refs_5_ = bf16[128,2048]{1,0:T(8,128)(2,1)S(1)} collective-permute-done((bf16[128,2048]{1,0:T(8,128)(2,1)}, bf16[128,2048]{1,0:T(8,128)(2,1)S(1)}, u32[]{:S(2)}, u32[]{:S(2)}) %collective-permute-start.25) | collective-permute-done | bytes 524320 | tf_op jit(solution)/shard_map/ppermute | solution.py:194
  329.7 5.2 %expand.8 = bf16[1,128,2048]{2,1,0:T(8,128)(2,1)} custom-call(s32[4]{0:T(128)} %xor_add_fusion.ids_ref, f32[1,16,128]{2,1,0:T(8,128)} %get-tuple-element.85.meta_ref, bf16[1,64,2048]{2,1,0:T(8,128)(2,1)} %get-tuple-element.76.refs_0_, bf16[1,64,2048]{2,1,0:T(8,128)(2,1)} %collective-permute-done.15.refs_1_, bf16[1,64,2048]{2,1,0:T(8,128)(2,1)} %copy-done.26, ...), custom_call_target="tpu_custom_call" | custom-call | tf_op jit(solution)/shard_map/expand/pallas_call | solution.py:165
  334.9 3.3 fusion.2
  338.2 3.4 fusion.1
  341.6 3.4 fusion
  (168 shorter events, 56.2 us)
Async XLA Ops:
  0.6 156.1 %copy-start = (bf16[1,384,2048]{2,1,0:T(8,128)(2,1)S(1)}, bf16[1,384,2048]{2,1,0:T(8,128)(2,1)}, u32[]{:S(2)}) copy-start(bf16[1,384,2048]{2,1,0:T(8,128)(2,1)} %param.13) | copy-start | bytes 4718596
  0.6 63.6 %copy-start.8 = (bf16[128,2048]{1,0:T(8,128)(2,1)S(1)}, bf16[128,2048]{1,0:T(8,128)(2,1)}, u32[]{:S(2)}) copy-start(bf16[128,2048]{1,0:T(8,128)(2,1)} %param.10) | copy-start | bytes 1572868
  2.8 14.9 %collective-permute-start.3 = (f32[16,128]{1,0:T(8,128)S(1)}, f32[16,128]{1,0:T(8,128)S(1)}, u32[]{:S(2)}, u32[]{:S(2)}) collective-permute-start(f32[16,128]{1,0:T(8,128)S(1)} %get-tuple-element.84), channel_id=1, source_target_pairs={{0,12},{1,13},{2,14},{3,15},{4,0},{5,1},{6,2},{7,3},{8,4},{9,5},{1... | collective-permute-start | bytes 24584 | tf_op jit(solution)/shard_map/ppermute | solution.py:194
  3.2 18.3 %collective-permute-start.4 = (f32[16,128]{1,0:T(8,128)S(1)}, f32[16,128]{1,0:T(8,128)S(1)}, u32[]{:S(2)}, u32[]{:S(2)}) collective-permute-start(f32[16,128]{1,0:T(8,128)S(1)} %get-tuple-element.84), channel_id=1, source_target_pairs={{0,4},{1,5},{2,6},{3,7},{4,8},{5,9},{6,10},{7,11},{8,12},{9,13},{1... | collective-permute-start | bytes 24584 | tf_op jit(solution)/shard_map/ppermute | solution.py:194
  4.8 68.5 %collective-permute-start.30 = (bf16[128,2048]{1,0:T(8,128)(2,1)}, bf16[128,2048]{1,0:T(8,128)(2,1)}, u32[]{:S(2)}, u32[]{:S(2)}) collective-permute-start(bf16[128,2048]{1,0:T(8,128)(2,1)} %param.10), channel_id=1, source_target_pairs={{0,12},{1,13},{2,14},{3,15},{4,0},{5,1},{6,2},{7,3},{8,4},{9,5},{1... | collective-permute-start | bytes 1572872 | tf_op jit(solution)/shard_map/ppermute | solution.py:194
  6.8 69.5 %collective-permute-start.31 = (bf16[128,2048]{1,0:T(8,128)(2,1)}, bf16[128,2048]{1,0:T(8,128)(2,1)}, u32[]{:S(2)}, u32[]{:S(2)}) collective-permute-start(bf16[128,2048]{1,0:T(8,128)(2,1)} %param.10), channel_id=1, source_target_pairs={{0,4},{1,5},{2,6},{3,7},{4,8},{5,9},{6,10},{7,11},{8,12},{9,13},{1... | collective-permute-start | bytes 1572872 | tf_op jit(solution)/shard_map/ppermute | solution.py:194
  10.6 11.5 %collective-permute-start.27 = (bf16[1,64,2048]{2,1,0:T(8,128)(2,1)}, bf16[1,64,2048]{2,1,0:T(8,128)(2,1)S(1)}, u32[]{:S(2)}, u32[]{:S(2)}) collective-permute-start(bf16[1,64,2048]{2,1,0:T(8,128)(2,1)} %get-tuple-element.42), channel_id=1, source_target_pairs={{0,3},{1,2},{2,1},{3,0},{4,7},{5,6},{6,5},{7,4},{8,11},{9,10},{10,... | collective-permute-start | bytes 786440 | tf_op jit(solution)/shard_map/ppermute | solution.py:199
  17.7 46.5 %collective-permute-start.5 = (bf16[128,2048]{1,0:T(8,128)(2,1)}, bf16[128,2048]{1,0:T(8,128)(2,1)S(1)}, u32[]{:S(2)}, u32[]{:S(2)}) collective-permute-start(bf16[128,2048]{1,0:T(8,128)(2,1)} %param.7), channel_id=1, source_target_pairs={{0,12},{1,13},{2,14},{3,15},{4,0},{5,1},{6,2},{7,3},{8,4},{9,5},{1... | collective-permute-start | bytes 1572872 | tf_op jit(solution)/shard_map/ppermute | solution.py:194
  21.5 42.7 %collective-permute-start.6 = (bf16[128,2048]{1,0:T(8,128)(2,1)}, bf16[128,2048]{1,0:T(8,128)(2,1)S(1)}, u32[]{:S(2)}, u32[]{:S(2)}) collective-permute-start(bf16[128,2048]{1,0:T(8,128)(2,1)} %param.7), channel_id=1, source_target_pairs={{0,4},{1,5},{2,6},{3,7},{4,8},{5,9},{6,10},{7,11},{8,12},{9,13},{1... | collective-permute-start | bytes 1572872 | tf_op jit(solution)/shard_map/ppermute | solution.py:194
  22.1 6.9 %collective-permute-start.28 = (bf16[1,64,2048]{2,1,0:T(8,128)(2,1)}, bf16[1,64,2048]{2,1,0:T(8,128)(2,1)S(1)}, u32[]{:S(2)}, u32[]{:S(2)}) collective-permute-start(bf16[1,64,2048]{2,1,0:T(8,128)(2,1)} %get-tuple-element.43), channel_id=1, source_target_pairs={{0,1},{1,0},{2,3},{3,2},{4,5},{5,4},{6,7},{7,6},{8,9},{9,8},{10,11... | collective-permute-start | bytes 786440 | tf_op jit(solution)/shard_map/ppermute | solution.py:199
  29.0 6.6 %collective-permute-start.29 = (bf16[1,64,2048]{2,1,0:T(8,128)(2,1)}, bf16[1,64,2048]{2,1,0:T(8,128)(2,1)S(1)}, u32[]{:S(2)}, u32[]{:S(2)}) collective-permute-start(bf16[1,64,2048]{2,1,0:T(8,128)(2,1)} %get-tuple-element.44), channel_id=1, source_target_pairs={{0,2},{1,3},{2,0},{3,1},{4,6},{5,7},{6,4},{7,5},{8,10},{9,11},{10,... | collective-permute-start | bytes 786440 | tf_op jit(solution)/shard_map/ppermute | solution.py:199
  35.6 8.2 %collective-permute-start = (bf16[1,64,2048]{2,1,0:T(8,128)(2,1)}, bf16[1,64,2048]{2,1,0:T(8,128)(2,1)S(1)}, u32[]{:S(2)}, u32[]{:S(2)}) collective-permute-start(bf16[1,64,2048]{2,1,0:T(8,128)(2,1)} %get-tuple-element.30), channel_id=1, source_target_pairs={{0,3},{1,2},{2,1},{3,0},{4,7},{5,6},{6,5},{7,4},{8,11},{9,10},{10,... | collective-permute-start | bytes 786440 | tf_op jit(solution)/shard_map/ppermute | solution.py:199
  43.7 6.6 %collective-permute-start.1 = (bf16[1,64,2048]{2,1,0:T(8,128)(2,1)}, bf16[1,64,2048]{2,1,0:T(8,128)(2,1)S(1)}, u32[]{:S(2)}, u32[]{:S(2)}) collective-permute-start(bf16[1,64,2048]{2,1,0:T(8,128)(2,1)} %get-tuple-element.31), channel_id=1, source_target_pairs={{0,1},{1,0},{2,3},{3,2},{4,5},{5,4},{6,7},{7,6},{8,9},{9,8},{10,11... | collective-permute-start | bytes 786440 | tf_op jit(solution)/shard_map/ppermute | solution.py:199
  50.3 6.9 %collective-permute-start.2 = (bf16[1,64,2048]{2,1,0:T(8,128)(2,1)}, bf16[1,64,2048]{2,1,0:T(8,128)(2,1)S(1)}, u32[]{:S(2)}, u32[]{:S(2)}) collective-permute-start(bf16[1,64,2048]{2,1,0:T(8,128)(2,1)} %get-tuple-element.32), channel_id=1, source_target_pairs={{0,2},{1,3},{2,0},{3,1},{4,6},{5,7},{6,4},{7,5},{8,10},{9,11},{10,... | collective-permute-start | bytes 786440 | tf_op jit(solution)/shard_map/ppermute | solution.py:199
  57.2 29.0 %collective-permute-start.10 = (f32[16,128]{1,0:T(8,128)S(1)}, f32[16,128]{1,0:T(8,128)S(1)}, u32[]{:S(2)}, u32[]{:S(2)}) collective-permute-start(f32[16,128]{1,0:T(8,128)S(1)} %get-tuple-element.84), channel_id=1, source_target_pairs={{0,8},{1,9},{2,10},{3,11},{4,12},{5,13},{6,14},{7,15},{8,0},{9,1},... | collective-permute-start | bytes 24584 | tf_op jit(solution)/shard_map/ppermute | solution.py:194
  64.2 28.1 %collective-permute-start.35 = (bf16[128,2048]{1,0:T(8,128)(2,1)S(1)}, bf16[128,2048]{1,0:T(8,128)(2,1)S(1)}, u32[]{:S(2)}, u32[]{:S(2)}) collective-permute-start(bf16[128,2048]{1,0:T(8,128)(2,1)S(1)} %copy-done.8), channel_id=1, source_target_pairs={{0,8},{1,9},{2,10},{3,11},{4,12},{5,13},{6,14},{7,15},{8,0},{9,1},... | collective-permute-start | bytes 1572872 | tf_op jit(solution)/shard_map/ppermute | solution.py:194
  64.2 39.2 %collective-permute-start.11 = (bf16[128,2048]{1,0:T(8,128)(2,1)}, bf16[128,2048]{1,0:T(8,128)(2,1)}, u32[]{:S(2)}, u32[]{:S(2)}) collective-permute-start(bf16[128,2048]{1,0:T(8,128)(2,1)} %param.7), channel_id=1, source_target_pairs={{0,8},{1,9},{2,10},{3,11},{4,12},{5,13},{6,14},{7,15},{8,0},{9,1},... | collective-permute-start | bytes 1572872 | tf_op jit(solution)/shard_map/ppermute | solution.py:194
  73.3 34.8 %collective-permute-start.7 = (bf16[2,64,2048]{2,1,0:T(8,128)(2,1)}, bf16[2,64,2048]{2,1,0:T(8,128)(2,1)}, u32[]{:S(2)}, u32[]{:S(2)}) collective-permute-start(bf16[2,64,2048]{2,1,0:T(8,128)(2,1)} %get-tuple-element.34), channel_id=1, source_target_pairs={{0,3},{1,2},{2,1},{3,0},{4,7},{5,6},{6,5},{7,4},{8,11},{9,10},{10,... | collective-permute-start | bytes 1572872 | tf_op jit(solution)/shard_map/ppermute | solution.py:199
  83.8 27.2 %collective-permute-start.8 = (bf16[2,64,2048]{2,1,0:T(8,128)(2,1)}, bf16[2,64,2048]{2,1,0:T(8,128)(2,1)}, u32[]{:S(2)}, u32[]{:S(2)}) collective-permute-start(bf16[2,64,2048]{2,1,0:T(8,128)(2,1)} %get-tuple-element.35), channel_id=1, source_target_pairs={{0,1},{1,0},{2,3},{3,2},{4,5},{5,4},{6,7},{7,6},{8,9},{9,8},{10,11... | collective-permute-start | bytes 1572872 | tf_op jit(solution)/shard_map/ppermute | solution.py:199
  86.2 27.8 %collective-permute-start.9 = (bf16[2,64,2048]{2,1,0:T(8,128)(2,1)}, bf16[2,64,2048]{2,1,0:T(8,128)(2,1)}, u32[]{:S(2)}, u32[]{:S(2)}) collective-permute-start(bf16[2,64,2048]{2,1,0:T(8,128)(2,1)} %get-tuple-element.36), channel_id=1, source_target_pairs={{0,2},{1,3},{2,0},{3,1},{4,6},{5,7},{6,4},{7,5},{8,10},{9,11},{10,... | collective-permute-start | bytes 1572872 | tf_op jit(solution)/shard_map/ppermute | solution.py:199
  92.3 47.2 %collective-permute-start.32 = (bf16[2,64,2048]{2,1,0:T(8,128)(2,1)}, bf16[2,64,2048]{2,1,0:T(8,128)(2,1)}, u32[]{:S(2)}, u32[]{:S(2)}) collective-permute-start(bf16[2,64,2048]{2,1,0:T(8,128)(2,1)} %get-tuple-element.46), channel_id=1, source_target_pairs={{0,3},{1,2},{2,1},{3,0},{4,7},{5,6},{6,5},{7,4},{8,11},{9,10},{10,... | collective-permute-start | bytes 1572872 | tf_op jit(solution)/shard_map/ppermute | solution.py:199
  93.7 55.8 %copy-start.2 = (bf16[1,2048,384]{2,1,0:T(8,128)(2,1)S(1)}, bf16[1,2048,384]{2,1,0:T(8,128)(2,1)}, u32[]{:S(2)}) copy-start(bf16[1,2048,384]{2,1,0:T(8,128)(2,1)} %param.11) | copy-start | bytes 4718596
  103.5 37.4 %collective-permute-start.33 = (bf16[2,64,2048]{2,1,0:T(8,128)(2,1)}, bf16[2,64,2048]{2,1,0:T(8,128)(2,1)}, u32[]{:S(2)}, u32[]{:S(2)}) collective-permute-start(bf16[2,64,2048]{2,1,0:T(8,128)(2,1)} %get-tuple-element.47), channel_id=1, source_target_pairs={{0,1},{1,0},{2,3},{3,2},{4,5},{5,4},{6,7},{7,6},{8,9},{9,8},{10,11... | collective-permute-start | bytes 1572872 | tf_op jit(solution)/shard_map/ppermute | solution.py:199
  108.2 48.4 %collective-permute-start.34 = (bf16[2,64,2048]{2,1,0:T(8,128)(2,1)}, bf16[2,64,2048]{2,1,0:T(8,128)(2,1)S(1)}, u32[]{:S(2)}, u32[]{:S(2)}) collective-permute-start(bf16[2,64,2048]{2,1,0:T(8,128)(2,1)} %get-tuple-element.48), channel_id=1, source_target_pairs={{0,2},{1,3},{2,0},{3,1},{4,6},{5,7},{6,4},{7,5},{8,10},{9,11},{10,... | collective-permute-start | bytes 1572872 | tf_op jit(solution)/shard_map/ppermute | solution.py:199
  111.0 45.6 %collective-permute-start.36 = (bf16[1,64,2048]{2,1,0:T(8,128)(2,1)}, bf16[1,64,2048]{2,1,0:T(8,128)(2,1)S(1)}, u32[]{:S(2)}, u32[]{:S(2)}) collective-permute-start(bf16[1,64,2048]{2,1,0:T(8,128)(2,1)} %get-tuple-element.50), channel_id=1, source_target_pairs={{0,3},{1,2},{2,1},{3,0},{4,7},{5,6},{6,5},{7,4},{8,11},{9,10},{10,... | collective-permute-start | bytes 786440 | tf_op jit(solution)/shard_map/ppermute | solution.py:199
  114.1 15.5 %collective-permute-start.12 = (bf16[1,64,2048]{2,1,0:T(8,128)(2,1)}, bf16[1,64,2048]{2,1,0:T(8,128)(2,1)S(1)}, u32[]{:S(2)}, u32[]{:S(2)}) collective-permute-start(bf16[1,64,2048]{2,1,0:T(8,128)(2,1)} %get-tuple-element.38), channel_id=1, source_target_pairs={{0,3},{1,2},{2,1},{3,0},{4,7},{5,6},{6,5},{7,4},{8,11},{9,10},{10,... | collective-permute-start | bytes 786440 | tf_op jit(solution)/shard_map/ppermute | solution.py:199
  129.6 7.7 %collective-permute-start.13 = (bf16[1,64,2048]{2,1,0:T(8,128)(2,1)}, bf16[1,64,2048]{2,1,0:T(8,128)(2,1)S(1)}, u32[]{:S(2)}, u32[]{:S(2)}) collective-permute-start(bf16[1,64,2048]{2,1,0:T(8,128)(2,1)} %get-tuple-element.39), channel_id=1, source_target_pairs={{0,1},{1,0},{2,3},{3,2},{4,5},{5,4},{6,7},{7,6},{8,9},{9,8},{10,11... | collective-permute-start | bytes 786440 | tf_op jit(solution)/shard_map/ppermute | solution.py:199
  137.3 19.4 %collective-permute-start.37 = (bf16[1,64,2048]{2,1,0:T(8,128)(2,1)}, bf16[1,64,2048]{2,1,0:T(8,128)(2,1)S(1)}, u32[]{:S(2)}, u32[]{:S(2)}) collective-permute-start(bf16[1,64,2048]{2,1,0:T(8,128)(2,1)} %get-tuple-element.51), channel_id=1, source_target_pairs={{0,1},{1,0},{2,3},{3,2},{4,5},{5,4},{6,7},{7,6},{8,9},{9,8},{10,11... | collective-permute-start | bytes 786440 | tf_op jit(solution)/shard_map/ppermute | solution.py:199
  139.5 9.3 %collective-permute-start.14 = (bf16[1,64,2048]{2,1,0:T(8,128)(2,1)}, bf16[1,64,2048]{2,1,0:T(8,128)(2,1)S(1)}, u32[]{:S(2)}, u32[]{:S(2)}) collective-permute-start(bf16[1,64,2048]{2,1,0:T(8,128)(2,1)} %get-tuple-element.40), channel_id=1, source_target_pairs={{0,2},{1,3},{2,0},{3,1},{4,6},{5,7},{6,4},{7,5},{8,10},{9,11},{10,... | collective-permute-start | bytes 786440 | tf_op jit(solution)/shard_map/ppermute | solution.py:199
  140.9 15.8 %collective-permute-start.38 = (bf16[1,64,2048]{2,1,0:T(8,128)(2,1)S(1)}, bf16[1,64,2048]{2,1,0:T(8,128)(2,1)S(1)}, u32[]{:S(2)}, u32[]{:S(2)}) collective-permute-start(bf16[1,64,2048]{2,1,0:T(8,128)(2,1)S(1)} %copy-done.31), channel_id=1, source_target_pairs={{0,2},{1,3},{2,0},{3,1},{4,6},{5,7},{6,4},{7,5},{8,10},{9,11},{10,... | collective-permute-start | bytes 786440 | tf_op jit(solution)/shard_map/ppermute | solution.py:199
  165.5 9.2 %collective-permute-start.42 = (bf16[1,64,2048]{2,1,0:T(8,128)(2,1)S(1)}, bf16[1,64,2048]{2,1,0:T(8,128)(2,1)S(1)}, u32[]{:S(2)}, u32[]{:S(2)}) collective-permute-start(bf16[1,64,2048]{2,1,0:T(8,128)(2,1)S(1)} %get-tuple-element.59), channel_id=1, source_target_pairs={{0,1},{1,0},{2,3},{3,2},{4,5},{5,4},{6,7},{7,6},{8,9},{9,8},{10,11... | collective-permute-start | bytes 786440 | tf_op jit(solution)/shard_map/ppermute | solution.py:199
  166.1 10.2 %collective-permute-start.43 = (bf16[1,64,2048]{2,1,0:T(8,128)(2,1)S(1)}, bf16[1,64,2048]{2,1,0:T(8,128)(2,1)S(1)}, u32[]{:S(2)}, u32[]{:S(2)}) collective-permute-start(bf16[1,64,2048]{2,1,0:T(8,128)(2,1)S(1)} %get-tuple-element.58), channel_id=1, source_target_pairs={{0,2},{1,3},{2,0},{3,1},{4,6},{5,7},{6,4},{7,5},{8,10},{9,11},{10,... | collective-permute-start | bytes 786440 | tf_op jit(solution)/shard_map/ppermute | solution.py:199
  166.4 13.7 %collective-permute-start.44 = (bf16[1,64,2048]{2,1,0:T(8,128)(2,1)S(1)}, bf16[1,64,2048]{2,1,0:T(8,128)(2,1)S(1)}, u32[]{:S(2)}, u32[]{:S(2)}) collective-permute-start(bf16[1,64,2048]{2,1,0:T(8,128)(2,1)S(1)} %get-tuple-element.57), channel_id=1, source_target_pairs={{0,3},{1,2},{2,1},{3,0},{4,7},{5,6},{6,5},{7,4},{8,11},{9,10},{10,... | collective-permute-start | bytes 786440 | tf_op jit(solution)/shard_map/ppermute | solution.py:199
  169.0 17.0 %collective-permute-start.39 = (bf16[1,64,2048]{2,1,0:T(8,128)(2,1)S(1)}, bf16[1,64,2048]{2,1,0:T(8,128)(2,1)S(1)}, u32[]{:S(2)}, u32[]{:S(2)}) collective-permute-start(bf16[1,64,2048]{2,1,0:T(8,128)(2,1)S(1)} %get-tuple-element.63), channel_id=1, source_target_pairs={{0,1},{1,0},{2,3},{3,2},{4,5},{5,4},{6,7},{7,6},{8,9},{9,8},{10,11... | collective-permute-start | bytes 786440 | tf_op jit(solution)/shard_map/ppermute | solution.py:199
  169.5 16.8 %collective-permute-start.40 = (bf16[1,64,2048]{2,1,0:T(8,128)(2,1)S(1)}, bf16[1,64,2048]{2,1,0:T(8,128)(2,1)S(1)}, u32[]{:S(2)}, u32[]{:S(2)}) collective-permute-start(bf16[1,64,2048]{2,1,0:T(8,128)(2,1)S(1)} %get-tuple-element.62), channel_id=1, source_target_pairs={{0,2},{1,3},{2,0},{3,1},{4,6},{5,7},{6,4},{7,5},{8,10},{9,11},{10,... | collective-permute-start | bytes 786440 | tf_op jit(solution)/shard_map/ppermute | solution.py:199
  174.8 16.9 %collective-permute-start.18 = (bf16[1,64,2048]{2,1,0:T(8,128)(2,1)S(1)}, bf16[1,64,2048]{2,1,0:T(8,128)(2,1)S(1)}, u32[]{:S(2)}, u32[]{:S(2)}) collective-permute-start(bf16[1,64,2048]{2,1,0:T(8,128)(2,1)S(1)} %get-tuple-element.71), channel_id=1, source_target_pairs={{0,1},{1,0},{2,3},{3,2},{4,5},{5,4},{6,7},{7,6},{8,9},{9,8},{10,11... | collective-permute-start | bytes 786440 | tf_op jit(solution)/shard_map/ppermute | solution.py:199
  176.3 49.2 %copy-start.19 = (bf16[1,64,2048]{2,1,0:T(8,128)(2,1)}, bf16[1,64,2048]{2,1,0:T(8,128)(2,1)S(1)}, u32[]{:S(2)}) copy-start(bf16[1,64,2048]{2,1,0:T(8,128)(2,1)S(1)} %collective-permute-done.43.refs_2_) | copy-start | bytes 786436
  176.3 43.8 %collective-permute-start.46 = (bf16[2,64,2048]{2,1,0:T(8,128)(2,1)S(1)}, bf16[2,64,2048]{2,1,0:T(8,128)(2,1)S(1)}, u32[]{:S(2)}, u32[]{:S(2)}) collective-permute-start(bf16[2,64,2048]{2,1,0:T(8,128)(2,1)S(1)} %bitcast.158), channel_id=1, source_target_pairs={{0,1},{1,0},{2,3},{3,2},{4,5},{5,4},{6,7},{7,6},{8,9},{9,8},{10,11... | collective-permute-start | bytes 1572872 | tf_op jit(solution)/shard_map/ppermute | solution.py:199
  180.1 45.4 %copy-start.20 = (bf16[1,64,2048]{2,1,0:T(8,128)(2,1)}, bf16[1,64,2048]{2,1,0:T(8,128)(2,1)S(1)}, u32[]{:S(2)}) copy-start(bf16[1,64,2048]{2,1,0:T(8,128)(2,1)S(1)} %collective-permute-done.44.refs_3_) | copy-start | bytes 786436
  180.1 41.6 %collective-permute-start.47 = (bf16[2,64,2048]{2,1,0:T(8,128)(2,1)S(1)}, bf16[2,64,2048]{2,1,0:T(8,128)(2,1)S(1)}, u32[]{:S(2)}, u32[]{:S(2)}) collective-permute-start(bf16[2,64,2048]{2,1,0:T(8,128)(2,1)S(1)} %bitcast.157), channel_id=1, source_target_pairs={{0,2},{1,3},{2,0},{3,1},{4,6},{5,7},{6,4},{7,5},{8,10},{9,11},{10,... | collective-permute-start | bytes 1572872 | tf_op jit(solution)/shard_map/ppermute | solution.py:199
  186.0 39.5 %copy-start.24 = (bf16[1,64,2048]{2,1,0:T(8,128)(2,1)}, bf16[1,64,2048]{2,1,0:T(8,128)(2,1)S(1)}, u32[]{:S(2)}) copy-start(bf16[1,64,2048]{2,1,0:T(8,128)(2,1)S(1)} %collective-permute-done.39.refs_1_) | copy-start | bytes 786436
  186.0 37.0 %collective-permute-start.48 = (bf16[2,64,2048]{2,1,0:T(8,128)(2,1)S(1)}, bf16[2,64,2048]{2,1,0:T(8,128)(2,1)S(1)}, u32[]{:S(2)}, u32[]{:S(2)}) collective-permute-start(bf16[2,64,2048]{2,1,0:T(8,128)(2,1)S(1)} %bitcast.156), channel_id=1, source_target_pairs={{0,3},{1,2},{2,1},{3,0},{4,7},{5,6},{6,5},{7,4},{8,11},{9,10},{10,... | collective-permute-start | bytes 1572872 | tf_op jit(solution)/shard_map/ppermute | solution.py:199
  186.4 39.1 %copy-start.25 = (bf16[1,64,2048]{2,1,0:T(8,128)(2,1)}, bf16[1,64,2048]{2,1,0:T(8,128)(2,1)S(1)}, u32[]{:S(2)}) copy-start(bf16[1,64,2048]{2,1,0:T(8,128)(2,1)S(1)} %collective-permute-done.40.refs_2_) | copy-start | bytes 786436
  186.4 27.3 %collective-permute-start.19 = (bf16[1,64,2048]{2,1,0:T(8,128)(2,1)S(1)}, bf16[1,64,2048]{2,1,0:T(8,128)(2,1)S(1)}, u32[]{:S(2)}, u32[]{:S(2)}) collective-permute-start(bf16[1,64,2048]{2,1,0:T(8,128)(2,1)S(1)} %get-tuple-element.70), channel_id=1, source_target_pairs={{0,2},{1,3},{2,0},{3,1},{4,6},{5,7},{6,4},{7,5},{8,10},{9,11},{10,... | collective-permute-start | bytes 786440 | tf_op jit(solution)/shard_map/ppermute | solution.py:199
  191.6 33.9 %copy-start.21 = (bf16[1,64,2048]{2,1,0:T(8,128)(2,1)}, bf16[1,64,2048]{2,1,0:T(8,128)(2,1)S(1)}, u32[]{:S(2)}) copy-start(bf16[1,64,2048]{2,1,0:T(8,128)(2,1)S(1)} %collective-permute-done.18.refs_1_) | copy-start | bytes 786436
  191.6 27.9 %collective-permute-start.20 = (bf16[1,64,2048]{2,1,0:T(8,128)(2,1)S(1)}, bf16[1,64,2048]{2,1,0:T(8,128)(2,1)S(1)}, u32[]{:S(2)}, u32[]{:S(2)}) collective-permute-start(bf16[1,64,2048]{2,1,0:T(8,128)(2,1)S(1)} %get-tuple-element.69), channel_id=1, source_target_pairs={{0,3},{1,2},{2,1},{3,0},{4,7},{5,6},{6,5},{7,4},{8,11},{9,10},{10,... | collective-permute-start | bytes 786440 | tf_op jit(solution)/shard_map/ppermute | solution.py:199
  213.7 27.1 %collective-permute-start.41 = (bf16[1,64,2048]{2,1,0:T(8,128)(2,1)}, bf16[1,64,2048]{2,1,0:T(8,128)(2,1)}, u32[]{:S(2)}, u32[]{:S(2)}) collective-permute-start(bf16[1,64,2048]{2,1,0:T(8,128)(2,1)} %get-tuple-element.61), channel_id=1, source_target_pairs={{0,3},{1,2},{2,1},{3,0},{4,7},{5,6},{6,5},{7,4},{8,11},{9,10},{10,... | collective-permute-start | bytes 786440 | tf_op jit(solution)/shard_map/ppermute | solution.py:199
  219.5 33.4 %collective-permute-start.22 = (bf16[2,64,2048]{2,1,0:T(8,128)(2,1)}, bf16[2,64,2048]{2,1,0:T(8,128)(2,1)}, u32[]{:S(2)}, u32[]{:S(2)}) collective-permute-start(bf16[2,64,2048]{2,1,0:T(8,128)(2,1)} %bitcast.35), channel_id=1, source_target_pairs={{0,1},{1,0},{2,3},{3,2},{4,5},{5,4},{6,7},{7,6},{8,9},{9,8},{10,11... | collective-permute-start | bytes 1572872 | tf_op jit(solution)/shard_map/ppermute | solution.py:199
  220.1 33.1 %collective-permute-start.23 = (bf16[2,64,2048]{2,1,0:T(8,128)(2,1)}, bf16[2,64,2048]{2,1,0:T(8,128)(2,1)}, u32[]{:S(2)}, u32[]{:S(2)}) collective-permute-start(bf16[2,64,2048]{2,1,0:T(8,128)(2,1)} %bitcast.36), channel_id=1, source_target_pairs={{0,2},{1,3},{2,0},{3,1},{4,6},{5,7},{6,4},{7,5},{8,10},{9,11},{10,... | collective-permute-start | bytes 1572872 | tf_op jit(solution)/shard_map/ppermute | solution.py:199
  221.7 31.8 %collective-permute-start.24 = (bf16[2,64,2048]{2,1,0:T(8,128)(2,1)}, bf16[2,64,2048]{2,1,0:T(8,128)(2,1)}, u32[]{:S(2)}, u32[]{:S(2)}) collective-permute-start(bf16[2,64,2048]{2,1,0:T(8,128)(2,1)} %bitcast.37), channel_id=1, source_target_pairs={{0,3},{1,2},{2,1},{3,0},{4,7},{5,6},{6,5},{7,4},{8,11},{9,10},{10,... | collective-permute-start | bytes 1572872 | tf_op jit(solution)/shard_map/ppermute | solution.py:199
  223.0 24.1 %collective-permute-start.15 = (bf16[1,64,2048]{2,1,0:T(8,128)(2,1)}, bf16[1,64,2048]{2,1,0:T(8,128)(2,1)}, u32[]{:S(2)}, u32[]{:S(2)}) collective-permute-start(bf16[1,64,2048]{2,1,0:T(8,128)(2,1)} %get-tuple-element.75), channel_id=1, source_target_pairs={{0,1},{1,0},{2,3},{3,2},{4,5},{5,4},{6,7},{7,6},{8,9},{9,8},{10,11... | collective-permute-start | bytes 786440 | tf_op jit(solution)/shard_map/ppermute | solution.py:199
  240.8 12.1 %collective-permute-start.16 = (bf16[1,64,2048]{2,1,0:T(8,128)(2,1)S(1)}, bf16[1,64,2048]{2,1,0:T(8,128)(2,1)S(1)}, u32[]{:S(2)}, u32[]{:S(2)}) collective-permute-start(bf16[1,64,2048]{2,1,0:T(8,128)(2,1)S(1)} %copy-done.16), channel_id=1, source_target_pairs={{0,2},{1,3},{2,0},{3,1},{4,6},{5,7},{6,4},{7,5},{8,10},{9,11},{10,... | collective-permute-start | bytes 786440 | tf_op jit(solution)/shard_map/ppermute | solution.py:199
  247.1 26.0 %collective-permute-start.45 = (bf16[128,2048]{1,0:T(8,128)(2,1)}, bf16[128,2048]{1,0:T(8,128)(2,1)}, u32[]{:S(2)}, u32[]{:S(2)}) collective-permute-start(bf16[128,2048]{1,0:T(8,128)(2,1)} %bitcast.149), channel_id=1, source_target_pairs={{0,8},{1,9},{2,10},{3,11},{4,12},{5,13},{6,14},{7,15},{8,0},{9,1},... | collective-permute-start | bytes 1572872 | tf_op jit(solution)/shard_map/ppermute | solution.py:194
  252.8 82.0 %collective-permute-start.53 = (bf16[384,2048]{1,0:T(8,128)(2,1)S(1)}, bf16[384,2048]{1,0:T(8,128)(2,1)}, u32[]{:S(2)}, u32[]{:S(2)}) collective-permute-start(bf16[384,2048]{1,0:T(8,128)(2,1)S(1)} %convolution_convert_fusion.1), channel_id=1, source_target_pairs={{0,16},{16,0},{1,17},{17,1},{2,18},{18,2},{3,19},{19,3},{4,20},{20... | collective-permute-start | bytes 4718600 | tf_op jit(solution)/shard_map/ppermute | solution.py:87
  252.9 14.6 %collective-permute-start.17 = (bf16[1,64,2048]{2,1,0:T(8,128)(2,1)S(1)}, bf16[1,64,2048]{2,1,0:T(8,128)(2,1)S(1)}, u32[]{:S(2)}, u32[]{:S(2)}) collective-permute-start(bf16[1,64,2048]{2,1,0:T(8,128)(2,1)S(1)} %get-tuple-element.73), channel_id=1, source_target_pairs={{0,3},{1,2},{2,1},{3,0},{4,7},{5,6},{6,5},{7,4},{8,11},{9,10},{10,... | collective-permute-start | bytes 786440 | tf_op jit(solution)/shard_map/ppermute | solution.py:199
  253.2 40.8 %collective-permute-start.21 = (bf16[128,2048]{1,0:T(8,128)(2,1)S(1)}, bf16[128,2048]{1,0:T(8,128)(2,1)}, u32[]{:S(2)}, u32[]{:S(2)}) collective-permute-start(bf16[128,2048]{1,0:T(8,128)(2,1)S(1)} %bitcast.147), channel_id=1, source_target_pairs={{0,8},{1,9},{2,10},{3,11},{4,12},{5,13},{6,14},{7,15},{8,0},{9,1},... | collective-permute-start | bytes 1572872 | tf_op jit(solution)/shard_map/ppermute | solution.py:194
  253.6 58.9 %collective-permute-start.49 = (bf16[128,2048]{1,0:T(8,128)(2,1)}, bf16[128,2048]{1,0:T(8,128)(2,1)}, u32[]{:S(2)}, u32[]{:S(2)}) collective-permute-start(bf16[128,2048]{1,0:T(8,128)(2,1)} %get-tuple-element.81), channel_id=1, source_target_pairs={{0,4},{1,5},{2,6},{3,7},{4,8},{5,9},{6,10},{7,11},{8,12},{9,13},{1... | collective-permute-start | bytes 1572872 | tf_op jit(solution)/shard_map/ppermute | solution.py:194
  259.3 53.1 %copy-start.5 = (bf16[1024,384]{1,0:T(8,128)(2,1)S(1)}, bf16[1024,384]{1,0:T(8,128)(2,1)}, u32[]{:S(2)}) copy-start(bf16[1024,384]{1,0:T(8,128)(2,1)} %copy-done.4) | copy-start | bytes 2359300
  267.4 50.7 %copy-start.27 = (bf16[1,64,2048]{2,1,0:T(8,128)(2,1)}, bf16[1,64,2048]{2,1,0:T(8,128)(2,1)S(1)}, u32[]{:S(2)}) copy-start(bf16[1,64,2048]{2,1,0:T(8,128)(2,1)S(1)} %collective-permute-done.17.refs_3_) | copy-start | bytes 786436
  267.4 70.7 %collective-permute-start.52 = (bf16[2048,384]{1,0:T(8,128)(2,1)}, bf16[2048,384]{1,0:T(8,128)(2,1)}, u32[]{:S(2)}, u32[]{:S(2)}) collective-permute-start(bf16[2048,384]{1,0:T(8,128)(2,1)} %convolution_convert_fusion.2), channel_id=1, source_target_pairs={{0,16},{16,0},{1,17},{17,1},{2,18},{18,2},{3,19},{19,3},{4,20},{20... | collective-permute-start | bytes 4718600 | tf_op jit(solution)/shard_map/ppermute | solution.py:87
  273.1 45.1 %collective-permute-start.50 = (bf16[128,2048]{1,0:T(8,128)(2,1)}, bf16[128,2048]{1,0:T(8,128)(2,1)}, u32[]{:S(2)}, u32[]{:S(2)}) collective-permute-start(bf16[128,2048]{1,0:T(8,128)(2,1)} %get-tuple-element.80), channel_id=1, source_target_pairs={{0,12},{1,13},{2,14},{3,15},{4,0},{5,1},{6,2},{7,3},{8,4},{9,5},{1... | collective-permute-start | bytes 1572872 | tf_op jit(solution)/shard_map/ppermute | solution.py:194
  294.0 34.6 %collective-permute-start.25 = (bf16[128,2048]{1,0:T(8,128)(2,1)}, bf16[128,2048]{1,0:T(8,128)(2,1)S(1)}, u32[]{:S(2)}, u32[]{:S(2)}) collective-permute-start(bf16[128,2048]{1,0:T(8,128)(2,1)} %get-tuple-element.83), channel_id=1, source_target_pairs={{0,4},{1,5},{2,6},{3,7},{4,8},{5,9},{6,10},{7,11},{8,12},{9,13},{1... | collective-permute-start | bytes 1572872 | tf_op jit(solution)/shard_map/ppermute | solution.py:194
  312.4 17.2 %collective-permute-start.26 = (bf16[128,2048]{1,0:T(8,128)(2,1)}, bf16[128,2048]{1,0:T(8,128)(2,1)}, u32[]{:S(2)}, u32[]{:S(2)}) collective-permute-start(bf16[128,2048]{1,0:T(8,128)(2,1)} %get-tuple-element.82), channel_id=1, source_target_pairs={{0,12},{1,13},{2,14},{3,15},{4,0},{5,1},{6,2},{7,3},{8,4},{9,5},{1... | collective-permute-start | bytes 1572872 | tf_op jit(solution)/shard_map/ppermute | solution.py:194
  318.1 23.5 %collective-permute-start.51 = (bf16[2048,384]{1,0:T(8,128)(2,1)}, bf16[2048,384]{1,0:T(8,128)(2,1)}, u32[]{:S(2)}, u32[]{:S(2)}) collective-permute-start(bf16[2048,384]{1,0:T(8,128)(2,1)} %convolution_convert_fusion.3), channel_id=1, source_target_pairs={{0,16},{16,0},{1,17},{17,1},{2,18},{18,2},{3,19},{19,3},{4,20},{20... | collective-permute-start | bytes 4718600 | tf_op jit(solution)/shard_map/ppermute | solution.py:87
  (22 other events, 225.1 us)

commit v2 on v0

v2 whole, which is shorter than its diff:
```python
import functools

import jax
import jax.numpy as jnp
from jax import lax
from jax.experimental import pallas as pl
from jax.experimental.pallas import tpu as pltpu
from jax.sharding import PartitionSpec as P

PLANE = 4
LEVELS = 4
LAG = 1
BF = jnp.bfloat16
F32 = jnp.float32


def slot_index(block_routes, expert_count, capacity):
    flat = block_routes.reshape(-1)
    onehot = (flat[:, None] == jnp.arange(expert_count, dtype=jnp.int32)[None, :]).astype(jnp.int32)
    before = jnp.cumsum(onehot, axis=0) - onehot
    ranks = jnp.sum(before * onehot, axis=1)
    return flat * capacity + ranks


def expert_forward(block, gate_mat, up_mat, down_mat):
    inputs = block.reshape(-1, block.shape[2])
    gate_pre = jnp.dot(inputs, gate_mat, preferred_element_type=jnp.float32)
    up_pre = jnp.dot(inputs, up_mat, preferred_element_type=jnp.float32)
    sigma = jax.nn.sigmoid(gate_pre)
    hidden = (gate_pre * sigma * up_pre).astype(jnp.bfloat16)
    outputs = jnp.dot(hidden, down_mat, preferred_element_type=jnp.float32).astype(jnp.bfloat16)
    return (gate_pre, up_pre, hidden, outputs)


def direct_plan(tokens, routes, gates, cotangent, w_gate, w_up, w_down):
    rows_dev, width = tokens.shape
    picks = routes.shape[1]
    experts = lax.axis_size("expert")
    capacity = rows_dev * picks // experts
    gate_mat = w_gate[0]
    up_mat = w_up[0]
    down_mat = w_down[0]
    slots = slot_index(routes, experts, capacity)
    flat_rows = jnp.arange(rows_dev * picks, dtype=jnp.int32) // picks
    token_of = jnp.full((experts * capacity,), rows_dev, jnp.int32).at[slots].set(flat_rows)
    weight_of = jnp.zeros((experts * capacity,), jnp.float32).at[slots].set(gates.reshape(-1))
    token_pad = jnp.concatenate([tokens, jnp.zeros((1, width), tokens.dtype)], axis=0)
    send = token_pad[token_of].reshape(experts, capacity, width)

    def exchange(rows):
        return lax.all_to_all(
            rows.reshape(experts, capacity, width), "expert", split_axis=0, concat_axis=0, tiled=True
        )

    block = exchange(send)
    gate_pre, up_pre, hidden, outputs = expert_forward(block, gate_mat, up_mat, down_mat)
    back_items = exchange(outputs)
    inputs = block.reshape(-1, width)
    gathered = back_items.reshape(-1, width)[slots].reshape(rows_dev, picks, width)
    mixed = jnp.sum(gates[:, :, None] * gathered.astype(jnp.float32), axis=1).astype(jnp.bfloat16)
    cot_pad = jnp.concatenate([cotangent, jnp.zeros((1, width), cotangent.dtype)], axis=0)
    cot_send = (weight_of[:, None] * cot_pad[token_of].astype(jnp.float32)).astype(jnp.bfloat16)
    slot_cot = exchange(cot_send).reshape(-1, width)
    down_part = jnp.dot(hidden.T, slot_cot, preferred_element_type=jnp.float32)
    hidden_grad = jnp.dot(slot_cot, down_mat.T, preferred_element_type=jnp.float32)
    sigma = jax.nn.sigmoid(gate_pre)
    gate_grad = (hidden_grad * up_pre * sigma * (1.0 + gate_pre * (1.0 - sigma))).astype(
        jnp.bfloat16
    )
    up_grad = (hidden_grad * gate_pre * sigma).astype(jnp.bfloat16)
    slot_grads = (
        jnp.dot(gate_grad, gate_mat.T, preferred_element_type=jnp.float32)
        + jnp.dot(up_grad, up_mat.T, preferred_element_type=jnp.float32)
    ).astype(jnp.bfloat16)
    grads_back = exchange(slot_grads)
    gate_part = jnp.dot(inputs.T, gate_grad, preferred_element_type=jnp.float32)
    up_part = jnp.dot(inputs.T, up_grad, preferred_element_type=jnp.float32)
    grad_rows = grads_back.reshape(-1, width)[slots].reshape(rows_dev, picks, width)
    input_grad = jnp.sum(grad_rows.astype(jnp.float32), axis=1).astype(jnp.bfloat16)
    return (mixed, input_grad) + relay_sums(gate_part, up_part, down_part)


def relay_sums(*parts):
    relays = lax.axis_size("pipe")
    sums = []
    for part in parts:
        part = part.astype(BF)
        if relays == 2:
            other = lax.ppermute(part, "pipe", [(0, 1), (1, 0)])
            total = (part.astype(F32) + other.astype(F32)).astype(BF)
        else:
            total = lax.psum(part, "pipe")
        sums.append(total[None])
    return tuple(sums)


def chosen_rows(ids_ref, meta, picks, capacity):
    columns = meta.astype(F32).T
    routes, high, low = (columns[n * picks : (n + 1) * picks] for n in range(3))
    rows = meta.shape[0]
    member, weights = [], []
    for k in range(PLANE):
        hit = routes == ids_ref[k].astype(F32)
        member.append(jnp.sum(jnp.where(hit, 1.0, 0.0), axis=0, keepdims=True))
        weights.append(
            [jnp.sum(jnp.where(hit, part, 0.0), axis=0, keepdims=True) for part in (high, low)]
        )
    stacked = jnp.concatenate(member + [jnp.zeros((16 - PLANE, rows), F32)], axis=0)
    first = lax.broadcasted_iota(jnp.int32, (rows, rows), 0)
    second = lax.broadcasted_iota(jnp.int32, (rows, rows), 1)
    ahead = jnp.where(first < second, 1.0, 0.0).astype(BF)
    rank = jnp.dot(stacked.astype(BF), ahead, preferred_element_type=F32)
    slot = lax.broadcasted_iota(jnp.int32, (capacity, rows), 0).astype(F32)
    pick, pick_high, pick_low = [], [], []
    for k in range(PLANE):
        chosen = slot == jnp.where(member[k] > 0.5, rank[k : k + 1], -1.0)
        pick.append(jnp.where(chosen, 1.0, 0.0))
        pick_high.append(jnp.where(chosen, weights[k][0], 0.0))
        pick_low.append(jnp.where(chosen, weights[k][1], 0.0))
    return [jnp.concatenate(part, axis=0) for part in (pick, pick_high, pick_low)]


def put(out_refs, n, start, picked, capacity):
    for k, out_ref in enumerate(out_refs):
        out_ref[n, start : start + capacity] = picked[k * capacity : (k + 1) * capacity]


def picked_rows(matrices, block):
    return sum(jnp.dot(m, block, preferred_element_type=F32) for m in matrices).astype(BF)


def token_kernel(ids_ref, *refs, blocks, halves, cots, picks, capacity):
    meta_refs, refs = refs[: blocks * halves], refs[blocks * halves :]
    row_refs, refs = refs[: blocks * halves], refs[blocks * halves :]
    cot_refs, refs = refs[:cots], refs[cots:]
    table_ref, turned_ref, *out_refs = refs
    for n in range(blocks):
        meta = sum(ref[...] for ref in meta_refs[n * halves : (n + 1) * halves])
        tables = chosen_rows(ids_ref, meta, picks, capacity)
        for m, table in enumerate(tables):
            table_ref[n, m] = table.astype(BF)
            turned_ref[n, m] = table.T.astype(BF)
        block = sum(ref[...] for ref in row_refs[n * halves : (n + 1) * halves])
        put(out_refs, n, 0, picked_rows([table_ref[n, 0]], block), capacity)
        if cots:
            rows = picked_rows([table_ref[n, 1], table_ref[n, 2]], cot_refs[n][...])
            put(out_refs, n, capacity, rows, capacity)


def token_rows(ids, blocks, picks, capacity, width, cots=()):
    halves = len(blocks[0])
    arrays = [a for block in blocks for a in block]
    rows = arrays[0].shape[0]
    count, tall = len(blocks), capacity * (2 if cots else 1)
    spec = [pl.BlockSpec((rows, 128), lambda i: (0, width // 128))] * len(arrays)
    spec += [pl.BlockSpec((rows, width), lambda i: (0, 0))] * (len(arrays) + len(cots))
    shapes = [(count, 3, PLANE * capacity, rows), (count, 3, rows, PLANE * capacity)]
    shapes += [(count, tall, width)] * PLANE
    work = 2 * count * PLANE * capacity * rows * width * (3 if cots else 1)
    moved = 2 * width * (rows * (len(arrays) + len(cots)) + count * PLANE * tall)
    table, turned, *out = pl.pallas_call(
        functools.partial(
            token_kernel, blocks=count, halves=halves, cots=len(cots), picks=picks, capacity=capacity
        ),
        grid=(1,),
        in_specs=[pl.BlockSpec(memory_space=pltpu.SMEM)] + spec,
        out_specs=[pl.BlockSpec(s, lambda i, d=len(s): (0,) * d) for s in shapes],
        out_shape=[jax.ShapeDtypeStruct(s, BF) for s in shapes],
        compiler_params=pltpu.CompilerParams(vmem_limit_bytes=28 << 20),
        cost_estimate=pl.CostEstimate(flops=work, bytes_accessed=moved, transcendentals=0),
        name="token_rows",
    )(ids, *arrays, *arrays, *cots)
    return table, turned, out


def cot_kernel(table_ref, *refs, blocks, halves):
    row_refs, out_refs = refs[: blocks * halves], refs[blocks * halves :]
    capacity = out_refs[0].shape[1]
    for n in range(blocks):
        block = sum(ref[...] for ref in row_refs[n * halves : (n + 1) * halves])
        put(out_refs, n, 0, picked_rows([table_ref[n, 1], table_ref[n, 2]], block), capacity)


def cot_rows(table, blocks):
    halves = len(blocks[0])
    arrays = [a for block in blocks for a in block]
    rows, width = arrays[0].shape
    shape = (len(blocks), table.shape[2] // PLANE, width)
    work = 4 * len(blocks) * table.shape[2] * rows * width
    moved = 2 * width * (rows * len(arrays) + len(blocks) * table.shape[2])
    return pl.pallas_call(
        functools.partial(cot_kernel, blocks=len(blocks), halves=halves),
        out_shape=[jax.ShapeDtypeStruct(shape, BF)] * PLANE,
        compiler_params=pltpu.CompilerParams(vmem_limit_bytes=28 << 20),
        cost_estimate=pl.CostEstimate(flops=work, bytes_accessed=moved, transcendentals=0),
        name="cot_rows",
    )(table, *arrays)


def expand_kernel(turned_ref, *refs, blocks, extras, parts):
    row_refs, extra_refs, out_refs = refs[:PLANE], refs[PLANE:-blocks], refs[-blocks:]
    for n in range(blocks):
        rows = jnp.concatenate([ref[n] for ref in row_refs], axis=0)
        total = sum(jnp.dot(turned_ref[n, m], rows, preferred_element_type=F32) for m in parts)
        for ref in extra_refs[n * extras : (n + 1) * extras]:
            total += ref[...].astype(F32)
        out_refs[n][...] = total.astype(BF)


def expand(turned, rows, weighted, extras):
    blocks, _, width = rows[0].shape
    rows_dev, slots = turned.shape[2:]
    flat = [e for extra in extras for e in extra]
    work = 2 * blocks * rows_dev * slots * width * (2 if weighted else 1)
    moved = 2 * width * (blocks * (slots + rows_dev) + len(flat) * rows_dev)
    return pl.pallas_call(
        functools.partial(
            expand_kernel,
            blocks=blocks,
            extras=len(extras[0]),
            parts=(1, 2) if weighted else (0,),
        ),
        out_shape=[jax.ShapeDtypeStruct((rows_dev, width), BF)] * blocks,
        compiler_params=pltpu.CompilerParams(vmem_limit_bytes=28 << 20),
        cost_estimate=pl.CostEstimate(flops=work, bytes_accessed=moved, transcendentals=0),
        name="expand",
    )(turned, *rows, *flat)


def nt_dot(a, b):
    return lax.dot_general(a, b, (((1,), (1,)), ((), ())), preferred_element_type=F32)


def forward_kernel(*refs, first):
    row_refs, (gate_ref, up_ref, down_ref), refs = refs[:PLANE], refs[PLANE : PLANE + 3], refs[PLANE + 3 :]
    gate_out, up_out, hidden_out, rows_out, *out_refs = refs
    count, capacity, width = out_refs[0].shape
    inputs = jnp.concatenate(
        [ref[n, :capacity] for ref in row_refs for n in range(count)], axis=0
    )
    rows_out[...] = inputs
    gate_pre = jnp.dot(inputs, gate_ref[...], preferred_element_type=F32)
    up_pre = jnp.dot(inputs, up_ref[...], preferred_element_type=F32)
    gate_out[...] = gate_pre
    up_out[...] = up_pre
    hidden = (gate_pre * jax.nn.sigmoid(gate_pre) * up_pre).astype(BF)
    hidden_out[...] = hidden
    outputs = jnp.dot(hidden, down_ref[...], preferred_element_type=F32).astype(BF)
    for k, out_ref in enumerate(out_refs):
        for n in range(count):
            at = (k * count + n) * capacity
            out_ref[n] = outputs[at : at + capacity]


def forward(rows, capacity, gate_mat, up_mat, down_mat):
    count, _, width = rows[0].shape
    inner = gate_mat.shape[1]
    total = PLANE * count * capacity
    return pl.pallas_call(
        functools.partial(forward_kernel, first=capacity),
        out_shape=[
            jax.ShapeDtypeStruct((total, inner), F32),
            jax.ShapeDtypeStruct((total, inner), F32),
            jax.ShapeDtypeStruct((total, inner), BF),
            jax.ShapeDtypeStruct((total, width), BF),
        ]
        + [jax.ShapeDtypeStruct((count, capacity, width), BF)] * PLANE,
        compiler_params=pltpu.CompilerParams(vmem_limit_bytes=36 << 20),
        cost_estimate=pl.CostEstimate(
            flops=6 * total * width * inner,
            bytes_accessed=6 * width * inner + 6 * total * width + 10 * total * inner,
            transcendentals=total * inner,
        ),
        name="expert_forward",
    )(*rows, gate_mat, up_mat, down_mat)


def backward_kernel(*refs, skip):
    cot_refs, refs = refs[:PLANE], refs[PLANE:]
    gate_pre_ref, up_pre_ref, gate_ref, up_ref, down_ref, *refs = refs
    gate_out, up_out, rows_out, *out_refs = refs
    count, capacity, width = out_refs[0].shape
    cots = jnp.concatenate(
        [ref[n, skip : skip + capacity] for ref in cot_refs for n in range(count)], axis=0
    )
    rows_out[...] = cots
    hidden_grad = nt_dot(cots, down_ref[...])
    gate_pre, up_pre = gate_pre_ref[...], up_pre_ref[...]
    sigma = jax.nn.sigmoid(gate_pre)
    gate_grad = (hidden_grad * up_pre * sigma * (1.0 + gate_pre * (1.0 - sigma))).astype(BF)
    up_grad = (hidden_grad * gate_pre * sigma).astype(BF)
    gate_out[...] = gate_grad
    up_out[...] = up_grad
    grads = (nt_dot(gate_grad, gate_ref[...]) + nt_dot(up_grad, up_ref[...])).astype(BF)
    for k, out_ref in enumerate(out_refs):
        for n in range(count):
            at = (k * count + n) * capacity
            out_ref[n] = grads[at : at + capacity]


def backward(cots, skip, capacity, gate_pre, up_pre, gate_mat, up_mat, down_mat):
    count, _, width = cots[0].shape
    total, inner = gate_pre.shape
    return pl.pallas_call(
        functools.partial(backward_kernel, skip=skip),
        out_shape=[
            jax.ShapeDtypeStruct((total, inner), BF),
            jax.ShapeDtypeStruct((total, inner), BF),
            jax.ShapeDtypeStruct((total, width), BF),
        ]
        + [jax.ShapeDtypeStruct((count, capacity, width), BF)] * PLANE,
        compiler_params=pltpu.CompilerParams(vmem_limit_bytes=36 << 20),
        cost_estimate=pl.CostEstimate(
            flops=6 * total * width * inner,
            bytes_accessed=6 * width * inner + 6 * total * width + 12 * total * inner,
            transcendentals=total * inner,
        ),
        name="expert_backward",
    )(*cots, gate_pre, up_pre, gate_mat, up_mat, down_mat)


def plane_plan(tokens, routes, gates, cotangent, w_gate, w_up, w_down):
    rows_dev, width = tokens.shape
    picks = routes.shape[1]
    experts = lax.axis_size("expert")
    capacity = rows_dev * picks // experts
    mats = (w_gate[0], w_up[0], w_down[0])
    here = lax.axis_index("expert")
    level, place = here // PLANE, here % PLANE
    ids = level * PLANE + (place ^ jnp.arange(PLANE, dtype=jnp.int32))

    def shift(value, levels, step):
        pairs = [
            (level * PLANE + p, (level + step) % LEVELS * PLANE + p)
            for level in levels
            for p in range(PLANE)
        ]
        return lax.ppermute(value, "expert", pairs)

    stages = []

    def across(rows):
        sent = tuple(rows[1:])
        if len(stages) >= LAG:
            sent, _ = lax.optimization_barrier((sent, stages[-LAG]))
        moved = {
            k: lax.ppermute(sent[k - 1], "expert", [(i, i ^ k) for i in range(experts)])
            for k in (3, 1, 2)
        }
        stages.append(tuple(moved[k] for k in range(1, PLANE)))
        return [rows[0], *stages[-1]]

    every = range(LEVELS)
    high = lax.reduce_precision(gates, 8, 7)
    low = lax.reduce_precision(gates - high, 8, 7)
    meta = jnp.concatenate([routes.astype(F32), high, low], axis=1).astype(BF)
    meta = jnp.pad(meta, ((0, 0), (0, 128 - meta.shape[1])))
    block = jnp.concatenate([tokens, meta], axis=1)

    def pick(blocks, cots=()):
        return token_rows(ids, blocks, picks, capacity, width, cots)

    above, below = shift(block, every, -1), shift(block, every, 1)
    table_a, turned_a, rows_a = pick([[block]], [cotangent])
    rows_a = across(rows_a)
    far = [shift(above, (1, 2), -1), shift(below, (1, 2), 1)]
    table_b, turned_b, rows_b = pick([[above], [below]])
    rows_b = across(rows_b)
    later, far = lax.optimization_barrier((cotangent, far))
    cot_above, cot_below = shift(later, every, -1), shift(later, every, 1)
    table_c, turned_c, rows_c = pick([far])
    rows_c = across(rows_c)
    cot_far = [shift(cot_above, (1, 2), -1), shift(cot_below, (1, 2), 1)]
    cots_b = across(cot_rows(table_b, [[cot_above], [cot_below]]))
    cots_c = across(cot_rows(table_c, [cot_far]))

    saved, outs = [], []
    for rows in (rows_a, rows_b, rows_c):
        gate_pre, up_pre, hidden, inputs, *out = forward(rows, capacity, *mats)
        saved.append((gate_pre, up_pre, hidden, inputs))
        outs.append(out)
    grads, grad_outs = [], []
    for cots, skip, (gate_pre, up_pre, _, _) in zip(
        (rows_a, cots_b, cots_c), (capacity, 0, 0), saved
    ):
        gate_grad, up_grad, flat, *out = backward(cots, skip, capacity, gate_pre, up_pre, *mats)
        grads.append((gate_grad, up_grad, flat))
        grad_outs.append(out)

    flows = ((outs, True), (grad_outs, False))
    relayed = []
    for rows, weighted in flows:
        (part,) = expand(turned_c, across(rows[2]), weighted, [[]])
        relayed.append((shift(part, (0, 1), 1), shift(part, (3, 2), -1)))
    arrived = []
    for (rows, weighted), (up, down) in zip(flows, relayed):
        near = expand(turned_b, across(rows[1]), weighted, [[up], [down]])
        arrived.append([shift(near[0], every, 1), shift(near[1], every, -1)])
    mixed, input_grad = (
        expand(turned_a, across(rows[0]), weighted, [extra])[0]
        for (rows, weighted), extra in zip(flows, arrived)
    )
    hidden, inputs = (jnp.concatenate([s[n] for s in saved]) for n in (2, 3))
    gate_grad, up_grad, slot_cot = (jnp.concatenate([g[n] for g in grads]) for n in range(3))
    down_part = jnp.dot(hidden.T, slot_cot, preferred_element_type=F32)
    gate_part = jnp.dot(inputs.T, gate_grad, preferred_element_type=F32)
    up_part = jnp.dot(inputs.T, up_grad, preferred_element_type=F32)
    return (mixed, input_grad) + relay_sums(gate_part, up_part, down_part)


def on_device(tokens, routes, *rest):
    experts, picks = lax.axis_size("expert"), routes.shape[1]
    if experts == LEVELS * PLANE and experts <= 2 * picks:
        return plane_plan(tokens, routes, *rest)
    return direct_plan(tokens, routes, *rest)


def solution(mesh):
    rows, stack = P(("pipe", "expert"), None), P("expert", None, None)
    return jax.shard_map(
        on_device,
        mesh=mesh,
        in_specs=(rows, rows, rows, rows, stack, stack, stack),
        out_specs=(rows, rows, stack, stack, stack),
        check_vma=False,
    )
```

time: 468 us -> 240 us (0.51)
  waiting for transfers between devices: 309 us -> 107 us
  starting transfers between devices: 22.8 us -> 84.5 us
  local copies, waits for them, and re-layouts: 52.1 us -> 3.99 us
  matrix products: 48.1 us -> 6.61 us
  Pallas kernels: 0 us -> 25.7 us
  other arithmetic: 21.6 us -> 7.35 us
  between operations: 14.2 us -> 1.03 us
    all_to_all x4 -> x0, waiting for transfers between devices: 309 us -> none  [the longest x1 84.6 us: on_device(): lax.all_to_all(outputs.reshape(experts, items, width), 'expert', split_ax...]
    ppermute x0 -> x52, waiting for transfers between devices: none -> 107 us  [the longest x33 67.6 us: across(): lax.ppermute(sent[k - 1], 'expert', [(i, i ^ k) for i in range(experts)])]
    ppermute x0 -> x52, starting transfers between devices: none -> 84.5 us  [the longest x33 52.6 us: across(): lax.ppermute(sent[k - 1], 'expert', [(i, i ^ k) for i in range(experts)])]
    dot_general x9 -> x3, matrix products: 48.1 us -> 6.61 us  [the longest x1 2.39 us: plane_plan(): gate_part = jnp.dot(inputs.T, gate_grad, preferred_element_type=F32)]
    gather x4 -> x0, local copies, waits for them, and re-layouts: 35.4 us -> none  [the longest x1 11.8 us: on_device(): back_items.reshape(-1, width)[slots].reshape(rows_dev, picks, width)]
    pallas_call x0 -> x17, Pallas kernels: none -> 25.7 us  [the longest x3 7.81 us: backward(): pl.pallas_call(functools.partial(backward_kernel, skip=skip), out_shape=[...]
    all_to_all x4 -> x0, starting transfers between devices: 22.7 us -> none  [the longest x1 7.27 us: on_device(): lax.all_to_all(send, 'expert', split_axis=0, concat_axis=0, tiled=True)]
    reduce_sum x3 -> x0, other arithmetic: 11.2 us -> none  [the longest x1 6.03 us: on_device(): jnp.sum(grad_rows.astype(jnp.float32), axis=1).astype(jnp.bfloat16)]
  transfers between devices with their start and end apart: 5 -> 52, of which waited for: 4 -> 26; matrix products, arithmetic and copies ran while one was open for 19% -> 6% of each run, Pallas kernels for 0% -> 10%
where the time goes in v2:
time: 240 us; the launch traced here: 236 us
  waiting for transfers between devices  107 us (45%)
  starting transfers between devices  84.5 us (35%)
  Pallas kernels  25.7 us (11%)
  other arithmetic  7.35 us (3%)
  matrix products  6.61 us (3%)
  local copies, waits for them, and re-layouts  3.99 us (2%)
    ppermute x33, waiting for transfers between devices, across(): lax.ppermute(sent[k - 1], 'expert', [(i, i ^ k) for i in range(experts)])  67.6 us
    ppermute x33, starting transfers between devices, across(): lax.ppermute(sent[k - 1], 'expert', [(i, i ^ k) for i in range(experts)])  52.6 us
    ppermute x16, waiting for transfers between devices, shift(): return lax.ppermute(value, 'expert', pairs)  39 us
    ppermute x16, starting transfers between devices, shift(): return lax.ppermute(value, 'expert', pairs)  31.6 us
    pallas_call x3, Pallas kernels, backward(): pl.pallas_call(functools.partial(backward_kernel, skip=skip), out_shape=[...  7.81 us
    pallas_call x3, Pallas kernels, forward(): pl.pallas_call(functools.partial(forward_kernel, first=capacity), out_sha...  7.2 us
    broadcast_in_dim x3, other arithmetic, relay_sums(): sums.append(total[None])  4.87 us
  transfers between devices with their start and end apart: 52, of which 26 were waited for; matrix products, arithmetic and copies ran while one was open for 6% of the time, Pallas kernels for 10%

profile of v2, /device:TPU:14, one launch (start us, length us, event | category | flops | bytes accessed | tf_op | source)
XLA Modules:
  0.0 235.8 jit_solution(11552291876023460692)
XLA Ops:
  3.7 1.6 collective-permute-start.4
  6.4 1.7 token_rows.3
  9.2 2.4 %collective-permute-start.2 = (bf16[1,128,2048]{2,1,0:T(8,128)(2,1)S(1)}, bf16[1,128,2048]{2,1,0:T(8,128)(2,1)S(1)}, u32[]{:S(2)}, u32[]{:S(2)}) collective-permute-start(bf16[1,128,2048]{2,1,0:T(8,128)(2,1)S(1)} %get-tuple-element.116), channel_id=1, source_target_pairs={{0,3},{1,2},{2,1},{3,0},{4,7},{5,6},{6,5},{7,4},{8,11},{9,10},{10,... | collective-permute-start | bytes 1572872 | tf_op jit(solution)/shard_map/ppermute | solution.py:347
  11.6 6.2 %collective-permute-done.3.refs_0_.refs_2_ = bf16[128,2176]{1,0:T(8,128)(2,1)S(1)} collective-permute-done((bf16[128,2176]{1,0:T(8,128)(2,1)S(1)}, bf16[128,2176]{1,0:T(8,128)(2,1)S(1)}, u32[]{:S(2)}, u32[]{:S(2)}) %collective-permute-start.3) | collective-permute-done | bytes 557088 | tf_op jit(solution)/shard_map/ppermute | solution.py:338
  17.8 4.5 %collective-permute-start.5 = (bf16[128,2176]{1,0:T(8,128)(2,1)S(1)}, bf16[128,2176]{1,0:T(8,128)(2,1)S(1)}, u32[]{:S(2)}, u32[]{:S(2)}) collective-permute-start(bf16[128,2176]{1,0:T(8,128)(2,1)S(1)} %collective-permute-done.3.refs_0_.refs_2_), channel_id=1, source_target_pairs={{4,0},{5,1},{6,2},{7,3},{8,4},{9,5},{10,6},{11,7},{20,16},{21,17},... | collective-permute-start | bytes 1671176 | tf_op jit(solution)/shard_map/ppermute | solution.py:338
  22.3 9.4 %collective-permute-done.4.refs_1_.refs_3_ = bf16[128,2176]{1,0:T(8,128)(2,1)S(1)} collective-permute-done((bf16[128,2176]{1,0:T(8,128)(2,1)S(1)}, bf16[128,2176]{1,0:T(8,128)(2,1)S(1)}, u32[]{:S(2)}, u32[]{:S(2)}) %collective-permute-start.4) | collective-permute-done | bytes 557088 | tf_op jit(solution)/shard_map/ppermute | solution.py:338
  31.7 1.6 collective-permute-start.6
  33.3 1.6 token_rows.4
  36.0 2.5 %collective-permute-start.11 = (bf16[2,64,2048]{2,1,0:T(8,128)(2,1)S(1)}, bf16[2,64,2048]{2,1,0:T(8,128)(2,1)S(1)}, u32[]{:S(2)}, u32[]{:S(2)}) collective-permute-start(bf16[2,64,2048]{2,1,0:T(8,128)(2,1)S(1)} %get-tuple-element.137), channel_id=1, source_target_pairs={{0,3},{1,2},{2,1},{3,0},{4,7},{5,6},{6,5},{7,4},{8,11},{9,10},{10,... | collective-permute-start | bytes 1572872 | tf_op jit(solution)/shard_map/ppermute | solution.py:347
  38.5 4.1 %collective-permute-done.5.refs_0_.refs_2_ = bf16[128,2176]{1,0:T(8,128)(2,1)S(1)} collective-permute-done((bf16[128,2176]{1,0:T(8,128)(2,1)S(1)}, bf16[128,2176]{1,0:T(8,128)(2,1)S(1)}, u32[]{:S(2)}, u32[]{:S(2)}) %collective-permute-start.5) | collective-permute-done | bytes 557088 | tf_op jit(solution)/shard_map/ppermute | solution.py:338
  42.5 1.7 collective-permute-done.6.refs_1_.refs_3_
  44.3 2.5 %collective-permute-start.8 = (bf16[128,2048]{1,0:T(8,128)(2,1)S(1)}, bf16[128,2048]{1,0:T(8,128)(2,1)S(1)}, u32[]{:S(2)}, u32[]{:S(2)}) collective-permute-start(bf16[128,2048]{1,0:T(8,128)(2,1)S(1)} %copy-done.4), channel_id=1, source_target_pairs={{0,4},{1,5},{2,6},{3,7},{4,8},{5,9},{6,10},{7,11},{8,12},{9,13},{1... | collective-permute-start | bytes 1572872 | tf_op jit(solution)/shard_map/ppermute | solution.py:338
  47.9 1.9 collective-permute-done.9.refs_1_
  49.9 9.2 %collective-permute-done.10.refs_2_ = bf16[2,64,2048]{2,1,0:T(8,128)(2,1)S(1)} collective-permute-done((bf16[2,64,2048]{2,1,0:T(8,128)(2,1)S(1)}, bf16[2,64,2048]{2,1,0:T(8,128)(2,1)S(1)}, u32[]{:S(2)}, u32[]{:S(2)}) %collective-permute-start.10) | collective-permute-done | bytes 524320 | tf_op jit(solution)/shard_map/ppermute | solution.py:347
  59.0 1.5 collective-permute-start.12
  61.0 1.5 collective-permute-start.14
  62.5 2.3 collective-permute-start.18
  64.8 4.9 %collective-permute-done.8.refs_1_ = bf16[128,2048]{1,0:T(8,128)(2,1)S(1)} collective-permute-done((bf16[128,2048]{1,0:T(8,128)(2,1)S(1)}, bf16[128,2048]{1,0:T(8,128)(2,1)S(1)}, u32[]{:S(2)}, u32[]{:S(2)}) %collective-permute-start.8) | collective-permute-done | bytes 524320 | tf_op jit(solution)/shard_map/ppermute | solution.py:338
  69.7 2.3 collective-permute-start.19
  74.4 2.4 %collective-permute-start.17 = (bf16[2,64,2048]{2,1,0:T(8,128)(2,1)S(1)}, bf16[2,64,2048]{2,1,0:T(8,128)(2,1)S(1)}, u32[]{:S(2)}, u32[]{:S(2)}) collective-permute-start(bf16[2,64,2048]{2,1,0:T(8,128)(2,1)S(1)} %get-tuple-element.143), channel_id=1, source_target_pairs={{0,3},{1,2},{2,1},{3,0},{4,7},{5,6},{6,5},{7,4},{8,11},{9,10},{10,... | collective-permute-start | bytes 1572872 | tf_op jit(solution)/shard_map/ppermute | solution.py:347
  76.8 1.9 expert_forward.3
  78.7 2.0 expert_backward.5
  82.6 5.6 %collective-permute-done.15.refs_1_ = bf16[2,64,2048]{2,1,0:T(8,128)(2,1)S(1)} collective-permute-done((bf16[2,64,2048]{2,1,0:T(8,128)(2,1)S(1)}, bf16[2,64,2048]{2,1,0:T(8,128)(2,1)S(1)}, u32[]{:S(2)}, u32[]{:S(2)}) %collective-permute-start.15) | collective-permute-done | bytes 524320 | tf_op jit(solution)/shard_map/ppermute | solution.py:347
  88.2 8.9 %collective-permute-done.16.refs_2_ = bf16[2,64,2048]{2,1,0:T(8,128)(2,1)S(1)} collective-permute-done((bf16[2,64,2048]{2,1,0:T(8,128)(2,1)S(1)}, bf16[2,64,2048]{2,1,0:T(8,128)(2,1)S(1)}, u32[]{:S(2)}, u32[]{:S(2)}) %collective-permute-start.16) | collective-permute-done | bytes 524320 | tf_op jit(solution)/shard_map/ppermute | solution.py:347
  100.6 3.4 %expert_forward.4 = (f32[512,384]{1,0:T(8,128)S(1)}, f32[512,384]{1,0:T(8,128)S(1)}, bf16[512,384]{1,0:T(8,128)(2,1)S(1)}, bf16[512,2048]{1,0:T(8,128)(2,1)S(1)}...) custom-call(bf16[2,64,2048]{2,1,0:T(8,128)(2,1)S(1)} %get-tuple-elem, ...), custom_call_target="tpu_custom_call" | custom-call | flops 2415919104 | bytes 12976128 | tf_op jit(solution)/shard_map/expert_forward/pallas_call | solution.py:259
  104.1 1.9 expert_forward.5
  106.0 2.9 %collective-permute-done.21.refs_2_ = bf16[1,64,2048]{2,1,0:T(8,128)(2,1)S(1)} collective-permute-done((bf16[1,64,2048]{2,1,0:T(8,128)(2,1)S(1)}, bf16[1,64,2048]{2,1,0:T(8,128)(2,1)S(1)}, u32[]{:S(2)}, u32[]{:S(2)}) %collective-permute-start.21) | collective-permute-done | bytes 262176 | tf_op jit(solution)/shard_map/ppermute | solution.py:347
  108.9 1.6 collective-permute-done.22.refs_3_
  110.5 1.9 collective-permute-start.24
  112.4 1.5 collective-permute-start.25
  114.0 1.6 constant_dynamic-update-slice_fusion.1
  115.6 2.0 expert_backward.4
  117.5 1.6 collective-permute-done.24.refs_2_
  119.1 3.5 %collective-permute-done.25.refs_3_ = bf16[1,64,2048]{2,1,0:T(8,128)(2,1)S(1)} collective-permute-done((bf16[1,64,2048]{2,1,0:T(8,128)(2,1)S(1)}, bf16[1,64,2048]{2,1,0:T(8,128)(2,1)S(1)}, u32[]{:S(2)}, u32[]{:S(2)}) %collective-permute-start.25) | collective-permute-done | bytes 262176 | tf_op jit(solution)/shard_map/ppermute | solution.py:347
  123.3 2.8 %collective-permute-start.28 = (bf16[1,64,2048]{2,1,0:T(8,128)(2,1)S(1)}, bf16[1,64,2048]{2,1,0:T(8,128)(2,1)S(1)}, u32[]{:S(2)}, u32[]{:S(2)}) collective-permute-start(bf16[1,64,2048]{2,1,0:T(8,128)(2,1)S(1)} %get-tuple-element.175), channel_id=1, source_target_pairs={{0,3},{1,2},{2,1},{3,0},{4,7},{5,6},{6,5},{7,4},{8,11},{9,10},{10,... | collective-permute-start | bytes 786440 | tf_op jit(solution)/shard_map/ppermute | solution.py:347
  126.2 3.9 %expert_backward.3 = (bf16[512,384]{1,0:T(8,128)(2,1)S(1)}, bf16[512,384]{1,0:T(8,128)(2,1)S(1)}, bf16[512,2048]{1,0:T(8,128)(2,1)S(1)}, bf16[2,64,2048]{2,1,0:T...) custom-call(bf16[2,64,2048]{2,1,0:T(8,128)(2,1)S(1)} %get-tuple-elem, ...), custom_call_target="tpu_custom_call" | custom-call | flops 2415919104 | bytes 13369344 | tf_op jit(solution)/shard_map/expert_backward/pallas_call | solution.py:304
  131.2 2.6 %collective-permute-done.28.refs_3_ = bf16[1,64,2048]{2,1,0:T(8,128)(2,1)S(1)} collective-permute-done((bf16[1,64,2048]{2,1,0:T(8,128)(2,1)S(1)}, bf16[1,64,2048]{2,1,0:T(8,128)(2,1)S(1)}, u32[]{:S(2)}, u32[]{:S(2)}) %collective-permute-start.28) | collective-permute-done | bytes 262176 | tf_op jit(solution)/shard_map/ppermute | solution.py:347
  134.9 1.6 collective-permute-start.30
  137.3 2.4 %convolution_convert_fusion.1 = bf16[2048,384]{1,0:T(8,128)(2,1)S(1)} fusion(bf16[1024,2048]{1,0:T(8,128)(2,1)S(1)} %constant_dynamic-update-slice_fusion, bf16[256,384]{1,0:T(8,128)(2,1)S(1)} %get-tuple-element.209, bf16[512,384]{1,0:T(8,128)(2,1)S(1)} %get-tuple-element.208, bf16[256,384]{1,0:T(8,128)(2,1)S(1)} %get-tuple-element.207), kind=kOutput, calls=%fused_computation.11 | convolution fusion | flops 1613758464 | bytes 6553600 | tf_op jit(solution)/shard_map/dot_general | solution.py:406
  140.2 4.3 %collective-permute-start.38 = (bf16[128,2048]{1,0:T(8,128)(2,1)S(1)}, bf16[128,2048]{1,0:T(8,128)(2,1)S(1)}, u32[]{:S(2)}, u32[]{:S(2)}) collective-permute-start(bf16[128,2048]{1,0:T(8,128)(2,1)S(1)} %expand.6), channel_id=1, source_target_pairs={{0,4},{1,5},{2,6},{3,7},{4,8},{5,9},{6,10},{7,11},{16,20},{17,21},... | collective-permute-start | bytes 1572872 | tf_op jit(solution)/shard_map/ppermute | solution.py:338
  144.5 4.2 %collective-permute-done.29.refs_1_ = bf16[2,64,2048]{2,1,0:T(8,128)(2,1)S(1)} collective-permute-done((bf16[2,64,2048]{2,1,0:T(8,128)(2,1)S(1)}, bf16[2,64,2048]{2,1,0:T(8,128)(2,1)S(1)}, u32[]{:S(2)}, u32[]{:S(2)}) %collective-permute-start.29) | collective-permute-done | bytes 524320 | tf_op jit(solution)/shard_map/ppermute | solution.py:347
  149.9 3.7 %collective-permute-done.30.refs_2_ = bf16[2,64,2048]{2,1,0:T(8,128)(2,1)S(1)} collective-permute-done((bf16[2,64,2048]{2,1,0:T(8,128)(2,1)S(1)}, bf16[2,64,2048]{2,1,0:T(8,128)(2,1)S(1)}, u32[]{:S(2)}, u32[]{:S(2)}) %collective-permute-start.30) | collective-permute-done | bytes 524320 | tf_op jit(solution)/shard_map/ppermute | solution.py:347
  153.6 2.8 %collective-permute-done.31.refs_3_ = bf16[2,64,2048]{2,1,0:T(8,128)(2,1)S(1)} collective-permute-done((bf16[2,64,2048]{2,1,0:T(8,128)(2,1)S(1)}, bf16[2,64,2048]{2,1,0:T(8,128)(2,1)S(1)}, u32[]{:S(2)}, u32[]{:S(2)}) %collective-permute-start.31) | collective-permute-done | bytes 524320 | tf_op jit(solution)/shard_map/ppermute | solution.py:347
  156.4 1.9 collective-permute-start.32
  158.3 2.0 collective-permute-start.33
  160.4 2.4 %convolution_convert_fusion = bf16[2048,384]{1,0:T(8,128)(2,1)S(1)} fusion(bf16[1024,2048]{1,0:T(8,128)(2,1)S(1)} %constant_dynamic-update-slice_fusion, bf16[256,384]{1,0:T(8,128)(2,1)S(1)} %get-tuple-element.212, bf16[512,384]{1,0:T(8,128)(2,1)S(1)} %get-tuple-element.211, bf16[256,384]{1,0:T(8,128)(2,1)S(1)} %get-tuple-element.210), kind=kOutput, calls=%fused_computation.10 | convolution fusion | flops 1613758464 | bytes 6553600 | tf_op jit(solution)/shard_map/dot_general | solution.py:407
  165.6 4.5 %collective-permute-start.45 = (bf16[128,2048]{1,0:T(8,128)(2,1)S(1)}, bf16[128,2048]{1,0:T(8,128)(2,1)S(1)}, u32[]{:S(2)}, u32[]{:S(2)}) collective-permute-start(bf16[128,2048]{1,0:T(8,128)(2,1)S(1)} %expand.9), channel_id=1, source_target_pairs={{0,4},{1,5},{2,6},{3,7},{4,8},{5,9},{6,10},{7,11},{16,20},{17,21},... | collective-permute-start | bytes 1572872 | tf_op jit(solution)/shard_map/ppermute | solution.py:338
  170.1 8.2 %collective-permute-done.33.refs_2_ = bf16[2,64,2048]{2,1,0:T(8,128)(2,1)S(1)} collective-permute-done((bf16[2,64,2048]{2,1,0:T(8,128)(2,1)S(1)}, bf16[2,64,2048]{2,1,0:T(8,128)(2,1)S(1)}, u32[]{:S(2)}, u32[]{:S(2)}) %collective-permute-start.33) | collective-permute-done | bytes 524320 | tf_op jit(solution)/shard_map/ppermute | solution.py:347
  179.6 1.8 fusion.6
  182.3 3.0 %collective-permute-start.40 = (bf16[128,2048]{1,0:T(8,128)(2,1)S(1)}, bf16[128,2048]{1,0:T(8,128)(2,1)S(1)}, u32[]{:S(2)}, u32[]{:S(2)}) collective-permute-start(bf16[128,2048]{1,0:T(8,128)(2,1)S(1)} %get-tuple-element.189), channel_id=1, source_target_pairs={{0,4},{1,5},{2,6},{3,7},{4,8},{5,9},{6,10},{7,11},{8,12},{9,13},{1... | collective-permute-start | bytes 1572872 | tf_op jit(solution)/shard_map/ppermute | solution.py:338
  185.3 8.5 %collective-permute-done.46.refs_5_ = bf16[128,2048]{1,0:T(8,128)(2,1)S(1)} collective-permute-done((bf16[128,2048]{1,0:T(8,128)(2,1)S(1)}, bf16[128,2048]{1,0:T(8,128)(2,1)S(1)}, u32[]{:S(2)}, u32[]{:S(2)}) %collective-permute-start.46) | collective-permute-done | bytes 524320 | tf_op jit(solution)/shard_map/ppermute | solution.py:338
  194.3 8.8 %collective-permute-start.35 = (bf16[1,64,2048]{2,1,0:T(8,128)(2,1)S(1)}, bf16[1,64,2048]{2,1,0:T(8,128)(2,1)S(1)}, u32[]{:S(2)}, u32[]{:S(2)}) collective-permute-start(bf16[1,64,2048]{2,1,0:T(8,128)(2,1)S(1)} %get-tuple-element.182), channel_id=1, source_target_pairs={{0,1},{1,0},{2,3},{3,2},{4,5},{5,4},{6,7},{7,6},{8,9},{9,8},{10,11... | collective-permute-start | bytes 786440 | tf_op jit(solution)/shard_map/ppermute | solution.py:347
  203.1 1.5 fusion.9
  204.6 2.8 %collective-permute-done.35.refs_1_ = bf16[1,64,2048]{2,1,0:T(8,128)(2,1)S(1)} collective-permute-done((bf16[1,64,2048]{2,1,0:T(8,128)(2,1)S(1)}, bf16[1,64,2048]{2,1,0:T(8,128)(2,1)S(1)}, u32[]{:S(2)}, u32[]{:S(2)}) %collective-permute-start.35) | collective-permute-done | bytes 262176 | tf_op jit(solution)/shard_map/ppermute | solution.py:347
  207.4 1.6 fusion.10
  209.0 2.0 collective-permute-done.36.refs_2_
  211.0 2.0 collective-permute-start.47
  213.0 4.0 %collective-permute-done.37.refs_3_ = bf16[1,64,2048]{2,1,0:T(8,128)(2,1)S(1)} collective-permute-done((bf16[1,64,2048]{2,1,0:T(8,128)(2,1)S(1)}, bf16[1,64,2048]{2,1,0:T(8,128)(2,1)S(1)}, u32[]{:S(2)}, u32[]{:S(2)}) %collective-permute-start.37) | collective-permute-done | bytes 262176 | tf_op jit(solution)/shard_map/ppermute | solution.py:347
  217.0 2.4 %collective-permute-start.42 = (bf16[1,64,2048]{2,1,0:T(8,128)(2,1)S(1)}, bf16[1,64,2048]{2,1,0:T(8,128)(2,1)S(1)}, u32[]{:S(2)}, u32[]{:S(2)}) collective-permute-start(bf16[1,64,2048]{2,1,0:T(8,128)(2,1)S(1)} %get-tuple-element.197), channel_id=1, source_target_pairs={{0,1},{1,0},{2,3},{3,2},{4,5},{5,4},{6,7},{7,6},{8,9},{9,8},{10,11... | collective-permute-start | bytes 786440 | tf_op jit(solution)/shard_map/ppermute | solution.py:347
  219.5 2.7 %collective-permute-done.41.refs_5_ = bf16[128,2048]{1,0:T(8,128)(2,1)S(1)} collective-permute-done((bf16[128,2048]{1,0:T(8,128)(2,1)S(1)}, bf16[128,2048]{1,0:T(8,128)(2,1)S(1)}, u32[]{:S(2)}, u32[]{:S(2)}) %collective-permute-start.41) | collective-permute-done | bytes 524320 | tf_op jit(solution)/shard_map/ppermute | solution.py:338
  222.2 2.5 %collective-permute-start.43 = (bf16[1,64,2048]{2,1,0:T(8,128)(2,1)S(1)}, bf16[1,64,2048]{2,1,0:T(8,128)(2,1)S(1)}, u32[]{:S(2)}, u32[]{:S(2)}) collective-permute-start(bf16[1,64,2048]{2,1,0:T(8,128)(2,1)S(1)} %get-tuple-element.198), channel_id=1, source_target_pairs={{0,2},{1,3},{2,0},{3,1},{4,6},{5,7},{6,4},{7,5},{8,10},{9,11},{10,... | collective-permute-start | bytes 786440 | tf_op jit(solution)/shard_map/ppermute | solution.py:347
  224.6 5.5 %collective-permute-start.44 = (bf16[1,64,2048]{2,1,0:T(8,128)(2,1)S(1)}, bf16[1,64,2048]{2,1,0:T(8,128)(2,1)S(1)}, u32[]{:S(2)}, u32[]{:S(2)}) collective-permute-start(bf16[1,64,2048]{2,1,0:T(8,128)(2,1)S(1)} %get-tuple-element.199), channel_id=1, source_target_pairs={{0,3},{1,2},{2,1},{3,0},{4,7},{5,6},{6,5},{7,4},{8,11},{9,10},{10,... | collective-permute-start | bytes 786440 | tf_op jit(solution)/shard_map/ppermute | solution.py:347
  230.1 1.7 fusion.11
  233.2 1.5 collective-permute-done.48.refs_5_
  (84 shorter events, 29.2 us)
Async XLA Ops:
  3.2 14.6 %collective-permute-start.3 = (bf16[128,2176]{1,0:T(8,128)(2,1)S(1)}, bf16[128,2176]{1,0:T(8,128)(2,1)S(1)}, u32[]{:S(2)}, u32[]{:S(2)}) collective-permute-start(bf16[128,2176]{1,0:T(8,128)(2,1)S(1)} %fusion.28.refs_0_.refs_1_), channel_id=1, source_target_pairs={{0,12},{1,13},{2,14},{3,15},{4,0},{5,1},{6,2},{7,3},{8,4},{9,5},{1... | collective-permute-start | bytes 1671176 | tf_op jit(solution)/shard_map/ppermute | solution.py:338
  3.7 27.9 %collective-permute-start.4 = (bf16[128,2176]{1,0:T(8,128)(2,1)S(1)}, bf16[128,2176]{1,0:T(8,128)(2,1)S(1)}, u32[]{:S(2)}, u32[]{:S(2)}) collective-permute-start(bf16[128,2176]{1,0:T(8,128)(2,1)S(1)} %fusion.28.refs_0_.refs_1_), channel_id=1, source_target_pairs={{0,4},{1,5},{2,6},{3,7},{4,8},{5,9},{6,10},{7,11},{8,12},{9,13},{1... | collective-permute-start | bytes 1671176 | tf_op jit(solution)/shard_map/ppermute | solution.py:338
  5.3 1.0 copy-start.3
  6.4 37.9 %copy-start.4 = (bf16[128,2048]{1,0:T(8,128)(2,1)S(1)}, bf16[128,2048]{1,0:T(8,128)(2,1)}, u32[]{:S(2)}) copy-start(bf16[128,2048]{1,0:T(8,128)(2,1)} %refs_2_.1) | copy-start | bytes 1572868
  8.1 26.8 %collective-permute-start = (bf16[1,128,2048]{2,1,0:T(8,128)(2,1)S(1)}, bf16[1,128,2048]{2,1,0:T(8,128)(2,1)S(1)}, u32[]{:S(2)}, u32[]{:S(2)}) collective-permute-start(bf16[1,128,2048]{2,1,0:T(8,128)(2,1)S(1)} %get-tuple-element.114), channel_id=1, source_target_pairs={{0,1},{1,0},{2,3},{3,2},{4,5},{5,4},{6,7},{7,6},{8,9},{9,8},{10,11... | collective-permute-start | bytes 1572872 | tf_op jit(solution)/shard_map/ppermute | solution.py:347
  8.7 26.2 %collective-permute-start.1 = (bf16[1,128,2048]{2,1,0:T(8,128)(2,1)S(1)}, bf16[1,128,2048]{2,1,0:T(8,128)(2,1)S(1)}, u32[]{:S(2)}, u32[]{:S(2)}) collective-permute-start(bf16[1,128,2048]{2,1,0:T(8,128)(2,1)S(1)} %get-tuple-element.115), channel_id=1, source_target_pairs={{0,2},{1,3},{2,0},{3,1},{4,6},{5,7},{6,4},{7,5},{8,10},{9,11},{10,... | collective-permute-start | bytes 1572872 | tf_op jit(solution)/shard_map/ppermute | solution.py:347
  9.2 25.7 %collective-permute-start.2 = (bf16[1,128,2048]{2,1,0:T(8,128)(2,1)S(1)}, bf16[1,128,2048]{2,1,0:T(8,128)(2,1)S(1)}, u32[]{:S(2)}, u32[]{:S(2)}) collective-permute-start(bf16[1,128,2048]{2,1,0:T(8,128)(2,1)S(1)} %get-tuple-element.116), channel_id=1, source_target_pairs={{0,3},{1,2},{2,1},{3,0},{4,7},{5,6},{6,5},{7,4},{8,11},{9,10},{10,... | collective-permute-start | bytes 1572872 | tf_op jit(solution)/shard_map/ppermute | solution.py:347
  17.8 24.8 %collective-permute-start.5 = (bf16[128,2176]{1,0:T(8,128)(2,1)S(1)}, bf16[128,2176]{1,0:T(8,128)(2,1)S(1)}, u32[]{:S(2)}, u32[]{:S(2)}) collective-permute-start(bf16[128,2176]{1,0:T(8,128)(2,1)S(1)} %collective-permute-done.3.refs_0_.refs_2_), channel_id=1, source_target_pairs={{4,0},{5,1},{6,2},{7,3},{8,4},{9,5},{10,6},{11,7},{20,16},{21,17},... | collective-permute-start | bytes 1671176 | tf_op jit(solution)/shard_map/ppermute | solution.py:338
  31.7 12.6 %collective-permute-start.6 = (bf16[128,2176]{1,0:T(8,128)(2,1)S(1)}, bf16[128,2176]{1,0:T(8,128)(2,1)S(1)}, u32[]{:S(2)}, u32[]{:S(2)}) collective-permute-start(bf16[128,2176]{1,0:T(8,128)(2,1)S(1)} %collective-permute-done.4.refs_1_.refs_3_), channel_id=1, source_target_pairs={{4,8},{5,9},{6,10},{7,11},{8,12},{9,13},{10,14},{11,15},{20,24},{2... | collective-permute-start | bytes 1671176 | tf_op jit(solution)/shard_map/ppermute | solution.py:338
  33.3 43.6 %copy-start.2 = (bf16[1,384,2048]{2,1,0:T(8,128)(2,1)S(1)}, bf16[1,384,2048]{2,1,0:T(8,128)(2,1)}, u32[]{:S(2)}) copy-start(bf16[1,384,2048]{2,1,0:T(8,128)(2,1)} %param.13) | copy-start | bytes 4718596
  34.9 41.9 %copy-start = (bf16[1,2048,384]{2,1,0:T(8,128)(2,1)S(1)}, bf16[1,2048,384]{2,1,0:T(8,128)(2,1)}, u32[]{:S(2)}) copy-start(bf16[1,2048,384]{2,1,0:T(8,128)(2,1)} %param.11) | copy-start | bytes 4718596
  34.9 41.9 %copy-start.1 = (bf16[1,2048,384]{2,1,0:T(8,128)(2,1)S(1)}, bf16[1,2048,384]{2,1,0:T(8,128)(2,1)}, u32[]{:S(2)}) copy-start(bf16[1,2048,384]{2,1,0:T(8,128)(2,1)} %param.12) | copy-start | bytes 4718596
  34.9 14.9 %collective-permute-start.9 = (bf16[2,64,2048]{2,1,0:T(8,128)(2,1)S(1)}, bf16[2,64,2048]{2,1,0:T(8,128)(2,1)S(1)}, u32[]{:S(2)}, u32[]{:S(2)}) collective-permute-start(bf16[2,64,2048]{2,1,0:T(8,128)(2,1)S(1)} %get-tuple-element.135), channel_id=1, source_target_pairs={{0,1},{1,0},{2,3},{3,2},{4,5},{5,4},{6,7},{7,6},{8,9},{9,8},{10,11... | collective-permute-start | bytes 1572872 | tf_op jit(solution)/shard_map/ppermute | solution.py:347
  35.5 23.5 %collective-permute-start.10 = (bf16[2,64,2048]{2,1,0:T(8,128)(2,1)S(1)}, bf16[2,64,2048]{2,1,0:T(8,128)(2,1)S(1)}, u32[]{:S(2)}, u32[]{:S(2)}) collective-permute-start(bf16[2,64,2048]{2,1,0:T(8,128)(2,1)S(1)} %get-tuple-element.136), channel_id=1, source_target_pairs={{0,2},{1,3},{2,0},{3,1},{4,6},{5,7},{6,4},{7,5},{8,10},{9,11},{10,... | collective-permute-start | bytes 1572872 | tf_op jit(solution)/shard_map/ppermute | solution.py:347
  36.0 23.0 %collective-permute-start.11 = (bf16[2,64,2048]{2,1,0:T(8,128)(2,1)S(1)}, bf16[2,64,2048]{2,1,0:T(8,128)(2,1)S(1)}, u32[]{:S(2)}, u32[]{:S(2)}) collective-permute-start(bf16[2,64,2048]{2,1,0:T(8,128)(2,1)S(1)} %get-tuple-element.137), channel_id=1, source_target_pairs={{0,3},{1,2},{2,1},{3,0},{4,7},{5,6},{6,5},{7,4},{8,11},{9,10},{10,... | collective-permute-start | bytes 1572872 | tf_op jit(solution)/shard_map/ppermute | solution.py:347
  44.3 18.3 %collective-permute-start.7 = (bf16[128,2048]{1,0:T(8,128)(2,1)S(1)}, bf16[128,2048]{1,0:T(8,128)(2,1)S(1)}, u32[]{:S(2)}, u32[]{:S(2)}) collective-permute-start(bf16[128,2048]{1,0:T(8,128)(2,1)S(1)} %copy-done.4), channel_id=1, source_target_pairs={{0,12},{1,13},{2,14},{3,15},{4,0},{5,1},{6,2},{7,3},{8,4},{9,5},{1... | collective-permute-start | bytes 1572872 | tf_op jit(solution)/shard_map/ppermute | solution.py:338
  44.3 25.4 %collective-permute-start.8 = (bf16[128,2048]{1,0:T(8,128)(2,1)S(1)}, bf16[128,2048]{1,0:T(8,128)(2,1)S(1)}, u32[]{:S(2)}, u32[]{:S(2)}) collective-permute-start(bf16[128,2048]{1,0:T(8,128)(2,1)S(1)} %copy-done.4), channel_id=1, source_target_pairs={{0,4},{1,5},{2,6},{3,7},{4,8},{5,9},{6,10},{7,11},{8,12},{9,13},{1... | collective-permute-start | bytes 1572872 | tf_op jit(solution)/shard_map/ppermute | solution.py:338
  59.0 14.2 %collective-permute-start.12 = (bf16[1,64,2048]{2,1,0:T(8,128)(2,1)S(1)}, bf16[1,64,2048]{2,1,0:T(8,128)(2,1)S(1)}, u32[]{:S(2)}, u32[]{:S(2)}) collective-permute-start(bf16[1,64,2048]{2,1,0:T(8,128)(2,1)S(1)} %get-tuple-element.138), channel_id=1, source_target_pairs={{0,1},{1,0},{2,3},{3,2},{4,5},{5,4},{6,7},{7,6},{8,9},{9,8},{10,11... | collective-permute-start | bytes 786440 | tf_op jit(solution)/shard_map/ppermute | solution.py:347
  60.5 12.7 %collective-permute-start.13 = (bf16[1,64,2048]{2,1,0:T(8,128)(2,1)S(1)}, bf16[1,64,2048]{2,1,0:T(8,128)(2,1)S(1)}, u32[]{:S(2)}, u32[]{:S(2)}) collective-permute-start(bf16[1,64,2048]{2,1,0:T(8,128)(2,1)S(1)} %get-tuple-element.139), channel_id=1, source_target_pairs={{0,2},{1,3},{2,0},{3,1},{4,6},{5,7},{6,4},{7,5},{8,10},{9,11},{10,... | collective-permute-start | bytes 786440 | tf_op jit(solution)/shard_map/ppermute | solution.py:347
  61.0 12.3 %collective-permute-start.14 = (bf16[1,64,2048]{2,1,0:T(8,128)(2,1)S(1)}, bf16[1,64,2048]{2,1,0:T(8,128)(2,1)S(1)}, u32[]{:S(2)}, u32[]{:S(2)}) collective-permute-start(bf16[1,64,2048]{2,1,0:T(8,128)(2,1)S(1)} %get-tuple-element.140), channel_id=1, source_target_pairs={{0,3},{1,2},{2,1},{3,0},{4,7},{5,6},{6,5},{7,4},{8,11},{9,10},{10,... | collective-permute-start | bytes 786440 | tf_op jit(solution)/shard_map/ppermute | solution.py:347
  62.5 19.3 %collective-permute-start.18 = (bf16[128,2048]{1,0:T(8,128)(2,1)S(1)}, bf16[128,2048]{1,0:T(8,128)(2,1)S(1)}, u32[]{:S(2)}, u32[]{:S(2)}) collective-permute-start(bf16[128,2048]{1,0:T(8,128)(2,1)S(1)} %collective-permute-done.7.refs_0_), channel_id=1, source_target_pairs={{4,0},{5,1},{6,2},{7,3},{8,4},{9,5},{10,6},{11,7},{20,16},{21,17},... | collective-permute-start | bytes 1572872 | tf_op jit(solution)/shard_map/ppermute | solution.py:338
  69.7 12.2 %collective-permute-start.19 = (bf16[128,2048]{1,0:T(8,128)(2,1)S(1)}, bf16[128,2048]{1,0:T(8,128)(2,1)S(1)}, u32[]{:S(2)}, u32[]{:S(2)}) collective-permute-start(bf16[128,2048]{1,0:T(8,128)(2,1)S(1)} %collective-permute-done.8.refs_1_), channel_id=1, source_target_pairs={{4,8},{5,9},{6,10},{7,11},{8,12},{9,13},{10,14},{11,15},{20,24},{2... | collective-permute-start | bytes 1572872 | tf_op jit(solution)/shard_map/ppermute | solution.py:338
  73.3 14.9 %collective-permute-start.15 = (bf16[2,64,2048]{2,1,0:T(8,128)(2,1)S(1)}, bf16[2,64,2048]{2,1,0:T(8,128)(2,1)S(1)}, u32[]{:S(2)}, u32[]{:S(2)}) collective-permute-start(bf16[2,64,2048]{2,1,0:T(8,128)(2,1)S(1)} %get-tuple-element.141), channel_id=1, source_target_pairs={{0,1},{1,0},{2,3},{3,2},{4,5},{5,4},{6,7},{7,6},{8,9},{9,8},{10,11... | collective-permute-start | bytes 1572872 | tf_op jit(solution)/shard_map/ppermute | solution.py:347
  73.9 23.2 %collective-permute-start.16 = (bf16[2,64,2048]{2,1,0:T(8,128)(2,1)S(1)}, bf16[2,64,2048]{2,1,0:T(8,128)(2,1)S(1)}, u32[]{:S(2)}, u32[]{:S(2)}) collective-permute-start(bf16[2,64,2048]{2,1,0:T(8,128)(2,1)S(1)} %get-tuple-element.142), channel_id=1, source_target_pairs={{0,2},{1,3},{2,0},{3,1},{4,6},{5,7},{6,4},{7,5},{8,10},{9,11},{10,... | collective-permute-start | bytes 1572872 | tf_op jit(solution)/shard_map/ppermute | solution.py:347
  74.4 22.7 %collective-permute-start.17 = (bf16[2,64,2048]{2,1,0:T(8,128)(2,1)S(1)}, bf16[2,64,2048]{2,1,0:T(8,128)(2,1)S(1)}, u32[]{:S(2)}, u32[]{:S(2)}) collective-permute-start(bf16[2,64,2048]{2,1,0:T(8,128)(2,1)S(1)} %get-tuple-element.143), channel_id=1, source_target_pairs={{0,3},{1,2},{2,1},{3,0},{4,7},{5,6},{6,5},{7,4},{8,11},{9,10},{10,... | collective-permute-start | bytes 1572872 | tf_op jit(solution)/shard_map/ppermute | solution.py:347
  97.1 8.8 %collective-permute-start.20 = (bf16[1,64,2048]{2,1,0:T(8,128)(2,1)S(1)}, bf16[1,64,2048]{2,1,0:T(8,128)(2,1)S(1)}, u32[]{:S(2)}, u32[]{:S(2)}) collective-permute-start(bf16[1,64,2048]{2,1,0:T(8,128)(2,1)S(1)} %get-tuple-element.158), channel_id=1, source_target_pairs={{0,1},{1,0},{2,3},{3,2},{4,5},{5,4},{6,7},{7,6},{8,9},{9,8},{10,11... | collective-permute-start | bytes 786440 | tf_op jit(solution)/shard_map/ppermute | solution.py:347
  98.6 10.3 %collective-permute-start.21 = (bf16[1,64,2048]{2,1,0:T(8,128)(2,1)S(1)}, bf16[1,64,2048]{2,1,0:T(8,128)(2,1)S(1)}, u32[]{:S(2)}, u32[]{:S(2)}) collective-permute-start(bf16[1,64,2048]{2,1,0:T(8,128)(2,1)S(1)} %get-tuple-element.159), channel_id=1, source_target_pairs={{0,2},{1,3},{2,0},{3,1},{4,6},{5,7},{6,4},{7,5},{8,10},{9,11},{10,... | collective-permute-start | bytes 786440 | tf_op jit(solution)/shard_map/ppermute | solution.py:347
  99.1 11.4 %collective-permute-start.22 = (bf16[1,64,2048]{2,1,0:T(8,128)(2,1)S(1)}, bf16[1,64,2048]{2,1,0:T(8,128)(2,1)S(1)}, u32[]{:S(2)}, u32[]{:S(2)}) collective-permute-start(bf16[1,64,2048]{2,1,0:T(8,128)(2,1)S(1)} %get-tuple-element.160), channel_id=1, source_target_pairs={{0,3},{1,2},{2,1},{3,0},{4,7},{5,6},{6,5},{7,4},{8,11},{9,10},{10,... | collective-permute-start | bytes 786440 | tf_op jit(solution)/shard_map/ppermute | solution.py:347
  110.5 7.0 %collective-permute-start.23 = (bf16[1,64,2048]{2,1,0:T(8,128)(2,1)S(1)}, bf16[1,64,2048]{2,1,0:T(8,128)(2,1)S(1)}, u32[]{:S(2)}, u32[]{:S(2)}) collective-permute-start(bf16[1,64,2048]{2,1,0:T(8,128)(2,1)S(1)} %get-tuple-element.170), channel_id=1, source_target_pairs={{0,1},{1,0},{2,3},{3,2},{4,5},{5,4},{6,7},{7,6},{8,9},{9,8},{10,11... | collective-permute-start | bytes 786440 | tf_op jit(solution)/shard_map/ppermute | solution.py:347
  110.5 8.6 %collective-permute-start.24 = (bf16[1,64,2048]{2,1,0:T(8,128)(2,1)S(1)}, bf16[1,64,2048]{2,1,0:T(8,128)(2,1)S(1)}, u32[]{:S(2)}, u32[]{:S(2)}) collective-permute-start(bf16[1,64,2048]{2,1,0:T(8,128)(2,1)S(1)} %get-tuple-element.171), channel_id=1, source_target_pairs={{0,2},{1,3},{2,0},{3,1},{4,6},{5,7},{6,4},{7,5},{8,10},{9,11},{10,... | collective-permute-start | bytes 786440 | tf_op jit(solution)/shard_map/ppermute | solution.py:347
  112.4 10.2 %collective-permute-start.25 = (bf16[1,64,2048]{2,1,0:T(8,128)(2,1)S(1)}, bf16[1,64,2048]{2,1,0:T(8,128)(2,1)S(1)}, u32[]{:S(2)}, u32[]{:S(2)}) collective-permute-start(bf16[1,64,2048]{2,1,0:T(8,128)(2,1)S(1)} %get-tuple-element.172), channel_id=1, source_target_pairs={{0,3},{1,2},{2,1},{3,0},{4,7},{5,6},{6,5},{7,4},{8,11},{9,10},{10,... | collective-permute-start | bytes 786440 | tf_op jit(solution)/shard_map/ppermute | solution.py:347
  115.5 10.6 %copy-start.5 = (bf16[1024,2048]{1,0:T(8,128)(2,1)S(1)}, bf16[1024,2048]{1,0:T(8,128)(2,1)}, u32[]{:S(2)}) copy-start(bf16[1024,2048]{1,0:T(8,128)(2,1)} %constant_dynamic-update-slice_fusion.1) | copy-start | bytes 12582916
  122.6 7.5 %collective-permute-start.26 = (bf16[1,64,2048]{2,1,0:T(8,128)(2,1)S(1)}, bf16[1,64,2048]{2,1,0:T(8,128)(2,1)S(1)}, u32[]{:S(2)}, u32[]{:S(2)}) collective-permute-start(bf16[1,64,2048]{2,1,0:T(8,128)(2,1)S(1)} %get-tuple-element.173), channel_id=1, source_target_pairs={{0,1},{1,0},{2,3},{3,2},{4,5},{5,4},{6,7},{7,6},{8,9},{9,8},{10,11... | collective-permute-start | bytes 786440 | tf_op jit(solution)/shard_map/ppermute | solution.py:347
  122.6 8.6 %collective-permute-start.27 = (bf16[1,64,2048]{2,1,0:T(8,128)(2,1)S(1)}, bf16[1,64,2048]{2,1,0:T(8,128)(2,1)S(1)}, u32[]{:S(2)}, u32[]{:S(2)}) collective-permute-start(bf16[1,64,2048]{2,1,0:T(8,128)(2,1)S(1)} %get-tuple-element.174), channel_id=1, source_target_pairs={{0,2},{1,3},{2,0},{3,1},{4,6},{5,7},{6,4},{7,5},{8,10},{9,11},{10,... | collective-permute-start | bytes 786440 | tf_op jit(solution)/shard_map/ppermute | solution.py:347
  123.3 10.4 %collective-permute-start.28 = (bf16[1,64,2048]{2,1,0:T(8,128)(2,1)S(1)}, bf16[1,64,2048]{2,1,0:T(8,128)(2,1)S(1)}, u32[]{:S(2)}, u32[]{:S(2)}) collective-permute-start(bf16[1,64,2048]{2,1,0:T(8,128)(2,1)S(1)} %get-tuple-element.175), channel_id=1, source_target_pairs={{0,3},{1,2},{2,1},{3,0},{4,7},{5,6},{6,5},{7,4},{8,11},{9,10},{10,... | collective-permute-start | bytes 786440 | tf_op jit(solution)/shard_map/ppermute | solution.py:347
  133.8 14.9 %collective-permute-start.29 = (bf16[2,64,2048]{2,1,0:T(8,128)(2,1)S(1)}, bf16[2,64,2048]{2,1,0:T(8,128)(2,1)S(1)}, u32[]{:S(2)}, u32[]{:S(2)}) collective-permute-start(bf16[2,64,2048]{2,1,0:T(8,128)(2,1)S(1)} %get-tuple-element.176), channel_id=1, source_target_pairs={{0,1},{1,0},{2,3},{3,2},{4,5},{5,4},{6,7},{7,6},{8,9},{9,8},{10,11... | collective-permute-start | bytes 1572872 | tf_op jit(solution)/shard_map/ppermute | solution.py:347
  134.9 18.7 %collective-permute-start.30 = (bf16[2,64,2048]{2,1,0:T(8,128)(2,1)S(1)}, bf16[2,64,2048]{2,1,0:T(8,128)(2,1)S(1)}, u32[]{:S(2)}, u32[]{:S(2)}) collective-permute-start(bf16[2,64,2048]{2,1,0:T(8,128)(2,1)S(1)} %get-tuple-element.177), channel_id=1, source_target_pairs={{0,2},{1,3},{2,0},{3,1},{4,6},{5,7},{6,4},{7,5},{8,10},{9,11},{10,... | collective-permute-start | bytes 1572872 | tf_op jit(solution)/shard_map/ppermute | solution.py:347
  136.5 19.9 %collective-permute-start.31 = (bf16[2,64,2048]{2,1,0:T(8,128)(2,1)S(1)}, bf16[2,64,2048]{2,1,0:T(8,128)(2,1)S(1)}, u32[]{:S(2)}, u32[]{:S(2)}) collective-permute-start(bf16[2,64,2048]{2,1,0:T(8,128)(2,1)S(1)} %get-tuple-element.178), channel_id=1, source_target_pairs={{0,3},{1,2},{2,1},{3,0},{4,7},{5,6},{6,5},{7,4},{8,11},{9,10},{10,... | collective-permute-start | bytes 1572872 | tf_op jit(solution)/shard_map/ppermute | solution.py:347
  139.7 54.7 %collective-permute-start.49 = (bf16[2048,384]{1,0:T(8,128)(2,1)S(1)}, bf16[2048,384]{1,0:T(8,128)(2,1)S(1)}, u32[]{:S(2)}, u32[]{:S(2)}) collective-permute-start(bf16[2048,384]{1,0:T(8,128)(2,1)S(1)} %convolution_convert_fusion.1), channel_id=1, source_target_pairs={{0,16},{16,0},{1,17},{17,1},{2,18},{18,2},{3,19},{19,3},{4,20},{20... | collective-permute-start | bytes 4718600 | tf_op jit(solution)/shard_map/ppermute | solution.py:89
  140.2 22.6 %collective-permute-start.38 = (bf16[128,2048]{1,0:T(8,128)(2,1)S(1)}, bf16[128,2048]{1,0:T(8,128)(2,1)S(1)}, u32[]{:S(2)}, u32[]{:S(2)}) collective-permute-start(bf16[128,2048]{1,0:T(8,128)(2,1)S(1)} %expand.6), channel_id=1, source_target_pairs={{0,4},{1,5},{2,6},{3,7},{4,8},{5,9},{6,10},{7,11},{16,20},{17,21},... | collective-permute-start | bytes 1572872 | tf_op jit(solution)/shard_map/ppermute | solution.py:338
  148.6 14.2 %collective-permute-start.39 = (bf16[128,2048]{1,0:T(8,128)(2,1)S(1)}, bf16[128,2048]{1,0:T(8,128)(2,1)S(1)}, u32[]{:S(2)}, u32[]{:S(2)}) collective-permute-start(bf16[128,2048]{1,0:T(8,128)(2,1)S(1)} %expand.6), channel_id=1, source_target_pairs={{12,8},{13,9},{14,10},{15,11},{8,4},{9,5},{10,6},{11,7},{28,24},{2... | collective-permute-start | bytes 1572872 | tf_op jit(solution)/shard_map/ppermute | solution.py:338
  156.4 9.2 %collective-permute-start.32 = (bf16[2,64,2048]{2,1,0:T(8,128)(2,1)S(1)}, bf16[2,64,2048]{2,1,0:T(8,128)(2,1)S(1)}, u32[]{:S(2)}, u32[]{:S(2)}) collective-permute-start(bf16[2,64,2048]{2,1,0:T(8,128)(2,1)S(1)} %get-tuple-element.179), channel_id=1, source_target_pairs={{0,1},{1,0},{2,3},{3,2},{4,5},{5,4},{6,7},{7,6},{8,9},{9,8},{10,11... | collective-permute-start | bytes 1572872 | tf_op jit(solution)/shard_map/ppermute | solution.py:347
  158.3 20.0 %collective-permute-start.33 = (bf16[2,64,2048]{2,1,0:T(8,128)(2,1)S(1)}, bf16[2,64,2048]{2,1,0:T(8,128)(2,1)S(1)}, u32[]{:S(2)}, u32[]{:S(2)}) collective-permute-start(bf16[2,64,2048]{2,1,0:T(8,128)(2,1)S(1)} %get-tuple-element.180), channel_id=1, source_target_pairs={{0,2},{1,3},{2,0},{3,1},{4,6},{5,7},{6,4},{7,5},{8,10},{9,11},{10,... | collective-permute-start | bytes 1572872 | tf_op jit(solution)/shard_map/ppermute | solution.py:347
  162.8 41.9 %collective-permute-start.50 = (bf16[2048,384]{1,0:T(8,128)(2,1)S(1)}, bf16[2048,384]{1,0:T(8,128)(2,1)S(1)}, u32[]{:S(2)}, u32[]{:S(2)}) collective-permute-start(bf16[2048,384]{1,0:T(8,128)(2,1)S(1)} %convolution_convert_fusion), channel_id=1, source_target_pairs={{0,16},{16,0},{1,17},{17,1},{2,18},{18,2},{3,19},{19,3},{4,20},{20... | collective-permute-start | bytes 4718600 | tf_op jit(solution)/shard_map/ppermute | solution.py:89
  162.9 18.6 %collective-permute-start.34 = (bf16[2,64,2048]{2,1,0:T(8,128)(2,1)S(1)}, bf16[2,64,2048]{2,1,0:T(8,128)(2,1)S(1)}, u32[]{:S(2)}, u32[]{:S(2)}) collective-permute-start(bf16[2,64,2048]{2,1,0:T(8,128)(2,1)S(1)} %get-tuple-element.181), channel_id=1, source_target_pairs={{0,3},{1,2},{2,1},{3,0},{4,7},{5,6},{6,5},{7,4},{8,11},{9,10},{10,... | collective-permute-start | bytes 1572872 | tf_op jit(solution)/shard_map/ppermute | solution.py:347
  165.6 16.7 %collective-permute-start.45 = (bf16[128,2048]{1,0:T(8,128)(2,1)S(1)}, bf16[128,2048]{1,0:T(8,128)(2,1)S(1)}, u32[]{:S(2)}, u32[]{:S(2)}) collective-permute-start(bf16[128,2048]{1,0:T(8,128)(2,1)S(1)} %expand.9), channel_id=1, source_target_pairs={{0,4},{1,5},{2,6},{3,7},{4,8},{5,9},{6,10},{7,11},{16,20},{17,21},... | collective-permute-start | bytes 1572872 | tf_op jit(solution)/shard_map/ppermute | solution.py:338
  178.3 15.5 %collective-permute-start.46 = (bf16[128,2048]{1,0:T(8,128)(2,1)S(1)}, bf16[128,2048]{1,0:T(8,128)(2,1)S(1)}, u32[]{:S(2)}, u32[]{:S(2)}) collective-permute-start(bf16[128,2048]{1,0:T(8,128)(2,1)S(1)} %expand.9), channel_id=1, source_target_pairs={{12,8},{13,9},{14,10},{15,11},{8,4},{9,5},{10,6},{11,7},{28,24},{2... | collective-permute-start | bytes 1572872 | tf_op jit(solution)/shard_map/ppermute | solution.py:338
  181.4 43.2 %collective-permute-start.51 = (bf16[384,2048]{1,0:T(8,128)(2,1)S(1)}, bf16[384,2048]{1,0:T(8,128)(2,1)S(1)}, u32[]{:S(2)}, u32[]{:S(2)}) collective-permute-start(bf16[384,2048]{1,0:T(8,128)(2,1)S(1)} %fusion.6), channel_id=1, source_target_pairs={{0,16},{16,0},{1,17},{17,1},{2,18},{18,2},{3,19},{19,3},{4,20},{20... | collective-permute-start | bytes 4718600 | tf_op jit(solution)/shard_map/ppermute | solution.py:89
  182.3 34.7 %collective-permute-start.40 = (bf16[128,2048]{1,0:T(8,128)(2,1)S(1)}, bf16[128,2048]{1,0:T(8,128)(2,1)S(1)}, u32[]{:S(2)}, u32[]{:S(2)}) collective-permute-start(bf16[128,2048]{1,0:T(8,128)(2,1)S(1)} %get-tuple-element.189), channel_id=1, source_target_pairs={{0,4},{1,5},{2,6},{3,7},{4,8},{5,9},{6,10},{7,11},{8,12},{9,13},{1... | collective-permute-start | bytes 1572872 | tf_op jit(solution)/shard_map/ppermute | solution.py:338
  193.9 28.3 %collective-permute-start.41 = (bf16[128,2048]{1,0:T(8,128)(2,1)S(1)}, bf16[128,2048]{1,0:T(8,128)(2,1)S(1)}, u32[]{:S(2)}, u32[]{:S(2)}) collective-permute-start(bf16[128,2048]{1,0:T(8,128)(2,1)S(1)} %get-tuple-element.190), channel_id=1, source_target_pairs={{0,12},{1,13},{2,14},{3,15},{4,0},{5,1},{6,2},{7,3},{8,4},{9,5},{1... | collective-permute-start | bytes 1572872 | tf_op jit(solution)/shard_map/ppermute | solution.py:338
  194.3 13.1 %collective-permute-start.35 = (bf16[1,64,2048]{2,1,0:T(8,128)(2,1)S(1)}, bf16[1,64,2048]{2,1,0:T(8,128)(2,1)S(1)}, u32[]{:S(2)}, u32[]{:S(2)}) collective-permute-start(bf16[1,64,2048]{2,1,0:T(8,128)(2,1)S(1)} %get-tuple-element.182), channel_id=1, source_target_pairs={{0,1},{1,0},{2,3},{3,2},{4,5},{5,4},{6,7},{7,6},{8,9},{9,8},{10,11... | collective-permute-start | bytes 786440 | tf_op jit(solution)/shard_map/ppermute | solution.py:347
  204.6 6.4 %collective-permute-start.36 = (bf16[1,64,2048]{2,1,0:T(8,128)(2,1)S(1)}, bf16[1,64,2048]{2,1,0:T(8,128)(2,1)S(1)}, u32[]{:S(2)}, u32[]{:S(2)}) collective-permute-start(bf16[1,64,2048]{2,1,0:T(8,128)(2,1)S(1)} %get-tuple-element.183), channel_id=1, source_target_pairs={{0,2},{1,3},{2,0},{3,1},{4,6},{5,7},{6,4},{7,5},{8,10},{9,11},{10,... | collective-permute-start | bytes 786440 | tf_op jit(solution)/shard_map/ppermute | solution.py:347
  207.4 9.6 %collective-permute-start.37 = (bf16[1,64,2048]{2,1,0:T(8,128)(2,1)S(1)}, bf16[1,64,2048]{2,1,0:T(8,128)(2,1)S(1)}, u32[]{:S(2)}, u32[]{:S(2)}) collective-permute-start(bf16[1,64,2048]{2,1,0:T(8,128)(2,1)S(1)} %get-tuple-element.184), channel_id=1, source_target_pairs={{0,3},{1,2},{2,1},{3,0},{4,7},{5,6},{6,5},{7,4},{8,11},{9,10},{10,... | collective-permute-start | bytes 786440 | tf_op jit(solution)/shard_map/ppermute | solution.py:347
  211.0 22.1 %collective-permute-start.47 = (bf16[128,2048]{1,0:T(8,128)(2,1)S(1)}, bf16[128,2048]{1,0:T(8,128)(2,1)S(1)}, u32[]{:S(2)}, u32[]{:S(2)}) collective-permute-start(bf16[128,2048]{1,0:T(8,128)(2,1)S(1)} %get-tuple-element.202), channel_id=1, source_target_pairs={{0,4},{1,5},{2,6},{3,7},{4,8},{5,9},{6,10},{7,11},{8,12},{9,13},{1... | collective-permute-start | bytes 1572872 | tf_op jit(solution)/shard_map/ppermute | solution.py:338
  217.0 17.7 %collective-permute-start.48 = (bf16[128,2048]{1,0:T(8,128)(2,1)S(1)}, bf16[128,2048]{1,0:T(8,128)(2,1)S(1)}, u32[]{:S(2)}, u32[]{:S(2)}) collective-permute-start(bf16[128,2048]{1,0:T(8,128)(2,1)S(1)} %get-tuple-element.203), channel_id=1, source_target_pairs={{0,12},{1,13},{2,14},{3,15},{4,0},{5,1},{6,2},{7,3},{8,4},{9,5},{1... | collective-permute-start | bytes 1572872 | tf_op jit(solution)/shard_map/ppermute | solution.py:338
  217.0 17.7 %collective-permute-start.42 = (bf16[1,64,2048]{2,1,0:T(8,128)(2,1)S(1)}, bf16[1,64,2048]{2,1,0:T(8,128)(2,1)S(1)}, u32[]{:S(2)}, u32[]{:S(2)}) collective-permute-start(bf16[1,64,2048]{2,1,0:T(8,128)(2,1)S(1)} %get-tuple-element.197), channel_id=1, source_target_pairs={{0,1},{1,0},{2,3},{3,2},{4,5},{5,4},{6,7},{7,6},{8,9},{9,8},{10,11... | collective-permute-start | bytes 786440 | tf_op jit(solution)/shard_map/ppermute | solution.py:347
  222.2 12.5 %collective-permute-start.43 = (bf16[1,64,2048]{2,1,0:T(8,128)(2,1)S(1)}, bf16[1,64,2048]{2,1,0:T(8,128)(2,1)S(1)}, u32[]{:S(2)}, u32[]{:S(2)}) collective-permute-start(bf16[1,64,2048]{2,1,0:T(8,128)(2,1)S(1)} %get-tuple-element.198), channel_id=1, source_target_pairs={{0,2},{1,3},{2,0},{3,1},{4,6},{5,7},{6,4},{7,5},{8,10},{9,11},{10,... | collective-permute-start | bytes 786440 | tf_op jit(solution)/shard_map/ppermute | solution.py:347
  224.6 10.0 %collective-permute-start.44 = (bf16[1,64,2048]{2,1,0:T(8,128)(2,1)S(1)}, bf16[1,64,2048]{2,1,0:T(8,128)(2,1)S(1)}, u32[]{:S(2)}, u32[]{:S(2)}) collective-permute-start(bf16[1,64,2048]{2,1,0:T(8,128)(2,1)S(1)} %get-tuple-element.199), channel_id=1, source_target_pairs={{0,3},{1,2},{2,1},{3,0},{4,7},{5,6},{6,5},{7,4},{8,11},{9,10},{10,... | collective-permute-start | bytes 786440 | tf_op jit(solution)/shard_map/ppermute | solution.py:347

commit v3 on v2

--- a/solution.py
+++ b/solution.py
@@ -9,7 +9,6 @@
 
 PLANE = 4
 LEVELS = 4
-LAG = 1
 BF = jnp.bfloat16
 F32 = jnp.float32
 
@@ -95,7 +94,7 @@
 
 
 def chosen_rows(ids_ref, meta, picks, capacity):
-    columns = meta.astype(F32).T
+    columns = meta.T
     routes, high, low = (columns[n * picks : (n + 1) * picks] for n in range(3))
     rows = meta.shape[0]
     member, weights = [], []
@@ -129,102 +128,143 @@
     return sum(jnp.dot(m, block, preferred_element_type=F32) for m in matrices).astype(BF)
 
 
-def token_kernel(ids_ref, *refs, blocks, halves, cots, picks, capacity):
-    meta_refs, refs = refs[: blocks * halves], refs[blocks * halves :]
-    row_refs, refs = refs[: blocks * halves], refs[blocks * halves :]
-    cot_refs, refs = refs[:cots], refs[cots:]
+def start_kernel(ids_ref, tokens_ref, routes_ref, gates_ref, cot_ref, block_ref, *refs, picks, capacity):
     table_ref, turned_ref, *out_refs = refs
+    rows, width = tokens_ref.shape
+    gates = gates_ref[...]
+    high = gates.astype(BF)
+    low = (gates - high.astype(F32)).astype(BF)
+    lane = lax.broadcasted_iota(jnp.int32, (picks, 128), 1)
+    row = lax.broadcasted_iota(jnp.int32, (picks, 128), 0)
+    meta = jnp.zeros((rows, 128), F32)
+    for n, part in enumerate((routes_ref[...].astype(F32).astype(BF), high, low)):
+        place = jnp.where(lane == row + n * picks, 1.0, 0.0).astype(BF)
+        meta += jnp.dot(part, place, preferred_element_type=F32)
+    block_ref[:, :width] = tokens_ref[...]
+    block_ref[:, width:] = meta.astype(BF)
+    write_tables(ids_ref, meta, table_ref, turned_ref, 0, picks, capacity)
+    put(out_refs, 0, 0, picked_rows([table_ref[0, 0]], tokens_ref[...]), capacity)
+    rows = picked_rows([table_ref[0, 1], table_ref[0, 2]], cot_ref[...])
+    put(out_refs, 0, capacity, rows, capacity)
+
+
+def write_tables(ids_ref, meta, table_ref, turned_ref, n, picks, capacity):
+    for m, table in enumerate(chosen_rows(ids_ref, meta, picks, capacity)):
+        table_ref[n, m] = table.astype(BF)
+        turned_ref[n, m] = table.T.astype(BF)
+
+
+def table_shapes(count, capacity, rows):
+    return [(count, 3, PLANE * capacity, rows), (count, 3, rows, PLANE * capacity)]
+
+
+def start_rows(ids, tokens, routes, gates, cotangent, capacity):
+    rows, width = tokens.shape
+    picks = routes.shape[1]
+    shapes = [(rows, width + 128)] + table_shapes(1, capacity, rows)
+    shapes += [(1, 2 * capacity, width)] * PLANE
+    block, table, turned, *out = pl.pallas_call(
+        functools.partial(start_kernel, picks=picks, capacity=capacity),
+        in_specs=[pl.BlockSpec(memory_space=pltpu.SMEM)]
+        + [pl.BlockSpec(memory_space=pltpu.VMEM)] * 4,
+        out_shape=[jax.ShapeDtypeStruct(s, BF) for s in shapes],
+        compiler_params=pltpu.CompilerParams(vmem_limit_bytes=28 << 20),
+        name="start_rows",
+    )(ids, tokens, routes, gates, cotangent)
+    return block, table, turned, out
+
+
+def token_kernel(ids_ref, *refs, blocks, picks, capacity):
+    meta_refs, row_refs, refs = refs[:blocks], refs[blocks : 2 * blocks], refs[2 * blocks :]
+    table_ref, turned_ref, *out_refs = refs
+    if blocks == 2:
+        *out_refs, pass_ref = out_refs
+        width = row_refs[0].shape[1]
+        first = ids_ref[PLANE] == 1
+        pass_ref[:, :width] = jnp.where(first, row_refs[0][...], row_refs[1][...])
+        pass_ref[:, width:] = jnp.where(first, meta_refs[0][...], meta_refs[1][...])
     for n in range(blocks):
-        meta = sum(ref[...] for ref in meta_refs[n * halves : (n + 1) * halves])
-        tables = chosen_rows(ids_ref, meta, picks, capacity)
-        for m, table in enumerate(tables):
-            table_ref[n, m] = table.astype(BF)
-            turned_ref[n, m] = table.T.astype(BF)
-        block = sum(ref[...] for ref in row_refs[n * halves : (n + 1) * halves])
-        put(out_refs, n, 0, picked_rows([table_ref[n, 0]], block), capacity)
-        if cots:
-            rows = picked_rows([table_ref[n, 1], table_ref[n, 2]], cot_refs[n][...])
-            put(out_refs, n, capacity, rows, capacity)
-
-
-def token_rows(ids, blocks, picks, capacity, width, cots=()):
-    halves = len(blocks[0])
-    arrays = [a for block in blocks for a in block]
-    rows = arrays[0].shape[0]
-    count, tall = len(blocks), capacity * (2 if cots else 1)
-    spec = [pl.BlockSpec((rows, 128), lambda i: (0, width // 128))] * len(arrays)
-    spec += [pl.BlockSpec((rows, width), lambda i: (0, 0))] * (len(arrays) + len(cots))
-    shapes = [(count, 3, PLANE * capacity, rows), (count, 3, rows, PLANE * capacity)]
-    shapes += [(count, tall, width)] * PLANE
-    work = 2 * count * PLANE * capacity * rows * width * (3 if cots else 1)
-    moved = 2 * width * (rows * (len(arrays) + len(cots)) + count * PLANE * tall)
+        meta = meta_refs[n][...].astype(F32)
+        write_tables(ids_ref, meta, table_ref, turned_ref, n, picks, capacity)
+        put(out_refs, n, 0, picked_rows([table_ref[n, 0]], row_refs[n][...]), capacity)
+
+
+def token_rows(ids, blocks, picks, capacity):
+    rows, wide = blocks[0].shape
+    width, count = wide - 128, len(blocks)
+    spec = [pl.BlockSpec((rows, 128), lambda i: (0, width // 128))] * count
+    spec += [pl.BlockSpec((rows, width), lambda i: (0, 0))] * count
+    shapes = table_shapes(count, capacity, rows) + [(count, capacity, width)] * PLANE
+    if count == 2:
+        shapes.append((rows, wide))
     table, turned, *out = pl.pallas_call(
-        functools.partial(
-            token_kernel, blocks=count, halves=halves, cots=len(cots), picks=picks, capacity=capacity
-        ),
+        functools.partial(token_kernel, blocks=count, picks=picks, capacity=capacity),
         grid=(1,),
         in_specs=[pl.BlockSpec(memory_space=pltpu.SMEM)] + spec,
         out_specs=[pl.BlockSpec(s, lambda i, d=len(s): (0,) * d) for s in shapes],
         out_shape=[jax.ShapeDtypeStruct(s, BF) for s in shapes],
         compiler_params=pltpu.CompilerParams(vmem_limit_bytes=28 << 20),
-        cost_estimate=pl.CostEstimate(flops=work, bytes_accessed=moved, transcendentals=0),
         name="token_rows",
-    )(ids, *arrays, *arrays, *cots)
+    )(ids, *blocks, *blocks)
     return table, turned, out
 
 
-def cot_kernel(table_ref, *refs, blocks, halves):
-    row_refs, out_refs = refs[: blocks * halves], refs[blocks * halves :]
-    capacity = out_refs[0].shape[1]
+def cot_kernel(ids_ref, table_ref, *refs, blocks):
+    row_refs, out_refs = refs[:blocks], refs[blocks:]
+    if blocks == 2:
+        *out_refs, pass_ref = out_refs
+        pass_ref[...] = jnp.where(ids_ref[PLANE] == 1, row_refs[0][...], row_refs[1][...])
     for n in range(blocks):
-        block = sum(ref[...] for ref in row_refs[n * halves : (n + 1) * halves])
-        put(out_refs, n, 0, picked_rows([table_ref[n, 1], table_ref[n, 2]], block), capacity)
-
-
-def cot_rows(table, blocks):
-    halves = len(blocks[0])
-    arrays = [a for block in blocks for a in block]
-    rows, width = arrays[0].shape
-    shape = (len(blocks), table.shape[2] // PLANE, width)
-    work = 4 * len(blocks) * table.shape[2] * rows * width
-    moved = 2 * width * (rows * len(arrays) + len(blocks) * table.shape[2])
+        rows = picked_rows([table_ref[n, 1], table_ref[n, 2]], row_refs[n][...])
+        put(out_refs, n, 0, rows, out_refs[0].shape[1])
+
+
+def cot_rows(ids, table, blocks):
+    rows, width = blocks[0].shape
+    shapes = [(len(blocks), table.shape[2] // PLANE, width)] * PLANE
+    if len(blocks) == 2:
+        shapes.append((rows, width))
     return pl.pallas_call(
-        functools.partial(cot_kernel, blocks=len(blocks), halves=halves),
-        out_shape=[jax.ShapeDtypeStruct(shape, BF)] * PLANE,
+        functools.partial(cot_kernel, blocks=len(blocks)),
+        in_specs=[pl.BlockSpec(memory_space=pltpu.SMEM)]
+        + [pl.BlockSpec(memory_space=pltpu.VMEM)] * (1 + len(blocks)),
+        out_shape=[jax.ShapeDtypeStruct(s, BF) for s in shapes],
         compiler_params=pltpu.CompilerParams(vmem_limit_bytes=28 << 20),
-        cost_estimate=pl.CostEstimate(flops=work, bytes_accessed=moved, transcendentals=0),
         name="cot_rows",
-    )(table, *arrays)
-
-
-def expand_kernel(turned_ref, *refs, blocks, extras, parts):
-    row_refs, extra_refs, out_refs = refs[:PLANE], refs[PLANE:-blocks], refs[-blocks:]
+    )(ids, table, *blocks)
+
+
+def expand_kernel(flags_ref, turned_ref, *refs, blocks, extras, parts, flagged):
+    row_refs, extra_refs, out_refs = refs[:PLANE], refs[PLANE : PLANE + extras], refs[-blocks:]
     for n in range(blocks):
         rows = jnp.concatenate([ref[n] for ref in row_refs], axis=0)
         total = sum(jnp.dot(turned_ref[n, m], rows, preferred_element_type=F32) for m in parts)
-        for ref in extra_refs[n * extras : (n + 1) * extras]:
-            total += ref[...].astype(F32)
+        for ref in extra_refs:
+            extra = ref[...].astype(F32)
+            total += jnp.where(flags_ref[n] == 1, extra, 0.0) if flagged else extra
         out_refs[n][...] = total.astype(BF)
 
 
-def expand(turned, rows, weighted, extras):
+def expand(turned, rows, weighted, extras=(), flags=None):
     blocks, _, width = rows[0].shape
     rows_dev, slots = turned.shape[2:]
-    flat = [e for extra in extras for e in extra]
     work = 2 * blocks * rows_dev * slots * width * (2 if weighted else 1)
-    moved = 2 * width * (blocks * (slots + rows_dev) + len(flat) * rows_dev)
+    moved = 2 * width * (blocks * (slots + rows_dev) + len(extras) * rows_dev)
     return pl.pallas_call(
         functools.partial(
             expand_kernel,
             blocks=blocks,
-            extras=len(extras[0]),
+            extras=len(extras),
             parts=(1, 2) if weighted else (0,),
+            flagged=flags is not None,
         ),
+        in_specs=[pl.BlockSpec(memory_space=pltpu.SMEM)]
+        + [pl.BlockSpec(memory_space=pltpu.VMEM)] * (1 + len(rows) + len(extras)),
         out_shape=[jax.ShapeDtypeStruct((rows_dev, width), BF)] * blocks,
         compiler_params=pltpu.CompilerParams(vmem_limit_bytes=28 << 20),
         cost_estimate=pl.CostEstimate(flops=work, bytes_accessed=moved, transcendentals=0),
         name="expand",
-    )(turned, *rows, *flat)
+    )(jnp.zeros((2,), jnp.int32) if flags is None else flags, turned, *rows, *extras)
 
 
 def nt_dot(a, b):
@@ -244,7 +284,7 @@
     gate_out[...] = gate_pre
     up_out[...] = up_pre
     hidden = (gate_pre * jax.nn.sigmoid(gate_pre) * up_pre).astype(BF)
-    hidden_out[...] = hidden
+    hidden_out[...] = hidden.astype(F32).T.astype(BF)
     outputs = jnp.dot(hidden, down_ref[...], preferred_element_type=F32).astype(BF)
     for k, out_ref in enumerate(out_refs):
         for n in range(count):
@@ -261,7 +301,7 @@
         out_shape=[
             jax.ShapeDtypeStruct((total, inner), F32),
             jax.ShapeDtypeStruct((total, inner), F32),
-            jax.ShapeDtypeStruct((total, inner), BF),
+            jax.ShapeDtypeStruct((inner, total), BF),
             jax.ShapeDtypeStruct((total, width), BF),
         ]
         + [jax.ShapeDtypeStruct((count, capacity, width), BF)] * PLANE,
@@ -289,8 +329,8 @@
     sigma = jax.nn.sigmoid(gate_pre)
     gate_grad = (hidden_grad * up_pre * sigma * (1.0 + gate_pre * (1.0 - sigma))).astype(BF)
     up_grad = (hidden_grad * gate_pre * sigma).astype(BF)
-    gate_out[...] = gate_grad
-    up_out[...] = up_grad
+    gate_out[...] = gate_grad.astype(F32).T.astype(BF)
+    up_out[...] = up_grad.astype(F32).T.astype(BF)
     grads = (nt_dot(gate_grad, gate_ref[...]) + nt_dot(up_grad, up_ref[...])).astype(BF)
     for k, out_ref in enumerate(out_refs):
         for n in range(count):
@@ -304,8 +344,8 @@
     return pl.pallas_call(
         functools.partial(backward_kernel, skip=skip),
         out_shape=[
-            jax.ShapeDtypeStruct((total, inner), BF),
-            jax.ShapeDtypeStruct((total, inner), BF),
+            jax.ShapeDtypeStruct((inner, total), BF),
+            jax.ShapeDtypeStruct((inner, total), BF),
             jax.ShapeDtypeStruct((total, width), BF),
         ]
         + [jax.ShapeDtypeStruct((count, capacity, width), BF)] * PLANE,
@@ -319,6 +359,76 @@
     )(*cots, gate_pre, up_pre, gate_mat, up_mat, down_mat)
 
 
+def partial_kernel(*refs):
+    out_ref = refs[-1]
+    chunks = (len(refs) - 1) // 5
+    hidden, gate_grad, up_grad, inputs, cots = (
+        refs[n * chunks : (n + 1) * chunks] for n in range(5)
+    )
+    for n, (left, right) in enumerate(((gate_grad, inputs), (up_grad, inputs), (hidden, cots))):
+        total = sum(
+            jnp.dot(a[...], b[...], preferred_element_type=F32) for a, b in zip(left, right)
+        )
+        out_ref[n] = total.astype(BF)
+
+
+def partial_sums(hidden, gate_grad, up_grad, inputs, cots):
+    inner, width = hidden[0].shape[0], inputs[0].shape[1]
+    total = sum(a.shape[0] for a in inputs)
+    tile = min(512, width)
+    small = [*hidden, *gate_grad, *up_grad]
+    large = [*inputs, *cots]
+    return pl.pallas_call(
+        partial_kernel,
+        grid=(width // tile,),
+        in_specs=[pl.BlockSpec(a.shape, lambda i: (0, 0)) for a in small]
+        + [pl.BlockSpec((a.shape[0], tile), lambda i: (0, i)) for a in large],
+        out_specs=pl.BlockSpec((3, inner, tile), lambda i: (0, 0, i)),
+        out_shape=jax.ShapeDtypeStruct((3, inner, width), BF),
+        compiler_params=pltpu.CompilerParams(vmem_limit_bytes=36 << 20),
+        cost_estimate=pl.CostEstimate(
+            flops=6 * total * inner * width,
+            bytes_accessed=6 * total * inner + 4 * total * width + 6 * inner * width,
+            transcendentals=0,
+        ),
+        name="partial_sums",
+    )(*small, *large)
+
+
+def turn_kernel(*refs):
+    *sum_refs, gate_ref, up_ref, down_ref = refs
+    for n, out_ref in enumerate((gate_ref, up_ref, down_ref)):
+        total = sum(ref[n].astype(F32) for ref in sum_refs)
+        out_ref[0] = (total if n == 2 else total.T).astype(BF)
+
+
+def weight_outputs(*sums):
+    _, inner, width = sums[0].shape
+    tile = min(512, width)
+    return pl.pallas_call(
+        turn_kernel,
+        grid=(width // tile,),
+        in_specs=[pl.BlockSpec((3, inner, tile), lambda i: (0, 0, i))] * len(sums),
+        out_specs=[
+            pl.BlockSpec((1, tile, inner), lambda i: (0, i, 0)),
+            pl.BlockSpec((1, tile, inner), lambda i: (0, i, 0)),
+            pl.BlockSpec((1, inner, tile), lambda i: (0, 0, i)),
+        ],
+        out_shape=[
+            jax.ShapeDtypeStruct((1, width, inner), BF),
+            jax.ShapeDtypeStruct((1, width, inner), BF),
+            jax.ShapeDtypeStruct((1, inner, width), BF),
+        ],
+        compiler_params=pltpu.CompilerParams(vmem_limit_bytes=28 << 20),
+        cost_estimate=pl.CostEstimate(
+            flops=6 * inner * width,
+            bytes_accessed=6 * inner * width * (1 + len(sums)),
+            transcendentals=0,
+        ),
+        name="weight_outputs",
+    )(*sums)
+
+
 def plane_plan(tokens, routes, gates, cotangent, w_gate, w_up, w_down):
     rows_dev, width = tokens.shape
     picks = routes.shape[1]
@@ -327,22 +437,28 @@
     mats = (w_gate[0], w_up[0], w_down[0])
     here = lax.axis_index("expert")
     level, place = here // PLANE, here % PLANE
-    ids = level * PLANE + (place ^ jnp.arange(PLANE, dtype=jnp.int32))
-
-    def shift(value, levels, step):
-        pairs = [
-            (level * PLANE + p, (level + step) % LEVELS * PLANE + p)
-            for level in levels
-            for p in range(PLANE)
-        ]
+    odd = level % 2
+    ids = jnp.stack([level * PLANE + (place ^ k) for k in range(PLANE)] + [odd])
+
+    def permute(value, step):
+        pairs = [(i, step(i // PLANE) % LEVELS * PLANE + i % PLANE) for i in range(experts)]
         return lax.ppermute(value, "expert", pairs)
 
+    def from_above(value):
+        return permute(value, lambda n: n - 1)
+
+    def from_below(value):
+        return permute(value, lambda n: n + 1)
+
+    def swap(value):
+        return permute(value, lambda n: n ^ 1)
+
     stages = []
 
-    def across(rows):
+    def across(rows, *deps):
         sent = tuple(rows[1:])
-        if len(stages) >= LAG:
-            sent, _ = lax.optimization_barrier((sent, stages[-LAG]))
+        if stages or deps:
+            sent, *_ = lax.optimization_barrier((sent, *stages[-1:], *deps))
         moved = {
             k: lax.ppermute(sent[k - 1], "expert", [(i, i ^ k) for i in range(experts)])
             for k in (3, 1, 2)
@@ -350,67 +466,66 @@
         stages.append(tuple(moved[k] for k in range(1, PLANE)))
         return [rows[0], *stages[-1]]
 
-    every = range(LEVELS)
-    high = lax.reduce_precision(gates, 8, 7)
-    low = lax.reduce_precision(gates - high, 8, 7)
-    meta = jnp.concatenate([routes.astype(F32), high, low], axis=1).astype(BF)
-    meta = jnp.pad(meta, ((0, 0), (0, 128 - meta.shape[1])))
-    block = jnp.concatenate([tokens, meta], axis=1)
-
-    def pick(blocks, cots=()):
-        return token_rows(ids, blocks, picks, capacity, width, cots)
-
-    above, below = shift(block, every, -1), shift(block, every, 1)
-    table_a, turned_a, rows_a = pick([[block]], [cotangent])
+    block, table_a, turned_a, rows_a = start_rows(ids, tokens, routes, gates, cotangent, capacity)
     rows_a = across(rows_a)
-    far = [shift(above, (1, 2), -1), shift(below, (1, 2), 1)]
-    table_b, turned_b, rows_b = pick([[above], [below]])
+    above, below = from_above(block), from_below(block)
+    table_b, turned_b, (*rows_b, far) = token_rows(ids, [above, below], picks, capacity)
+    far = swap(far)
     rows_b = across(rows_b)
     later, far = lax.optimization_barrier((cotangent, far))
-    cot_above, cot_below = shift(later, every, -1), shift(later, every, 1)
-    table_c, turned_c, rows_c = pick([far])
+    cot_above, cot_below = from_above(later), from_below(later)
+    table_c, turned_c, rows_c = token_rows(ids, [far], picks, capacity)
     rows_c = across(rows_c)
-    cot_far = [shift(cot_above, (1, 2), -1), shift(cot_below, (1, 2), 1)]
-    cots_b = across(cot_rows(table_b, [[cot_above], [cot_below]]))
-    cots_c = across(cot_rows(table_c, [cot_far]))
-
-    saved, outs = [], []
-    for rows in (rows_a, rows_b, rows_c):
-        gate_pre, up_pre, hidden, inputs, *out = forward(rows, capacity, *mats)
-        saved.append((gate_pre, up_pre, hidden, inputs))
-        outs.append(out)
-    grads, grad_outs = [], []
-    for cots, skip, (gate_pre, up_pre, _, _) in zip(
-        (rows_a, cots_b, cots_c), (capacity, 0, 0), saved
-    ):
-        gate_grad, up_grad, flat, *out = backward(cots, skip, capacity, gate_pre, up_pre, *mats)
-        grads.append((gate_grad, up_grad, flat))
-        grad_outs.append(out)
-
-    flows = ((outs, True), (grad_outs, False))
-    relayed = []
-    for rows, weighted in flows:
-        (part,) = expand(turned_c, across(rows[2]), weighted, [[]])
-        relayed.append((shift(part, (0, 1), 1), shift(part, (3, 2), -1)))
-    arrived = []
-    for (rows, weighted), (up, down) in zip(flows, relayed):
-        near = expand(turned_b, across(rows[1]), weighted, [[up], [down]])
-        arrived.append([shift(near[0], every, 1), shift(near[1], every, -1)])
-    mixed, input_grad = (
-        expand(turned_a, across(rows[0]), weighted, [extra])[0]
-        for (rows, weighted), extra in zip(flows, arrived)
+    *cots_b, cot_far = cot_rows(ids, table_b, [cot_above, cot_below])
+    cot_far = swap(cot_far)
+    cots_b = across(cots_b)
+
+    saved = [forward(rows, capacity, *mats) for rows in (rows_a, rows_b, rows_c)]
+    outs = [s[4:] for s in saved]
+
+    def back(cots, skip, forth):
+        return backward(cots, skip, capacity, forth[0], forth[1], *mats)
+
+    back_a = back(rows_a, capacity, saved[0])
+    cots_c = across(cot_rows(ids, table_c, [cot_far]), saved, back_a)
+    back_b = back(cots_b, 0, saved[1])
+    mixed_c = across(outs[2], back_b)
+    back_c = back(cots_c, 0, saved[2])
+    backs = (back_a, back_b, back_c)
+    partial = partial_sums(
+        [s[2] for s in saved],
+        [b[0] for b in backs],
+        [b[1] for b in backs],
+        [s[3] for s in saved],
+        [b[2] for b in backs],
     )
-    hidden, inputs = (jnp.concatenate([s[n] for s in saved]) for n in (2, 3))
-    gate_grad, up_grad, slot_cot = (jnp.concatenate([g[n] for g in grads]) for n in range(3))
-    down_part = jnp.dot(hidden.T, slot_cot, preferred_element_type=F32)
-    gate_part = jnp.dot(inputs.T, gate_grad, preferred_element_type=F32)
-    up_part = jnp.dot(inputs.T, up_grad, preferred_element_type=F32)
-    return (mixed, input_grad) + relay_sums(gate_part, up_part, down_part)
+    grads_c = across(back_c[3:], partial)
+    passed = jnp.stack([odd, 1 - odd])
+
+    def send_near(rows, weighted, far, *deps):
+        near = expand(turned_b, rows, weighted, [far], passed)
+        near, *_ = lax.optimization_barrier((near, *deps))
+        return from_below(near[0]), from_above(near[1])
+
+    mixed_far = swap(*expand(turned_c, mixed_c, True))
+    sent, _ = lax.optimization_barrier((partial, mixed_c))
+    other = lax.ppermute(sent, "pipe", [(0, 1), (1, 0)])
+    mixed_b = across(outs[1])
+    grads_far = swap(*expand(turned_c, grads_c, False))
+    weight_grads = weight_outputs(partial, other)
+    grads_b = across(back_b[3:], mixed_far, grads_far, weight_grads)
+    mixed_near = send_near(mixed_b, True, mixed_far, grads_far)
+    mixed_a = across(outs[0])
+    grads_near = send_near(grads_b, False, grads_far, mixed_near)
+    grads_a = across(back_a[3:], mixed_near)
+    mixed = expand(turned_a, mixed_a, True, mixed_near)
+    input_grad = expand(turned_a, grads_a, False, grads_near)
+    return (*mixed, *input_grad, *weight_grads)
 
 
 def on_device(tokens, routes, *rest):
     experts, picks = lax.axis_size("expert"), routes.shape[1]
-    if experts == LEVELS * PLANE and experts <= 2 * picks:
+    if experts == LEVELS * PLANE and lax.axis_size("pipe") == 2 and experts <= 2 * picks:
         return plane_plan(tokens, routes, *rest)
     return direct_plan(tokens, routes, *rest)
 

time: 240 us -> 227 us (0.946)
  starting transfers between devices: 84.5 us -> 52.1 us
  Pallas kernels: 25.7 us -> 43.9 us
  local copies, waits for them, and re-layouts: 3.99 us -> 16.4 us
  other arithmetic: 7.35 us -> 0.07 us
  matrix products: 6.61 us -> 0 us
  waiting for transfers between devices: 107 us -> 110 us
    ppermute x19 -> x13, starting transfers between devices: 31.8 us -> 12 us  [the longest x12 12 us: permute(): return lax.ppermute(value, 'expert', pairs)]
    unnamed x14 -> x66, local copies, waits for them, and re-layouts: 3.77 us -> 16.3 us
    ppermute x33, starting transfers between devices: 52.6 us -> 40.1 us  [across(): lax.ppermute(sent[k - 1], 'expert', [(i, i ^ k) for i in range(experts)])]
    pallas_call x5 -> x7, Pallas kernels: 6.37 us -> 17.8 us  [the longest x1 6.58 us: partial_sums(): pl.pallas_call(partial_kernel, grid=(width // tile,), in_specs=[pl.BlockS...]
    ppermute x19 -> x13, waiting for transfers between devices: 39 us -> 45.8 us  [the longest x12 45.8 us: permute(): return lax.ppermute(value, 'expert', pairs)]
    dot_general x3 -> x0, matrix products: 6.61 us -> none  [the longest x1 2.39 us: plane_plan(): gate_part = jnp.dot(inputs.T, gate_grad, preferred_element_type=F32)]
    pallas_call x6, Pallas kernels: 4.37 us -> 9.98 us  [expand(): pl.pallas_call(functools.partial(expand_kernel, blocks=blocks, extras=len...]
    broadcast_in_dim x3 -> x0, other arithmetic: 4.87 us -> none  [relay_sums(): sums.append(total[None])]
  transfers between devices with their start and end apart: 52 -> 46, of which waited for: 26 -> 21; matrix products, arithmetic and copies ran while one was open for 6% -> 0% of each run, Pallas kernels for 10% -> 18%
where the time goes in v3:
time: 227 us; the launch traced here: 223 us
  waiting for transfers between devices  110 us (48%)
  starting transfers between devices  52.1 us (23%)
  Pallas kernels  43.9 us (19%)
  local copies, waits for them, and re-layouts  16.4 us (7%)
    ppermute x33, waiting for transfers between devices, across(): lax.ppermute(sent[k - 1], 'expert', [(i, i ^ k) for i in range(experts)])  63.7 us
    ppermute x12, waiting for transfers between devices, permute(): return lax.ppermute(value, 'expert', pairs)  45.8 us
    ppermute x33, starting transfers between devices, across(): lax.ppermute(sent[k - 1], 'expert', [(i, i ^ k) for i in range(experts)])  40.1 us
    unnamed x66, local copies, waits for them, and re-layouts  16.3 us
    ppermute x12, starting transfers between devices, permute(): return lax.ppermute(value, 'expert', pairs)  12 us
    pallas_call x6, Pallas kernels, expand(): pl.pallas_call(functools.partial(expand_kernel, blocks=blocks, extras=len...  9.98 us
    pallas_call x3, Pallas kernels, forward(): pl.pallas_call(functools.partial(forward_kernel, first=capacity), out_sha...  8.24 us
    pallas_call x3, Pallas kernels, backward(): pl.pallas_call(functools.partial(backward_kernel, skip=skip), out_shape=[...  7.88 us
  transfers between devices with their start and end apart: 46, of which 21 were waited for; matrix products, arithmetic and copies ran while one was open for 0% of the time, Pallas kernels for 18%

profile of v3, /device:TPU:14, one launch (start us, length us, event | category | flops | bytes accessed | tf_op | source)
XLA Modules:
  0.0 223.1 jit_solution(4280446461894358734)
XLA Ops:
  2.3 1.0 copy-done.7
  4.4 1.9 start_rows.1
  6.8 1.6 collective-permute-start.4
  9.4 2.5 %collective-permute-start.2 = (bf16[1,128,2048]{2,1,0:T(8,128)(2,1)S(1)}, bf16[1,128,2048]{2,1,0:T(8,128)(2,1)S(1)}, u32[]{:S(2)}, u32[]{:S(2)}) collective-permute-start(bf16[1,128,2048]{2,1,0:T(8,128)(2,1)S(1)} %get-tuple-element.126), channel_id=1, source_target_pairs={{0,3},{1,2},{2,1},{3,0},{4,7},{5,6},{6,5},{7,4},{8,11},{9,10},{10,... | collective-permute-start | bytes 1572872 | tf_op jit(solution)/shard_map/ppermute | solution.py:463
  11.9 9.0 %collective-permute-done.3.refs_0_.refs_2_ = bf16[128,2176]{1,0:T(8,128)(2,1)S(1)} collective-permute-done((bf16[128,2176]{1,0:T(8,128)(2,1)S(1)}, bf16[128,2176]{1,0:T(8,128)(2,1)S(1)}, u32[]{:S(2)}, u32[]{:S(2)}) %collective-permute-start.3) | collective-permute-done | bytes 557088 | tf_op jit(solution)/shard_map/ppermute | solution.py:445
  20.8 13.9 %collective-permute-done.4.refs_1_.refs_3_ = bf16[128,2176]{1,0:T(8,128)(2,1)S(1)} collective-permute-done((bf16[128,2176]{1,0:T(8,128)(2,1)S(1)}, bf16[128,2176]{1,0:T(8,128)(2,1)S(1)}, u32[]{:S(2)}, u32[]{:S(2)}) %collective-permute-start.4) | collective-permute-done | bytes 557088 | tf_op jit(solution)/shard_map/ppermute | solution.py:445
  34.7 1.6 token_rows.2
  37.9 2.5 %collective-permute-start.10 = (bf16[2,64,2048]{2,1,0:T(8,128)(2,1)S(1)}, bf16[2,64,2048]{2,1,0:T(8,128)(2,1)S(1)}, u32[]{:S(2)}, u32[]{:S(2)}) collective-permute-start(bf16[2,64,2048]{2,1,0:T(8,128)(2,1)S(1)} %get-tuple-element.148), channel_id=1, source_target_pairs={{0,3},{1,2},{2,1},{3,0},{4,7},{5,6},{6,5},{7,4},{8,11},{9,10},{10,... | collective-permute-start | bytes 1572872 | tf_op jit(solution)/shard_map/ppermute | solution.py:463
  40.4 9.6 %collective-permute-done.5.refs_0_.refs_1_ = bf16[128,2176]{1,0:T(8,128)(2,1)S(1)} collective-permute-done((bf16[128,2176]{1,0:T(8,128)(2,1)S(1)}, bf16[128,2176]{1,0:T(8,128)(2,1)S(1)}, u32[]{:S(2)}, u32[]{:S(2)}) %collective-permute-start.5) | collective-permute-done | bytes 557088 | tf_op jit(solution)/shard_map/ppermute | solution.py:445
  50.3 1.7 collective-permute-start.7
  52.0 1.2 token_rows.3
  53.1 7.8 %collective-permute-done.9.refs_2_ = bf16[2,64,2048]{2,1,0:T(8,128)(2,1)S(1)} collective-permute-done((bf16[2,64,2048]{2,1,0:T(8,128)(2,1)S(1)}, bf16[2,64,2048]{2,1,0:T(8,128)(2,1)S(1)}, u32[]{:S(2)}, u32[]{:S(2)}) %collective-permute-start.9) | collective-permute-done | bytes 524320 | tf_op jit(solution)/shard_map/ppermute | solution.py:463
  60.9 1.5 collective-permute-start.11
  62.9 1.5 collective-permute-start.13
  64.4 8.7 %collective-permute-done.6.refs_0_ = bf16[128,2048]{1,0:T(8,128)(2,1)S(1)} collective-permute-done((bf16[128,2048]{1,0:T(8,128)(2,1)S(1)}, bf16[128,2048]{1,0:T(8,128)(2,1)S(1)}, u32[]{:S(2)}, u32[]{:S(2)}) %collective-permute-start.6) | collective-permute-done | bytes 524320 | tf_op jit(solution)/shard_map/ppermute | solution.py:445
  73.1 1.8 cot_rows.2
  76.1 2.4 %collective-permute-start.16 = (bf16[2,64,2048]{2,1,0:T(8,128)(2,1)S(1)}, bf16[2,64,2048]{2,1,0:T(8,128)(2,1)S(1)}, u32[]{:S(2)}, u32[]{:S(2)}) collective-permute-start(bf16[2,64,2048]{2,1,0:T(8,128)(2,1)S(1)} %get-tuple-element.154), channel_id=1, source_target_pairs={{0,3},{1,2},{2,1},{3,0},{4,7},{5,6},{6,5},{7,4},{8,11},{9,10},{10,... | collective-permute-start | bytes 1572872 | tf_op jit(solution)/shard_map/ppermute | solution.py:463
  78.9 1.9 expert_forward.3
  82.2 2.0 expert_backward.4
  86.4 4.5 %expert_forward.4 = (f32[512,384]{1,0:T(8,128)S(1)}, f32[512,384]{1,0:T(8,128)S(1)}, bf16[384,512]{1,0:T(8,128)(2,1)S(1)}, bf16[512,2048]{1,0:T(8,128)(2,1)S(1)}...) custom-call(bf16[2,64,2048]{2,1,0:T(8,128)(2,1)S(1)} %get-tuple-elem, ...), custom_call_target="tpu_custom_call" | custom-call | flops 2415919104 | bytes 12976128 | tf_op jit(solution)/shard_map/expert_forward/pallas_call | solution.py:299
  90.9 1.9 expert_forward.5
  92.7 1.2 cot_rows.3
  94.0 4.7 %collective-permute-done.15.refs_2_ = bf16[2,64,2048]{2,1,0:T(8,128)(2,1)S(1)} collective-permute-done((bf16[2,64,2048]{2,1,0:T(8,128)(2,1)S(1)}, bf16[2,64,2048]{2,1,0:T(8,128)(2,1)S(1)}, u32[]{:S(2)}, u32[]{:S(2)}) %collective-permute-start.15) | collective-permute-done | bytes 524320 | tf_op jit(solution)/shard_map/ppermute | solution.py:463
  98.7 1.5 collective-permute-start.18
  100.7 1.5 collective-permute-start.20
  102.2 3.9 %expert_backward.3 = (bf16[384,512]{1,0:T(8,128)(2,1)S(1)}, bf16[384,512]{1,0:T(8,128)(2,1)S(1)}, bf16[512,2048]{1,0:T(8,128)(2,1)S(1)}, bf16[2,64,2048]{2,1,0:T...) custom-call(bf16[2,64,2048]{2,1,0:T(8,128)(2,1)S(1)} %get-tuple-elem, ...), custom_call_target="tpu_custom_call" | custom-call | flops 2415919104 | bytes 13369344 | tf_op jit(solution)/shard_map/expert_backward/pallas_call | solution.py:344
  107.0 3.3 %collective-permute-done.19.refs_2_ = bf16[1,64,2048]{2,1,0:T(8,128)(2,1)S(1)} collective-permute-done((bf16[1,64,2048]{2,1,0:T(8,128)(2,1)S(1)}, bf16[1,64,2048]{2,1,0:T(8,128)(2,1)S(1)}, u32[]{:S(2)}, u32[]{:S(2)}) %collective-permute-start.19) | collective-permute-done | bytes 262176 | tf_op jit(solution)/shard_map/ppermute | solution.py:463
  110.2 2.0 collective-permute-done.20.refs_3_
  112.2 1.8 collective-permute-start.22
  114.0 1.6 collective-permute-start.23
  115.7 2.0 expert_backward.5
  117.7 6.6 %partial_sums.1.refs_0_ = bf16[3,384,2048]{2,1,0:T(8,128)(2,1)S(1)} custom-call(bf16[384,256]{1,0:T(8,128)(2,1)S(1)} %get-tuple-element.172.refs_0_, bf16[384,512]{1,0:T(8,128)(2,1)S(1)} %get-tuple-element.174.refs_1_, bf16[384,256]{1,0:T(8,128)(2,1)S(1)} %get-tuple-element.180.refs_2_, bf16[384,256]{1,0:T(8,128)(2,1)S(1)} %get-tuple-element.186.refs_3_, ...), custom_call_target="tpu_custom_call" | custom-call | flops 4831838208 | bytes 15466496 | tf_op jit(solution)/shard_map/partial_sums/pallas_call | solution.py:381
  124.4 2.2 copy-done.3
  126.6 1.8 collective-permute-start.25
  128.4 1.6 collective-permute-start.26
  130.1 1.8 expand.6
  131.9 3.8 %collective-permute-done.24.refs_1_ = bf16[1,64,2048]{2,1,0:T(8,128)(2,1)S(1)} collective-permute-done((bf16[1,64,2048]{2,1,0:T(8,128)(2,1)S(1)}, bf16[1,64,2048]{2,1,0:T(8,128)(2,1)S(1)}, u32[]{:S(2)}, u32[]{:S(2)}) %collective-permute-start.24) | collective-permute-done | bytes 262176 | tf_op jit(solution)/shard_map/ppermute | solution.py:463
  135.7 5.2 %collective-permute-done.25.refs_2_ = bf16[1,64,2048]{2,1,0:T(8,128)(2,1)S(1)} collective-permute-done((bf16[1,64,2048]{2,1,0:T(8,128)(2,1)S(1)}, bf16[1,64,2048]{2,1,0:T(8,128)(2,1)S(1)}, u32[]{:S(2)}, u32[]{:S(2)}) %collective-permute-start.25) | collective-permute-done | bytes 262176 | tf_op jit(solution)/shard_map/ppermute | solution.py:463
  140.9 1.7 collective-permute-start.27
  143.0 1.5 collective-permute-start.29
  144.4 1.7 expand.7
  146.1 2.2 copy-done.5
  148.4 2.3 %copy-done.4 = bf16[3,384,2048]{2,1,0:T(8,128)(2,1)S(1)} copy-done((bf16[3,384,2048]{2,1,0:T(8,128)(2,1)S(1)}, bf16[3,384,2048]{2,1,0:T(8,128)(2,1)}, u32[]{:S(2)}) %copy-start.4) | copy-done | bytes 4718616
  150.7 2.3 %copy-done.6 = bf16[3,384,2048]{2,1,0:T(8,128)(2,1)S(1)} copy-done((bf16[3,384,2048]{2,1,0:T(8,128)(2,1)S(1)}, bf16[3,384,2048]{2,1,0:T(8,128)(2,1)}, u32[]{:S(2)}) %copy-start.6) | copy-done | bytes 4718616
  153.1 3.6 %weight_outputs.1 = (bf16[1,2048,384]{2,1,0:T(8,128)(2,1)}, bf16[1,2048,384]{2,1,0:T(8,128)(2,1)}, bf16[1,384,2048]{2,1,0:T(8,128)(2,1)}) custom-call(bf16[3,384,2048]{2,1,0:T(8,128)(2,1)S(1)} %copy-done.4, bf16[3,384,2048]{2,1,0:T(8,128)(2,1)S(1)} %copy-done.6), custom_call_target="tpu_custom_call" | custom-call | flops 4718592 | bytes 14155776 | tf_op jit(solution)/shard_map/weight_outputs/pallas_call | solution.py:408
  156.6 8.6 %collective-permute-done.28.refs_2_ = bf16[2,64,2048]{2,1,0:T(8,128)(2,1)} collective-permute-done((bf16[2,64,2048]{2,1,0:T(8,128)(2,1)}, bf16[2,64,2048]{2,1,0:T(8,128)(2,1)}, u32[]{:S(2)}, u32[]{:S(2)}) %collective-permute-start.28) | collective-permute-done | bytes 524320 | tf_op jit(solution)/shard_map/ppermute | solution.py:463
  165.3 1.8 collective-permute-done.29.refs_3_
  167.5 1.8 collective-permute-start.34
  169.3 1.2 collective-permute-start.35
  170.6 1.9 expand.8
  172.6 3.2 %collective-permute-start.39 = (bf16[128,2048]{1,0:T(8,128)(2,1)S(1)}, bf16[128,2048]{1,0:T(8,128)(2,1)S(1)}, u32[]{:S(2)}, u32[]{:S(2)}) collective-permute-start(bf16[128,2048]{1,0:T(8,128)(2,1)S(1)} %get-tuple-element.230), channel_id=1, source_target_pairs={{0,4},{1,5},{2,6},{3,7},{4,8},{5,9},{6,10},{7,11},{8,12},{9,13},{1... | collective-permute-start | bytes 1572872 | tf_op jit(solution)/shard_map/ppermute | solution.py:445
  175.8 6.1 %collective-permute-done.33.refs_1_ = bf16[2,64,2048]{2,1,0:T(8,128)(2,1)S(1)} collective-permute-done((bf16[2,64,2048]{2,1,0:T(8,128)(2,1)S(1)}, bf16[2,64,2048]{2,1,0:T(8,128)(2,1)S(1)}, u32[]{:S(2)}, u32[]{:S(2)}) %collective-permute-start.33) | collective-permute-done | bytes 524320 | tf_op jit(solution)/shard_map/ppermute | solution.py:463
  181.9 9.1 %collective-permute-done.34.refs_2_ = bf16[2,64,2048]{2,1,0:T(8,128)(2,1)S(1)} collective-permute-done((bf16[2,64,2048]{2,1,0:T(8,128)(2,1)S(1)}, bf16[2,64,2048]{2,1,0:T(8,128)(2,1)S(1)}, u32[]{:S(2)}, u32[]{:S(2)}) %collective-permute-start.34) | collective-permute-done | bytes 524320 | tf_op jit(solution)/shard_map/ppermute | solution.py:463
  191.1 1.5 collective-permute-start.36
  193.3 1.5 collective-permute-start.38
  194.8 1.0 expand.10
  196.3 3.7 %collective-permute-start.44 = (bf16[128,2048]{1,0:T(8,128)(2,1)S(1)}, bf16[128,2048]{1,0:T(8,128)(2,1)S(1)}, u32[]{:S(2)}, u32[]{:S(2)}) collective-permute-start(bf16[128,2048]{1,0:T(8,128)(2,1)S(1)} %get-tuple-element.237), channel_id=1, source_target_pairs={{0,4},{1,5},{2,6},{3,7},{4,8},{5,9},{6,10},{7,11},{8,12},{9,13},{1... | collective-permute-start | bytes 1572872 | tf_op jit(solution)/shard_map/ppermute | solution.py:445
  200.1 2.1 collective-permute-done.37.refs_2_
  202.2 2.8 %collective-permute-done.38.refs_3_ = bf16[1,64,2048]{2,1,0:T(8,128)(2,1)S(1)} collective-permute-done((bf16[1,64,2048]{2,1,0:T(8,128)(2,1)S(1)}, bf16[1,64,2048]{2,1,0:T(8,128)(2,1)S(1)}, u32[]{:S(2)}, u32[]{:S(2)}) %collective-permute-start.38) | collective-permute-done | bytes 262176 | tf_op jit(solution)/shard_map/ppermute | solution.py:463
  205.1 4.8 %collective-permute-start.42 = (bf16[1,64,2048]{2,1,0:T(8,128)(2,1)S(1)}, bf16[1,64,2048]{2,1,0:T(8,128)(2,1)S(1)}, u32[]{:S(2)}, u32[]{:S(2)}) collective-permute-start(bf16[1,64,2048]{2,1,0:T(8,128)(2,1)S(1)} %copy-done.21), channel_id=1, source_target_pairs={{0,2},{1,3},{2,0},{3,1},{4,6},{5,7},{6,4},{7,5},{8,10},{9,11},{10,... | collective-permute-start | bytes 786440 | tf_op jit(solution)/shard_map/ppermute | solution.py:463
  209.9 1.8 expand.9
  211.7 4.9 %collective-permute-done.42.refs_2_ = bf16[1,64,2048]{2,1,0:T(8,128)(2,1)S(1)} collective-permute-done((bf16[1,64,2048]{2,1,0:T(8,128)(2,1)S(1)}, bf16[1,64,2048]{2,1,0:T(8,128)(2,1)S(1)}, u32[]{:S(2)}, u32[]{:S(2)}) %collective-permute-start.42) | collective-permute-done | bytes 262176 | tf_op jit(solution)/shard_map/ppermute | solution.py:463
  217.2 4.2 %collective-permute-done.45.refs_5_ = bf16[128,2048]{1,0:T(8,128)(2,1)S(1)} collective-permute-done((bf16[128,2048]{1,0:T(8,128)(2,1)S(1)}, bf16[128,2048]{1,0:T(8,128)(2,1)S(1)}, u32[]{:S(2)}, u32[]{:S(2)}) %collective-permute-start.45) | collective-permute-done | bytes 524320 | tf_op jit(solution)/shard_map/ppermute | solution.py:445
  221.4 1.7 expand.11
  (116 shorter events, 15.9 us)
Async XLA Ops:
  4.4 45.5 %copy-start.9 = (bf16[128,2048]{1,0:T(8,128)(2,1)S(1)}, bf16[128,2048]{1,0:T(8,128)(2,1)}, u32[]{:S(2)}) copy-start(bf16[128,2048]{1,0:T(8,128)(2,1)} %cot_ref.1) | copy-start | bytes 1572868
  6.3 14.5 %collective-permute-start.3 = (bf16[128,2176]{1,0:T(8,128)(2,1)S(1)}, bf16[128,2176]{1,0:T(8,128)(2,1)S(1)}, u32[]{:S(2)}, u32[]{:S(2)}) collective-permute-start(bf16[128,2176]{1,0:T(8,128)(2,1)S(1)} %get-tuple-element.131), channel_id=1, source_target_pairs={{0,12},{1,13},{2,14},{3,15},{4,0},{5,1},{6,2},{7,3},{8,4},{9,5},{1... | collective-permute-start | bytes 1671176 | tf_op jit(solution)/shard_map/ppermute | solution.py:445
  6.8 27.9 %collective-permute-start.4 = (bf16[128,2176]{1,0:T(8,128)(2,1)S(1)}, bf16[128,2176]{1,0:T(8,128)(2,1)S(1)}, u32[]{:S(2)}, u32[]{:S(2)}) collective-permute-start(bf16[128,2176]{1,0:T(8,128)(2,1)S(1)} %get-tuple-element.131), channel_id=1, source_target_pairs={{0,4},{1,5},{2,6},{3,7},{4,8},{5,9},{6,10},{7,11},{8,12},{9,13},{1... | collective-permute-start | bytes 1671176 | tf_op jit(solution)/shard_map/ppermute | solution.py:445
  8.4 28.4 %collective-permute-start = (bf16[1,128,2048]{2,1,0:T(8,128)(2,1)S(1)}, bf16[1,128,2048]{2,1,0:T(8,128)(2,1)S(1)}, u32[]{:S(2)}, u32[]{:S(2)}) collective-permute-start(bf16[1,128,2048]{2,1,0:T(8,128)(2,1)S(1)} %get-tuple-element.124), channel_id=1, source_target_pairs={{0,1},{1,0},{2,3},{3,2},{4,5},{5,4},{6,7},{7,6},{8,9},{9,8},{10,11... | collective-permute-start | bytes 1572872 | tf_op jit(solution)/shard_map/ppermute | solution.py:463
  8.9 27.9 %collective-permute-start.1 = (bf16[1,128,2048]{2,1,0:T(8,128)(2,1)S(1)}, bf16[1,128,2048]{2,1,0:T(8,128)(2,1)S(1)}, u32[]{:S(2)}, u32[]{:S(2)}) collective-permute-start(bf16[1,128,2048]{2,1,0:T(8,128)(2,1)S(1)} %get-tuple-element.125), channel_id=1, source_target_pairs={{0,2},{1,3},{2,0},{3,1},{4,6},{5,7},{6,4},{7,5},{8,10},{9,11},{10,... | collective-permute-start | bytes 1572872 | tf_op jit(solution)/shard_map/ppermute | solution.py:463
  9.4 27.4 %collective-permute-start.2 = (bf16[1,128,2048]{2,1,0:T(8,128)(2,1)S(1)}, bf16[1,128,2048]{2,1,0:T(8,128)(2,1)S(1)}, u32[]{:S(2)}, u32[]{:S(2)}) collective-permute-start(bf16[1,128,2048]{2,1,0:T(8,128)(2,1)S(1)} %get-tuple-element.126), channel_id=1, source_target_pairs={{0,3},{1,2},{2,1},{3,0},{4,7},{5,6},{6,5},{7,4},{8,11},{9,10},{10,... | collective-permute-start | bytes 1572872 | tf_op jit(solution)/shard_map/ppermute | solution.py:463
  34.7 44.2 %copy-start.1 = (bf16[1,2048,384]{2,1,0:T(8,128)(2,1)S(1)}, bf16[1,2048,384]{2,1,0:T(8,128)(2,1)}, u32[]{:S(2)}) copy-start(bf16[1,2048,384]{2,1,0:T(8,128)(2,1)} %param.12) | copy-start | bytes 4718596
  34.7 44.2 %copy-start.2 = (bf16[1,384,2048]{2,1,0:T(8,128)(2,1)S(1)}, bf16[1,384,2048]{2,1,0:T(8,128)(2,1)}, u32[]{:S(2)}) copy-start(bf16[1,384,2048]{2,1,0:T(8,128)(2,1)} %param.13) | copy-start | bytes 4718596
  36.3 42.6 %copy-start = (bf16[1,2048,384]{2,1,0:T(8,128)(2,1)S(1)}, bf16[1,2048,384]{2,1,0:T(8,128)(2,1)}, u32[]{:S(2)}) copy-start(bf16[1,2048,384]{2,1,0:T(8,128)(2,1)} %param.11) | copy-start | bytes 4718596
  36.3 13.6 %collective-permute-start.5 = (bf16[128,2176]{1,0:T(8,128)(2,1)S(1)}, bf16[128,2176]{1,0:T(8,128)(2,1)S(1)}, u32[]{:S(2)}, u32[]{:S(2)}) collective-permute-start(bf16[128,2176]{1,0:T(8,128)(2,1)S(1)} %get-tuple-element.133), channel_id=1, source_target_pairs={{0,4},{1,5},{2,6},{3,7},{4,0},{5,1},{6,2},{7,3},{8,12},{9,13},{10,... | collective-permute-start | bytes 1671176 | tf_op jit(solution)/shard_map/ppermute | solution.py:445
  36.8 16.3 %collective-permute-start.8 = (bf16[2,64,2048]{2,1,0:T(8,128)(2,1)S(1)}, bf16[2,64,2048]{2,1,0:T(8,128)(2,1)S(1)}, u32[]{:S(2)}, u32[]{:S(2)}) collective-permute-start(bf16[2,64,2048]{2,1,0:T(8,128)(2,1)S(1)} %get-tuple-element.146), channel_id=1, source_target_pairs={{0,1},{1,0},{2,3},{3,2},{4,5},{5,4},{6,7},{7,6},{8,9},{9,8},{10,11... | collective-permute-start | bytes 1572872 | tf_op jit(solution)/shard_map/ppermute | solution.py:463
  37.4 23.5 %collective-permute-start.9 = (bf16[2,64,2048]{2,1,0:T(8,128)(2,1)S(1)}, bf16[2,64,2048]{2,1,0:T(8,128)(2,1)S(1)}, u32[]{:S(2)}, u32[]{:S(2)}) collective-permute-start(bf16[2,64,2048]{2,1,0:T(8,128)(2,1)S(1)} %get-tuple-element.147), channel_id=1, source_target_pairs={{0,2},{1,3},{2,0},{3,1},{4,6},{5,7},{6,4},{7,5},{8,10},{9,11},{10,... | collective-permute-start | bytes 1572872 | tf_op jit(solution)/shard_map/ppermute | solution.py:463
  37.9 23.0 %collective-permute-start.10 = (bf16[2,64,2048]{2,1,0:T(8,128)(2,1)S(1)}, bf16[2,64,2048]{2,1,0:T(8,128)(2,1)S(1)}, u32[]{:S(2)}, u32[]{:S(2)}) collective-permute-start(bf16[2,64,2048]{2,1,0:T(8,128)(2,1)S(1)} %get-tuple-element.148), channel_id=1, source_target_pairs={{0,3},{1,2},{2,1},{3,0},{4,7},{5,6},{6,5},{7,4},{8,11},{9,10},{10,... | collective-permute-start | bytes 1572872 | tf_op jit(solution)/shard_map/ppermute | solution.py:463
  49.9 23.1 %collective-permute-start.6 = (bf16[128,2048]{1,0:T(8,128)(2,1)S(1)}, bf16[128,2048]{1,0:T(8,128)(2,1)S(1)}, u32[]{:S(2)}, u32[]{:S(2)}) collective-permute-start(bf16[128,2048]{1,0:T(8,128)(2,1)S(1)} %copy-done.9), channel_id=1, source_target_pairs={{0,12},{1,13},{2,14},{3,15},{4,0},{5,1},{6,2},{7,3},{8,4},{9,5},{1... | collective-permute-start | bytes 1572872 | tf_op jit(solution)/shard_map/ppermute | solution.py:445
  50.3 22.8 %collective-permute-start.7 = (bf16[128,2048]{1,0:T(8,128)(2,1)S(1)}, bf16[128,2048]{1,0:T(8,128)(2,1)S(1)}, u32[]{:S(2)}, u32[]{:S(2)}) collective-permute-start(bf16[128,2048]{1,0:T(8,128)(2,1)S(1)} %copy-done.9), channel_id=1, source_target_pairs={{0,4},{1,5},{2,6},{3,7},{4,8},{5,9},{6,10},{7,11},{8,12},{9,13},{1... | collective-permute-start | bytes 1572872 | tf_op jit(solution)/shard_map/ppermute | solution.py:445
  60.9 14.0 %collective-permute-start.11 = (bf16[1,64,2048]{2,1,0:T(8,128)(2,1)S(1)}, bf16[1,64,2048]{2,1,0:T(8,128)(2,1)S(1)}, u32[]{:S(2)}, u32[]{:S(2)}) collective-permute-start(bf16[1,64,2048]{2,1,0:T(8,128)(2,1)S(1)} %get-tuple-element.149), channel_id=1, source_target_pairs={{0,1},{1,0},{2,3},{3,2},{4,5},{5,4},{6,7},{7,6},{8,9},{9,8},{10,11... | collective-permute-start | bytes 786440 | tf_op jit(solution)/shard_map/ppermute | solution.py:463
  62.4 12.5 %collective-permute-start.12 = (bf16[1,64,2048]{2,1,0:T(8,128)(2,1)S(1)}, bf16[1,64,2048]{2,1,0:T(8,128)(2,1)S(1)}, u32[]{:S(2)}, u32[]{:S(2)}) collective-permute-start(bf16[1,64,2048]{2,1,0:T(8,128)(2,1)S(1)} %get-tuple-element.150), channel_id=1, source_target_pairs={{0,2},{1,3},{2,0},{3,1},{4,6},{5,7},{6,4},{7,5},{8,10},{9,11},{10,... | collective-permute-start | bytes 786440 | tf_op jit(solution)/shard_map/ppermute | solution.py:463
  62.9 12.0 %collective-permute-start.13 = (bf16[1,64,2048]{2,1,0:T(8,128)(2,1)S(1)}, bf16[1,64,2048]{2,1,0:T(8,128)(2,1)S(1)}, u32[]{:S(2)}, u32[]{:S(2)}) collective-permute-start(bf16[1,64,2048]{2,1,0:T(8,128)(2,1)S(1)} %get-tuple-element.151), channel_id=1, source_target_pairs={{0,3},{1,2},{2,1},{3,0},{4,7},{5,6},{6,5},{7,4},{8,11},{9,10},{10,... | collective-permute-start | bytes 786440 | tf_op jit(solution)/shard_map/ppermute | solution.py:463
  74.9 19.0 %collective-permute-start.14 = (bf16[2,64,2048]{2,1,0:T(8,128)(2,1)S(1)}, bf16[2,64,2048]{2,1,0:T(8,128)(2,1)S(1)}, u32[]{:S(2)}, u32[]{:S(2)}) collective-permute-start(bf16[2,64,2048]{2,1,0:T(8,128)(2,1)S(1)} %get-tuple-element.152), channel_id=1, source_target_pairs={{0,1},{1,0},{2,3},{3,2},{4,5},{5,4},{6,7},{7,6},{8,9},{9,8},{10,11... | collective-permute-start | bytes 1572872 | tf_op jit(solution)/shard_map/ppermute | solution.py:463
  75.6 23.2 %collective-permute-start.15 = (bf16[2,64,2048]{2,1,0:T(8,128)(2,1)S(1)}, bf16[2,64,2048]{2,1,0:T(8,128)(2,1)S(1)}, u32[]{:S(2)}, u32[]{:S(2)}) collective-permute-start(bf16[2,64,2048]{2,1,0:T(8,128)(2,1)S(1)} %get-tuple-element.153), channel_id=1, source_target_pairs={{0,2},{1,3},{2,0},{3,1},{4,6},{5,7},{6,4},{7,5},{8,10},{9,11},{10,... | collective-permute-start | bytes 1572872 | tf_op jit(solution)/shard_map/ppermute | solution.py:463
  76.1 22.7 %collective-permute-start.16 = (bf16[2,64,2048]{2,1,0:T(8,128)(2,1)S(1)}, bf16[2,64,2048]{2,1,0:T(8,128)(2,1)S(1)}, u32[]{:S(2)}, u32[]{:S(2)}) collective-permute-start(bf16[2,64,2048]{2,1,0:T(8,128)(2,1)S(1)} %get-tuple-element.154), channel_id=1, source_target_pairs={{0,3},{1,2},{2,1},{3,0},{4,7},{5,6},{6,5},{7,4},{8,11},{9,10},{10,... | collective-permute-start | bytes 1572872 | tf_op jit(solution)/shard_map/ppermute | solution.py:463
  78.5 14.2 %collective-permute-start.17 = (bf16[128,2048]{1,0:T(8,128)(2,1)S(1)}, bf16[128,2048]{1,0:T(8,128)(2,1)S(1)}, u32[]{:S(2)}, u32[]{:S(2)}) collective-permute-start(bf16[128,2048]{1,0:T(8,128)(2,1)S(1)} %get-tuple-element.165), channel_id=1, source_target_pairs={{0,4},{1,5},{2,6},{3,7},{4,0},{5,1},{6,2},{7,3},{8,12},{9,13},{10,... | collective-permute-start | bytes 1572872 | tf_op jit(solution)/shard_map/ppermute | solution.py:445
  98.7 8.2 %collective-permute-start.18 = (bf16[1,64,2048]{2,1,0:T(8,128)(2,1)S(1)}, bf16[1,64,2048]{2,1,0:T(8,128)(2,1)S(1)}, u32[]{:S(2)}, u32[]{:S(2)}) collective-permute-start(bf16[1,64,2048]{2,1,0:T(8,128)(2,1)S(1)} %get-tuple-element.193), channel_id=1, source_target_pairs={{0,1},{1,0},{2,3},{3,2},{4,5},{5,4},{6,7},{7,6},{8,9},{9,8},{10,11... | collective-permute-start | bytes 786440 | tf_op jit(solution)/shard_map/ppermute | solution.py:463
  100.2 10.0 %collective-permute-start.19 = (bf16[1,64,2048]{2,1,0:T(8,128)(2,1)S(1)}, bf16[1,64,2048]{2,1,0:T(8,128)(2,1)S(1)}, u32[]{:S(2)}, u32[]{:S(2)}) collective-permute-start(bf16[1,64,2048]{2,1,0:T(8,128)(2,1)S(1)} %get-tuple-element.194), channel_id=1, source_target_pairs={{0,2},{1,3},{2,0},{3,1},{4,6},{5,7},{6,4},{7,5},{8,10},{9,11},{10,... | collective-permute-start | bytes 786440 | tf_op jit(solution)/shard_map/ppermute | solution.py:463
  100.7 11.5 %collective-permute-start.20 = (bf16[1,64,2048]{2,1,0:T(8,128)(2,1)S(1)}, bf16[1,64,2048]{2,1,0:T(8,128)(2,1)S(1)}, u32[]{:S(2)}, u32[]{:S(2)}) collective-permute-start(bf16[1,64,2048]{2,1,0:T(8,128)(2,1)S(1)} %get-tuple-element.195), channel_id=1, source_target_pairs={{0,3},{1,2},{2,1},{3,0},{4,7},{5,6},{6,5},{7,4},{8,11},{9,10},{10,... | collective-permute-start | bytes 786440 | tf_op jit(solution)/shard_map/ppermute | solution.py:463
  106.1 11.6 %copy-start.12 = (bf16[2,64,2048]{2,1,0:T(8,128)(2,1)}, bf16[2,64,2048]{2,1,0:T(8,128)(2,1)S(1)}, u32[]{:S(2)}) copy-start(bf16[2,64,2048]{2,1,0:T(8,128)(2,1)S(1)} %get-tuple-element.223) | copy-start | bytes 1572868
  106.1 11.6 %copy-start.14 = (bf16[2,64,2048]{2,1,0:T(8,128)(2,1)}, bf16[2,64,2048]{2,1,0:T(8,128)(2,1)S(1)}, u32[]{:S(2)}) copy-start(bf16[2,64,2048]{2,1,0:T(8,128)(2,1)S(1)} %get-tuple-element.222) | copy-start | bytes 1572868
  106.1 11.6 %copy-start.16 = (bf16[2,64,2048]{2,1,0:T(8,128)(2,1)}, bf16[2,64,2048]{2,1,0:T(8,128)(2,1)S(1)}, u32[]{:S(2)}) copy-start(bf16[2,64,2048]{2,1,0:T(8,128)(2,1)S(1)} %get-tuple-element.221) | copy-start | bytes 1572868
  112.2 12.1 %collective-permute-start.21 = (bf16[1,64,2048]{2,1,0:T(8,128)(2,1)S(1)}, bf16[1,64,2048]{2,1,0:T(8,128)(2,1)S(1)}, u32[]{:S(2)}, u32[]{:S(2)}) collective-permute-start(bf16[1,64,2048]{2,1,0:T(8,128)(2,1)S(1)} %get-tuple-element.203), channel_id=1, source_target_pairs={{0,1},{1,0},{2,3},{3,2},{4,5},{5,4},{6,7},{7,6},{8,9},{9,8},{10,11... | collective-permute-start | bytes 786440 | tf_op jit(solution)/shard_map/ppermute | solution.py:463
  112.2 12.1 %collective-permute-start.22 = (bf16[1,64,2048]{2,1,0:T(8,128)(2,1)S(1)}, bf16[1,64,2048]{2,1,0:T(8,128)(2,1)S(1)}, u32[]{:S(2)}, u32[]{:S(2)}) collective-permute-start(bf16[1,64,2048]{2,1,0:T(8,128)(2,1)S(1)} %get-tuple-element.204), channel_id=1, source_target_pairs={{0,2},{1,3},{2,0},{3,1},{4,6},{5,7},{6,4},{7,5},{8,10},{9,11},{10,... | collective-permute-start | bytes 786440 | tf_op jit(solution)/shard_map/ppermute | solution.py:463
  114.0 10.3 %collective-permute-start.23 = (bf16[1,64,2048]{2,1,0:T(8,128)(2,1)S(1)}, bf16[1,64,2048]{2,1,0:T(8,128)(2,1)S(1)}, u32[]{:S(2)}, u32[]{:S(2)}) collective-permute-start(bf16[1,64,2048]{2,1,0:T(8,128)(2,1)S(1)} %get-tuple-element.205), channel_id=1, source_target_pairs={{0,3},{1,2},{2,1},{3,0},{4,7},{5,6},{6,5},{7,4},{8,11},{9,10},{10,... | collective-permute-start | bytes 786440 | tf_op jit(solution)/shard_map/ppermute | solution.py:463
  124.3 21.7 %collective-permute-start.32 = (bf16[3,384,2048]{2,1,0:T(8,128)(2,1)S(1)}, bf16[3,384,2048]{2,1,0:T(8,128)(2,1)S(1)}, u32[]{:S(2)}, u32[]{:S(2)}) collective-permute-start(bf16[3,384,2048]{2,1,0:T(8,128)(2,1)S(1)} %partial_sums.1.refs_0_), channel_id=1, source_target_pairs={{0,16},{16,0},{1,17},{17,1},{2,18},{18,2},{3,19},{19,3},{4,20},{20... | collective-permute-start | bytes 14155784 | tf_op jit(solution)/shard_map/ppermute | solution.py:512
  126.6 9.1 %collective-permute-start.24 = (bf16[1,64,2048]{2,1,0:T(8,128)(2,1)S(1)}, bf16[1,64,2048]{2,1,0:T(8,128)(2,1)S(1)}, u32[]{:S(2)}, u32[]{:S(2)}) collective-permute-start(bf16[1,64,2048]{2,1,0:T(8,128)(2,1)S(1)} %get-tuple-element.209), channel_id=1, source_target_pairs={{0,1},{1,0},{2,3},{3,2},{4,5},{5,4},{6,7},{7,6},{8,9},{9,8},{10,11... | collective-permute-start | bytes 786440 | tf_op jit(solution)/shard_map/ppermute | solution.py:463
  126.6 14.3 %collective-permute-start.25 = (bf16[1,64,2048]{2,1,0:T(8,128)(2,1)S(1)}, bf16[1,64,2048]{2,1,0:T(8,128)(2,1)S(1)}, u32[]{:S(2)}, u32[]{:S(2)}) collective-permute-start(bf16[1,64,2048]{2,1,0:T(8,128)(2,1)S(1)} %get-tuple-element.210), channel_id=1, source_target_pairs={{0,2},{1,3},{2,0},{3,1},{4,6},{5,7},{6,4},{7,5},{8,10},{9,11},{10,... | collective-permute-start | bytes 786440 | tf_op jit(solution)/shard_map/ppermute | solution.py:463
  128.4 12.5 %collective-permute-start.26 = (bf16[1,64,2048]{2,1,0:T(8,128)(2,1)S(1)}, bf16[1,64,2048]{2,1,0:T(8,128)(2,1)S(1)}, u32[]{:S(2)}, u32[]{:S(2)}) collective-permute-start(bf16[1,64,2048]{2,1,0:T(8,128)(2,1)S(1)} %get-tuple-element.211), channel_id=1, source_target_pairs={{0,3},{1,2},{2,1},{3,0},{4,7},{5,6},{6,5},{7,4},{8,11},{9,10},{10,... | collective-permute-start | bytes 786440 | tf_op jit(solution)/shard_map/ppermute | solution.py:463
  131.9 24.7 %collective-permute-start.30 = (bf16[128,2048]{1,0:T(8,128)(2,1)}, bf16[128,2048]{1,0:T(8,128)(2,1)S(1)}, u32[]{:S(2)}, u32[]{:S(2)}) collective-permute-start(bf16[128,2048]{1,0:T(8,128)(2,1)} %expand.6), channel_id=1, source_target_pairs={{0,4},{1,5},{2,6},{3,7},{4,0},{5,1},{6,2},{7,3},{8,12},{9,13},{10,... | collective-permute-start | bytes 1572872 | tf_op jit(solution)/shard_map/ppermute | solution.py:445
  140.9 15.7 %collective-permute-start.27 = (bf16[2,64,2048]{2,1,0:T(8,128)(2,1)}, bf16[2,64,2048]{2,1,0:T(8,128)(2,1)S(1)}, u32[]{:S(2)}, u32[]{:S(2)}) collective-permute-start(bf16[2,64,2048]{2,1,0:T(8,128)(2,1)} %get-tuple-element.212), channel_id=1, source_target_pairs={{0,1},{1,0},{2,3},{3,2},{4,5},{5,4},{6,7},{7,6},{8,9},{9,8},{10,11... | collective-permute-start | bytes 1572872 | tf_op jit(solution)/shard_map/ppermute | solution.py:463
  142.7 22.6 %collective-permute-start.28 = (bf16[2,64,2048]{2,1,0:T(8,128)(2,1)}, bf16[2,64,2048]{2,1,0:T(8,128)(2,1)}, u32[]{:S(2)}, u32[]{:S(2)}) collective-permute-start(bf16[2,64,2048]{2,1,0:T(8,128)(2,1)} %get-tuple-element.213), channel_id=1, source_target_pairs={{0,2},{1,3},{2,0},{3,1},{4,6},{5,7},{6,4},{7,5},{8,10},{9,11},{10,... | collective-permute-start | bytes 1572872 | tf_op jit(solution)/shard_map/ppermute | solution.py:463
  143.0 24.1 %collective-permute-start.29 = (bf16[2,64,2048]{2,1,0:T(8,128)(2,1)}, bf16[2,64,2048]{2,1,0:T(8,128)(2,1)}, u32[]{:S(2)}, u32[]{:S(2)}) collective-permute-start(bf16[2,64,2048]{2,1,0:T(8,128)(2,1)} %get-tuple-element.214), channel_id=1, source_target_pairs={{0,3},{1,2},{2,1},{3,0},{4,7},{5,6},{6,5},{7,4},{8,11},{9,10},{10,... | collective-permute-start | bytes 1572872 | tf_op jit(solution)/shard_map/ppermute | solution.py:463
  148.3 18.8 %collective-permute-start.31 = (bf16[128,2048]{1,0:T(8,128)(2,1)}, bf16[128,2048]{1,0:T(8,128)(2,1)S(1)}, u32[]{:S(2)}, u32[]{:S(2)}) collective-permute-start(bf16[128,2048]{1,0:T(8,128)(2,1)} %expand.7), channel_id=1, source_target_pairs={{0,4},{1,5},{2,6},{3,7},{4,0},{5,1},{6,2},{7,3},{8,12},{9,13},{10,... | collective-permute-start | bytes 1572872 | tf_op jit(solution)/shard_map/ppermute | solution.py:445
  148.4 2.3 %copy-start.4 = (bf16[3,384,2048]{2,1,0:T(8,128)(2,1)S(1)}, bf16[3,384,2048]{2,1,0:T(8,128)(2,1)}, u32[]{:S(2)}) copy-start(bf16[3,384,2048]{2,1,0:T(8,128)(2,1)} %copy-done.3) | copy-start | bytes 14155780
  153.1 14.0 %copy-start.17 = (bf16[2,64,2048]{2,1,0:T(8,128)(2,1)S(1)}, bf16[2,64,2048]{2,1,0:T(8,128)(2,1)}, u32[]{:S(2)}) copy-start(bf16[2,64,2048]{2,1,0:T(8,128)(2,1)} %copy-done.16) | copy-start | bytes 1572868
  153.1 14.5 %copy-start.15 = (bf16[2,64,2048]{2,1,0:T(8,128)(2,1)S(1)}, bf16[2,64,2048]{2,1,0:T(8,128)(2,1)}, u32[]{:S(2)}) copy-start(bf16[2,64,2048]{2,1,0:T(8,128)(2,1)} %copy-done.14) | copy-start | bytes 1572868
  153.1 16.3 %copy-start.13 = (bf16[2,64,2048]{2,1,0:T(8,128)(2,1)S(1)}, bf16[2,64,2048]{2,1,0:T(8,128)(2,1)}, u32[]{:S(2)}) copy-start(bf16[2,64,2048]{2,1,0:T(8,128)(2,1)} %copy-done.12) | copy-start | bytes 1572868
  156.6 34.4 %copy-start.29 = (bf16[1,64,2048]{2,1,0:T(8,128)(2,1)S(1)}, bf16[1,64,2048]{2,1,0:T(8,128)(2,1)}, u32[]{:S(2)}) copy-start(bf16[1,64,2048]{2,1,0:T(8,128)(2,1)} %copy-done.28) | copy-start | bytes 786436
  156.6 36.0 %copy-start.27 = (bf16[1,64,2048]{2,1,0:T(8,128)(2,1)S(1)}, bf16[1,64,2048]{2,1,0:T(8,128)(2,1)}, u32[]{:S(2)}) copy-start(bf16[1,64,2048]{2,1,0:T(8,128)(2,1)} %copy-done.26) | copy-start | bytes 786436
  156.6 36.7 %copy-start.25 = (bf16[1,64,2048]{2,1,0:T(8,128)(2,1)S(1)}, bf16[1,64,2048]{2,1,0:T(8,128)(2,1)}, u32[]{:S(2)}) copy-start(bf16[1,64,2048]{2,1,0:T(8,128)(2,1)} %copy-done.24) | copy-start | bytes 786436
  167.1 14.9 %collective-permute-start.33 = (bf16[2,64,2048]{2,1,0:T(8,128)(2,1)S(1)}, bf16[2,64,2048]{2,1,0:T(8,128)(2,1)S(1)}, u32[]{:S(2)}, u32[]{:S(2)}) collective-permute-start(bf16[2,64,2048]{2,1,0:T(8,128)(2,1)S(1)} %copy-done.17), channel_id=1, source_target_pairs={{0,1},{1,0},{2,3},{3,2},{4,5},{5,4},{6,7},{7,6},{8,9},{9,8},{10,11... | collective-permute-start | bytes 1572872 | tf_op jit(solution)/shard_map/ppermute | solution.py:463
  167.5 23.5 %collective-permute-start.34 = (bf16[2,64,2048]{2,1,0:T(8,128)(2,1)S(1)}, bf16[2,64,2048]{2,1,0:T(8,128)(2,1)S(1)}, u32[]{:S(2)}, u32[]{:S(2)}) collective-permute-start(bf16[2,64,2048]{2,1,0:T(8,128)(2,1)S(1)} %copy-done.15), channel_id=1, source_target_pairs={{0,2},{1,3},{2,0},{3,1},{4,6},{5,7},{6,4},{7,5},{8,10},{9,11},{10,... | collective-permute-start | bytes 1572872 | tf_op jit(solution)/shard_map/ppermute | solution.py:463
  169.3 21.7 %collective-permute-start.35 = (bf16[2,64,2048]{2,1,0:T(8,128)(2,1)S(1)}, bf16[2,64,2048]{2,1,0:T(8,128)(2,1)S(1)}, u32[]{:S(2)}, u32[]{:S(2)}) collective-permute-start(bf16[2,64,2048]{2,1,0:T(8,128)(2,1)S(1)} %copy-done.13), channel_id=1, source_target_pairs={{0,3},{1,2},{2,1},{3,0},{4,7},{5,6},{6,5},{7,4},{8,11},{9,10},{10,... | collective-permute-start | bytes 1572872 | tf_op jit(solution)/shard_map/ppermute | solution.py:463
  172.5 32.5 %copy-start.23 = (bf16[1,64,2048]{2,1,0:T(8,128)(2,1)S(1)}, bf16[1,64,2048]{2,1,0:T(8,128)(2,1)}, u32[]{:S(2)}) copy-start(bf16[1,64,2048]{2,1,0:T(8,128)(2,1)} %copy-done.22) | copy-start | bytes 786436
  172.5 32.5 %copy-start.21 = (bf16[1,64,2048]{2,1,0:T(8,128)(2,1)S(1)}, bf16[1,64,2048]{2,1,0:T(8,128)(2,1)}, u32[]{:S(2)}) copy-start(bf16[1,64,2048]{2,1,0:T(8,128)(2,1)} %copy-done.20) | copy-start | bytes 786436
  172.5 37.4 %copy-start.19 = (bf16[1,64,2048]{2,1,0:T(8,128)(2,1)S(1)}, bf16[1,64,2048]{2,1,0:T(8,128)(2,1)}, u32[]{:S(2)}) copy-start(bf16[1,64,2048]{2,1,0:T(8,128)(2,1)} %copy-done.18) | copy-start | bytes 786436
  172.5 37.4 %copy-start.11 = (bf16[1,64,2048]{2,1,0:T(8,128)(2,1)S(1)}, bf16[1,64,2048]{2,1,0:T(8,128)(2,1)}, u32[]{:S(2)}) copy-start(bf16[1,64,2048]{2,1,0:T(8,128)(2,1)} %copy-done.10) | copy-start | bytes 786436
  172.6 23.3 %collective-permute-start.39 = (bf16[128,2048]{1,0:T(8,128)(2,1)S(1)}, bf16[128,2048]{1,0:T(8,128)(2,1)S(1)}, u32[]{:S(2)}, u32[]{:S(2)}) collective-permute-start(bf16[128,2048]{1,0:T(8,128)(2,1)S(1)} %get-tuple-element.230), channel_id=1, source_target_pairs={{0,4},{1,5},{2,6},{3,7},{4,8},{5,9},{6,10},{7,11},{8,12},{9,13},{1... | collective-permute-start | bytes 1572872 | tf_op jit(solution)/shard_map/ppermute | solution.py:445
  175.8 20.5 %collective-permute-start.40 = (bf16[128,2048]{1,0:T(8,128)(2,1)S(1)}, bf16[128,2048]{1,0:T(8,128)(2,1)S(1)}, u32[]{:S(2)}, u32[]{:S(2)}) collective-permute-start(bf16[128,2048]{1,0:T(8,128)(2,1)S(1)} %get-tuple-element.231), channel_id=1, source_target_pairs={{0,12},{1,13},{2,14},{3,15},{4,0},{5,1},{6,2},{7,3},{8,4},{9,5},{1... | collective-permute-start | bytes 1572872 | tf_op jit(solution)/shard_map/ppermute | solution.py:445
  191.1 9.0 %collective-permute-start.36 = (bf16[1,64,2048]{2,1,0:T(8,128)(2,1)S(1)}, bf16[1,64,2048]{2,1,0:T(8,128)(2,1)S(1)}, u32[]{:S(2)}, u32[]{:S(2)}) collective-permute-start(bf16[1,64,2048]{2,1,0:T(8,128)(2,1)S(1)} %copy-done.29), channel_id=1, source_target_pairs={{0,1},{1,0},{2,3},{3,2},{4,5},{5,4},{6,7},{7,6},{8,9},{9,8},{10,11... | collective-permute-start | bytes 786440 | tf_op jit(solution)/shard_map/ppermute | solution.py:463
  192.6 9.6 %collective-permute-start.37 = (bf16[1,64,2048]{2,1,0:T(8,128)(2,1)S(1)}, bf16[1,64,2048]{2,1,0:T(8,128)(2,1)S(1)}, u32[]{:S(2)}, u32[]{:S(2)}) collective-permute-start(bf16[1,64,2048]{2,1,0:T(8,128)(2,1)S(1)} %copy-done.27), channel_id=1, source_target_pairs={{0,2},{1,3},{2,0},{3,1},{4,6},{5,7},{6,4},{7,5},{8,10},{9,11},{10,... | collective-permute-start | bytes 786440 | tf_op jit(solution)/shard_map/ppermute | solution.py:463
  193.3 11.7 %collective-permute-start.38 = (bf16[1,64,2048]{2,1,0:T(8,128)(2,1)S(1)}, bf16[1,64,2048]{2,1,0:T(8,128)(2,1)S(1)}, u32[]{:S(2)}, u32[]{:S(2)}) collective-permute-start(bf16[1,64,2048]{2,1,0:T(8,128)(2,1)S(1)} %copy-done.25), channel_id=1, source_target_pairs={{0,3},{1,2},{2,1},{3,0},{4,7},{5,6},{6,5},{7,4},{8,11},{9,10},{10,... | collective-permute-start | bytes 786440 | tf_op jit(solution)/shard_map/ppermute | solution.py:463
  196.3 20.8 %collective-permute-start.44 = (bf16[128,2048]{1,0:T(8,128)(2,1)S(1)}, bf16[128,2048]{1,0:T(8,128)(2,1)S(1)}, u32[]{:S(2)}, u32[]{:S(2)}) collective-permute-start(bf16[128,2048]{1,0:T(8,128)(2,1)S(1)} %get-tuple-element.237), channel_id=1, source_target_pairs={{0,4},{1,5},{2,6},{3,7},{4,8},{5,9},{6,10},{7,11},{8,12},{9,13},{1... | collective-permute-start | bytes 1572872 | tf_op jit(solution)/shard_map/ppermute | solution.py:445
  200.1 21.4 %collective-permute-start.45 = (bf16[128,2048]{1,0:T(8,128)(2,1)S(1)}, bf16[128,2048]{1,0:T(8,128)(2,1)S(1)}, u32[]{:S(2)}, u32[]{:S(2)}) collective-permute-start(bf16[128,2048]{1,0:T(8,128)(2,1)S(1)} %get-tuple-element.238), channel_id=1, source_target_pairs={{0,12},{1,13},{2,14},{3,15},{4,0},{5,1},{6,2},{7,3},{8,4},{9,5},{1... | collective-permute-start | bytes 1572872 | tf_op jit(solution)/shard_map/ppermute | solution.py:445
  205.0 6.7 %collective-permute-start.41 = (bf16[1,64,2048]{2,1,0:T(8,128)(2,1)S(1)}, bf16[1,64,2048]{2,1,0:T(8,128)(2,1)S(1)}, u32[]{:S(2)}, u32[]{:S(2)}) collective-permute-start(bf16[1,64,2048]{2,1,0:T(8,128)(2,1)S(1)} %copy-done.23), channel_id=1, source_target_pairs={{0,1},{1,0},{2,3},{3,2},{4,5},{5,4},{6,7},{7,6},{8,9},{9,8},{10,11... | collective-permute-start | bytes 786440 | tf_op jit(solution)/shard_map/ppermute | solution.py:463
  205.1 11.5 %collective-permute-start.42 = (bf16[1,64,2048]{2,1,0:T(8,128)(2,1)S(1)}, bf16[1,64,2048]{2,1,0:T(8,128)(2,1)S(1)}, u32[]{:S(2)}, u32[]{:S(2)}) collective-permute-start(bf16[1,64,2048]{2,1,0:T(8,128)(2,1)S(1)} %copy-done.21), channel_id=1, source_target_pairs={{0,2},{1,3},{2,0},{3,1},{4,6},{5,7},{6,4},{7,5},{8,10},{9,11},{10,... | collective-permute-start | bytes 786440 | tf_op jit(solution)/shard_map/ppermute | solution.py:463
  209.9 7.3 %collective-permute-start.43 = (bf16[1,64,2048]{2,1,0:T(8,128)(2,1)S(1)}, bf16[1,64,2048]{2,1,0:T(8,128)(2,1)S(1)}, u32[]{:S(2)}, u32[]{:S(2)}) collective-permute-start(bf16[1,64,2048]{2,1,0:T(8,128)(2,1)S(1)} %copy-done.19), channel_id=1, source_target_pairs={{0,3},{1,2},{2,1},{3,0},{4,7},{5,6},{6,5},{7,4},{8,11},{9,10},{10,... | collective-permute-start | bytes 786440 | tf_op jit(solution)/shard_map/ppermute | solution.py:463
  (14 other events, 20.3 us)

commit v4 on v3

--- a/solution.py
+++ b/solution.py
@@ -132,14 +132,10 @@
     table_ref, turned_ref, *out_refs = refs
     rows, width = tokens_ref.shape
     gates = gates_ref[...]
-    high = gates.astype(BF)
-    low = (gates - high.astype(F32)).astype(BF)
-    lane = lax.broadcasted_iota(jnp.int32, (picks, 128), 1)
-    row = lax.broadcasted_iota(jnp.int32, (picks, 128), 0)
-    meta = jnp.zeros((rows, 128), F32)
-    for n, part in enumerate((routes_ref[...].astype(F32).astype(BF), high, low)):
-        place = jnp.where(lane == row + n * picks, 1.0, 0.0).astype(BF)
-        meta += jnp.dot(part, place, preferred_element_type=F32)
+    high = gates.astype(BF).astype(F32)
+    low = (gates - high).astype(BF).astype(F32)
+    beside = [routes_ref[...].astype(F32), high, low, jnp.zeros((128 - 3 * picks, rows), F32)]
+    meta = jnp.concatenate(beside, axis=0).T
     block_ref[:, :width] = tokens_ref[...]
     block_ref[:, width:] = meta.astype(BF)
     write_tables(ids_ref, meta, table_ref, turned_ref, 0, picks, capacity)
@@ -168,9 +164,9 @@
         in_specs=[pl.BlockSpec(memory_space=pltpu.SMEM)]
         + [pl.BlockSpec(memory_space=pltpu.VMEM)] * 4,
         out_shape=[jax.ShapeDtypeStruct(s, BF) for s in shapes],
-        compiler_params=pltpu.CompilerParams(vmem_limit_bytes=28 << 20),
+        compiler_params=pltpu.CompilerParams(vmem_limit_bytes=16 << 20),
         name="start_rows",
-    )(ids, tokens, routes, gates, cotangent)
+    )(ids, tokens, routes.T, gates.T, cotangent)
     return block, table, turned, out
 
 
@@ -203,7 +199,7 @@
         in_specs=[pl.BlockSpec(memory_space=pltpu.SMEM)] + spec,
         out_specs=[pl.BlockSpec(s, lambda i, d=len(s): (0,) * d) for s in shapes],
         out_shape=[jax.ShapeDtypeStruct(s, BF) for s in shapes],
-        compiler_params=pltpu.CompilerParams(vmem_limit_bytes=28 << 20),
+        compiler_params=pltpu.CompilerParams(vmem_limit_bytes=16 << 20),
         name="token_rows",
     )(ids, *blocks, *blocks)
     return table, turned, out
@@ -229,7 +225,7 @@
         in_specs=[pl.BlockSpec(memory_space=pltpu.SMEM)]
         + [pl.BlockSpec(memory_space=pltpu.VMEM)] * (1 + len(blocks)),
         out_shape=[jax.ShapeDtypeStruct(s, BF) for s in shapes],
-        compiler_params=pltpu.CompilerParams(vmem_limit_bytes=28 << 20),
+        compiler_params=pltpu.CompilerParams(vmem_limit_bytes=16 << 20),
         name="cot_rows",
     )(ids, table, *blocks)
 
@@ -261,7 +257,7 @@
         in_specs=[pl.BlockSpec(memory_space=pltpu.SMEM)]
         + [pl.BlockSpec(memory_space=pltpu.VMEM)] * (1 + len(rows) + len(extras)),
         out_shape=[jax.ShapeDtypeStruct((rows_dev, width), BF)] * blocks,
-        compiler_params=pltpu.CompilerParams(vmem_limit_bytes=28 << 20),
+        compiler_params=pltpu.CompilerParams(vmem_limit_bytes=16 << 20),
         cost_estimate=pl.CostEstimate(flops=work, bytes_accessed=moved, transcendentals=0),
         name="expand",
     )(jnp.zeros((2,), jnp.int32) if flags is None else flags, turned, *rows, *extras)
@@ -305,7 +301,7 @@
             jax.ShapeDtypeStruct((total, width), BF),
         ]
         + [jax.ShapeDtypeStruct((count, capacity, width), BF)] * PLANE,
-        compiler_params=pltpu.CompilerParams(vmem_limit_bytes=36 << 20),
+        compiler_params=pltpu.CompilerParams(vmem_limit_bytes=24 << 20),
         cost_estimate=pl.CostEstimate(
             flops=6 * total * width * inner,
             bytes_accessed=6 * width * inner + 6 * total * width + 10 * total * inner,
@@ -349,7 +345,7 @@
             jax.ShapeDtypeStruct((total, width), BF),
         ]
         + [jax.ShapeDtypeStruct((count, capacity, width), BF)] * PLANE,
-        compiler_params=pltpu.CompilerParams(vmem_limit_bytes=36 << 20),
+        compiler_params=pltpu.CompilerParams(vmem_limit_bytes=24 << 20),
         cost_estimate=pl.CostEstimate(
             flops=6 * total * width * inner,
             bytes_accessed=6 * width * inner + 6 * total * width + 12 * total * inner,
@@ -384,8 +380,8 @@
         in_specs=[pl.BlockSpec(a.shape, lambda i: (0, 0)) for a in small]
         + [pl.BlockSpec((a.shape[0], tile), lambda i: (0, i)) for a in large],
         out_specs=pl.BlockSpec((3, inner, tile), lambda i: (0, 0, i)),
-        out_shape=jax.ShapeDtypeStruct((3, inner, width), BF),
-        compiler_params=pltpu.CompilerParams(vmem_limit_bytes=36 << 20),
+        out_shape=pltpu.HBM((3, inner, width), BF),
+        compiler_params=pltpu.CompilerParams(vmem_limit_bytes=24 << 20),
         cost_estimate=pl.CostEstimate(
             flops=6 * total * inner * width,
             bytes_accessed=6 * total * inner + 4 * total * width + 6 * inner * width,
@@ -419,7 +415,7 @@
             jax.ShapeDtypeStruct((1, width, inner), BF),
             jax.ShapeDtypeStruct((1, inner, width), BF),
         ],
-        compiler_params=pltpu.CompilerParams(vmem_limit_bytes=28 << 20),
+        compiler_params=pltpu.CompilerParams(vmem_limit_bytes=16 << 20),
         cost_estimate=pl.CostEstimate(
             flops=6 * inner * width,
             bytes_accessed=6 * inner * width * (1 + len(sums)),

time: 227 us -> 225 us (level)
  starting transfers between devices: 52.1 us -> 49.6 us
    ppermute x12, waiting for transfers between devices: 45.8 us -> 49 us  [permute(): return lax.ppermute(value, 'expert', pairs)]
    unnamed x66 -> x62, local copies, waits for them, and re-layouts: 16.3 us -> 14.7 us
  transfers between devices with their start and end apart: 46 -> 46, of which waited for: 21 -> 20; matrix products, arithmetic and copies ran while one was open for 0% -> 0% of each run, Pallas kernels for 18% -> 19%
where the time goes in v4:
time: 225 us; the launch traced here: 221 us
  waiting for transfers between devices  111 us (49%)
  starting transfers between devices  49.6 us (22%)
  Pallas kernels  44.5 us (20%)
  local copies, waits for them, and re-layouts  14.8 us (7%)
    ppermute x33, waiting for transfers between devices, across(): lax.ppermute(sent[k - 1], 'expert', [(i, i ^ k) for i in range(experts)])  62.2 us
    ppermute x12, waiting for transfers between devices, permute(): return lax.ppermute(value, 'expert', pairs)  49 us
    ppermute x33, starting transfers between devices, across(): lax.ppermute(sent[k - 1], 'expert', [(i, i ^ k) for i in range(experts)])  38.6 us
    unnamed x62, local copies, waits for them, and re-layouts  14.7 us
    ppermute x12, starting transfers between devices, permute(): return lax.ppermute(value, 'expert', pairs)  10.9 us
    pallas_call x6, Pallas kernels, expand(): pl.pallas_call(functools.partial(expand_kernel, blocks=blocks, extras=len...  9.97 us
    pallas_call x3, Pallas kernels, forward(): pl.pallas_call(functools.partial(forward_kernel, first=capacity), out_sha...  8.23 us
    pallas_call x3, Pallas kernels, backward(): pl.pallas_call(functools.partial(backward_kernel, skip=skip), out_shape=[...  7.88 us
  transfers between devices with their start and end apart: 46, of which 20 were waited for; matrix products, arithmetic and copies ran while one was open for 0% of the time, Pallas kernels for 19%

profile of v4, /device:TPU:14, one launch (start us, length us, event | category | flops | bytes accessed | tf_op | source)
XLA Modules:
  0.0 221.2 jit_solution(15329083543153521214)
XLA Ops:
  4.2 1.7 start_rows.1
  6.4 1.6 collective-permute-start.4
  9.0 2.4 %collective-permute-start.2 = (bf16[1,128,2048]{2,1,0:T(8,128)(2,1)S(1)}, bf16[1,128,2048]{2,1,0:T(8,128)(2,1)S(1)}, u32[]{:S(2)}, u32[]{:S(2)}) collective-permute-start(bf16[1,128,2048]{2,1,0:T(8,128)(2,1)S(1)} %get-tuple-element.126), channel_id=1, source_target_pairs={{0,3},{1,2},{2,1},{3,0},{4,7},{5,6},{6,5},{7,4},{8,11},{9,10},{10,... | collective-permute-start | bytes 1572872 | tf_op jit(solution)/shard_map/ppermute | solution.py:459
  11.5 9.0 %collective-permute-done.3.refs_0_.refs_2_ = bf16[128,2176]{1,0:T(8,128)(2,1)S(1)} collective-permute-done((bf16[128,2176]{1,0:T(8,128)(2,1)S(1)}, bf16[128,2176]{1,0:T(8,128)(2,1)S(1)}, u32[]{:S(2)}, u32[]{:S(2)}) %collective-permute-start.3) | collective-permute-done | bytes 557088 | tf_op jit(solution)/shard_map/ppermute | solution.py:441
  20.4 13.9 %collective-permute-done.4.refs_1_.refs_3_ = bf16[128,2176]{1,0:T(8,128)(2,1)S(1)} collective-permute-done((bf16[128,2176]{1,0:T(8,128)(2,1)S(1)}, bf16[128,2176]{1,0:T(8,128)(2,1)S(1)}, u32[]{:S(2)}, u32[]{:S(2)}) %collective-permute-start.4) | collective-permute-done | bytes 557088 | tf_op jit(solution)/shard_map/ppermute | solution.py:441
  34.3 1.6 token_rows.2
  37.5 2.4 %collective-permute-start.10 = (bf16[2,64,2048]{2,1,0:T(8,128)(2,1)S(1)}, bf16[2,64,2048]{2,1,0:T(8,128)(2,1)S(1)}, u32[]{:S(2)}, u32[]{:S(2)}) collective-permute-start(bf16[2,64,2048]{2,1,0:T(8,128)(2,1)S(1)} %get-tuple-element.148), channel_id=1, source_target_pairs={{0,3},{1,2},{2,1},{3,0},{4,7},{5,6},{6,5},{7,4},{8,11},{9,10},{10,... | collective-permute-start | bytes 1572872 | tf_op jit(solution)/shard_map/ppermute | solution.py:459
  40.0 9.6 %collective-permute-done.5.refs_0_.refs_1_ = bf16[128,2176]{1,0:T(8,128)(2,1)S(1)} collective-permute-done((bf16[128,2176]{1,0:T(8,128)(2,1)S(1)}, bf16[128,2176]{1,0:T(8,128)(2,1)S(1)}, u32[]{:S(2)}, u32[]{:S(2)}) %collective-permute-start.5) | collective-permute-done | bytes 557088 | tf_op jit(solution)/shard_map/ppermute | solution.py:441
  49.9 1.7 collective-permute-start.7
  51.6 1.2 token_rows.3
  52.8 7.7 %collective-permute-done.9.refs_2_ = bf16[2,64,2048]{2,1,0:T(8,128)(2,1)S(1)} collective-permute-done((bf16[2,64,2048]{2,1,0:T(8,128)(2,1)S(1)}, bf16[2,64,2048]{2,1,0:T(8,128)(2,1)S(1)}, u32[]{:S(2)}, u32[]{:S(2)}) %collective-permute-start.9) | collective-permute-done | bytes 524320 | tf_op jit(solution)/shard_map/ppermute | solution.py:459
  60.5 1.5 collective-permute-start.11
  62.5 1.5 collective-permute-start.13
  64.0 8.7 %collective-permute-done.6.refs_0_ = bf16[128,2048]{1,0:T(8,128)(2,1)S(1)} collective-permute-done((bf16[128,2048]{1,0:T(8,128)(2,1)S(1)}, bf16[128,2048]{1,0:T(8,128)(2,1)S(1)}, u32[]{:S(2)}, u32[]{:S(2)}) %collective-permute-start.6) | collective-permute-done | bytes 524320 | tf_op jit(solution)/shard_map/ppermute | solution.py:441
  72.7 1.8 cot_rows.2
  75.7 2.5 %collective-permute-start.16 = (bf16[2,64,2048]{2,1,0:T(8,128)(2,1)S(1)}, bf16[2,64,2048]{2,1,0:T(8,128)(2,1)S(1)}, u32[]{:S(2)}, u32[]{:S(2)}) collective-permute-start(bf16[2,64,2048]{2,1,0:T(8,128)(2,1)S(1)} %get-tuple-element.154), channel_id=1, source_target_pairs={{0,3},{1,2},{2,1},{3,0},{4,7},{5,6},{6,5},{7,4},{8,11},{9,10},{10,... | collective-permute-start | bytes 1572872 | tf_op jit(solution)/shard_map/ppermute | solution.py:459
  78.5 1.9 expert_forward.3
  81.9 2.0 expert_backward.4
  86.0 4.5 %expert_forward.4 = (f32[512,384]{1,0:T(8,128)S(1)}, f32[512,384]{1,0:T(8,128)S(1)}, bf16[384,512]{1,0:T(8,128)(2,1)S(1)}, bf16[512,2048]{1,0:T(8,128)(2,1)S(1)}...) custom-call(bf16[2,64,2048]{2,1,0:T(8,128)(2,1)S(1)} %get-tuple-elem, ...), custom_call_target="tpu_custom_call" | custom-call | flops 2415919104 | bytes 12976128 | tf_op jit(solution)/shard_map/expert_forward/pallas_call | solution.py:295
  90.5 1.9 expert_forward.5
  92.4 1.2 cot_rows.3
  93.6 4.7 %collective-permute-done.15.refs_2_ = bf16[2,64,2048]{2,1,0:T(8,128)(2,1)S(1)} collective-permute-done((bf16[2,64,2048]{2,1,0:T(8,128)(2,1)S(1)}, bf16[2,64,2048]{2,1,0:T(8,128)(2,1)S(1)}, u32[]{:S(2)}, u32[]{:S(2)}) %collective-permute-start.15) | collective-permute-done | bytes 524320 | tf_op jit(solution)/shard_map/ppermute | solution.py:459
  98.3 1.5 collective-permute-start.18
  100.3 1.5 collective-permute-start.20
  101.8 3.9 %expert_backward.3 = (bf16[384,512]{1,0:T(8,128)(2,1)S(1)}, bf16[384,512]{1,0:T(8,128)(2,1)S(1)}, bf16[512,2048]{1,0:T(8,128)(2,1)S(1)}, bf16[2,64,2048]{2,1,0:T...) custom-call(bf16[2,64,2048]{2,1,0:T(8,128)(2,1)S(1)} %get-tuple-elem, ...), custom_call_target="tpu_custom_call" | custom-call | flops 2415919104 | bytes 13369344 | tf_op jit(solution)/shard_map/expert_backward/pallas_call | solution.py:340
  106.6 3.3 %collective-permute-done.19.refs_2_ = bf16[1,64,2048]{2,1,0:T(8,128)(2,1)S(1)} collective-permute-done((bf16[1,64,2048]{2,1,0:T(8,128)(2,1)S(1)}, bf16[1,64,2048]{2,1,0:T(8,128)(2,1)S(1)}, u32[]{:S(2)}, u32[]{:S(2)}) %collective-permute-start.19) | collective-permute-done | bytes 262176 | tf_op jit(solution)/shard_map/ppermute | solution.py:459
  109.9 1.8 collective-permute-done.20.refs_3_
  111.7 1.9 collective-permute-start.22
  113.6 1.6 collective-permute-start.23
  115.2 2.0 expert_backward.5
  117.2 7.4 %partial_sums.1.refs_0_ = bf16[3,384,2048]{2,1,0:T(8,128)(2,1)} custom-call(bf16[384,256]{1,0:T(8,128)(2,1)S(1)} %get-tuple-element.172.refs_0_, bf16[384,512]{1,0:T(8,128)(2,1)S(1)} %get-tuple-element.174.refs_1_, bf16[384,256]{1,0:T(8,128)(2,1)S(1)} %get-tuple-element.180.refs_2_, bf16[384,256]{1,0:T(8,128)(2,1)S(1)} %get-tuple-element.186.refs_3_, ...), custom_call_target="tpu_custom_call" | custom-call | flops 4831838208 | bytes 15466496 | tf_op jit(solution)/shard_map/partial_sums/pallas_call | solution.py:377
  124.8 1.9 collective-permute-start.25
  126.6 1.6 collective-permute-start.26
  128.2 1.8 expand.6
  130.0 3.8 %collective-permute-done.24.refs_1_ = bf16[1,64,2048]{2,1,0:T(8,128)(2,1)S(1)} collective-permute-done((bf16[1,64,2048]{2,1,0:T(8,128)(2,1)S(1)}, bf16[1,64,2048]{2,1,0:T(8,128)(2,1)S(1)}, u32[]{:S(2)}, u32[]{:S(2)}) %collective-permute-start.24) | collective-permute-done | bytes 262176 | tf_op jit(solution)/shard_map/ppermute | solution.py:459
  133.8 5.2 %collective-permute-done.25.refs_2_ = bf16[1,64,2048]{2,1,0:T(8,128)(2,1)S(1)} collective-permute-done((bf16[1,64,2048]{2,1,0:T(8,128)(2,1)S(1)}, bf16[1,64,2048]{2,1,0:T(8,128)(2,1)S(1)}, u32[]{:S(2)}, u32[]{:S(2)}) %collective-permute-start.25) | collective-permute-done | bytes 262176 | tf_op jit(solution)/shard_map/ppermute | solution.py:459
  139.0 1.8 collective-permute-start.27
  141.0 1.4 collective-permute-start.29
  142.5 1.7 expand.7
  144.1 2.2 %copy-done.4 = bf16[3,384,2048]{2,1,0:T(8,128)(2,1)} copy-done((bf16[3,384,2048]{2,1,0:T(8,128)(2,1)}, bf16[3,384,2048]{2,1,0:T(8,128)(2,1)S(1)}, u32[]{:S(2)}) %copy-start.4) | copy-done | bytes 4718616
  146.4 2.3 %copy-done.3 = bf16[3,384,2048]{2,1,0:T(8,128)(2,1)S(1)} copy-done((bf16[3,384,2048]{2,1,0:T(8,128)(2,1)S(1)}, bf16[3,384,2048]{2,1,0:T(8,128)(2,1)}, u32[]{:S(2)}) %copy-start.3) | copy-done | bytes 4718616
  148.8 2.3 %copy-done.5 = bf16[3,384,2048]{2,1,0:T(8,128)(2,1)S(1)} copy-done((bf16[3,384,2048]{2,1,0:T(8,128)(2,1)S(1)}, bf16[3,384,2048]{2,1,0:T(8,128)(2,1)}, u32[]{:S(2)}) %copy-start.5) | copy-done | bytes 4718616
  151.1 3.6 %weight_outputs.1 = (bf16[1,2048,384]{2,1,0:T(8,128)(2,1)}, bf16[1,2048,384]{2,1,0:T(8,128)(2,1)}, bf16[1,384,2048]{2,1,0:T(8,128)(2,1)}) custom-call(bf16[3,384,2048]{2,1,0:T(8,128)(2,1)S(1)} %copy-done.3, bf16[3,384,2048]{2,1,0:T(8,128)(2,1)S(1)} %copy-done.5), custom_call_target="tpu_custom_call" | custom-call | flops 4718592 | bytes 14155776 | tf_op jit(solution)/shard_map/weight_outputs/pallas_call | solution.py:404
  154.7 10.4 %collective-permute-done.28.refs_2_ = bf16[2,64,2048]{2,1,0:T(8,128)(2,1)} collective-permute-done((bf16[2,64,2048]{2,1,0:T(8,128)(2,1)}, bf16[2,64,2048]{2,1,0:T(8,128)(2,1)}, u32[]{:S(2)}, u32[]{:S(2)}) %collective-permute-start.28) | collective-permute-done | bytes 524320 | tf_op jit(solution)/shard_map/ppermute | solution.py:459
  165.7 1.7 collective-permute-start.34
  167.4 1.3 collective-permute-start.35
  168.7 1.9 expand.8
  170.7 3.2 %collective-permute-start.39 = (bf16[128,2048]{1,0:T(8,128)(2,1)S(1)}, bf16[128,2048]{1,0:T(8,128)(2,1)S(1)}, u32[]{:S(2)}, u32[]{:S(2)}) collective-permute-start(bf16[128,2048]{1,0:T(8,128)(2,1)S(1)} %get-tuple-element.230), channel_id=1, source_target_pairs={{0,4},{1,5},{2,6},{3,7},{4,8},{5,9},{6,10},{7,11},{8,12},{9,13},{1... | collective-permute-start | bytes 1572872 | tf_op jit(solution)/shard_map/ppermute | solution.py:441
  173.9 6.2 %collective-permute-done.33.refs_1_ = bf16[2,64,2048]{2,1,0:T(8,128)(2,1)S(1)} collective-permute-done((bf16[2,64,2048]{2,1,0:T(8,128)(2,1)S(1)}, bf16[2,64,2048]{2,1,0:T(8,128)(2,1)S(1)}, u32[]{:S(2)}, u32[]{:S(2)}) %collective-permute-start.33) | collective-permute-done | bytes 524320 | tf_op jit(solution)/shard_map/ppermute | solution.py:459
  180.1 8.8 %collective-permute-done.34.refs_2_ = bf16[2,64,2048]{2,1,0:T(8,128)(2,1)S(1)} collective-permute-done((bf16[2,64,2048]{2,1,0:T(8,128)(2,1)S(1)}, bf16[2,64,2048]{2,1,0:T(8,128)(2,1)S(1)}, u32[]{:S(2)}, u32[]{:S(2)}) %collective-permute-start.34) | collective-permute-done | bytes 524320 | tf_op jit(solution)/shard_map/ppermute | solution.py:459
  188.8 1.7 collective-permute-start.36
  190.7 1.6 collective-permute-start.38
  192.3 1.0 expand.10
  193.4 1.1 collective-permute-done.40.refs_5_
  194.4 2.7 %collective-permute-start.44 = (bf16[128,2048]{1,0:T(8,128)(2,1)S(1)}, bf16[128,2048]{1,0:T(8,128)(2,1)S(1)}, u32[]{:S(2)}, u32[]{:S(2)}) collective-permute-start(bf16[128,2048]{1,0:T(8,128)(2,1)S(1)} %get-tuple-element.237), channel_id=1, source_target_pairs={{0,4},{1,5},{2,6},{3,7},{4,8},{5,9},{6,10},{7,11},{8,12},{9,13},{1... | collective-permute-start | bytes 1572872 | tf_op jit(solution)/shard_map/ppermute | solution.py:441
  197.2 2.9 %collective-permute-done.37.refs_2_ = bf16[1,64,2048]{2,1,0:T(8,128)(2,1)S(1)} collective-permute-done((bf16[1,64,2048]{2,1,0:T(8,128)(2,1)S(1)}, bf16[1,64,2048]{2,1,0:T(8,128)(2,1)S(1)}, u32[]{:S(2)}, u32[]{:S(2)}) %collective-permute-start.37) | collective-permute-done | bytes 262176 | tf_op jit(solution)/shard_map/ppermute | solution.py:459
  200.1 2.2 %collective-permute-done.38.refs_3_ = bf16[1,64,2048]{2,1,0:T(8,128)(2,1)S(1)} collective-permute-done((bf16[1,64,2048]{2,1,0:T(8,128)(2,1)S(1)}, bf16[1,64,2048]{2,1,0:T(8,128)(2,1)S(1)}, u32[]{:S(2)}, u32[]{:S(2)}) %collective-permute-start.38) | collective-permute-done | bytes 262176 | tf_op jit(solution)/shard_map/ppermute | solution.py:459
  202.4 1.7 collective-permute-start.42
  204.1 1.8 collective-permute-start.43
  205.9 1.8 expand.9
  207.7 1.1 collective-permute-done.41.refs_1_
  208.7 4.0 %collective-permute-done.42.refs_2_ = bf16[1,64,2048]{2,1,0:T(8,128)(2,1)S(1)} collective-permute-done((bf16[1,64,2048]{2,1,0:T(8,128)(2,1)S(1)}, bf16[1,64,2048]{2,1,0:T(8,128)(2,1)S(1)}, u32[]{:S(2)}, u32[]{:S(2)}) %collective-permute-start.42) | collective-permute-done | bytes 262176 | tf_op jit(solution)/shard_map/ppermute | solution.py:459
  212.7 6.8 %collective-permute-done.45.refs_5_ = bf16[128,2048]{1,0:T(8,128)(2,1)S(1)} collective-permute-done((bf16[128,2048]{1,0:T(8,128)(2,1)S(1)}, bf16[128,2048]{1,0:T(8,128)(2,1)S(1)}, u32[]{:S(2)}, u32[]{:S(2)}) %collective-permute-start.45) | collective-permute-done | bytes 524320 | tf_op jit(solution)/shard_map/ppermute | solution.py:441
  219.5 1.7 expand.11
  (112 shorter events, 15.4 us)
Async XLA Ops:
  4.2 45.3 %copy-start.8 = (bf16[128,2048]{1,0:T(8,128)(2,1)S(1)}, bf16[128,2048]{1,0:T(8,128)(2,1)}, u32[]{:S(2)}) copy-start(bf16[128,2048]{1,0:T(8,128)(2,1)} %cot_ref.1) | copy-start | bytes 1572868
  5.9 14.6 %collective-permute-start.3 = (bf16[128,2176]{1,0:T(8,128)(2,1)S(1)}, bf16[128,2176]{1,0:T(8,128)(2,1)S(1)}, u32[]{:S(2)}, u32[]{:S(2)}) collective-permute-start(bf16[128,2176]{1,0:T(8,128)(2,1)S(1)} %get-tuple-element.131), channel_id=1, source_target_pairs={{0,12},{1,13},{2,14},{3,15},{4,0},{5,1},{6,2},{7,3},{8,4},{9,5},{1... | collective-permute-start | bytes 1671176 | tf_op jit(solution)/shard_map/ppermute | solution.py:441
  6.4 27.9 %collective-permute-start.4 = (bf16[128,2176]{1,0:T(8,128)(2,1)S(1)}, bf16[128,2176]{1,0:T(8,128)(2,1)S(1)}, u32[]{:S(2)}, u32[]{:S(2)}) collective-permute-start(bf16[128,2176]{1,0:T(8,128)(2,1)S(1)} %get-tuple-element.131), channel_id=1, source_target_pairs={{0,4},{1,5},{2,6},{3,7},{4,8},{5,9},{6,10},{7,11},{8,12},{9,13},{1... | collective-permute-start | bytes 1671176 | tf_op jit(solution)/shard_map/ppermute | solution.py:441
  8.0 28.4 %collective-permute-start = (bf16[1,128,2048]{2,1,0:T(8,128)(2,1)S(1)}, bf16[1,128,2048]{2,1,0:T(8,128)(2,1)S(1)}, u32[]{:S(2)}, u32[]{:S(2)}) collective-permute-start(bf16[1,128,2048]{2,1,0:T(8,128)(2,1)S(1)} %get-tuple-element.124), channel_id=1, source_target_pairs={{0,1},{1,0},{2,3},{3,2},{4,5},{5,4},{6,7},{7,6},{8,9},{9,8},{10,11... | collective-permute-start | bytes 1572872 | tf_op jit(solution)/shard_map/ppermute | solution.py:459
  8.5 27.9 %collective-permute-start.1 = (bf16[1,128,2048]{2,1,0:T(8,128)(2,1)S(1)}, bf16[1,128,2048]{2,1,0:T(8,128)(2,1)S(1)}, u32[]{:S(2)}, u32[]{:S(2)}) collective-permute-start(bf16[1,128,2048]{2,1,0:T(8,128)(2,1)S(1)} %get-tuple-element.125), channel_id=1, source_target_pairs={{0,2},{1,3},{2,0},{3,1},{4,6},{5,7},{6,4},{7,5},{8,10},{9,11},{10,... | collective-permute-start | bytes 1572872 | tf_op jit(solution)/shard_map/ppermute | solution.py:459
  9.0 27.4 %collective-permute-start.2 = (bf16[1,128,2048]{2,1,0:T(8,128)(2,1)S(1)}, bf16[1,128,2048]{2,1,0:T(8,128)(2,1)S(1)}, u32[]{:S(2)}, u32[]{:S(2)}) collective-permute-start(bf16[1,128,2048]{2,1,0:T(8,128)(2,1)S(1)} %get-tuple-element.126), channel_id=1, source_target_pairs={{0,3},{1,2},{2,1},{3,0},{4,7},{5,6},{6,5},{7,4},{8,11},{9,10},{10,... | collective-permute-start | bytes 1572872 | tf_op jit(solution)/shard_map/ppermute | solution.py:459
  34.3 44.2 %copy-start.1 = (bf16[1,2048,384]{2,1,0:T(8,128)(2,1)S(1)}, bf16[1,2048,384]{2,1,0:T(8,128)(2,1)}, u32[]{:S(2)}) copy-start(bf16[1,2048,384]{2,1,0:T(8,128)(2,1)} %param.12) | copy-start | bytes 4718596
  34.3 44.2 %copy-start.2 = (bf16[1,384,2048]{2,1,0:T(8,128)(2,1)S(1)}, bf16[1,384,2048]{2,1,0:T(8,128)(2,1)}, u32[]{:S(2)}) copy-start(bf16[1,384,2048]{2,1,0:T(8,128)(2,1)} %param.13) | copy-start | bytes 4718596
  35.9 42.6 %copy-start = (bf16[1,2048,384]{2,1,0:T(8,128)(2,1)S(1)}, bf16[1,2048,384]{2,1,0:T(8,128)(2,1)}, u32[]{:S(2)}) copy-start(bf16[1,2048,384]{2,1,0:T(8,128)(2,1)} %param.11) | copy-start | bytes 4718596
  36.0 13.6 %collective-permute-start.5 = (bf16[128,2176]{1,0:T(8,128)(2,1)S(1)}, bf16[128,2176]{1,0:T(8,128)(2,1)S(1)}, u32[]{:S(2)}, u32[]{:S(2)}) collective-permute-start(bf16[128,2176]{1,0:T(8,128)(2,1)S(1)} %get-tuple-element.133), channel_id=1, source_target_pairs={{0,4},{1,5},{2,6},{3,7},{4,0},{5,1},{6,2},{7,3},{8,12},{9,13},{10,... | collective-permute-start | bytes 1671176 | tf_op jit(solution)/shard_map/ppermute | solution.py:441
  36.4 16.3 %collective-permute-start.8 = (bf16[2,64,2048]{2,1,0:T(8,128)(2,1)S(1)}, bf16[2,64,2048]{2,1,0:T(8,128)(2,1)S(1)}, u32[]{:S(2)}, u32[]{:S(2)}) collective-permute-start(bf16[2,64,2048]{2,1,0:T(8,128)(2,1)S(1)} %get-tuple-element.146), channel_id=1, source_target_pairs={{0,1},{1,0},{2,3},{3,2},{4,5},{5,4},{6,7},{7,6},{8,9},{9,8},{10,11... | collective-permute-start | bytes 1572872 | tf_op jit(solution)/shard_map/ppermute | solution.py:459
  37.0 23.5 %collective-permute-start.9 = (bf16[2,64,2048]{2,1,0:T(8,128)(2,1)S(1)}, bf16[2,64,2048]{2,1,0:T(8,128)(2,1)S(1)}, u32[]{:S(2)}, u32[]{:S(2)}) collective-permute-start(bf16[2,64,2048]{2,1,0:T(8,128)(2,1)S(1)} %get-tuple-element.147), channel_id=1, source_target_pairs={{0,2},{1,3},{2,0},{3,1},{4,6},{5,7},{6,4},{7,5},{8,10},{9,11},{10,... | collective-permute-start | bytes 1572872 | tf_op jit(solution)/shard_map/ppermute | solution.py:459
  37.5 23.0 %collective-permute-start.10 = (bf16[2,64,2048]{2,1,0:T(8,128)(2,1)S(1)}, bf16[2,64,2048]{2,1,0:T(8,128)(2,1)S(1)}, u32[]{:S(2)}, u32[]{:S(2)}) collective-permute-start(bf16[2,64,2048]{2,1,0:T(8,128)(2,1)S(1)} %get-tuple-element.148), channel_id=1, source_target_pairs={{0,3},{1,2},{2,1},{3,0},{4,7},{5,6},{6,5},{7,4},{8,11},{9,10},{10,... | collective-permute-start | bytes 1572872 | tf_op jit(solution)/shard_map/ppermute | solution.py:459
  49.6 23.1 %collective-permute-start.6 = (bf16[128,2048]{1,0:T(8,128)(2,1)S(1)}, bf16[128,2048]{1,0:T(8,128)(2,1)S(1)}, u32[]{:S(2)}, u32[]{:S(2)}) collective-permute-start(bf16[128,2048]{1,0:T(8,128)(2,1)S(1)} %copy-done.8), channel_id=1, source_target_pairs={{0,12},{1,13},{2,14},{3,15},{4,0},{5,1},{6,2},{7,3},{8,4},{9,5},{1... | collective-permute-start | bytes 1572872 | tf_op jit(solution)/shard_map/ppermute | solution.py:441
  49.9 22.8 %collective-permute-start.7 = (bf16[128,2048]{1,0:T(8,128)(2,1)S(1)}, bf16[128,2048]{1,0:T(8,128)(2,1)S(1)}, u32[]{:S(2)}, u32[]{:S(2)}) collective-permute-start(bf16[128,2048]{1,0:T(8,128)(2,1)S(1)} %copy-done.8), channel_id=1, source_target_pairs={{0,4},{1,5},{2,6},{3,7},{4,8},{5,9},{6,10},{7,11},{8,12},{9,13},{1... | collective-permute-start | bytes 1572872 | tf_op jit(solution)/shard_map/ppermute | solution.py:441
  60.5 14.0 %collective-permute-start.11 = (bf16[1,64,2048]{2,1,0:T(8,128)(2,1)S(1)}, bf16[1,64,2048]{2,1,0:T(8,128)(2,1)S(1)}, u32[]{:S(2)}, u32[]{:S(2)}) collective-permute-start(bf16[1,64,2048]{2,1,0:T(8,128)(2,1)S(1)} %get-tuple-element.149), channel_id=1, source_target_pairs={{0,1},{1,0},{2,3},{3,2},{4,5},{5,4},{6,7},{7,6},{8,9},{9,8},{10,11... | collective-permute-start | bytes 786440 | tf_op jit(solution)/shard_map/ppermute | solution.py:459
  62.0 12.6 %collective-permute-start.12 = (bf16[1,64,2048]{2,1,0:T(8,128)(2,1)S(1)}, bf16[1,64,2048]{2,1,0:T(8,128)(2,1)S(1)}, u32[]{:S(2)}, u32[]{:S(2)}) collective-permute-start(bf16[1,64,2048]{2,1,0:T(8,128)(2,1)S(1)} %get-tuple-element.150), channel_id=1, source_target_pairs={{0,2},{1,3},{2,0},{3,1},{4,6},{5,7},{6,4},{7,5},{8,10},{9,11},{10,... | collective-permute-start | bytes 786440 | tf_op jit(solution)/shard_map/ppermute | solution.py:459
  62.5 12.1 %collective-permute-start.13 = (bf16[1,64,2048]{2,1,0:T(8,128)(2,1)S(1)}, bf16[1,64,2048]{2,1,0:T(8,128)(2,1)S(1)}, u32[]{:S(2)}, u32[]{:S(2)}) collective-permute-start(bf16[1,64,2048]{2,1,0:T(8,128)(2,1)S(1)} %get-tuple-element.151), channel_id=1, source_target_pairs={{0,3},{1,2},{2,1},{3,0},{4,7},{5,6},{6,5},{7,4},{8,11},{9,10},{10,... | collective-permute-start | bytes 786440 | tf_op jit(solution)/shard_map/ppermute | solution.py:459
  74.6 19.1 %collective-permute-start.14 = (bf16[2,64,2048]{2,1,0:T(8,128)(2,1)S(1)}, bf16[2,64,2048]{2,1,0:T(8,128)(2,1)S(1)}, u32[]{:S(2)}, u32[]{:S(2)}) collective-permute-start(bf16[2,64,2048]{2,1,0:T(8,128)(2,1)S(1)} %get-tuple-element.152), channel_id=1, source_target_pairs={{0,1},{1,0},{2,3},{3,2},{4,5},{5,4},{6,7},{7,6},{8,9},{9,8},{10,11... | collective-permute-start | bytes 1572872 | tf_op jit(solution)/shard_map/ppermute | solution.py:459
  75.2 23.2 %collective-permute-start.15 = (bf16[2,64,2048]{2,1,0:T(8,128)(2,1)S(1)}, bf16[2,64,2048]{2,1,0:T(8,128)(2,1)S(1)}, u32[]{:S(2)}, u32[]{:S(2)}) collective-permute-start(bf16[2,64,2048]{2,1,0:T(8,128)(2,1)S(1)} %get-tuple-element.153), channel_id=1, source_target_pairs={{0,2},{1,3},{2,0},{3,1},{4,6},{5,7},{6,4},{7,5},{8,10},{9,11},{10,... | collective-permute-start | bytes 1572872 | tf_op jit(solution)/shard_map/ppermute | solution.py:459
  75.7 22.7 %collective-permute-start.16 = (bf16[2,64,2048]{2,1,0:T(8,128)(2,1)S(1)}, bf16[2,64,2048]{2,1,0:T(8,128)(2,1)S(1)}, u32[]{:S(2)}, u32[]{:S(2)}) collective-permute-start(bf16[2,64,2048]{2,1,0:T(8,128)(2,1)S(1)} %get-tuple-element.154), channel_id=1, source_target_pairs={{0,3},{1,2},{2,1},{3,0},{4,7},{5,6},{6,5},{7,4},{8,11},{9,10},{10,... | collective-permute-start | bytes 1572872 | tf_op jit(solution)/shard_map/ppermute | solution.py:459
  78.1 14.3 %collective-permute-start.17 = (bf16[128,2048]{1,0:T(8,128)(2,1)S(1)}, bf16[128,2048]{1,0:T(8,128)(2,1)S(1)}, u32[]{:S(2)}, u32[]{:S(2)}) collective-permute-start(bf16[128,2048]{1,0:T(8,128)(2,1)S(1)} %get-tuple-element.165), channel_id=1, source_target_pairs={{0,4},{1,5},{2,6},{3,7},{4,0},{5,1},{6,2},{7,3},{8,12},{9,13},{10,... | collective-permute-start | bytes 1572872 | tf_op jit(solution)/shard_map/ppermute | solution.py:441
  98.3 8.3 %collective-permute-start.18 = (bf16[1,64,2048]{2,1,0:T(8,128)(2,1)S(1)}, bf16[1,64,2048]{2,1,0:T(8,128)(2,1)S(1)}, u32[]{:S(2)}, u32[]{:S(2)}) collective-permute-start(bf16[1,64,2048]{2,1,0:T(8,128)(2,1)S(1)} %get-tuple-element.193), channel_id=1, source_target_pairs={{0,1},{1,0},{2,3},{3,2},{4,5},{5,4},{6,7},{7,6},{8,9},{9,8},{10,11... | collective-permute-start | bytes 786440 | tf_op jit(solution)/shard_map/ppermute | solution.py:459
  99.8 10.1 %collective-permute-start.19 = (bf16[1,64,2048]{2,1,0:T(8,128)(2,1)S(1)}, bf16[1,64,2048]{2,1,0:T(8,128)(2,1)S(1)}, u32[]{:S(2)}, u32[]{:S(2)}) collective-permute-start(bf16[1,64,2048]{2,1,0:T(8,128)(2,1)S(1)} %get-tuple-element.194), channel_id=1, source_target_pairs={{0,2},{1,3},{2,0},{3,1},{4,6},{5,7},{6,4},{7,5},{8,10},{9,11},{10,... | collective-permute-start | bytes 786440 | tf_op jit(solution)/shard_map/ppermute | solution.py:459
  100.3 11.3 %collective-permute-start.20 = (bf16[1,64,2048]{2,1,0:T(8,128)(2,1)S(1)}, bf16[1,64,2048]{2,1,0:T(8,128)(2,1)S(1)}, u32[]{:S(2)}, u32[]{:S(2)}) collective-permute-start(bf16[1,64,2048]{2,1,0:T(8,128)(2,1)S(1)} %get-tuple-element.195), channel_id=1, source_target_pairs={{0,3},{1,2},{2,1},{3,0},{4,7},{5,6},{6,5},{7,4},{8,11},{9,10},{10,... | collective-permute-start | bytes 786440 | tf_op jit(solution)/shard_map/ppermute | solution.py:459
  106.5 10.6 %copy-start.13 = (bf16[2,64,2048]{2,1,0:T(8,128)(2,1)}, bf16[2,64,2048]{2,1,0:T(8,128)(2,1)S(1)}, u32[]{:S(2)}) copy-start(bf16[2,64,2048]{2,1,0:T(8,128)(2,1)S(1)} %get-tuple-element.223) | copy-start | bytes 1572868
  106.5 10.6 %copy-start.15 = (bf16[2,64,2048]{2,1,0:T(8,128)(2,1)}, bf16[2,64,2048]{2,1,0:T(8,128)(2,1)S(1)}, u32[]{:S(2)}) copy-start(bf16[2,64,2048]{2,1,0:T(8,128)(2,1)S(1)} %get-tuple-element.222) | copy-start | bytes 1572868
  111.7 12.9 %collective-permute-start.21 = (bf16[1,64,2048]{2,1,0:T(8,128)(2,1)S(1)}, bf16[1,64,2048]{2,1,0:T(8,128)(2,1)S(1)}, u32[]{:S(2)}, u32[]{:S(2)}) collective-permute-start(bf16[1,64,2048]{2,1,0:T(8,128)(2,1)S(1)} %get-tuple-element.203), channel_id=1, source_target_pairs={{0,1},{1,0},{2,3},{3,2},{4,5},{5,4},{6,7},{7,6},{8,9},{9,8},{10,11... | collective-permute-start | bytes 786440 | tf_op jit(solution)/shard_map/ppermute | solution.py:459
  111.7 12.8 %collective-permute-start.22 = (bf16[1,64,2048]{2,1,0:T(8,128)(2,1)S(1)}, bf16[1,64,2048]{2,1,0:T(8,128)(2,1)S(1)}, u32[]{:S(2)}, u32[]{:S(2)}) collective-permute-start(bf16[1,64,2048]{2,1,0:T(8,128)(2,1)S(1)} %get-tuple-element.204), channel_id=1, source_target_pairs={{0,2},{1,3},{2,0},{3,1},{4,6},{5,7},{6,4},{7,5},{8,10},{9,11},{10,... | collective-permute-start | bytes 786440 | tf_op jit(solution)/shard_map/ppermute | solution.py:459
  113.6 11.0 %collective-permute-start.23 = (bf16[1,64,2048]{2,1,0:T(8,128)(2,1)S(1)}, bf16[1,64,2048]{2,1,0:T(8,128)(2,1)S(1)}, u32[]{:S(2)}, u32[]{:S(2)}) collective-permute-start(bf16[1,64,2048]{2,1,0:T(8,128)(2,1)S(1)} %get-tuple-element.205), channel_id=1, source_target_pairs={{0,3},{1,2},{2,1},{3,0},{4,7},{5,6},{6,5},{7,4},{8,11},{9,10},{10,... | collective-permute-start | bytes 786440 | tf_op jit(solution)/shard_map/ppermute | solution.py:459
  124.6 19.6 %collective-permute-start.32 = (bf16[3,384,2048]{2,1,0:T(8,128)(2,1)}, bf16[3,384,2048]{2,1,0:T(8,128)(2,1)S(1)}, u32[]{:S(2)}, u32[]{:S(2)}) collective-permute-start(bf16[3,384,2048]{2,1,0:T(8,128)(2,1)} %partial_sums.1.refs_0_), channel_id=1, source_target_pairs={{0,16},{16,0},{1,17},{17,1},{2,18},{18,2},{3,19},{19,3},{4,20},{20... | collective-permute-start | bytes 14155784 | tf_op jit(solution)/shard_map/ppermute | solution.py:508
  124.6 9.2 %collective-permute-start.24 = (bf16[1,64,2048]{2,1,0:T(8,128)(2,1)S(1)}, bf16[1,64,2048]{2,1,0:T(8,128)(2,1)S(1)}, u32[]{:S(2)}, u32[]{:S(2)}) collective-permute-start(bf16[1,64,2048]{2,1,0:T(8,128)(2,1)S(1)} %get-tuple-element.209), channel_id=1, source_target_pairs={{0,1},{1,0},{2,3},{3,2},{4,5},{5,4},{6,7},{7,6},{8,9},{9,8},{10,11... | collective-permute-start | bytes 786440 | tf_op jit(solution)/shard_map/ppermute | solution.py:459
  124.8 14.2 %collective-permute-start.25 = (bf16[1,64,2048]{2,1,0:T(8,128)(2,1)S(1)}, bf16[1,64,2048]{2,1,0:T(8,128)(2,1)S(1)}, u32[]{:S(2)}, u32[]{:S(2)}) collective-permute-start(bf16[1,64,2048]{2,1,0:T(8,128)(2,1)S(1)} %get-tuple-element.210), channel_id=1, source_target_pairs={{0,2},{1,3},{2,0},{3,1},{4,6},{5,7},{6,4},{7,5},{8,10},{9,11},{10,... | collective-permute-start | bytes 786440 | tf_op jit(solution)/shard_map/ppermute | solution.py:459
  126.6 12.4 %collective-permute-start.26 = (bf16[1,64,2048]{2,1,0:T(8,128)(2,1)S(1)}, bf16[1,64,2048]{2,1,0:T(8,128)(2,1)S(1)}, u32[]{:S(2)}, u32[]{:S(2)}) collective-permute-start(bf16[1,64,2048]{2,1,0:T(8,128)(2,1)S(1)} %get-tuple-element.211), channel_id=1, source_target_pairs={{0,3},{1,2},{2,1},{3,0},{4,7},{5,6},{6,5},{7,4},{8,11},{9,10},{10,... | collective-permute-start | bytes 786440 | tf_op jit(solution)/shard_map/ppermute | solution.py:459
  130.0 24.7 %collective-permute-start.30 = (bf16[128,2048]{1,0:T(8,128)(2,1)}, bf16[128,2048]{1,0:T(8,128)(2,1)S(1)}, u32[]{:S(2)}, u32[]{:S(2)}) collective-permute-start(bf16[128,2048]{1,0:T(8,128)(2,1)} %expand.6), channel_id=1, source_target_pairs={{0,4},{1,5},{2,6},{3,7},{4,0},{5,1},{6,2},{7,3},{8,12},{9,13},{10,... | collective-permute-start | bytes 1572872 | tf_op jit(solution)/shard_map/ppermute | solution.py:441
  139.0 15.7 %collective-permute-start.27 = (bf16[2,64,2048]{2,1,0:T(8,128)(2,1)}, bf16[2,64,2048]{2,1,0:T(8,128)(2,1)S(1)}, u32[]{:S(2)}, u32[]{:S(2)}) collective-permute-start(bf16[2,64,2048]{2,1,0:T(8,128)(2,1)} %get-tuple-element.212), channel_id=1, source_target_pairs={{0,1},{1,0},{2,3},{3,2},{4,5},{5,4},{6,7},{7,6},{8,9},{9,8},{10,11... | collective-permute-start | bytes 1572872 | tf_op jit(solution)/shard_map/ppermute | solution.py:459
  140.7 24.4 %collective-permute-start.28 = (bf16[2,64,2048]{2,1,0:T(8,128)(2,1)}, bf16[2,64,2048]{2,1,0:T(8,128)(2,1)}, u32[]{:S(2)}, u32[]{:S(2)}) collective-permute-start(bf16[2,64,2048]{2,1,0:T(8,128)(2,1)} %get-tuple-element.213), channel_id=1, source_target_pairs={{0,2},{1,3},{2,0},{3,1},{4,6},{5,7},{6,4},{7,5},{8,10},{9,11},{10,... | collective-permute-start | bytes 1572872 | tf_op jit(solution)/shard_map/ppermute | solution.py:459
  141.0 24.1 %collective-permute-start.29 = (bf16[2,64,2048]{2,1,0:T(8,128)(2,1)}, bf16[2,64,2048]{2,1,0:T(8,128)(2,1)}, u32[]{:S(2)}, u32[]{:S(2)}) collective-permute-start(bf16[2,64,2048]{2,1,0:T(8,128)(2,1)} %get-tuple-element.214), channel_id=1, source_target_pairs={{0,3},{1,2},{2,1},{3,0},{4,7},{5,6},{6,5},{7,4},{8,11},{9,10},{10,... | collective-permute-start | bytes 1572872 | tf_op jit(solution)/shard_map/ppermute | solution.py:459
  146.4 18.8 %collective-permute-start.31 = (bf16[128,2048]{1,0:T(8,128)(2,1)}, bf16[128,2048]{1,0:T(8,128)(2,1)S(1)}, u32[]{:S(2)}, u32[]{:S(2)}) collective-permute-start(bf16[128,2048]{1,0:T(8,128)(2,1)} %expand.7), channel_id=1, source_target_pairs={{0,4},{1,5},{2,6},{3,7},{4,0},{5,1},{6,2},{7,3},{8,12},{9,13},{10,... | collective-permute-start | bytes 1572872 | tf_op jit(solution)/shard_map/ppermute | solution.py:441
  146.4 2.3 %copy-start.3 = (bf16[3,384,2048]{2,1,0:T(8,128)(2,1)S(1)}, bf16[3,384,2048]{2,1,0:T(8,128)(2,1)}, u32[]{:S(2)}) copy-start(bf16[3,384,2048]{2,1,0:T(8,128)(2,1)} %partial_sums.1.refs_0_) | copy-start | bytes 14155780
  148.8 2.3 %copy-start.5 = (bf16[3,384,2048]{2,1,0:T(8,128)(2,1)S(1)}, bf16[3,384,2048]{2,1,0:T(8,128)(2,1)}, u32[]{:S(2)}) copy-start(bf16[3,384,2048]{2,1,0:T(8,128)(2,1)} %copy-done.4) | copy-start | bytes 14155780
  151.1 14.0 %copy-start.18 = (bf16[2,64,2048]{2,1,0:T(8,128)(2,1)S(1)}, bf16[2,64,2048]{2,1,0:T(8,128)(2,1)}, u32[]{:S(2)}) copy-start(bf16[2,64,2048]{2,1,0:T(8,128)(2,1)} %copy-done.17) | copy-start | bytes 1572868
  151.1 14.5 %copy-start.16 = (bf16[2,64,2048]{2,1,0:T(8,128)(2,1)S(1)}, bf16[2,64,2048]{2,1,0:T(8,128)(2,1)}, u32[]{:S(2)}) copy-start(bf16[2,64,2048]{2,1,0:T(8,128)(2,1)} %copy-done.15) | copy-start | bytes 1572868
  151.1 16.2 %copy-start.14 = (bf16[2,64,2048]{2,1,0:T(8,128)(2,1)S(1)}, bf16[2,64,2048]{2,1,0:T(8,128)(2,1)}, u32[]{:S(2)}) copy-start(bf16[2,64,2048]{2,1,0:T(8,128)(2,1)} %copy-done.13) | copy-start | bytes 1572868
  154.7 34.2 %copy-start.30 = (bf16[1,64,2048]{2,1,0:T(8,128)(2,1)S(1)}, bf16[1,64,2048]{2,1,0:T(8,128)(2,1)}, u32[]{:S(2)}) copy-start(bf16[1,64,2048]{2,1,0:T(8,128)(2,1)} %copy-done.29) | copy-start | bytes 786436
  154.7 35.9 %copy-start.28 = (bf16[1,64,2048]{2,1,0:T(8,128)(2,1)S(1)}, bf16[1,64,2048]{2,1,0:T(8,128)(2,1)}, u32[]{:S(2)}) copy-start(bf16[1,64,2048]{2,1,0:T(8,128)(2,1)} %copy-done.27) | copy-start | bytes 786436
  154.7 36.1 %copy-start.26 = (bf16[1,64,2048]{2,1,0:T(8,128)(2,1)S(1)}, bf16[1,64,2048]{2,1,0:T(8,128)(2,1)}, u32[]{:S(2)}) copy-start(bf16[1,64,2048]{2,1,0:T(8,128)(2,1)} %copy-done.25) | copy-start | bytes 786436
  165.1 14.9 %collective-permute-start.33 = (bf16[2,64,2048]{2,1,0:T(8,128)(2,1)S(1)}, bf16[2,64,2048]{2,1,0:T(8,128)(2,1)S(1)}, u32[]{:S(2)}, u32[]{:S(2)}) collective-permute-start(bf16[2,64,2048]{2,1,0:T(8,128)(2,1)S(1)} %copy-done.18), channel_id=1, source_target_pairs={{0,1},{1,0},{2,3},{3,2},{4,5},{5,4},{6,7},{7,6},{8,9},{9,8},{10,11... | collective-permute-start | bytes 1572872 | tf_op jit(solution)/shard_map/ppermute | solution.py:459
  165.7 23.2 %collective-permute-start.34 = (bf16[2,64,2048]{2,1,0:T(8,128)(2,1)S(1)}, bf16[2,64,2048]{2,1,0:T(8,128)(2,1)S(1)}, u32[]{:S(2)}, u32[]{:S(2)}) collective-permute-start(bf16[2,64,2048]{2,1,0:T(8,128)(2,1)S(1)} %copy-done.16), channel_id=1, source_target_pairs={{0,2},{1,3},{2,0},{3,1},{4,6},{5,7},{6,4},{7,5},{8,10},{9,11},{10,... | collective-permute-start | bytes 1572872 | tf_op jit(solution)/shard_map/ppermute | solution.py:459
  167.4 21.5 %collective-permute-start.35 = (bf16[2,64,2048]{2,1,0:T(8,128)(2,1)S(1)}, bf16[2,64,2048]{2,1,0:T(8,128)(2,1)S(1)}, u32[]{:S(2)}, u32[]{:S(2)}) collective-permute-start(bf16[2,64,2048]{2,1,0:T(8,128)(2,1)S(1)} %copy-done.14), channel_id=1, source_target_pairs={{0,3},{1,2},{2,1},{3,0},{4,7},{5,6},{6,5},{7,4},{8,11},{9,10},{10,... | collective-permute-start | bytes 1572872 | tf_op jit(solution)/shard_map/ppermute | solution.py:459
  170.7 31.7 %copy-start.24 = (bf16[1,64,2048]{2,1,0:T(8,128)(2,1)S(1)}, bf16[1,64,2048]{2,1,0:T(8,128)(2,1)}, u32[]{:S(2)}) copy-start(bf16[1,64,2048]{2,1,0:T(8,128)(2,1)} %copy-done.23) | copy-start | bytes 786436
  170.7 31.7 %copy-start.22 = (bf16[1,64,2048]{2,1,0:T(8,128)(2,1)S(1)}, bf16[1,64,2048]{2,1,0:T(8,128)(2,1)}, u32[]{:S(2)}) copy-start(bf16[1,64,2048]{2,1,0:T(8,128)(2,1)} %copy-done.21) | copy-start | bytes 786436
  170.7 33.4 %copy-start.20 = (bf16[1,64,2048]{2,1,0:T(8,128)(2,1)S(1)}, bf16[1,64,2048]{2,1,0:T(8,128)(2,1)}, u32[]{:S(2)}) copy-start(bf16[1,64,2048]{2,1,0:T(8,128)(2,1)} %copy-done.19) | copy-start | bytes 786436
  170.7 35.2 %copy-start.10 = (bf16[1,64,2048]{2,1,0:T(8,128)(2,1)S(1)}, bf16[1,64,2048]{2,1,0:T(8,128)(2,1)}, u32[]{:S(2)}) copy-start(bf16[1,64,2048]{2,1,0:T(8,128)(2,1)} %copy-done.9) | copy-start | bytes 786436
  170.7 22.7 %collective-permute-start.39 = (bf16[128,2048]{1,0:T(8,128)(2,1)S(1)}, bf16[128,2048]{1,0:T(8,128)(2,1)S(1)}, u32[]{:S(2)}, u32[]{:S(2)}) collective-permute-start(bf16[128,2048]{1,0:T(8,128)(2,1)S(1)} %get-tuple-element.230), channel_id=1, source_target_pairs={{0,4},{1,5},{2,6},{3,7},{4,8},{5,9},{6,10},{7,11},{8,12},{9,13},{1... | collective-permute-start | bytes 1572872 | tf_op jit(solution)/shard_map/ppermute | solution.py:441
  173.9 20.6 %collective-permute-start.40 = (bf16[128,2048]{1,0:T(8,128)(2,1)S(1)}, bf16[128,2048]{1,0:T(8,128)(2,1)S(1)}, u32[]{:S(2)}, u32[]{:S(2)}) collective-permute-start(bf16[128,2048]{1,0:T(8,128)(2,1)S(1)} %get-tuple-element.231), channel_id=1, source_target_pairs={{0,12},{1,13},{2,14},{3,15},{4,0},{5,1},{6,2},{7,3},{8,4},{9,5},{1... | collective-permute-start | bytes 1572872 | tf_op jit(solution)/shard_map/ppermute | solution.py:441
  188.8 8.4 %collective-permute-start.36 = (bf16[1,64,2048]{2,1,0:T(8,128)(2,1)S(1)}, bf16[1,64,2048]{2,1,0:T(8,128)(2,1)S(1)}, u32[]{:S(2)}, u32[]{:S(2)}) collective-permute-start(bf16[1,64,2048]{2,1,0:T(8,128)(2,1)S(1)} %copy-done.30), channel_id=1, source_target_pairs={{0,1},{1,0},{2,3},{3,2},{4,5},{5,4},{6,7},{7,6},{8,9},{9,8},{10,11... | collective-permute-start | bytes 786440 | tf_op jit(solution)/shard_map/ppermute | solution.py:459
  190.6 9.6 %collective-permute-start.37 = (bf16[1,64,2048]{2,1,0:T(8,128)(2,1)S(1)}, bf16[1,64,2048]{2,1,0:T(8,128)(2,1)S(1)}, u32[]{:S(2)}, u32[]{:S(2)}) collective-permute-start(bf16[1,64,2048]{2,1,0:T(8,128)(2,1)S(1)} %copy-done.28), channel_id=1, source_target_pairs={{0,2},{1,3},{2,0},{3,1},{4,6},{5,7},{6,4},{7,5},{8,10},{9,11},{10,... | collective-permute-start | bytes 786440 | tf_op jit(solution)/shard_map/ppermute | solution.py:459
  190.7 11.6 %collective-permute-start.38 = (bf16[1,64,2048]{2,1,0:T(8,128)(2,1)S(1)}, bf16[1,64,2048]{2,1,0:T(8,128)(2,1)S(1)}, u32[]{:S(2)}, u32[]{:S(2)}) collective-permute-start(bf16[1,64,2048]{2,1,0:T(8,128)(2,1)S(1)} %copy-done.26), channel_id=1, source_target_pairs={{0,3},{1,2},{2,1},{3,0},{4,7},{5,6},{6,5},{7,4},{8,11},{9,10},{10,... | collective-permute-start | bytes 786440 | tf_op jit(solution)/shard_map/ppermute | solution.py:459
  194.4 18.3 %collective-permute-start.44 = (bf16[128,2048]{1,0:T(8,128)(2,1)S(1)}, bf16[128,2048]{1,0:T(8,128)(2,1)S(1)}, u32[]{:S(2)}, u32[]{:S(2)}) collective-permute-start(bf16[128,2048]{1,0:T(8,128)(2,1)S(1)} %get-tuple-element.237), channel_id=1, source_target_pairs={{0,4},{1,5},{2,6},{3,7},{4,8},{5,9},{6,10},{7,11},{8,12},{9,13},{1... | collective-permute-start | bytes 1572872 | tf_op jit(solution)/shard_map/ppermute | solution.py:441
  197.2 22.3 %collective-permute-start.45 = (bf16[128,2048]{1,0:T(8,128)(2,1)S(1)}, bf16[128,2048]{1,0:T(8,128)(2,1)S(1)}, u32[]{:S(2)}, u32[]{:S(2)}) collective-permute-start(bf16[128,2048]{1,0:T(8,128)(2,1)S(1)} %get-tuple-element.238), channel_id=1, source_target_pairs={{0,12},{1,13},{2,14},{3,15},{4,0},{5,1},{6,2},{7,3},{8,4},{9,5},{1... | collective-permute-start | bytes 1572872 | tf_op jit(solution)/shard_map/ppermute | solution.py:441
  202.4 6.4 %collective-permute-start.41 = (bf16[1,64,2048]{2,1,0:T(8,128)(2,1)S(1)}, bf16[1,64,2048]{2,1,0:T(8,128)(2,1)S(1)}, u32[]{:S(2)}, u32[]{:S(2)}) collective-permute-start(bf16[1,64,2048]{2,1,0:T(8,128)(2,1)S(1)} %copy-done.24), channel_id=1, source_target_pairs={{0,1},{1,0},{2,3},{3,2},{4,5},{5,4},{6,7},{7,6},{8,9},{9,8},{10,11... | collective-permute-start | bytes 786440 | tf_op jit(solution)/shard_map/ppermute | solution.py:459
  202.4 10.3 %collective-permute-start.42 = (bf16[1,64,2048]{2,1,0:T(8,128)(2,1)S(1)}, bf16[1,64,2048]{2,1,0:T(8,128)(2,1)S(1)}, u32[]{:S(2)}, u32[]{:S(2)}) collective-permute-start(bf16[1,64,2048]{2,1,0:T(8,128)(2,1)S(1)} %copy-done.22), channel_id=1, source_target_pairs={{0,2},{1,3},{2,0},{3,1},{4,6},{5,7},{6,4},{7,5},{8,10},{9,11},{10,... | collective-permute-start | bytes 786440 | tf_op jit(solution)/shard_map/ppermute | solution.py:459
  204.1 8.6 %collective-permute-start.43 = (bf16[1,64,2048]{2,1,0:T(8,128)(2,1)S(1)}, bf16[1,64,2048]{2,1,0:T(8,128)(2,1)S(1)}, u32[]{:S(2)}, u32[]{:S(2)}) collective-permute-start(bf16[1,64,2048]{2,1,0:T(8,128)(2,1)S(1)} %copy-done.20), channel_id=1, source_target_pairs={{0,3},{1,2},{2,1},{3,0},{4,7},{5,6},{6,5},{7,4},{8,11},{9,10},{10,... | collective-permute-start | bytes 786440 | tf_op jit(solution)/shard_map/ppermute | solution.py:459
  (13 other events, 14.1 us)

commit v5 on v4

--- a/solution.py
+++ b/solution.py
@@ -128,8 +128,18 @@
     return sum(jnp.dot(m, block, preferred_element_type=F32) for m in matrices).astype(BF)
 
 
-def start_kernel(ids_ref, tokens_ref, routes_ref, gates_ref, cot_ref, block_ref, *refs, picks, capacity):
-    table_ref, turned_ref, *out_refs = refs
+def start_kernel(ids_ref, *refs, picks, capacity):
+    sources, block_ref, table_ref, turned_ref = refs[:4], *refs[4:7]
+    out_refs, held, arrived = refs[7 : 7 + PLANE], refs[7 + PLANE : -1], refs[-1]
+    copies = [
+        pltpu.make_async_copy(source, target, arrived.at[n])
+        for n, (source, target) in enumerate(zip(sources, held))
+    ]
+    for copy in copies:
+        copy.start()
+    for copy in copies:
+        copy.wait()
+    tokens_ref, routes_ref, gates_ref, cot_ref = held
     rows, width = tokens_ref.shape
     gates = gates_ref[...]
     high = gates.astype(BF).astype(F32)
@@ -162,11 +172,18 @@
     block, table, turned, *out = pl.pallas_call(
         functools.partial(start_kernel, picks=picks, capacity=capacity),
         in_specs=[pl.BlockSpec(memory_space=pltpu.SMEM)]
-        + [pl.BlockSpec(memory_space=pltpu.VMEM)] * 4,
+        + [pl.BlockSpec(memory_space=pltpu.HBM)] * 4,
         out_shape=[jax.ShapeDtypeStruct(s, BF) for s in shapes],
+        scratch_shapes=[
+            pltpu.VMEM((rows, width), BF),
+            pltpu.VMEM((picks, rows), routes.dtype),
+            pltpu.VMEM((picks, rows), gates.dtype),
+            pltpu.VMEM((rows, width), BF),
+            pltpu.SemaphoreType.DMA((4,)),
+        ],
         compiler_params=pltpu.CompilerParams(vmem_limit_bytes=16 << 20),
         name="start_rows",
-    )(ids, tokens, routes.T, gates.T, cotangent)
+    )(ids, *(pltpu.with_memory_space_constraint(v, pltpu.HBM) for v in (tokens, routes.T, gates.T, cotangent)))
     return block, table, turned, out
 
 

time: 225 us -> 223 us (level)
  local copies, waits for them, and re-layouts: 14.8 us -> 11.4 us
    unnamed x62 -> x54, local copies, waits for them, and re-layouts: 14.7 us -> 11.3 us
  transfers between devices with their start and end apart: 46 -> 46, of which waited for: 20 -> 21; matrix products, arithmetic and copies ran while one was open for 0% -> 0% of each run, Pallas kernels for 19% -> 19%
where the time goes in v5:
time: 223 us; the launch traced here: 219 us
  waiting for transfers between devices  111 us (50%)
  starting transfers between devices  49.8 us (22%)
  Pallas kernels  45.7 us (20%)
  local copies, waits for them, and re-layouts  11.4 us (5%)
    ppermute x33, waiting for transfers between devices, across(): lax.ppermute(sent[k - 1], 'expert', [(i, i ^ k) for i in range(experts)])  61.8 us
    ppermute x12, waiting for transfers between devices, permute(): return lax.ppermute(value, 'expert', pairs)  49.3 us
    ppermute x33, starting transfers between devices, across(): lax.ppermute(sent[k - 1], 'expert', [(i, i ^ k) for i in range(experts)])  38.6 us
    unnamed x54, local copies, waits for them, and re-layouts  11.3 us
    ppermute x12, starting transfers between devices, permute(): return lax.ppermute(value, 'expert', pairs)  11.1 us
    pallas_call x6, Pallas kernels, expand(): pl.pallas_call(functools.partial(expand_kernel, blocks=blocks, extras=len...  9.96 us
    pallas_call x3, Pallas kernels, forward(): pl.pallas_call(functools.partial(forward_kernel, first=capacity), out_sha...  8.24 us
    pallas_call x3, Pallas kernels, backward(): pl.pallas_call(functools.partial(backward_kernel, skip=skip), out_shape=[...  7.88 us
  transfers between devices with their start and end apart: 46, of which 21 were waited for; matrix products, arithmetic and copies ran while one was open for 0% of the time, Pallas kernels for 19%

profile of v5, /device:TPU:14, one launch (start us, length us, event | category | flops | bytes accessed | tf_op | source)
XLA Modules:
  0.0 219.0 jit_solution(16290979607709265590)
XLA Ops:
  0.8 2.9 %start_rows.1 = (bf16[128,2176]{1,0:T(8,128)(2,1)S(1)}, bf16[1,3,256,128]{3,2,1,0:T(8,128)(2,1)}, bf16[1,3,128,256]{3,2,1,0:T(8,128)(2,1)S(1)}, bf16[1,128,2048]...) custom-call(s32[5]{0:T(128)S(1)} %stack.30.ids_ref, ...), custom_call_target="tpu_custom_call" | custom-call | tf_op jit(solution)/shard_map/start_rows/pallas_call | solution.py:172
  4.2 1.6 collective-permute-start.4
  6.8 2.5 %collective-permute-start.2 = (bf16[1,128,2048]{2,1,0:T(8,128)(2,1)S(1)}, bf16[1,128,2048]{2,1,0:T(8,128)(2,1)S(1)}, u32[]{:S(2)}, u32[]{:S(2)}) collective-permute-start(bf16[1,128,2048]{2,1,0:T(8,128)(2,1)S(1)} %get-tuple-element.126), channel_id=1, source_target_pairs={{0,3},{1,2},{2,1},{3,0},{4,7},{5,6},{6,5},{7,4},{8,11},{9,10},{10,... | collective-permute-start | bytes 1572872 | tf_op jit(solution)/shard_map/ppermute | solution.py:476
  9.3 9.0 %collective-permute-done.3.refs_0_.refs_2_ = bf16[128,2176]{1,0:T(8,128)(2,1)S(1)} collective-permute-done((bf16[128,2176]{1,0:T(8,128)(2,1)S(1)}, bf16[128,2176]{1,0:T(8,128)(2,1)S(1)}, u32[]{:S(2)}, u32[]{:S(2)}) %collective-permute-start.3) | collective-permute-done | bytes 557088 | tf_op jit(solution)/shard_map/ppermute | solution.py:458
  18.3 13.9 %collective-permute-done.4.refs_1_.refs_3_ = bf16[128,2176]{1,0:T(8,128)(2,1)S(1)} collective-permute-done((bf16[128,2176]{1,0:T(8,128)(2,1)S(1)}, bf16[128,2176]{1,0:T(8,128)(2,1)S(1)}, u32[]{:S(2)}, u32[]{:S(2)}) %collective-permute-start.4) | collective-permute-done | bytes 557088 | tf_op jit(solution)/shard_map/ppermute | solution.py:458
  32.1 1.6 token_rows.2
  35.3 2.4 %collective-permute-start.10 = (bf16[2,64,2048]{2,1,0:T(8,128)(2,1)S(1)}, bf16[2,64,2048]{2,1,0:T(8,128)(2,1)S(1)}, u32[]{:S(2)}, u32[]{:S(2)}) collective-permute-start(bf16[2,64,2048]{2,1,0:T(8,128)(2,1)S(1)} %get-tuple-element.148), channel_id=1, source_target_pairs={{0,3},{1,2},{2,1},{3,0},{4,7},{5,6},{6,5},{7,4},{8,11},{9,10},{10,... | collective-permute-start | bytes 1572872 | tf_op jit(solution)/shard_map/ppermute | solution.py:476
  37.8 9.6 %collective-permute-done.5.refs_0_.refs_1_ = bf16[128,2176]{1,0:T(8,128)(2,1)S(1)} collective-permute-done((bf16[128,2176]{1,0:T(8,128)(2,1)S(1)}, bf16[128,2176]{1,0:T(8,128)(2,1)S(1)}, u32[]{:S(2)}, u32[]{:S(2)}) %collective-permute-start.5) | collective-permute-done | bytes 557088 | tf_op jit(solution)/shard_map/ppermute | solution.py:458
  47.7 1.7 collective-permute-start.7
  49.4 1.2 token_rows.3
  50.6 7.7 %collective-permute-done.9.refs_2_ = bf16[2,64,2048]{2,1,0:T(8,128)(2,1)S(1)} collective-permute-done((bf16[2,64,2048]{2,1,0:T(8,128)(2,1)S(1)}, bf16[2,64,2048]{2,1,0:T(8,128)(2,1)S(1)}, u32[]{:S(2)}, u32[]{:S(2)}) %collective-permute-start.9) | collective-permute-done | bytes 524320 | tf_op jit(solution)/shard_map/ppermute | solution.py:476
  58.3 1.5 collective-permute-start.11
  60.3 1.5 collective-permute-start.13
  61.8 8.7 %collective-permute-done.6.refs_0_ = bf16[128,2048]{1,0:T(8,128)(2,1)S(1)} collective-permute-done((bf16[128,2048]{1,0:T(8,128)(2,1)S(1)}, bf16[128,2048]{1,0:T(8,128)(2,1)S(1)}, u32[]{:S(2)}, u32[]{:S(2)}) %collective-permute-start.6) | collective-permute-done | bytes 524320 | tf_op jit(solution)/shard_map/ppermute | solution.py:458
  70.5 1.8 cot_rows.2
  73.5 2.4 %collective-permute-start.16 = (bf16[2,64,2048]{2,1,0:T(8,128)(2,1)S(1)}, bf16[2,64,2048]{2,1,0:T(8,128)(2,1)S(1)}, u32[]{:S(2)}, u32[]{:S(2)}) collective-permute-start(bf16[2,64,2048]{2,1,0:T(8,128)(2,1)S(1)} %get-tuple-element.154), channel_id=1, source_target_pairs={{0,3},{1,2},{2,1},{3,0},{4,7},{5,6},{6,5},{7,4},{8,11},{9,10},{10,... | collective-permute-start | bytes 1572872 | tf_op jit(solution)/shard_map/ppermute | solution.py:476
  76.4 1.9 expert_forward.3
  79.7 2.0 expert_backward.4
  83.9 4.5 %expert_forward.4 = (f32[512,384]{1,0:T(8,128)S(1)}, f32[512,384]{1,0:T(8,128)S(1)}, bf16[384,512]{1,0:T(8,128)(2,1)S(1)}, bf16[512,2048]{1,0:T(8,128)(2,1)S(1)}...) custom-call(bf16[2,64,2048]{2,1,0:T(8,128)(2,1)S(1)} %get-tuple-elem, ...), custom_call_target="tpu_custom_call" | custom-call | flops 2415919104 | bytes 12976128 | tf_op jit(solution)/shard_map/expert_forward/pallas_call | solution.py:312
  88.4 1.9 expert_forward.5
  90.2 1.2 cot_rows.3
  91.5 4.7 %collective-permute-done.15.refs_2_ = bf16[2,64,2048]{2,1,0:T(8,128)(2,1)S(1)} collective-permute-done((bf16[2,64,2048]{2,1,0:T(8,128)(2,1)S(1)}, bf16[2,64,2048]{2,1,0:T(8,128)(2,1)S(1)}, u32[]{:S(2)}, u32[]{:S(2)}) %collective-permute-start.15) | collective-permute-done | bytes 524320 | tf_op jit(solution)/shard_map/ppermute | solution.py:476
  96.1 1.5 collective-permute-start.18
  98.2 1.5 collective-permute-start.20
  99.6 3.9 %expert_backward.3 = (bf16[384,512]{1,0:T(8,128)(2,1)S(1)}, bf16[384,512]{1,0:T(8,128)(2,1)S(1)}, bf16[512,2048]{1,0:T(8,128)(2,1)S(1)}, bf16[2,64,2048]{2,1,0:T...) custom-call(bf16[2,64,2048]{2,1,0:T(8,128)(2,1)S(1)} %get-tuple-elem, ...), custom_call_target="tpu_custom_call" | custom-call | flops 2415919104 | bytes 13369344 | tf_op jit(solution)/shard_map/expert_backward/pallas_call | solution.py:357
  104.4 3.3 %collective-permute-done.19.refs_2_ = bf16[1,64,2048]{2,1,0:T(8,128)(2,1)S(1)} collective-permute-done((bf16[1,64,2048]{2,1,0:T(8,128)(2,1)S(1)}, bf16[1,64,2048]{2,1,0:T(8,128)(2,1)S(1)}, u32[]{:S(2)}, u32[]{:S(2)}) %collective-permute-start.19) | collective-permute-done | bytes 262176 | tf_op jit(solution)/shard_map/ppermute | solution.py:476
  107.8 1.6 collective-permute-done.20.refs_3_
  109.6 1.7 collective-permute-start.22
  111.3 1.6 collective-permute-start.23
  112.8 2.0 expert_backward.5
  114.9 7.4 %partial_sums.1.refs_0_ = bf16[3,384,2048]{2,1,0:T(8,128)(2,1)} custom-call(bf16[384,256]{1,0:T(8,128)(2,1)S(1)} %get-tuple-element.172.refs_0_, bf16[384,512]{1,0:T(8,128)(2,1)S(1)} %get-tuple-element.174.refs_1_, bf16[384,256]{1,0:T(8,128)(2,1)S(1)} %get-tuple-element.180.refs_2_, bf16[384,256]{1,0:T(8,128)(2,1)S(1)} %get-tuple-element.186.refs_3_, ...), custom_call_target="tpu_custom_call" | custom-call | flops 4831838208 | bytes 15466496 | tf_op jit(solution)/shard_map/partial_sums/pallas_call | solution.py:394
  122.7 1.7 collective-permute-start.25
  124.3 1.6 collective-permute-start.26
  125.9 1.8 expand.6
  127.7 3.8 %collective-permute-done.24.refs_1_ = bf16[1,64,2048]{2,1,0:T(8,128)(2,1)S(1)} collective-permute-done((bf16[1,64,2048]{2,1,0:T(8,128)(2,1)S(1)}, bf16[1,64,2048]{2,1,0:T(8,128)(2,1)S(1)}, u32[]{:S(2)}, u32[]{:S(2)}) %collective-permute-start.24) | collective-permute-done | bytes 262176 | tf_op jit(solution)/shard_map/ppermute | solution.py:476
  131.5 5.2 %collective-permute-done.25.refs_2_ = bf16[1,64,2048]{2,1,0:T(8,128)(2,1)S(1)} collective-permute-done((bf16[1,64,2048]{2,1,0:T(8,128)(2,1)S(1)}, bf16[1,64,2048]{2,1,0:T(8,128)(2,1)S(1)}, u32[]{:S(2)}, u32[]{:S(2)}) %collective-permute-start.25) | collective-permute-done | bytes 262176 | tf_op jit(solution)/shard_map/ppermute | solution.py:476
  136.7 1.8 collective-permute-start.27
  138.7 1.4 collective-permute-start.29
  140.2 1.7 expand.7
  141.8 2.2 %copy-done.4 = bf16[3,384,2048]{2,1,0:T(8,128)(2,1)} copy-done((bf16[3,384,2048]{2,1,0:T(8,128)(2,1)}, bf16[3,384,2048]{2,1,0:T(8,128)(2,1)S(1)}, u32[]{:S(2)}) %copy-start.4) | copy-done | bytes 4718616
  144.1 2.3 %copy-done.3 = bf16[3,384,2048]{2,1,0:T(8,128)(2,1)S(1)} copy-done((bf16[3,384,2048]{2,1,0:T(8,128)(2,1)S(1)}, bf16[3,384,2048]{2,1,0:T(8,128)(2,1)}, u32[]{:S(2)}) %copy-start.3) | copy-done | bytes 4718616
  146.5 2.3 %copy-done.5 = bf16[3,384,2048]{2,1,0:T(8,128)(2,1)S(1)} copy-done((bf16[3,384,2048]{2,1,0:T(8,128)(2,1)S(1)}, bf16[3,384,2048]{2,1,0:T(8,128)(2,1)}, u32[]{:S(2)}) %copy-start.5) | copy-done | bytes 4718616
  148.8 3.6 %weight_outputs.1 = (bf16[1,2048,384]{2,1,0:T(8,128)(2,1)}, bf16[1,2048,384]{2,1,0:T(8,128)(2,1)}, bf16[1,384,2048]{2,1,0:T(8,128)(2,1)}) custom-call(bf16[3,384,2048]{2,1,0:T(8,128)(2,1)S(1)} %copy-done.3, bf16[3,384,2048]{2,1,0:T(8,128)(2,1)S(1)} %copy-done.5), custom_call_target="tpu_custom_call" | custom-call | flops 4718592 | bytes 14155776 | tf_op jit(solution)/shard_map/weight_outputs/pallas_call | solution.py:421
  152.4 10.5 %collective-permute-done.28.refs_2_ = bf16[2,64,2048]{2,1,0:T(8,128)(2,1)} collective-permute-done((bf16[2,64,2048]{2,1,0:T(8,128)(2,1)}, bf16[2,64,2048]{2,1,0:T(8,128)(2,1)}, u32[]{:S(2)}, u32[]{:S(2)}) %collective-permute-start.28) | collective-permute-done | bytes 524320 | tf_op jit(solution)/shard_map/ppermute | solution.py:476
  163.4 1.7 collective-permute-start.34
  165.1 1.4 collective-permute-start.35
  166.4 1.9 expand.8
  168.4 3.3 %collective-permute-start.39 = (bf16[128,2048]{1,0:T(8,128)(2,1)S(1)}, bf16[128,2048]{1,0:T(8,128)(2,1)S(1)}, u32[]{:S(2)}, u32[]{:S(2)}) collective-permute-start(bf16[128,2048]{1,0:T(8,128)(2,1)S(1)} %get-tuple-element.230), channel_id=1, source_target_pairs={{0,4},{1,5},{2,6},{3,7},{4,8},{5,9},{6,10},{7,11},{8,12},{9,13},{1... | collective-permute-start | bytes 1572872 | tf_op jit(solution)/shard_map/ppermute | solution.py:458
  171.7 6.1 %collective-permute-done.33.refs_1_ = bf16[2,64,2048]{2,1,0:T(8,128)(2,1)S(1)} collective-permute-done((bf16[2,64,2048]{2,1,0:T(8,128)(2,1)S(1)}, bf16[2,64,2048]{2,1,0:T(8,128)(2,1)S(1)}, u32[]{:S(2)}, u32[]{:S(2)}) %collective-permute-start.33) | collective-permute-done | bytes 524320 | tf_op jit(solution)/shard_map/ppermute | solution.py:476
  177.8 8.7 %collective-permute-done.34.refs_2_ = bf16[2,64,2048]{2,1,0:T(8,128)(2,1)S(1)} collective-permute-done((bf16[2,64,2048]{2,1,0:T(8,128)(2,1)S(1)}, bf16[2,64,2048]{2,1,0:T(8,128)(2,1)S(1)}, u32[]{:S(2)}, u32[]{:S(2)}) %collective-permute-start.34) | collective-permute-done | bytes 524320 | tf_op jit(solution)/shard_map/ppermute | solution.py:476
  186.5 1.8 collective-permute-start.36
  188.4 1.5 collective-permute-start.38
  190.0 1.0 expand.10
  191.1 1.1 collective-permute-done.40.refs_5_
  192.3 2.8 %collective-permute-start.44 = (bf16[128,2048]{1,0:T(8,128)(2,1)S(1)}, bf16[128,2048]{1,0:T(8,128)(2,1)S(1)}, u32[]{:S(2)}, u32[]{:S(2)}) collective-permute-start(bf16[128,2048]{1,0:T(8,128)(2,1)S(1)} %get-tuple-element.237), channel_id=1, source_target_pairs={{0,4},{1,5},{2,6},{3,7},{4,8},{5,9},{6,10},{7,11},{8,12},{9,13},{1... | collective-permute-start | bytes 1572872 | tf_op jit(solution)/shard_map/ppermute | solution.py:458
  195.0 3.3 %collective-permute-done.37.refs_2_ = bf16[1,64,2048]{2,1,0:T(8,128)(2,1)S(1)} collective-permute-done((bf16[1,64,2048]{2,1,0:T(8,128)(2,1)S(1)}, bf16[1,64,2048]{2,1,0:T(8,128)(2,1)S(1)}, u32[]{:S(2)}, u32[]{:S(2)}) %collective-permute-start.37) | collective-permute-done | bytes 262176 | tf_op jit(solution)/shard_map/ppermute | solution.py:476
  198.3 1.7 collective-permute-done.38.refs_3_
  200.0 1.6 collective-permute-start.42
  201.6 1.9 collective-permute-start.43
  203.5 1.8 expand.9
  205.4 1.1 collective-permute-done.41.refs_1_
  206.4 4.0 %collective-permute-done.42.refs_2_ = bf16[1,64,2048]{2,1,0:T(8,128)(2,1)S(1)} collective-permute-done((bf16[1,64,2048]{2,1,0:T(8,128)(2,1)S(1)}, bf16[1,64,2048]{2,1,0:T(8,128)(2,1)S(1)}, u32[]{:S(2)}, u32[]{:S(2)}) %collective-permute-start.42) | collective-permute-done | bytes 262176 | tf_op jit(solution)/shard_map/ppermute | solution.py:476
  210.5 6.9 %collective-permute-done.45.refs_5_ = bf16[128,2048]{1,0:T(8,128)(2,1)S(1)} collective-permute-done((bf16[128,2048]{1,0:T(8,128)(2,1)S(1)}, bf16[128,2048]{1,0:T(8,128)(2,1)S(1)}, u32[]{:S(2)}, u32[]{:S(2)}) %collective-permute-start.45) | collective-permute-done | bytes 524320 | tf_op jit(solution)/shard_map/ppermute | solution.py:458
  217.3 1.7 expand.11
  (104 shorter events, 12.5 us)
Async XLA Ops:
  0.8 46.6 %copy-start.26 = (bf16[128,2048]{1,0:T(8,128)(2,1)S(1)}, bf16[128,2048]{1,0:T(8,128)(2,1)}, u32[]{:S(2)}) copy-start(bf16[128,2048]{1,0:T(8,128)(2,1)} %refs_3_.1) | copy-start | bytes 1572868
  3.7 14.6 %collective-permute-start.3 = (bf16[128,2176]{1,0:T(8,128)(2,1)S(1)}, bf16[128,2176]{1,0:T(8,128)(2,1)S(1)}, u32[]{:S(2)}, u32[]{:S(2)}) collective-permute-start(bf16[128,2176]{1,0:T(8,128)(2,1)S(1)} %get-tuple-element.131), channel_id=1, source_target_pairs={{0,12},{1,13},{2,14},{3,15},{4,0},{5,1},{6,2},{7,3},{8,4},{9,5},{1... | collective-permute-start | bytes 1671176 | tf_op jit(solution)/shard_map/ppermute | solution.py:458
  4.2 27.9 %collective-permute-start.4 = (bf16[128,2176]{1,0:T(8,128)(2,1)S(1)}, bf16[128,2176]{1,0:T(8,128)(2,1)S(1)}, u32[]{:S(2)}, u32[]{:S(2)}) collective-permute-start(bf16[128,2176]{1,0:T(8,128)(2,1)S(1)} %get-tuple-element.131), channel_id=1, source_target_pairs={{0,4},{1,5},{2,6},{3,7},{4,8},{5,9},{6,10},{7,11},{8,12},{9,13},{1... | collective-permute-start | bytes 1671176 | tf_op jit(solution)/shard_map/ppermute | solution.py:458
  5.8 28.4 %collective-permute-start = (bf16[1,128,2048]{2,1,0:T(8,128)(2,1)S(1)}, bf16[1,128,2048]{2,1,0:T(8,128)(2,1)S(1)}, u32[]{:S(2)}, u32[]{:S(2)}) collective-permute-start(bf16[1,128,2048]{2,1,0:T(8,128)(2,1)S(1)} %get-tuple-element.124), channel_id=1, source_target_pairs={{0,1},{1,0},{2,3},{3,2},{4,5},{5,4},{6,7},{7,6},{8,9},{9,8},{10,11... | collective-permute-start | bytes 1572872 | tf_op jit(solution)/shard_map/ppermute | solution.py:476
  6.3 27.9 %collective-permute-start.1 = (bf16[1,128,2048]{2,1,0:T(8,128)(2,1)S(1)}, bf16[1,128,2048]{2,1,0:T(8,128)(2,1)S(1)}, u32[]{:S(2)}, u32[]{:S(2)}) collective-permute-start(bf16[1,128,2048]{2,1,0:T(8,128)(2,1)S(1)} %get-tuple-element.125), channel_id=1, source_target_pairs={{0,2},{1,3},{2,0},{3,1},{4,6},{5,7},{6,4},{7,5},{8,10},{9,11},{10,... | collective-permute-start | bytes 1572872 | tf_op jit(solution)/shard_map/ppermute | solution.py:476
  6.8 27.4 %collective-permute-start.2 = (bf16[1,128,2048]{2,1,0:T(8,128)(2,1)S(1)}, bf16[1,128,2048]{2,1,0:T(8,128)(2,1)S(1)}, u32[]{:S(2)}, u32[]{:S(2)}) collective-permute-start(bf16[1,128,2048]{2,1,0:T(8,128)(2,1)S(1)} %get-tuple-element.126), channel_id=1, source_target_pairs={{0,3},{1,2},{2,1},{3,0},{4,7},{5,6},{6,5},{7,4},{8,11},{9,10},{10,... | collective-permute-start | bytes 1572872 | tf_op jit(solution)/shard_map/ppermute | solution.py:476
  32.1 44.3 %copy-start.1 = (bf16[1,2048,384]{2,1,0:T(8,128)(2,1)S(1)}, bf16[1,2048,384]{2,1,0:T(8,128)(2,1)}, u32[]{:S(2)}) copy-start(bf16[1,2048,384]{2,1,0:T(8,128)(2,1)} %param.12) | copy-start | bytes 4718596
  32.1 44.3 %copy-start.2 = (bf16[1,384,2048]{2,1,0:T(8,128)(2,1)S(1)}, bf16[1,384,2048]{2,1,0:T(8,128)(2,1)}, u32[]{:S(2)}) copy-start(bf16[1,384,2048]{2,1,0:T(8,128)(2,1)} %param.13) | copy-start | bytes 4718596
  33.7 42.7 %copy-start = (bf16[1,2048,384]{2,1,0:T(8,128)(2,1)S(1)}, bf16[1,2048,384]{2,1,0:T(8,128)(2,1)}, u32[]{:S(2)}) copy-start(bf16[1,2048,384]{2,1,0:T(8,128)(2,1)} %param.11) | copy-start | bytes 4718596
  33.8 13.6 %collective-permute-start.5 = (bf16[128,2176]{1,0:T(8,128)(2,1)S(1)}, bf16[128,2176]{1,0:T(8,128)(2,1)S(1)}, u32[]{:S(2)}, u32[]{:S(2)}) collective-permute-start(bf16[128,2176]{1,0:T(8,128)(2,1)S(1)} %get-tuple-element.133), channel_id=1, source_target_pairs={{0,4},{1,5},{2,6},{3,7},{4,0},{5,1},{6,2},{7,3},{8,12},{9,13},{10,... | collective-permute-start | bytes 1671176 | tf_op jit(solution)/shard_map/ppermute | solution.py:458
  34.2 16.3 %collective-permute-start.8 = (bf16[2,64,2048]{2,1,0:T(8,128)(2,1)S(1)}, bf16[2,64,2048]{2,1,0:T(8,128)(2,1)S(1)}, u32[]{:S(2)}, u32[]{:S(2)}) collective-permute-start(bf16[2,64,2048]{2,1,0:T(8,128)(2,1)S(1)} %get-tuple-element.146), channel_id=1, source_target_pairs={{0,1},{1,0},{2,3},{3,2},{4,5},{5,4},{6,7},{7,6},{8,9},{9,8},{10,11... | collective-permute-start | bytes 1572872 | tf_op jit(solution)/shard_map/ppermute | solution.py:476
  34.8 23.5 %collective-permute-start.9 = (bf16[2,64,2048]{2,1,0:T(8,128)(2,1)S(1)}, bf16[2,64,2048]{2,1,0:T(8,128)(2,1)S(1)}, u32[]{:S(2)}, u32[]{:S(2)}) collective-permute-start(bf16[2,64,2048]{2,1,0:T(8,128)(2,1)S(1)} %get-tuple-element.147), channel_id=1, source_target_pairs={{0,2},{1,3},{2,0},{3,1},{4,6},{5,7},{6,4},{7,5},{8,10},{9,11},{10,... | collective-permute-start | bytes 1572872 | tf_op jit(solution)/shard_map/ppermute | solution.py:476
  35.3 23.0 %collective-permute-start.10 = (bf16[2,64,2048]{2,1,0:T(8,128)(2,1)S(1)}, bf16[2,64,2048]{2,1,0:T(8,128)(2,1)S(1)}, u32[]{:S(2)}, u32[]{:S(2)}) collective-permute-start(bf16[2,64,2048]{2,1,0:T(8,128)(2,1)S(1)} %get-tuple-element.148), channel_id=1, source_target_pairs={{0,3},{1,2},{2,1},{3,0},{4,7},{5,6},{6,5},{7,4},{8,11},{9,10},{10,... | collective-permute-start | bytes 1572872 | tf_op jit(solution)/shard_map/ppermute | solution.py:476
  47.4 23.1 %collective-permute-start.6 = (bf16[128,2048]{1,0:T(8,128)(2,1)S(1)}, bf16[128,2048]{1,0:T(8,128)(2,1)S(1)}, u32[]{:S(2)}, u32[]{:S(2)}) collective-permute-start(bf16[128,2048]{1,0:T(8,128)(2,1)S(1)} %copy-done.26), channel_id=1, source_target_pairs={{0,12},{1,13},{2,14},{3,15},{4,0},{5,1},{6,2},{7,3},{8,4},{9,5},{1... | collective-permute-start | bytes 1572872 | tf_op jit(solution)/shard_map/ppermute | solution.py:458
  47.7 22.8 %collective-permute-start.7 = (bf16[128,2048]{1,0:T(8,128)(2,1)S(1)}, bf16[128,2048]{1,0:T(8,128)(2,1)S(1)}, u32[]{:S(2)}, u32[]{:S(2)}) collective-permute-start(bf16[128,2048]{1,0:T(8,128)(2,1)S(1)} %copy-done.26), channel_id=1, source_target_pairs={{0,4},{1,5},{2,6},{3,7},{4,8},{5,9},{6,10},{7,11},{8,12},{9,13},{1... | collective-permute-start | bytes 1572872 | tf_op jit(solution)/shard_map/ppermute | solution.py:458
  58.3 14.0 %collective-permute-start.11 = (bf16[1,64,2048]{2,1,0:T(8,128)(2,1)S(1)}, bf16[1,64,2048]{2,1,0:T(8,128)(2,1)S(1)}, u32[]{:S(2)}, u32[]{:S(2)}) collective-permute-start(bf16[1,64,2048]{2,1,0:T(8,128)(2,1)S(1)} %get-tuple-element.149), channel_id=1, source_target_pairs={{0,1},{1,0},{2,3},{3,2},{4,5},{5,4},{6,7},{7,6},{8,9},{9,8},{10,11... | collective-permute-start | bytes 786440 | tf_op jit(solution)/shard_map/ppermute | solution.py:476
  59.8 12.6 %collective-permute-start.12 = (bf16[1,64,2048]{2,1,0:T(8,128)(2,1)S(1)}, bf16[1,64,2048]{2,1,0:T(8,128)(2,1)S(1)}, u32[]{:S(2)}, u32[]{:S(2)}) collective-permute-start(bf16[1,64,2048]{2,1,0:T(8,128)(2,1)S(1)} %get-tuple-element.150), channel_id=1, source_target_pairs={{0,2},{1,3},{2,0},{3,1},{4,6},{5,7},{6,4},{7,5},{8,10},{9,11},{10,... | collective-permute-start | bytes 786440 | tf_op jit(solution)/shard_map/ppermute | solution.py:476
  60.3 12.1 %collective-permute-start.13 = (bf16[1,64,2048]{2,1,0:T(8,128)(2,1)S(1)}, bf16[1,64,2048]{2,1,0:T(8,128)(2,1)S(1)}, u32[]{:S(2)}, u32[]{:S(2)}) collective-permute-start(bf16[1,64,2048]{2,1,0:T(8,128)(2,1)S(1)} %get-tuple-element.151), channel_id=1, source_target_pairs={{0,3},{1,2},{2,1},{3,0},{4,7},{5,6},{6,5},{7,4},{8,11},{9,10},{10,... | collective-permute-start | bytes 786440 | tf_op jit(solution)/shard_map/ppermute | solution.py:476
  72.4 19.1 %collective-permute-start.14 = (bf16[2,64,2048]{2,1,0:T(8,128)(2,1)S(1)}, bf16[2,64,2048]{2,1,0:T(8,128)(2,1)S(1)}, u32[]{:S(2)}, u32[]{:S(2)}) collective-permute-start(bf16[2,64,2048]{2,1,0:T(8,128)(2,1)S(1)} %get-tuple-element.152), channel_id=1, source_target_pairs={{0,1},{1,0},{2,3},{3,2},{4,5},{5,4},{6,7},{7,6},{8,9},{9,8},{10,11... | collective-permute-start | bytes 1572872 | tf_op jit(solution)/shard_map/ppermute | solution.py:476
  73.0 23.2 %collective-permute-start.15 = (bf16[2,64,2048]{2,1,0:T(8,128)(2,1)S(1)}, bf16[2,64,2048]{2,1,0:T(8,128)(2,1)S(1)}, u32[]{:S(2)}, u32[]{:S(2)}) collective-permute-start(bf16[2,64,2048]{2,1,0:T(8,128)(2,1)S(1)} %get-tuple-element.153), channel_id=1, source_target_pairs={{0,2},{1,3},{2,0},{3,1},{4,6},{5,7},{6,4},{7,5},{8,10},{9,11},{10,... | collective-permute-start | bytes 1572872 | tf_op jit(solution)/shard_map/ppermute | solution.py:476
  73.5 22.7 %collective-permute-start.16 = (bf16[2,64,2048]{2,1,0:T(8,128)(2,1)S(1)}, bf16[2,64,2048]{2,1,0:T(8,128)(2,1)S(1)}, u32[]{:S(2)}, u32[]{:S(2)}) collective-permute-start(bf16[2,64,2048]{2,1,0:T(8,128)(2,1)S(1)} %get-tuple-element.154), channel_id=1, source_target_pairs={{0,3},{1,2},{2,1},{3,0},{4,7},{5,6},{6,5},{7,4},{8,11},{9,10},{10,... | collective-permute-start | bytes 1572872 | tf_op jit(solution)/shard_map/ppermute | solution.py:476
  75.9 14.3 %collective-permute-start.17 = (bf16[128,2048]{1,0:T(8,128)(2,1)S(1)}, bf16[128,2048]{1,0:T(8,128)(2,1)S(1)}, u32[]{:S(2)}, u32[]{:S(2)}) collective-permute-start(bf16[128,2048]{1,0:T(8,128)(2,1)S(1)} %get-tuple-element.165), channel_id=1, source_target_pairs={{0,4},{1,5},{2,6},{3,7},{4,0},{5,1},{6,2},{7,3},{8,12},{9,13},{10,... | collective-permute-start | bytes 1572872 | tf_op jit(solution)/shard_map/ppermute | solution.py:458
  96.1 8.3 %collective-permute-start.18 = (bf16[1,64,2048]{2,1,0:T(8,128)(2,1)S(1)}, bf16[1,64,2048]{2,1,0:T(8,128)(2,1)S(1)}, u32[]{:S(2)}, u32[]{:S(2)}) collective-permute-start(bf16[1,64,2048]{2,1,0:T(8,128)(2,1)S(1)} %get-tuple-element.193), channel_id=1, source_target_pairs={{0,1},{1,0},{2,3},{3,2},{4,5},{5,4},{6,7},{7,6},{8,9},{9,8},{10,11... | collective-permute-start | bytes 786440 | tf_op jit(solution)/shard_map/ppermute | solution.py:476
  97.6 10.2 %collective-permute-start.19 = (bf16[1,64,2048]{2,1,0:T(8,128)(2,1)S(1)}, bf16[1,64,2048]{2,1,0:T(8,128)(2,1)S(1)}, u32[]{:S(2)}, u32[]{:S(2)}) collective-permute-start(bf16[1,64,2048]{2,1,0:T(8,128)(2,1)S(1)} %get-tuple-element.194), channel_id=1, source_target_pairs={{0,2},{1,3},{2,0},{3,1},{4,6},{5,7},{6,4},{7,5},{8,10},{9,11},{10,... | collective-permute-start | bytes 786440 | tf_op jit(solution)/shard_map/ppermute | solution.py:476
  98.2 11.2 %collective-permute-start.20 = (bf16[1,64,2048]{2,1,0:T(8,128)(2,1)S(1)}, bf16[1,64,2048]{2,1,0:T(8,128)(2,1)S(1)}, u32[]{:S(2)}, u32[]{:S(2)}) collective-permute-start(bf16[1,64,2048]{2,1,0:T(8,128)(2,1)S(1)} %get-tuple-element.195), channel_id=1, source_target_pairs={{0,3},{1,2},{2,1},{3,0},{4,7},{5,6},{6,5},{7,4},{8,11},{9,10},{10,... | collective-permute-start | bytes 786440 | tf_op jit(solution)/shard_map/ppermute | solution.py:476
  104.3 10.5 %copy-start.8 = (bf16[2,64,2048]{2,1,0:T(8,128)(2,1)}, bf16[2,64,2048]{2,1,0:T(8,128)(2,1)S(1)}, u32[]{:S(2)}) copy-start(bf16[2,64,2048]{2,1,0:T(8,128)(2,1)S(1)} %get-tuple-element.223) | copy-start | bytes 1572868
  104.3 10.5 %copy-start.10 = (bf16[2,64,2048]{2,1,0:T(8,128)(2,1)}, bf16[2,64,2048]{2,1,0:T(8,128)(2,1)S(1)}, u32[]{:S(2)}) copy-start(bf16[2,64,2048]{2,1,0:T(8,128)(2,1)S(1)} %get-tuple-element.222) | copy-start | bytes 1572868
  109.4 12.9 %collective-permute-start.21 = (bf16[1,64,2048]{2,1,0:T(8,128)(2,1)S(1)}, bf16[1,64,2048]{2,1,0:T(8,128)(2,1)S(1)}, u32[]{:S(2)}, u32[]{:S(2)}) collective-permute-start(bf16[1,64,2048]{2,1,0:T(8,128)(2,1)S(1)} %get-tuple-element.203), channel_id=1, source_target_pairs={{0,1},{1,0},{2,3},{3,2},{4,5},{5,4},{6,7},{7,6},{8,9},{9,8},{10,11... | collective-permute-start | bytes 786440 | tf_op jit(solution)/shard_map/ppermute | solution.py:476
  109.6 12.6 %collective-permute-start.22 = (bf16[1,64,2048]{2,1,0:T(8,128)(2,1)S(1)}, bf16[1,64,2048]{2,1,0:T(8,128)(2,1)S(1)}, u32[]{:S(2)}, u32[]{:S(2)}) collective-permute-start(bf16[1,64,2048]{2,1,0:T(8,128)(2,1)S(1)} %get-tuple-element.204), channel_id=1, source_target_pairs={{0,2},{1,3},{2,0},{3,1},{4,6},{5,7},{6,4},{7,5},{8,10},{9,11},{10,... | collective-permute-start | bytes 786440 | tf_op jit(solution)/shard_map/ppermute | solution.py:476
  111.3 11.0 %collective-permute-start.23 = (bf16[1,64,2048]{2,1,0:T(8,128)(2,1)S(1)}, bf16[1,64,2048]{2,1,0:T(8,128)(2,1)S(1)}, u32[]{:S(2)}, u32[]{:S(2)}) collective-permute-start(bf16[1,64,2048]{2,1,0:T(8,128)(2,1)S(1)} %get-tuple-element.205), channel_id=1, source_target_pairs={{0,3},{1,2},{2,1},{3,0},{4,7},{5,6},{6,5},{7,4},{8,11},{9,10},{10,... | collective-permute-start | bytes 786440 | tf_op jit(solution)/shard_map/ppermute | solution.py:476
  122.3 19.6 %collective-permute-start.32 = (bf16[3,384,2048]{2,1,0:T(8,128)(2,1)}, bf16[3,384,2048]{2,1,0:T(8,128)(2,1)S(1)}, u32[]{:S(2)}, u32[]{:S(2)}) collective-permute-start(bf16[3,384,2048]{2,1,0:T(8,128)(2,1)} %partial_sums.1.refs_0_), channel_id=1, source_target_pairs={{0,16},{16,0},{1,17},{17,1},{2,18},{18,2},{3,19},{19,3},{4,20},{20... | collective-permute-start | bytes 14155784 | tf_op jit(solution)/shard_map/ppermute | solution.py:525
  122.3 9.2 %collective-permute-start.24 = (bf16[1,64,2048]{2,1,0:T(8,128)(2,1)S(1)}, bf16[1,64,2048]{2,1,0:T(8,128)(2,1)S(1)}, u32[]{:S(2)}, u32[]{:S(2)}) collective-permute-start(bf16[1,64,2048]{2,1,0:T(8,128)(2,1)S(1)} %get-tuple-element.209), channel_id=1, source_target_pairs={{0,1},{1,0},{2,3},{3,2},{4,5},{5,4},{6,7},{7,6},{8,9},{9,8},{10,11... | collective-permute-start | bytes 786440 | tf_op jit(solution)/shard_map/ppermute | solution.py:476
  122.7 14.0 %collective-permute-start.25 = (bf16[1,64,2048]{2,1,0:T(8,128)(2,1)S(1)}, bf16[1,64,2048]{2,1,0:T(8,128)(2,1)S(1)}, u32[]{:S(2)}, u32[]{:S(2)}) collective-permute-start(bf16[1,64,2048]{2,1,0:T(8,128)(2,1)S(1)} %get-tuple-element.210), channel_id=1, source_target_pairs={{0,2},{1,3},{2,0},{3,1},{4,6},{5,7},{6,4},{7,5},{8,10},{9,11},{10,... | collective-permute-start | bytes 786440 | tf_op jit(solution)/shard_map/ppermute | solution.py:476
  124.3 12.3 %collective-permute-start.26 = (bf16[1,64,2048]{2,1,0:T(8,128)(2,1)S(1)}, bf16[1,64,2048]{2,1,0:T(8,128)(2,1)S(1)}, u32[]{:S(2)}, u32[]{:S(2)}) collective-permute-start(bf16[1,64,2048]{2,1,0:T(8,128)(2,1)S(1)} %get-tuple-element.211), channel_id=1, source_target_pairs={{0,3},{1,2},{2,1},{3,0},{4,7},{5,6},{6,5},{7,4},{8,11},{9,10},{10,... | collective-permute-start | bytes 786440 | tf_op jit(solution)/shard_map/ppermute | solution.py:476
  127.7 24.7 %collective-permute-start.30 = (bf16[128,2048]{1,0:T(8,128)(2,1)}, bf16[128,2048]{1,0:T(8,128)(2,1)S(1)}, u32[]{:S(2)}, u32[]{:S(2)}) collective-permute-start(bf16[128,2048]{1,0:T(8,128)(2,1)} %expand.6), channel_id=1, source_target_pairs={{0,4},{1,5},{2,6},{3,7},{4,0},{5,1},{6,2},{7,3},{8,12},{9,13},{10,... | collective-permute-start | bytes 1572872 | tf_op jit(solution)/shard_map/ppermute | solution.py:458
  136.7 15.7 %collective-permute-start.27 = (bf16[2,64,2048]{2,1,0:T(8,128)(2,1)}, bf16[2,64,2048]{2,1,0:T(8,128)(2,1)S(1)}, u32[]{:S(2)}, u32[]{:S(2)}) collective-permute-start(bf16[2,64,2048]{2,1,0:T(8,128)(2,1)} %get-tuple-element.212), channel_id=1, source_target_pairs={{0,1},{1,0},{2,3},{3,2},{4,5},{5,4},{6,7},{7,6},{8,9},{9,8},{10,11... | collective-permute-start | bytes 1572872 | tf_op jit(solution)/shard_map/ppermute | solution.py:476
  138.4 24.4 %collective-permute-start.28 = (bf16[2,64,2048]{2,1,0:T(8,128)(2,1)}, bf16[2,64,2048]{2,1,0:T(8,128)(2,1)}, u32[]{:S(2)}, u32[]{:S(2)}) collective-permute-start(bf16[2,64,2048]{2,1,0:T(8,128)(2,1)} %get-tuple-element.213), channel_id=1, source_target_pairs={{0,2},{1,3},{2,0},{3,1},{4,6},{5,7},{6,4},{7,5},{8,10},{9,11},{10,... | collective-permute-start | bytes 1572872 | tf_op jit(solution)/shard_map/ppermute | solution.py:476
  138.7 24.1 %collective-permute-start.29 = (bf16[2,64,2048]{2,1,0:T(8,128)(2,1)}, bf16[2,64,2048]{2,1,0:T(8,128)(2,1)}, u32[]{:S(2)}, u32[]{:S(2)}) collective-permute-start(bf16[2,64,2048]{2,1,0:T(8,128)(2,1)} %get-tuple-element.214), channel_id=1, source_target_pairs={{0,3},{1,2},{2,1},{3,0},{4,7},{5,6},{6,5},{7,4},{8,11},{9,10},{10,... | collective-permute-start | bytes 1572872 | tf_op jit(solution)/shard_map/ppermute | solution.py:476
  144.0 18.8 %collective-permute-start.31 = (bf16[128,2048]{1,0:T(8,128)(2,1)}, bf16[128,2048]{1,0:T(8,128)(2,1)S(1)}, u32[]{:S(2)}, u32[]{:S(2)}) collective-permute-start(bf16[128,2048]{1,0:T(8,128)(2,1)} %expand.7), channel_id=1, source_target_pairs={{0,4},{1,5},{2,6},{3,7},{4,0},{5,1},{6,2},{7,3},{8,12},{9,13},{10,... | collective-permute-start | bytes 1572872 | tf_op jit(solution)/shard_map/ppermute | solution.py:458
  144.1 2.3 %copy-start.3 = (bf16[3,384,2048]{2,1,0:T(8,128)(2,1)S(1)}, bf16[3,384,2048]{2,1,0:T(8,128)(2,1)}, u32[]{:S(2)}) copy-start(bf16[3,384,2048]{2,1,0:T(8,128)(2,1)} %partial_sums.1.refs_0_) | copy-start | bytes 14155780
  146.5 2.3 %copy-start.5 = (bf16[3,384,2048]{2,1,0:T(8,128)(2,1)S(1)}, bf16[3,384,2048]{2,1,0:T(8,128)(2,1)}, u32[]{:S(2)}) copy-start(bf16[3,384,2048]{2,1,0:T(8,128)(2,1)} %copy-done.4) | copy-start | bytes 14155780
  148.8 14.1 %copy-start.13 = (bf16[2,64,2048]{2,1,0:T(8,128)(2,1)S(1)}, bf16[2,64,2048]{2,1,0:T(8,128)(2,1)}, u32[]{:S(2)}) copy-start(bf16[2,64,2048]{2,1,0:T(8,128)(2,1)} %copy-done.12) | copy-start | bytes 1572868
  148.8 14.6 %copy-start.11 = (bf16[2,64,2048]{2,1,0:T(8,128)(2,1)S(1)}, bf16[2,64,2048]{2,1,0:T(8,128)(2,1)}, u32[]{:S(2)}) copy-start(bf16[2,64,2048]{2,1,0:T(8,128)(2,1)} %copy-done.10) | copy-start | bytes 1572868
  148.8 16.3 %copy-start.9 = (bf16[2,64,2048]{2,1,0:T(8,128)(2,1)S(1)}, bf16[2,64,2048]{2,1,0:T(8,128)(2,1)}, u32[]{:S(2)}) copy-start(bf16[2,64,2048]{2,1,0:T(8,128)(2,1)} %copy-done.8) | copy-start | bytes 1572868
  152.4 34.1 %copy-start.25 = (bf16[1,64,2048]{2,1,0:T(8,128)(2,1)S(1)}, bf16[1,64,2048]{2,1,0:T(8,128)(2,1)}, u32[]{:S(2)}) copy-start(bf16[1,64,2048]{2,1,0:T(8,128)(2,1)} %copy-done.24) | copy-start | bytes 786436
  152.4 35.9 %copy-start.23 = (bf16[1,64,2048]{2,1,0:T(8,128)(2,1)S(1)}, bf16[1,64,2048]{2,1,0:T(8,128)(2,1)}, u32[]{:S(2)}) copy-start(bf16[1,64,2048]{2,1,0:T(8,128)(2,1)} %copy-done.22) | copy-start | bytes 786436
  152.4 36.1 %copy-start.21 = (bf16[1,64,2048]{2,1,0:T(8,128)(2,1)S(1)}, bf16[1,64,2048]{2,1,0:T(8,128)(2,1)}, u32[]{:S(2)}) copy-start(bf16[1,64,2048]{2,1,0:T(8,128)(2,1)} %copy-done.20) | copy-start | bytes 786436
  162.8 14.9 %collective-permute-start.33 = (bf16[2,64,2048]{2,1,0:T(8,128)(2,1)S(1)}, bf16[2,64,2048]{2,1,0:T(8,128)(2,1)S(1)}, u32[]{:S(2)}, u32[]{:S(2)}) collective-permute-start(bf16[2,64,2048]{2,1,0:T(8,128)(2,1)S(1)} %copy-done.13), channel_id=1, source_target_pairs={{0,1},{1,0},{2,3},{3,2},{4,5},{5,4},{6,7},{7,6},{8,9},{9,8},{10,11... | collective-permute-start | bytes 1572872 | tf_op jit(solution)/shard_map/ppermute | solution.py:476
  163.4 23.1 %collective-permute-start.34 = (bf16[2,64,2048]{2,1,0:T(8,128)(2,1)S(1)}, bf16[2,64,2048]{2,1,0:T(8,128)(2,1)S(1)}, u32[]{:S(2)}, u32[]{:S(2)}) collective-permute-start(bf16[2,64,2048]{2,1,0:T(8,128)(2,1)S(1)} %copy-done.11), channel_id=1, source_target_pairs={{0,2},{1,3},{2,0},{3,1},{4,6},{5,7},{6,4},{7,5},{8,10},{9,11},{10,... | collective-permute-start | bytes 1572872 | tf_op jit(solution)/shard_map/ppermute | solution.py:476
  165.1 21.4 %collective-permute-start.35 = (bf16[2,64,2048]{2,1,0:T(8,128)(2,1)S(1)}, bf16[2,64,2048]{2,1,0:T(8,128)(2,1)S(1)}, u32[]{:S(2)}, u32[]{:S(2)}) collective-permute-start(bf16[2,64,2048]{2,1,0:T(8,128)(2,1)S(1)} %copy-done.9), channel_id=1, source_target_pairs={{0,3},{1,2},{2,1},{3,0},{4,7},{5,6},{6,5},{7,4},{8,11},{9,10},{10,... | collective-permute-start | bytes 1572872 | tf_op jit(solution)/shard_map/ppermute | solution.py:476
  168.4 31.7 %copy-start.19 = (bf16[1,64,2048]{2,1,0:T(8,128)(2,1)S(1)}, bf16[1,64,2048]{2,1,0:T(8,128)(2,1)}, u32[]{:S(2)}) copy-start(bf16[1,64,2048]{2,1,0:T(8,128)(2,1)} %copy-done.18) | copy-start | bytes 786436
  168.4 31.7 %copy-start.17 = (bf16[1,64,2048]{2,1,0:T(8,128)(2,1)S(1)}, bf16[1,64,2048]{2,1,0:T(8,128)(2,1)}, u32[]{:S(2)}) copy-start(bf16[1,64,2048]{2,1,0:T(8,128)(2,1)} %copy-done.16) | copy-start | bytes 786436
  168.4 33.2 %copy-start.15 = (bf16[1,64,2048]{2,1,0:T(8,128)(2,1)S(1)}, bf16[1,64,2048]{2,1,0:T(8,128)(2,1)}, u32[]{:S(2)}) copy-start(bf16[1,64,2048]{2,1,0:T(8,128)(2,1)} %copy-done.14) | copy-start | bytes 786436
  168.4 35.1 %copy-start.7 = (bf16[1,64,2048]{2,1,0:T(8,128)(2,1)S(1)}, bf16[1,64,2048]{2,1,0:T(8,128)(2,1)}, u32[]{:S(2)}) copy-start(bf16[1,64,2048]{2,1,0:T(8,128)(2,1)} %copy-done.6) | copy-start | bytes 786436
  168.4 22.7 %collective-permute-start.39 = (bf16[128,2048]{1,0:T(8,128)(2,1)S(1)}, bf16[128,2048]{1,0:T(8,128)(2,1)S(1)}, u32[]{:S(2)}, u32[]{:S(2)}) collective-permute-start(bf16[128,2048]{1,0:T(8,128)(2,1)S(1)} %get-tuple-element.230), channel_id=1, source_target_pairs={{0,4},{1,5},{2,6},{3,7},{4,8},{5,9},{6,10},{7,11},{8,12},{9,13},{1... | collective-permute-start | bytes 1572872 | tf_op jit(solution)/shard_map/ppermute | solution.py:458
  171.7 20.6 %collective-permute-start.40 = (bf16[128,2048]{1,0:T(8,128)(2,1)S(1)}, bf16[128,2048]{1,0:T(8,128)(2,1)S(1)}, u32[]{:S(2)}, u32[]{:S(2)}) collective-permute-start(bf16[128,2048]{1,0:T(8,128)(2,1)S(1)} %get-tuple-element.231), channel_id=1, source_target_pairs={{0,12},{1,13},{2,14},{3,15},{4,0},{5,1},{6,2},{7,3},{8,4},{9,5},{1... | collective-permute-start | bytes 1572872 | tf_op jit(solution)/shard_map/ppermute | solution.py:458
  186.5 8.6 %collective-permute-start.36 = (bf16[1,64,2048]{2,1,0:T(8,128)(2,1)S(1)}, bf16[1,64,2048]{2,1,0:T(8,128)(2,1)S(1)}, u32[]{:S(2)}, u32[]{:S(2)}) collective-permute-start(bf16[1,64,2048]{2,1,0:T(8,128)(2,1)S(1)} %copy-done.25), channel_id=1, source_target_pairs={{0,1},{1,0},{2,3},{3,2},{4,5},{5,4},{6,7},{7,6},{8,9},{9,8},{10,11... | collective-permute-start | bytes 786440 | tf_op jit(solution)/shard_map/ppermute | solution.py:476
  188.3 10.0 %collective-permute-start.37 = (bf16[1,64,2048]{2,1,0:T(8,128)(2,1)S(1)}, bf16[1,64,2048]{2,1,0:T(8,128)(2,1)S(1)}, u32[]{:S(2)}, u32[]{:S(2)}) collective-permute-start(bf16[1,64,2048]{2,1,0:T(8,128)(2,1)S(1)} %copy-done.23), channel_id=1, source_target_pairs={{0,2},{1,3},{2,0},{3,1},{4,6},{5,7},{6,4},{7,5},{8,10},{9,11},{10,... | collective-permute-start | bytes 786440 | tf_op jit(solution)/shard_map/ppermute | solution.py:476
  188.4 11.6 %collective-permute-start.38 = (bf16[1,64,2048]{2,1,0:T(8,128)(2,1)S(1)}, bf16[1,64,2048]{2,1,0:T(8,128)(2,1)S(1)}, u32[]{:S(2)}, u32[]{:S(2)}) collective-permute-start(bf16[1,64,2048]{2,1,0:T(8,128)(2,1)S(1)} %copy-done.21), channel_id=1, source_target_pairs={{0,3},{1,2},{2,1},{3,0},{4,7},{5,6},{6,5},{7,4},{8,11},{9,10},{10,... | collective-permute-start | bytes 786440 | tf_op jit(solution)/shard_map/ppermute | solution.py:476
  192.3 18.2 %collective-permute-start.44 = (bf16[128,2048]{1,0:T(8,128)(2,1)S(1)}, bf16[128,2048]{1,0:T(8,128)(2,1)S(1)}, u32[]{:S(2)}, u32[]{:S(2)}) collective-permute-start(bf16[128,2048]{1,0:T(8,128)(2,1)S(1)} %get-tuple-element.237), channel_id=1, source_target_pairs={{0,4},{1,5},{2,6},{3,7},{4,8},{5,9},{6,10},{7,11},{8,12},{9,13},{1... | collective-permute-start | bytes 1572872 | tf_op jit(solution)/shard_map/ppermute | solution.py:458
  195.0 22.3 %collective-permute-start.45 = (bf16[128,2048]{1,0:T(8,128)(2,1)S(1)}, bf16[128,2048]{1,0:T(8,128)(2,1)S(1)}, u32[]{:S(2)}, u32[]{:S(2)}) collective-permute-start(bf16[128,2048]{1,0:T(8,128)(2,1)S(1)} %get-tuple-element.238), channel_id=1, source_target_pairs={{0,12},{1,13},{2,14},{3,15},{4,0},{5,1},{6,2},{7,3},{8,4},{9,5},{1... | collective-permute-start | bytes 1572872 | tf_op jit(solution)/shard_map/ppermute | solution.py:458
  200.0 6.4 %collective-permute-start.41 = (bf16[1,64,2048]{2,1,0:T(8,128)(2,1)S(1)}, bf16[1,64,2048]{2,1,0:T(8,128)(2,1)S(1)}, u32[]{:S(2)}, u32[]{:S(2)}) collective-permute-start(bf16[1,64,2048]{2,1,0:T(8,128)(2,1)S(1)} %copy-done.19), channel_id=1, source_target_pairs={{0,1},{1,0},{2,3},{3,2},{4,5},{5,4},{6,7},{7,6},{8,9},{9,8},{10,11... | collective-permute-start | bytes 786440 | tf_op jit(solution)/shard_map/ppermute | solution.py:476
  200.0 10.4 %collective-permute-start.42 = (bf16[1,64,2048]{2,1,0:T(8,128)(2,1)S(1)}, bf16[1,64,2048]{2,1,0:T(8,128)(2,1)S(1)}, u32[]{:S(2)}, u32[]{:S(2)}) collective-permute-start(bf16[1,64,2048]{2,1,0:T(8,128)(2,1)S(1)} %copy-done.17), channel_id=1, source_target_pairs={{0,2},{1,3},{2,0},{3,1},{4,6},{5,7},{6,4},{7,5},{8,10},{9,11},{10,... | collective-permute-start | bytes 786440 | tf_op jit(solution)/shard_map/ppermute | solution.py:476
  201.6 8.8 %collective-permute-start.43 = (bf16[1,64,2048]{2,1,0:T(8,128)(2,1)S(1)}, bf16[1,64,2048]{2,1,0:T(8,128)(2,1)S(1)}, u32[]{:S(2)}, u32[]{:S(2)}) collective-permute-start(bf16[1,64,2048]{2,1,0:T(8,128)(2,1)S(1)} %copy-done.15), channel_id=1, source_target_pairs={{0,3},{1,2},{2,1},{3,0},{4,7},{5,6},{6,5},{7,4},{8,11},{9,10},{10,... | collective-permute-start | bytes 786440 | tf_op jit(solution)/shard_map/ppermute | solution.py:476
  (9 other events, 10.6 us)

commit v6 on v5

--- a/solution.py
+++ b/solution.py
@@ -439,7 +439,7 @@
             transcendentals=0,
         ),
         name="weight_outputs",
-    )(*sums)
+    )(*(pltpu.with_memory_space_constraint(v, pltpu.HBM) for v in sums))
 
 
 def plane_plan(tokens, routes, gates, cotangent, w_gate, w_up, w_down):

time: 223 us -> 223 us (level)
  local copies, waits for them, and re-layouts: 11.4 us -> 4.46 us
  waiting for transfers between devices: 111 us -> 115 us
  Pallas kernels: 45.7 us -> 48.7 us
    unnamed x54 -> x48, local copies, waits for them, and re-layouts: 11.3 us -> 4.38 us
    ppermute x33, waiting for transfers between devices: 61.8 us -> 65.7 us  [across(): lax.ppermute(sent[k - 1], 'expert', [(i, i ^ k) for i in range(experts)])]
    pallas_call x1, Pallas kernels: 3.55 us -> 6.48 us  [weight_outputs(): pl.pallas_call(turn_kernel, grid=(width // tile,), in_specs=[pl.BlockSpec...]
  transfers between devices with their start and end apart: 46 -> 46, of which waited for: 21 -> 22; matrix products, arithmetic and copies ran while one was open for 0% -> 0% of each run, Pallas kernels for 19% -> 20%
where the time goes in v6:
time: 223 us; the launch traced here: 219 us
  waiting for transfers between devices  115 us (52%)
  starting transfers between devices  49.9 us (22%)
  Pallas kernels  48.7 us (22%)
  local copies, waits for them, and re-layouts  4.46 us (2%)
    ppermute x33, waiting for transfers between devices, across(): lax.ppermute(sent[k - 1], 'expert', [(i, i ^ k) for i in range(experts)])  65.7 us
    ppermute x12, waiting for transfers between devices, permute(): return lax.ppermute(value, 'expert', pairs)  49.3 us
    ppermute x33, starting transfers between devices, across(): lax.ppermute(sent[k - 1], 'expert', [(i, i ^ k) for i in range(experts)])  38.6 us
    ppermute x12, starting transfers between devices, permute(): return lax.ppermute(value, 'expert', pairs)  11.2 us
    pallas_call x6, Pallas kernels, expand(): pl.pallas_call(functools.partial(expand_kernel, blocks=blocks, extras=len...  9.98 us
    pallas_call x3, Pallas kernels, forward(): pl.pallas_call(functools.partial(forward_kernel, first=capacity), out_sha...  8.24 us
    pallas_call x3, Pallas kernels, backward(): pl.pallas_call(functools.partial(backward_kernel, skip=skip), out_shape=[...  7.88 us
    pallas_call x1, Pallas kernels, partial_sums(): pl.pallas_call(partial_kernel, grid=(width // tile,), in_specs=[pl.BlockS...  7.35 us
  transfers between devices with their start and end apart: 46, of which 22 were waited for; matrix products, arithmetic and copies ran while one was open for 0% of the time, Pallas kernels for 20%

profile of v6, /device:TPU:14, one launch (start us, length us, event | category | flops | bytes accessed | tf_op | source)
XLA Modules:
  0.0 219.0 jit_solution(9284570987395746489)
XLA Ops:
  0.8 2.9 %start_rows.1 = (bf16[128,2176]{1,0:T(8,128)(2,1)S(1)}, bf16[1,3,256,128]{3,2,1,0:T(8,128)(2,1)}, bf16[1,3,128,256]{3,2,1,0:T(8,128)(2,1)S(1)}, bf16[1,128,2048]...) custom-call(s32[5]{0:T(128)S(1)} %stack.30.ids_ref, ...), custom_call_target="tpu_custom_call" | custom-call | tf_op jit(solution)/shard_map/start_rows/pallas_call | solution.py:172
  4.2 1.6 collective-permute-start.4
  6.8 2.5 %collective-permute-start.2 = (bf16[1,128,2048]{2,1,0:T(8,128)(2,1)S(1)}, bf16[1,128,2048]{2,1,0:T(8,128)(2,1)S(1)}, u32[]{:S(2)}, u32[]{:S(2)}) collective-permute-start(bf16[1,128,2048]{2,1,0:T(8,128)(2,1)S(1)} %get-tuple-element.126), channel_id=1, source_target_pairs={{0,3},{1,2},{2,1},{3,0},{4,7},{5,6},{6,5},{7,4},{8,11},{9,10},{10,... | collective-permute-start | bytes 1572872 | tf_op jit(solution)/shard_map/ppermute | solution.py:476
  9.3 9.0 %collective-permute-done.3.refs_0_.refs_2_ = bf16[128,2176]{1,0:T(8,128)(2,1)S(1)} collective-permute-done((bf16[128,2176]{1,0:T(8,128)(2,1)S(1)}, bf16[128,2176]{1,0:T(8,128)(2,1)S(1)}, u32[]{:S(2)}, u32[]{:S(2)}) %collective-permute-start.3) | collective-permute-done | bytes 557088 | tf_op jit(solution)/shard_map/ppermute | solution.py:458
  18.3 13.9 %collective-permute-done.4.refs_1_.refs_3_ = bf16[128,2176]{1,0:T(8,128)(2,1)S(1)} collective-permute-done((bf16[128,2176]{1,0:T(8,128)(2,1)S(1)}, bf16[128,2176]{1,0:T(8,128)(2,1)S(1)}, u32[]{:S(2)}, u32[]{:S(2)}) %collective-permute-start.4) | collective-permute-done | bytes 557088 | tf_op jit(solution)/shard_map/ppermute | solution.py:458
  32.1 1.6 token_rows.2
  35.3 2.4 %collective-permute-start.10 = (bf16[2,64,2048]{2,1,0:T(8,128)(2,1)S(1)}, bf16[2,64,2048]{2,1,0:T(8,128)(2,1)S(1)}, u32[]{:S(2)}, u32[]{:S(2)}) collective-permute-start(bf16[2,64,2048]{2,1,0:T(8,128)(2,1)S(1)} %get-tuple-element.148), channel_id=1, source_target_pairs={{0,3},{1,2},{2,1},{3,0},{4,7},{5,6},{6,5},{7,4},{8,11},{9,10},{10,... | collective-permute-start | bytes 1572872 | tf_op jit(solution)/shard_map/ppermute | solution.py:476
  37.8 9.6 %collective-permute-done.5.refs_0_.refs_1_ = bf16[128,2176]{1,0:T(8,128)(2,1)S(1)} collective-permute-done((bf16[128,2176]{1,0:T(8,128)(2,1)S(1)}, bf16[128,2176]{1,0:T(8,128)(2,1)S(1)}, u32[]{:S(2)}, u32[]{:S(2)}) %collective-permute-start.5) | collective-permute-done | bytes 557088 | tf_op jit(solution)/shard_map/ppermute | solution.py:458
  47.7 1.7 collective-permute-start.7
  49.4 1.2 token_rows.3
  50.6 7.7 %collective-permute-done.9.refs_2_ = bf16[2,64,2048]{2,1,0:T(8,128)(2,1)S(1)} collective-permute-done((bf16[2,64,2048]{2,1,0:T(8,128)(2,1)S(1)}, bf16[2,64,2048]{2,1,0:T(8,128)(2,1)S(1)}, u32[]{:S(2)}, u32[]{:S(2)}) %collective-permute-start.9) | collective-permute-done | bytes 524320 | tf_op jit(solution)/shard_map/ppermute | solution.py:476
  58.3 1.5 collective-permute-start.11
  60.3 1.5 collective-permute-start.13
  61.8 8.7 %collective-permute-done.6.refs_0_ = bf16[128,2048]{1,0:T(8,128)(2,1)S(1)} collective-permute-done((bf16[128,2048]{1,0:T(8,128)(2,1)S(1)}, bf16[128,2048]{1,0:T(8,128)(2,1)S(1)}, u32[]{:S(2)}, u32[]{:S(2)}) %collective-permute-start.6) | collective-permute-done | bytes 524320 | tf_op jit(solution)/shard_map/ppermute | solution.py:458
  70.5 1.8 cot_rows.2
  73.5 2.4 %collective-permute-start.16 = (bf16[2,64,2048]{2,1,0:T(8,128)(2,1)S(1)}, bf16[2,64,2048]{2,1,0:T(8,128)(2,1)S(1)}, u32[]{:S(2)}, u32[]{:S(2)}) collective-permute-start(bf16[2,64,2048]{2,1,0:T(8,128)(2,1)S(1)} %get-tuple-element.154), channel_id=1, source_target_pairs={{0,3},{1,2},{2,1},{3,0},{4,7},{5,6},{6,5},{7,4},{8,11},{9,10},{10,... | collective-permute-start | bytes 1572872 | tf_op jit(solution)/shard_map/ppermute | solution.py:476
  76.4 1.9 expert_forward.3
  79.7 2.0 expert_backward.4
  83.1 0.7 copy-done.15
  83.9 4.5 %expert_forward.4 = (f32[512,384]{1,0:T(8,128)S(1)}, f32[512,384]{1,0:T(8,128)S(1)}, bf16[384,512]{1,0:T(8,128)(2,1)S(1)}, bf16[512,2048]{1,0:T(8,128)(2,1)S(1)}...) custom-call(bf16[2,64,2048]{2,1,0:T(8,128)(2,1)S(1)} %get-tuple-elem, ...), custom_call_target="tpu_custom_call" | custom-call | flops 2415919104 | bytes 12976128 | tf_op jit(solution)/shard_map/expert_forward/pallas_call | solution.py:312
  88.4 1.9 expert_forward.5
  90.2 1.2 cot_rows.3
  91.5 4.7 %collective-permute-done.15.refs_2_ = bf16[2,64,2048]{2,1,0:T(8,128)(2,1)S(1)} collective-permute-done((bf16[2,64,2048]{2,1,0:T(8,128)(2,1)S(1)}, bf16[2,64,2048]{2,1,0:T(8,128)(2,1)S(1)}, u32[]{:S(2)}, u32[]{:S(2)}) %collective-permute-start.15) | collective-permute-done | bytes 524320 | tf_op jit(solution)/shard_map/ppermute | solution.py:476
  96.1 1.5 collective-permute-start.18
  98.2 1.5 collective-permute-start.20
  99.6 3.9 %expert_backward.3 = (bf16[384,512]{1,0:T(8,128)(2,1)S(1)}, bf16[384,512]{1,0:T(8,128)(2,1)S(1)}, bf16[512,2048]{1,0:T(8,128)(2,1)S(1)}, bf16[2,64,2048]{2,1,0:T...) custom-call(bf16[2,64,2048]{2,1,0:T(8,128)(2,1)S(1)} %get-tuple-elem, ...), custom_call_target="tpu_custom_call" | custom-call | flops 2415919104 | bytes 13369344 | tf_op jit(solution)/shard_map/expert_backward/pallas_call | solution.py:357
  103.5 0.8 copy-done.9
  104.4 3.3 %collective-permute-done.19.refs_2_ = bf16[1,64,2048]{2,1,0:T(8,128)(2,1)S(1)} collective-permute-done((bf16[1,64,2048]{2,1,0:T(8,128)(2,1)S(1)}, bf16[1,64,2048]{2,1,0:T(8,128)(2,1)S(1)}, u32[]{:S(2)}, u32[]{:S(2)}) %collective-permute-start.19) | collective-permute-done | bytes 262176 | tf_op jit(solution)/shard_map/ppermute | solution.py:476
  107.8 1.6 collective-permute-done.20.refs_3_
  109.6 1.7 collective-permute-start.22
  111.3 1.6 collective-permute-start.23
  112.8 2.0 expert_backward.5
  114.9 7.3 %partial_sums.1.refs_0_ = bf16[3,384,2048]{2,1,0:T(8,128)(2,1)} custom-call(bf16[384,256]{1,0:T(8,128)(2,1)S(1)} %get-tuple-element.172.refs_0_, bf16[384,512]{1,0:T(8,128)(2,1)S(1)} %get-tuple-element.174.refs_1_, bf16[384,256]{1,0:T(8,128)(2,1)S(1)} %get-tuple-element.180.refs_2_, bf16[384,256]{1,0:T(8,128)(2,1)S(1)} %get-tuple-element.186.refs_3_, ...), custom_call_target="tpu_custom_call" | custom-call | flops 4831838208 | bytes 15466496 | tf_op jit(solution)/shard_map/partial_sums/pallas_call | solution.py:394
  122.6 1.7 collective-permute-start.25
  124.3 1.6 collective-permute-start.26
  125.9 1.8 expand.6
  127.7 3.8 %collective-permute-done.24.refs_1_ = bf16[1,64,2048]{2,1,0:T(8,128)(2,1)S(1)} collective-permute-done((bf16[1,64,2048]{2,1,0:T(8,128)(2,1)S(1)}, bf16[1,64,2048]{2,1,0:T(8,128)(2,1)S(1)}, u32[]{:S(2)}, u32[]{:S(2)}) %collective-permute-start.24) | collective-permute-done | bytes 262176 | tf_op jit(solution)/shard_map/ppermute | solution.py:476
  131.5 5.2 %collective-permute-done.25.refs_2_ = bf16[1,64,2048]{2,1,0:T(8,128)(2,1)S(1)} collective-permute-done((bf16[1,64,2048]{2,1,0:T(8,128)(2,1)S(1)}, bf16[1,64,2048]{2,1,0:T(8,128)(2,1)S(1)}, u32[]{:S(2)}, u32[]{:S(2)}) %collective-permute-start.25) | collective-permute-done | bytes 262176 | tf_op jit(solution)/shard_map/ppermute | solution.py:476
  136.6 1.8 collective-permute-start.27
  138.7 1.4 collective-permute-start.29
  140.1 1.7 expand.7
  141.9 6.5 %weight_outputs.1 = (bf16[1,2048,384]{2,1,0:T(8,128)(2,1)}, bf16[1,2048,384]{2,1,0:T(8,128)(2,1)}, bf16[1,384,2048]{2,1,0:T(8,128)(2,1)}) custom-call(bf16[3,384,2048]{2,1,0:T(8,128)(2,1)} %partial_sums.1.refs_0_, bf16[3,384,2048]{2,1,0:T(8,128)(2,1)} %collective-permute-done.32.refs_1_), custom_call_target="tpu_custom_call" | custom-call | flops 4718592 | bytes 14155776 | tf_op jit(solution)/shard_map/weight_outputs/pallas_call | solution.py:421
  148.4 3.3 %collective-permute-done.27.refs_1_ = bf16[2,64,2048]{2,1,0:T(8,128)(2,1)S(1)} collective-permute-done((bf16[2,64,2048]{2,1,0:T(8,128)(2,1)}, bf16[2,64,2048]{2,1,0:T(8,128)(2,1)S(1)}, u32[]{:S(2)}, u32[]{:S(2)}) %collective-permute-start.27) | collective-permute-done | bytes 524320 | tf_op jit(solution)/shard_map/ppermute | solution.py:476
  151.7 11.1 %collective-permute-done.28.refs_2_ = bf16[2,64,2048]{2,1,0:T(8,128)(2,1)} collective-permute-done((bf16[2,64,2048]{2,1,0:T(8,128)(2,1)}, bf16[2,64,2048]{2,1,0:T(8,128)(2,1)}, u32[]{:S(2)}, u32[]{:S(2)}) %collective-permute-start.28) | collective-permute-done | bytes 524320 | tf_op jit(solution)/shard_map/ppermute | solution.py:476
  163.3 1.7 collective-permute-start.34
  165.0 1.4 collective-permute-start.35
  166.4 1.9 expand.8
  168.4 3.3 %collective-permute-start.39 = (bf16[128,2048]{1,0:T(8,128)(2,1)S(1)}, bf16[128,2048]{1,0:T(8,128)(2,1)S(1)}, u32[]{:S(2)}, u32[]{:S(2)}) collective-permute-start(bf16[128,2048]{1,0:T(8,128)(2,1)S(1)} %get-tuple-element.230), channel_id=1, source_target_pairs={{0,4},{1,5},{2,6},{3,7},{4,8},{5,9},{6,10},{7,11},{8,12},{9,13},{1... | collective-permute-start | bytes 1572872 | tf_op jit(solution)/shard_map/ppermute | solution.py:458
  171.7 6.1 %collective-permute-done.33.refs_1_ = bf16[2,64,2048]{2,1,0:T(8,128)(2,1)S(1)} collective-permute-done((bf16[2,64,2048]{2,1,0:T(8,128)(2,1)S(1)}, bf16[2,64,2048]{2,1,0:T(8,128)(2,1)S(1)}, u32[]{:S(2)}, u32[]{:S(2)}) %collective-permute-start.33) | collective-permute-done | bytes 524320 | tf_op jit(solution)/shard_map/ppermute | solution.py:476
  177.8 8.7 %collective-permute-done.34.refs_2_ = bf16[2,64,2048]{2,1,0:T(8,128)(2,1)S(1)} collective-permute-done((bf16[2,64,2048]{2,1,0:T(8,128)(2,1)S(1)}, bf16[2,64,2048]{2,1,0:T(8,128)(2,1)S(1)}, u32[]{:S(2)}, u32[]{:S(2)}) %collective-permute-start.34) | collective-permute-done | bytes 524320 | tf_op jit(solution)/shard_map/ppermute | solution.py:476
  186.5 1.8 collective-permute-start.36
  188.4 1.5 collective-permute-start.38
  190.0 1.0 expand.10
  191.1 1.1 collective-permute-done.40.refs_5_
  192.2 2.8 %collective-permute-start.44 = (bf16[128,2048]{1,0:T(8,128)(2,1)S(1)}, bf16[128,2048]{1,0:T(8,128)(2,1)S(1)}, u32[]{:S(2)}, u32[]{:S(2)}) collective-permute-start(bf16[128,2048]{1,0:T(8,128)(2,1)S(1)} %get-tuple-element.237), channel_id=1, source_target_pairs={{0,4},{1,5},{2,6},{3,7},{4,8},{5,9},{6,10},{7,11},{8,12},{9,13},{1... | collective-permute-start | bytes 1572872 | tf_op jit(solution)/shard_map/ppermute | solution.py:458
  195.1 3.2 %collective-permute-done.37.refs_2_ = bf16[1,64,2048]{2,1,0:T(8,128)(2,1)S(1)} collective-permute-done((bf16[1,64,2048]{2,1,0:T(8,128)(2,1)S(1)}, bf16[1,64,2048]{2,1,0:T(8,128)(2,1)S(1)}, u32[]{:S(2)}, u32[]{:S(2)}) %collective-permute-start.37) | collective-permute-done | bytes 262176 | tf_op jit(solution)/shard_map/ppermute | solution.py:476
  198.3 1.7 collective-permute-done.38.refs_3_
  200.0 1.6 collective-permute-start.42
  201.6 1.9 collective-permute-start.43
  203.5 1.8 expand.9
  205.3 1.1 collective-permute-done.41.refs_1_
  206.4 4.0 %collective-permute-done.42.refs_2_ = bf16[1,64,2048]{2,1,0:T(8,128)(2,1)S(1)} collective-permute-done((bf16[1,64,2048]{2,1,0:T(8,128)(2,1)S(1)}, bf16[1,64,2048]{2,1,0:T(8,128)(2,1)S(1)}, u32[]{:S(2)}, u32[]{:S(2)}) %collective-permute-start.42) | collective-permute-done | bytes 262176 | tf_op jit(solution)/shard_map/ppermute | solution.py:476
  210.4 6.9 %collective-permute-done.45.refs_5_ = bf16[128,2048]{1,0:T(8,128)(2,1)S(1)} collective-permute-done((bf16[128,2048]{1,0:T(8,128)(2,1)S(1)}, bf16[128,2048]{1,0:T(8,128)(2,1)S(1)}, u32[]{:S(2)}, u32[]{:S(2)}) %collective-permute-start.45) | collective-permute-done | bytes 524320 | tf_op jit(solution)/shard_map/ppermute | solution.py:458
  217.3 1.7 expand.11
  (98 shorter events, 11.0 us)
Async XLA Ops:
  0.8 46.6 %copy-start.23 = (bf16[128,2048]{1,0:T(8,128)(2,1)S(1)}, bf16[128,2048]{1,0:T(8,128)(2,1)}, u32[]{:S(2)}) copy-start(bf16[128,2048]{1,0:T(8,128)(2,1)} %refs_3_.1) | copy-start | bytes 1572868
  3.7 14.6 %collective-permute-start.3 = (bf16[128,2176]{1,0:T(8,128)(2,1)S(1)}, bf16[128,2176]{1,0:T(8,128)(2,1)S(1)}, u32[]{:S(2)}, u32[]{:S(2)}) collective-permute-start(bf16[128,2176]{1,0:T(8,128)(2,1)S(1)} %get-tuple-element.131), channel_id=1, source_target_pairs={{0,12},{1,13},{2,14},{3,15},{4,0},{5,1},{6,2},{7,3},{8,4},{9,5},{1... | collective-permute-start | bytes 1671176 | tf_op jit(solution)/shard_map/ppermute | solution.py:458
  4.2 27.9 %collective-permute-start.4 = (bf16[128,2176]{1,0:T(8,128)(2,1)S(1)}, bf16[128,2176]{1,0:T(8,128)(2,1)S(1)}, u32[]{:S(2)}, u32[]{:S(2)}) collective-permute-start(bf16[128,2176]{1,0:T(8,128)(2,1)S(1)} %get-tuple-element.131), channel_id=1, source_target_pairs={{0,4},{1,5},{2,6},{3,7},{4,8},{5,9},{6,10},{7,11},{8,12},{9,13},{1... | collective-permute-start | bytes 1671176 | tf_op jit(solution)/shard_map/ppermute | solution.py:458
  5.8 28.4 %collective-permute-start = (bf16[1,128,2048]{2,1,0:T(8,128)(2,1)S(1)}, bf16[1,128,2048]{2,1,0:T(8,128)(2,1)S(1)}, u32[]{:S(2)}, u32[]{:S(2)}) collective-permute-start(bf16[1,128,2048]{2,1,0:T(8,128)(2,1)S(1)} %get-tuple-element.124), channel_id=1, source_target_pairs={{0,1},{1,0},{2,3},{3,2},{4,5},{5,4},{6,7},{7,6},{8,9},{9,8},{10,11... | collective-permute-start | bytes 1572872 | tf_op jit(solution)/shard_map/ppermute | solution.py:476
  6.3 27.9 %collective-permute-start.1 = (bf16[1,128,2048]{2,1,0:T(8,128)(2,1)S(1)}, bf16[1,128,2048]{2,1,0:T(8,128)(2,1)S(1)}, u32[]{:S(2)}, u32[]{:S(2)}) collective-permute-start(bf16[1,128,2048]{2,1,0:T(8,128)(2,1)S(1)} %get-tuple-element.125), channel_id=1, source_target_pairs={{0,2},{1,3},{2,0},{3,1},{4,6},{5,7},{6,4},{7,5},{8,10},{9,11},{10,... | collective-permute-start | bytes 1572872 | tf_op jit(solution)/shard_map/ppermute | solution.py:476
  6.8 27.4 %collective-permute-start.2 = (bf16[1,128,2048]{2,1,0:T(8,128)(2,1)S(1)}, bf16[1,128,2048]{2,1,0:T(8,128)(2,1)S(1)}, u32[]{:S(2)}, u32[]{:S(2)}) collective-permute-start(bf16[1,128,2048]{2,1,0:T(8,128)(2,1)S(1)} %get-tuple-element.126), channel_id=1, source_target_pairs={{0,3},{1,2},{2,1},{3,0},{4,7},{5,6},{6,5},{7,4},{8,11},{9,10},{10,... | collective-permute-start | bytes 1572872 | tf_op jit(solution)/shard_map/ppermute | solution.py:476
  32.1 44.3 %copy-start.1 = (bf16[1,2048,384]{2,1,0:T(8,128)(2,1)S(1)}, bf16[1,2048,384]{2,1,0:T(8,128)(2,1)}, u32[]{:S(2)}) copy-start(bf16[1,2048,384]{2,1,0:T(8,128)(2,1)} %param.12) | copy-start | bytes 4718596
  32.1 44.3 %copy-start.2 = (bf16[1,384,2048]{2,1,0:T(8,128)(2,1)S(1)}, bf16[1,384,2048]{2,1,0:T(8,128)(2,1)}, u32[]{:S(2)}) copy-start(bf16[1,384,2048]{2,1,0:T(8,128)(2,1)} %param.13) | copy-start | bytes 4718596
  33.7 42.7 %copy-start = (bf16[1,2048,384]{2,1,0:T(8,128)(2,1)S(1)}, bf16[1,2048,384]{2,1,0:T(8,128)(2,1)}, u32[]{:S(2)}) copy-start(bf16[1,2048,384]{2,1,0:T(8,128)(2,1)} %param.11) | copy-start | bytes 4718596
  33.8 13.6 %collective-permute-start.5 = (bf16[128,2176]{1,0:T(8,128)(2,1)S(1)}, bf16[128,2176]{1,0:T(8,128)(2,1)S(1)}, u32[]{:S(2)}, u32[]{:S(2)}) collective-permute-start(bf16[128,2176]{1,0:T(8,128)(2,1)S(1)} %get-tuple-element.133), channel_id=1, source_target_pairs={{0,4},{1,5},{2,6},{3,7},{4,0},{5,1},{6,2},{7,3},{8,12},{9,13},{10,... | collective-permute-start | bytes 1671176 | tf_op jit(solution)/shard_map/ppermute | solution.py:458
  34.2 16.3 %collective-permute-start.8 = (bf16[2,64,2048]{2,1,0:T(8,128)(2,1)S(1)}, bf16[2,64,2048]{2,1,0:T(8,128)(2,1)S(1)}, u32[]{:S(2)}, u32[]{:S(2)}) collective-permute-start(bf16[2,64,2048]{2,1,0:T(8,128)(2,1)S(1)} %get-tuple-element.146), channel_id=1, source_target_pairs={{0,1},{1,0},{2,3},{3,2},{4,5},{5,4},{6,7},{7,6},{8,9},{9,8},{10,11... | collective-permute-start | bytes 1572872 | tf_op jit(solution)/shard_map/ppermute | solution.py:476
  34.8 23.5 %collective-permute-start.9 = (bf16[2,64,2048]{2,1,0:T(8,128)(2,1)S(1)}, bf16[2,64,2048]{2,1,0:T(8,128)(2,1)S(1)}, u32[]{:S(2)}, u32[]{:S(2)}) collective-permute-start(bf16[2,64,2048]{2,1,0:T(8,128)(2,1)S(1)} %get-tuple-element.147), channel_id=1, source_target_pairs={{0,2},{1,3},{2,0},{3,1},{4,6},{5,7},{6,4},{7,5},{8,10},{9,11},{10,... | collective-permute-start | bytes 1572872 | tf_op jit(solution)/shard_map/ppermute | solution.py:476
  35.3 23.0 %collective-permute-start.10 = (bf16[2,64,2048]{2,1,0:T(8,128)(2,1)S(1)}, bf16[2,64,2048]{2,1,0:T(8,128)(2,1)S(1)}, u32[]{:S(2)}, u32[]{:S(2)}) collective-permute-start(bf16[2,64,2048]{2,1,0:T(8,128)(2,1)S(1)} %get-tuple-element.148), channel_id=1, source_target_pairs={{0,3},{1,2},{2,1},{3,0},{4,7},{5,6},{6,5},{7,4},{8,11},{9,10},{10,... | collective-permute-start | bytes 1572872 | tf_op jit(solution)/shard_map/ppermute | solution.py:476
  47.4 23.1 %collective-permute-start.6 = (bf16[128,2048]{1,0:T(8,128)(2,1)S(1)}, bf16[128,2048]{1,0:T(8,128)(2,1)S(1)}, u32[]{:S(2)}, u32[]{:S(2)}) collective-permute-start(bf16[128,2048]{1,0:T(8,128)(2,1)S(1)} %copy-done.23), channel_id=1, source_target_pairs={{0,12},{1,13},{2,14},{3,15},{4,0},{5,1},{6,2},{7,3},{8,4},{9,5},{1... | collective-permute-start | bytes 1572872 | tf_op jit(solution)/shard_map/ppermute | solution.py:458
  47.7 22.8 %collective-permute-start.7 = (bf16[128,2048]{1,0:T(8,128)(2,1)S(1)}, bf16[128,2048]{1,0:T(8,128)(2,1)S(1)}, u32[]{:S(2)}, u32[]{:S(2)}) collective-permute-start(bf16[128,2048]{1,0:T(8,128)(2,1)S(1)} %copy-done.23), channel_id=1, source_target_pairs={{0,4},{1,5},{2,6},{3,7},{4,8},{5,9},{6,10},{7,11},{8,12},{9,13},{1... | collective-permute-start | bytes 1572872 | tf_op jit(solution)/shard_map/ppermute | solution.py:458
  58.3 14.0 %collective-permute-start.11 = (bf16[1,64,2048]{2,1,0:T(8,128)(2,1)S(1)}, bf16[1,64,2048]{2,1,0:T(8,128)(2,1)S(1)}, u32[]{:S(2)}, u32[]{:S(2)}) collective-permute-start(bf16[1,64,2048]{2,1,0:T(8,128)(2,1)S(1)} %get-tuple-element.149), channel_id=1, source_target_pairs={{0,1},{1,0},{2,3},{3,2},{4,5},{5,4},{6,7},{7,6},{8,9},{9,8},{10,11... | collective-permute-start | bytes 786440 | tf_op jit(solution)/shard_map/ppermute | solution.py:476
  59.8 12.6 %collective-permute-start.12 = (bf16[1,64,2048]{2,1,0:T(8,128)(2,1)S(1)}, bf16[1,64,2048]{2,1,0:T(8,128)(2,1)S(1)}, u32[]{:S(2)}, u32[]{:S(2)}) collective-permute-start(bf16[1,64,2048]{2,1,0:T(8,128)(2,1)S(1)} %get-tuple-element.150), channel_id=1, source_target_pairs={{0,2},{1,3},{2,0},{3,1},{4,6},{5,7},{6,4},{7,5},{8,10},{9,11},{10,... | collective-permute-start | bytes 786440 | tf_op jit(solution)/shard_map/ppermute | solution.py:476
  60.3 12.1 %collective-permute-start.13 = (bf16[1,64,2048]{2,1,0:T(8,128)(2,1)S(1)}, bf16[1,64,2048]{2,1,0:T(8,128)(2,1)S(1)}, u32[]{:S(2)}, u32[]{:S(2)}) collective-permute-start(bf16[1,64,2048]{2,1,0:T(8,128)(2,1)S(1)} %get-tuple-element.151), channel_id=1, source_target_pairs={{0,3},{1,2},{2,1},{3,0},{4,7},{5,6},{6,5},{7,4},{8,11},{9,10},{10,... | collective-permute-start | bytes 786440 | tf_op jit(solution)/shard_map/ppermute | solution.py:476
  72.4 19.1 %collective-permute-start.14 = (bf16[2,64,2048]{2,1,0:T(8,128)(2,1)S(1)}, bf16[2,64,2048]{2,1,0:T(8,128)(2,1)S(1)}, u32[]{:S(2)}, u32[]{:S(2)}) collective-permute-start(bf16[2,64,2048]{2,1,0:T(8,128)(2,1)S(1)} %get-tuple-element.152), channel_id=1, source_target_pairs={{0,1},{1,0},{2,3},{3,2},{4,5},{5,4},{6,7},{7,6},{8,9},{9,8},{10,11... | collective-permute-start | bytes 1572872 | tf_op jit(solution)/shard_map/ppermute | solution.py:476
  73.0 23.2 %collective-permute-start.15 = (bf16[2,64,2048]{2,1,0:T(8,128)(2,1)S(1)}, bf16[2,64,2048]{2,1,0:T(8,128)(2,1)S(1)}, u32[]{:S(2)}, u32[]{:S(2)}) collective-permute-start(bf16[2,64,2048]{2,1,0:T(8,128)(2,1)S(1)} %get-tuple-element.153), channel_id=1, source_target_pairs={{0,2},{1,3},{2,0},{3,1},{4,6},{5,7},{6,4},{7,5},{8,10},{9,11},{10,... | collective-permute-start | bytes 1572872 | tf_op jit(solution)/shard_map/ppermute | solution.py:476
  73.5 22.7 %collective-permute-start.16 = (bf16[2,64,2048]{2,1,0:T(8,128)(2,1)S(1)}, bf16[2,64,2048]{2,1,0:T(8,128)(2,1)S(1)}, u32[]{:S(2)}, u32[]{:S(2)}) collective-permute-start(bf16[2,64,2048]{2,1,0:T(8,128)(2,1)S(1)} %get-tuple-element.154), channel_id=1, source_target_pairs={{0,3},{1,2},{2,1},{3,0},{4,7},{5,6},{6,5},{7,4},{8,11},{9,10},{10,... | collective-permute-start | bytes 1572872 | tf_op jit(solution)/shard_map/ppermute | solution.py:476
  75.9 14.3 %collective-permute-start.17 = (bf16[128,2048]{1,0:T(8,128)(2,1)S(1)}, bf16[128,2048]{1,0:T(8,128)(2,1)S(1)}, u32[]{:S(2)}, u32[]{:S(2)}) collective-permute-start(bf16[128,2048]{1,0:T(8,128)(2,1)S(1)} %get-tuple-element.165), channel_id=1, source_target_pairs={{0,4},{1,5},{2,6},{3,7},{4,0},{5,1},{6,2},{7,3},{8,12},{9,13},{10,... | collective-permute-start | bytes 1572872 | tf_op jit(solution)/shard_map/ppermute | solution.py:458
  79.7 2.0 copy-start.19
  79.7 2.0 copy-start.21
  96.1 8.3 %collective-permute-start.18 = (bf16[1,64,2048]{2,1,0:T(8,128)(2,1)S(1)}, bf16[1,64,2048]{2,1,0:T(8,128)(2,1)S(1)}, u32[]{:S(2)}, u32[]{:S(2)}) collective-permute-start(bf16[1,64,2048]{2,1,0:T(8,128)(2,1)S(1)} %get-tuple-element.193), channel_id=1, source_target_pairs={{0,1},{1,0},{2,3},{3,2},{4,5},{5,4},{6,7},{7,6},{8,9},{9,8},{10,11... | collective-permute-start | bytes 786440 | tf_op jit(solution)/shard_map/ppermute | solution.py:476
  97.6 10.2 %collective-permute-start.19 = (bf16[1,64,2048]{2,1,0:T(8,128)(2,1)S(1)}, bf16[1,64,2048]{2,1,0:T(8,128)(2,1)S(1)}, u32[]{:S(2)}, u32[]{:S(2)}) collective-permute-start(bf16[1,64,2048]{2,1,0:T(8,128)(2,1)S(1)} %get-tuple-element.194), channel_id=1, source_target_pairs={{0,2},{1,3},{2,0},{3,1},{4,6},{5,7},{6,4},{7,5},{8,10},{9,11},{10,... | collective-permute-start | bytes 786440 | tf_op jit(solution)/shard_map/ppermute | solution.py:476
  98.2 11.2 %collective-permute-start.20 = (bf16[1,64,2048]{2,1,0:T(8,128)(2,1)S(1)}, bf16[1,64,2048]{2,1,0:T(8,128)(2,1)S(1)}, u32[]{:S(2)}, u32[]{:S(2)}) collective-permute-start(bf16[1,64,2048]{2,1,0:T(8,128)(2,1)S(1)} %get-tuple-element.195), channel_id=1, source_target_pairs={{0,3},{1,2},{2,1},{3,0},{4,7},{5,6},{6,5},{7,4},{8,11},{9,10},{10,... | collective-permute-start | bytes 786440 | tf_op jit(solution)/shard_map/ppermute | solution.py:476
  104.3 10.5 %copy-start.5 = (bf16[2,64,2048]{2,1,0:T(8,128)(2,1)}, bf16[2,64,2048]{2,1,0:T(8,128)(2,1)S(1)}, u32[]{:S(2)}) copy-start(bf16[2,64,2048]{2,1,0:T(8,128)(2,1)S(1)} %get-tuple-element.223) | copy-start | bytes 1572868
  104.3 10.6 %copy-start.7 = (bf16[2,64,2048]{2,1,0:T(8,128)(2,1)}, bf16[2,64,2048]{2,1,0:T(8,128)(2,1)S(1)}, u32[]{:S(2)}) copy-start(bf16[2,64,2048]{2,1,0:T(8,128)(2,1)S(1)} %get-tuple-element.222) | copy-start | bytes 1572868
  109.4 12.9 %collective-permute-start.21 = (bf16[1,64,2048]{2,1,0:T(8,128)(2,1)S(1)}, bf16[1,64,2048]{2,1,0:T(8,128)(2,1)S(1)}, u32[]{:S(2)}, u32[]{:S(2)}) collective-permute-start(bf16[1,64,2048]{2,1,0:T(8,128)(2,1)S(1)} %get-tuple-element.203), channel_id=1, source_target_pairs={{0,1},{1,0},{2,3},{3,2},{4,5},{5,4},{6,7},{7,6},{8,9},{9,8},{10,11... | collective-permute-start | bytes 786440 | tf_op jit(solution)/shard_map/ppermute | solution.py:476
  109.6 12.6 %collective-permute-start.22 = (bf16[1,64,2048]{2,1,0:T(8,128)(2,1)S(1)}, bf16[1,64,2048]{2,1,0:T(8,128)(2,1)S(1)}, u32[]{:S(2)}, u32[]{:S(2)}) collective-permute-start(bf16[1,64,2048]{2,1,0:T(8,128)(2,1)S(1)} %get-tuple-element.204), channel_id=1, source_target_pairs={{0,2},{1,3},{2,0},{3,1},{4,6},{5,7},{6,4},{7,5},{8,10},{9,11},{10,... | collective-permute-start | bytes 786440 | tf_op jit(solution)/shard_map/ppermute | solution.py:476
  111.3 10.9 %collective-permute-start.23 = (bf16[1,64,2048]{2,1,0:T(8,128)(2,1)S(1)}, bf16[1,64,2048]{2,1,0:T(8,128)(2,1)S(1)}, u32[]{:S(2)}, u32[]{:S(2)}) collective-permute-start(bf16[1,64,2048]{2,1,0:T(8,128)(2,1)S(1)} %get-tuple-element.205), channel_id=1, source_target_pairs={{0,3},{1,2},{2,1},{3,0},{4,7},{5,6},{6,5},{7,4},{8,11},{9,10},{10,... | collective-permute-start | bytes 786440 | tf_op jit(solution)/shard_map/ppermute | solution.py:476
  122.2 19.6 %collective-permute-start.32 = (bf16[3,384,2048]{2,1,0:T(8,128)(2,1)}, bf16[3,384,2048]{2,1,0:T(8,128)(2,1)}, u32[]{:S(2)}, u32[]{:S(2)}) collective-permute-start(bf16[3,384,2048]{2,1,0:T(8,128)(2,1)} %partial_sums.1.refs_0_), channel_id=1, source_target_pairs={{0,16},{16,0},{1,17},{17,1},{2,18},{18,2},{3,19},{19,3},{4,20},{20... | collective-permute-start | bytes 14155784 | tf_op jit(solution)/shard_map/ppermute | solution.py:525
  122.3 9.2 %collective-permute-start.24 = (bf16[1,64,2048]{2,1,0:T(8,128)(2,1)S(1)}, bf16[1,64,2048]{2,1,0:T(8,128)(2,1)S(1)}, u32[]{:S(2)}, u32[]{:S(2)}) collective-permute-start(bf16[1,64,2048]{2,1,0:T(8,128)(2,1)S(1)} %get-tuple-element.209), channel_id=1, source_target_pairs={{0,1},{1,0},{2,3},{3,2},{4,5},{5,4},{6,7},{7,6},{8,9},{9,8},{10,11... | collective-permute-start | bytes 786440 | tf_op jit(solution)/shard_map/ppermute | solution.py:476
  122.6 14.0 %collective-permute-start.25 = (bf16[1,64,2048]{2,1,0:T(8,128)(2,1)S(1)}, bf16[1,64,2048]{2,1,0:T(8,128)(2,1)S(1)}, u32[]{:S(2)}, u32[]{:S(2)}) collective-permute-start(bf16[1,64,2048]{2,1,0:T(8,128)(2,1)S(1)} %get-tuple-element.210), channel_id=1, source_target_pairs={{0,2},{1,3},{2,0},{3,1},{4,6},{5,7},{6,4},{7,5},{8,10},{9,11},{10,... | collective-permute-start | bytes 786440 | tf_op jit(solution)/shard_map/ppermute | solution.py:476
  124.3 12.3 %collective-permute-start.26 = (bf16[1,64,2048]{2,1,0:T(8,128)(2,1)S(1)}, bf16[1,64,2048]{2,1,0:T(8,128)(2,1)S(1)}, u32[]{:S(2)}, u32[]{:S(2)}) collective-permute-start(bf16[1,64,2048]{2,1,0:T(8,128)(2,1)S(1)} %get-tuple-element.211), channel_id=1, source_target_pairs={{0,3},{1,2},{2,1},{3,0},{4,7},{5,6},{6,5},{7,4},{8,11},{9,10},{10,... | collective-permute-start | bytes 786440 | tf_op jit(solution)/shard_map/ppermute | solution.py:476
  127.7 20.7 %collective-permute-start.30 = (bf16[128,2048]{1,0:T(8,128)(2,1)}, bf16[128,2048]{1,0:T(8,128)(2,1)S(1)}, u32[]{:S(2)}, u32[]{:S(2)}) collective-permute-start(bf16[128,2048]{1,0:T(8,128)(2,1)} %expand.6), channel_id=1, source_target_pairs={{0,4},{1,5},{2,6},{3,7},{4,0},{5,1},{6,2},{7,3},{8,12},{9,13},{10,... | collective-permute-start | bytes 1572872 | tf_op jit(solution)/shard_map/ppermute | solution.py:458
  136.6 15.1 %collective-permute-start.27 = (bf16[2,64,2048]{2,1,0:T(8,128)(2,1)}, bf16[2,64,2048]{2,1,0:T(8,128)(2,1)S(1)}, u32[]{:S(2)}, u32[]{:S(2)}) collective-permute-start(bf16[2,64,2048]{2,1,0:T(8,128)(2,1)} %get-tuple-element.212), channel_id=1, source_target_pairs={{0,1},{1,0},{2,3},{3,2},{4,5},{5,4},{6,7},{7,6},{8,9},{9,8},{10,11... | collective-permute-start | bytes 1572872 | tf_op jit(solution)/shard_map/ppermute | solution.py:476
  138.4 24.4 %collective-permute-start.28 = (bf16[2,64,2048]{2,1,0:T(8,128)(2,1)}, bf16[2,64,2048]{2,1,0:T(8,128)(2,1)}, u32[]{:S(2)}, u32[]{:S(2)}) collective-permute-start(bf16[2,64,2048]{2,1,0:T(8,128)(2,1)} %get-tuple-element.213), channel_id=1, source_target_pairs={{0,2},{1,3},{2,0},{3,1},{4,6},{5,7},{6,4},{7,5},{8,10},{9,11},{10,... | collective-permute-start | bytes 1572872 | tf_op jit(solution)/shard_map/ppermute | solution.py:476
  138.7 24.1 %collective-permute-start.29 = (bf16[2,64,2048]{2,1,0:T(8,128)(2,1)}, bf16[2,64,2048]{2,1,0:T(8,128)(2,1)}, u32[]{:S(2)}, u32[]{:S(2)}) collective-permute-start(bf16[2,64,2048]{2,1,0:T(8,128)(2,1)} %get-tuple-element.214), channel_id=1, source_target_pairs={{0,3},{1,2},{2,1},{3,0},{4,7},{5,6},{6,5},{7,4},{8,11},{9,10},{10,... | collective-permute-start | bytes 1572872 | tf_op jit(solution)/shard_map/ppermute | solution.py:476
  141.8 21.0 %collective-permute-start.31 = (bf16[128,2048]{1,0:T(8,128)(2,1)}, bf16[128,2048]{1,0:T(8,128)(2,1)S(1)}, u32[]{:S(2)}, u32[]{:S(2)}) collective-permute-start(bf16[128,2048]{1,0:T(8,128)(2,1)} %expand.7), channel_id=1, source_target_pairs={{0,4},{1,5},{2,6},{3,7},{4,0},{5,1},{6,2},{7,3},{8,12},{9,13},{10,... | collective-permute-start | bytes 1572872 | tf_op jit(solution)/shard_map/ppermute | solution.py:458
  141.9 20.9 %copy-start.10 = (bf16[2,64,2048]{2,1,0:T(8,128)(2,1)S(1)}, bf16[2,64,2048]{2,1,0:T(8,128)(2,1)}, u32[]{:S(2)}) copy-start(bf16[2,64,2048]{2,1,0:T(8,128)(2,1)} %copy-done.9) | copy-start | bytes 1572868
  141.9 21.5 %copy-start.8 = (bf16[2,64,2048]{2,1,0:T(8,128)(2,1)S(1)}, bf16[2,64,2048]{2,1,0:T(8,128)(2,1)}, u32[]{:S(2)}) copy-start(bf16[2,64,2048]{2,1,0:T(8,128)(2,1)} %copy-done.7) | copy-start | bytes 1572868
  141.9 23.1 %copy-start.6 = (bf16[2,64,2048]{2,1,0:T(8,128)(2,1)S(1)}, bf16[2,64,2048]{2,1,0:T(8,128)(2,1)}, u32[]{:S(2)}) copy-start(bf16[2,64,2048]{2,1,0:T(8,128)(2,1)} %copy-done.5) | copy-start | bytes 1572868
  148.4 38.1 %copy-start.22 = (bf16[1,64,2048]{2,1,0:T(8,128)(2,1)S(1)}, bf16[1,64,2048]{2,1,0:T(8,128)(2,1)}, u32[]{:S(2)}) copy-start(bf16[1,64,2048]{2,1,0:T(8,128)(2,1)} %copy-done.21) | copy-start | bytes 786436
  148.4 39.9 %copy-start.20 = (bf16[1,64,2048]{2,1,0:T(8,128)(2,1)S(1)}, bf16[1,64,2048]{2,1,0:T(8,128)(2,1)}, u32[]{:S(2)}) copy-start(bf16[1,64,2048]{2,1,0:T(8,128)(2,1)} %copy-done.19) | copy-start | bytes 786436
  148.4 40.0 %copy-start.18 = (bf16[1,64,2048]{2,1,0:T(8,128)(2,1)S(1)}, bf16[1,64,2048]{2,1,0:T(8,128)(2,1)}, u32[]{:S(2)}) copy-start(bf16[1,64,2048]{2,1,0:T(8,128)(2,1)} %copy-done.17) | copy-start | bytes 786436
  162.8 14.9 %collective-permute-start.33 = (bf16[2,64,2048]{2,1,0:T(8,128)(2,1)S(1)}, bf16[2,64,2048]{2,1,0:T(8,128)(2,1)S(1)}, u32[]{:S(2)}, u32[]{:S(2)}) collective-permute-start(bf16[2,64,2048]{2,1,0:T(8,128)(2,1)S(1)} %copy-done.10), channel_id=1, source_target_pairs={{0,1},{1,0},{2,3},{3,2},{4,5},{5,4},{6,7},{7,6},{8,9},{9,8},{10,11... | collective-permute-start | bytes 1572872 | tf_op jit(solution)/shard_map/ppermute | solution.py:476
  163.3 23.1 %collective-permute-start.34 = (bf16[2,64,2048]{2,1,0:T(8,128)(2,1)S(1)}, bf16[2,64,2048]{2,1,0:T(8,128)(2,1)S(1)}, u32[]{:S(2)}, u32[]{:S(2)}) collective-permute-start(bf16[2,64,2048]{2,1,0:T(8,128)(2,1)S(1)} %copy-done.8), channel_id=1, source_target_pairs={{0,2},{1,3},{2,0},{3,1},{4,6},{5,7},{6,4},{7,5},{8,10},{9,11},{10,... | collective-permute-start | bytes 1572872 | tf_op jit(solution)/shard_map/ppermute | solution.py:476
  165.0 21.4 %collective-permute-start.35 = (bf16[2,64,2048]{2,1,0:T(8,128)(2,1)S(1)}, bf16[2,64,2048]{2,1,0:T(8,128)(2,1)S(1)}, u32[]{:S(2)}, u32[]{:S(2)}) collective-permute-start(bf16[2,64,2048]{2,1,0:T(8,128)(2,1)S(1)} %copy-done.6), channel_id=1, source_target_pairs={{0,3},{1,2},{2,1},{3,0},{4,7},{5,6},{6,5},{7,4},{8,11},{9,10},{10,... | collective-permute-start | bytes 1572872 | tf_op jit(solution)/shard_map/ppermute | solution.py:476
  168.3 31.7 %copy-start.16 = (bf16[1,64,2048]{2,1,0:T(8,128)(2,1)S(1)}, bf16[1,64,2048]{2,1,0:T(8,128)(2,1)}, u32[]{:S(2)}) copy-start(bf16[1,64,2048]{2,1,0:T(8,128)(2,1)} %copy-done.15) | copy-start | bytes 786436
  168.3 31.7 %copy-start.14 = (bf16[1,64,2048]{2,1,0:T(8,128)(2,1)S(1)}, bf16[1,64,2048]{2,1,0:T(8,128)(2,1)}, u32[]{:S(2)}) copy-start(bf16[1,64,2048]{2,1,0:T(8,128)(2,1)} %copy-done.13) | copy-start | bytes 786436
  168.4 33.2 %copy-start.12 = (bf16[1,64,2048]{2,1,0:T(8,128)(2,1)S(1)}, bf16[1,64,2048]{2,1,0:T(8,128)(2,1)}, u32[]{:S(2)}) copy-start(bf16[1,64,2048]{2,1,0:T(8,128)(2,1)} %copy-done.11) | copy-start | bytes 786436
  168.4 35.1 %copy-start.4 = (bf16[1,64,2048]{2,1,0:T(8,128)(2,1)S(1)}, bf16[1,64,2048]{2,1,0:T(8,128)(2,1)}, u32[]{:S(2)}) copy-start(bf16[1,64,2048]{2,1,0:T(8,128)(2,1)} %copy-done.3) | copy-start | bytes 786436
  168.4 22.7 %collective-permute-start.39 = (bf16[128,2048]{1,0:T(8,128)(2,1)S(1)}, bf16[128,2048]{1,0:T(8,128)(2,1)S(1)}, u32[]{:S(2)}, u32[]{:S(2)}) collective-permute-start(bf16[128,2048]{1,0:T(8,128)(2,1)S(1)} %get-tuple-element.230), channel_id=1, source_target_pairs={{0,4},{1,5},{2,6},{3,7},{4,8},{5,9},{6,10},{7,11},{8,12},{9,13},{1... | collective-permute-start | bytes 1572872 | tf_op jit(solution)/shard_map/ppermute | solution.py:458
  171.7 20.6 %collective-permute-start.40 = (bf16[128,2048]{1,0:T(8,128)(2,1)S(1)}, bf16[128,2048]{1,0:T(8,128)(2,1)S(1)}, u32[]{:S(2)}, u32[]{:S(2)}) collective-permute-start(bf16[128,2048]{1,0:T(8,128)(2,1)S(1)} %get-tuple-element.231), channel_id=1, source_target_pairs={{0,12},{1,13},{2,14},{3,15},{4,0},{5,1},{6,2},{7,3},{8,4},{9,5},{1... | collective-permute-start | bytes 1572872 | tf_op jit(solution)/shard_map/ppermute | solution.py:458
  186.5 8.6 %collective-permute-start.36 = (bf16[1,64,2048]{2,1,0:T(8,128)(2,1)S(1)}, bf16[1,64,2048]{2,1,0:T(8,128)(2,1)S(1)}, u32[]{:S(2)}, u32[]{:S(2)}) collective-permute-start(bf16[1,64,2048]{2,1,0:T(8,128)(2,1)S(1)} %copy-done.22), channel_id=1, source_target_pairs={{0,1},{1,0},{2,3},{3,2},{4,5},{5,4},{6,7},{7,6},{8,9},{9,8},{10,11... | collective-permute-start | bytes 786440 | tf_op jit(solution)/shard_map/ppermute | solution.py:476
  188.2 10.0 %collective-permute-start.37 = (bf16[1,64,2048]{2,1,0:T(8,128)(2,1)S(1)}, bf16[1,64,2048]{2,1,0:T(8,128)(2,1)S(1)}, u32[]{:S(2)}, u32[]{:S(2)}) collective-permute-start(bf16[1,64,2048]{2,1,0:T(8,128)(2,1)S(1)} %copy-done.20), channel_id=1, source_target_pairs={{0,2},{1,3},{2,0},{3,1},{4,6},{5,7},{6,4},{7,5},{8,10},{9,11},{10,... | collective-permute-start | bytes 786440 | tf_op jit(solution)/shard_map/ppermute | solution.py:476
  188.4 11.6 %collective-permute-start.38 = (bf16[1,64,2048]{2,1,0:T(8,128)(2,1)S(1)}, bf16[1,64,2048]{2,1,0:T(8,128)(2,1)S(1)}, u32[]{:S(2)}, u32[]{:S(2)}) collective-permute-start(bf16[1,64,2048]{2,1,0:T(8,128)(2,1)S(1)} %copy-done.18), channel_id=1, source_target_pairs={{0,3},{1,2},{2,1},{3,0},{4,7},{5,6},{6,5},{7,4},{8,11},{9,10},{10,... | collective-permute-start | bytes 786440 | tf_op jit(solution)/shard_map/ppermute | solution.py:476
  192.2 18.2 %collective-permute-start.44 = (bf16[128,2048]{1,0:T(8,128)(2,1)S(1)}, bf16[128,2048]{1,0:T(8,128)(2,1)S(1)}, u32[]{:S(2)}, u32[]{:S(2)}) collective-permute-start(bf16[128,2048]{1,0:T(8,128)(2,1)S(1)} %get-tuple-element.237), channel_id=1, source_target_pairs={{0,4},{1,5},{2,6},{3,7},{4,8},{5,9},{6,10},{7,11},{8,12},{9,13},{1... | collective-permute-start | bytes 1572872 | tf_op jit(solution)/shard_map/ppermute | solution.py:458
  195.1 22.2 %collective-permute-start.45 = (bf16[128,2048]{1,0:T(8,128)(2,1)S(1)}, bf16[128,2048]{1,0:T(8,128)(2,1)S(1)}, u32[]{:S(2)}, u32[]{:S(2)}) collective-permute-start(bf16[128,2048]{1,0:T(8,128)(2,1)S(1)} %get-tuple-element.238), channel_id=1, source_target_pairs={{0,12},{1,13},{2,14},{3,15},{4,0},{5,1},{6,2},{7,3},{8,4},{9,5},{1... | collective-permute-start | bytes 1572872 | tf_op jit(solution)/shard_map/ppermute | solution.py:458
  200.0 6.4 %collective-permute-start.41 = (bf16[1,64,2048]{2,1,0:T(8,128)(2,1)S(1)}, bf16[1,64,2048]{2,1,0:T(8,128)(2,1)S(1)}, u32[]{:S(2)}, u32[]{:S(2)}) collective-permute-start(bf16[1,64,2048]{2,1,0:T(8,128)(2,1)S(1)} %copy-done.16), channel_id=1, source_target_pairs={{0,1},{1,0},{2,3},{3,2},{4,5},{5,4},{6,7},{7,6},{8,9},{9,8},{10,11... | collective-permute-start | bytes 786440 | tf_op jit(solution)/shard_map/ppermute | solution.py:476
  200.0 10.4 %collective-permute-start.42 = (bf16[1,64,2048]{2,1,0:T(8,128)(2,1)S(1)}, bf16[1,64,2048]{2,1,0:T(8,128)(2,1)S(1)}, u32[]{:S(2)}, u32[]{:S(2)}) collective-permute-start(bf16[1,64,2048]{2,1,0:T(8,128)(2,1)S(1)} %copy-done.14), channel_id=1, source_target_pairs={{0,2},{1,3},{2,0},{3,1},{4,6},{5,7},{6,4},{7,5},{8,10},{9,11},{10,... | collective-permute-start | bytes 786440 | tf_op jit(solution)/shard_map/ppermute | solution.py:476
  201.6 8.8 %collective-permute-start.43 = (bf16[1,64,2048]{2,1,0:T(8,128)(2,1)S(1)}, bf16[1,64,2048]{2,1,0:T(8,128)(2,1)S(1)}, u32[]{:S(2)}, u32[]{:S(2)}) collective-permute-start(bf16[1,64,2048]{2,1,0:T(8,128)(2,1)S(1)} %copy-done.12), channel_id=1, source_target_pairs={{0,3},{1,2},{2,1},{3,0},{4,7},{5,6},{6,5},{7,4},{8,11},{9,10},{10,... | collective-permute-start | bytes 786440 | tf_op jit(solution)/shard_map/ppermute | solution.py:476
  (6 other events, 4.3 us)
